TPU v7x, 32 devices: a whole 2x2x4 slice. The times are simulated.
32 devices in a mesh: wide: 8 (over y, x, core), narrow: 4 (over z).
Axes of the slice: x: 2, y: 2, z: 4, core: 2. Of those that a mesh axis runs over, the one named last changes fastest.
Arguments:
- tokens: bfloat16 [256, 128, 768], P(('wide', 'narrow')), may hold values from -6 to 6
- segments: int32 [256, 128], P(('wide', 'narrow')), may hold values from 0 to 7, never falling along the last dimension, each value on 1 to 32 neighbouring positions
- destination: int32 [256], P(('wide', 'narrow')), may hold values from -1 to 7, as said below
- pair_index: int32 [1024, 2], P(('wide', 'narrow')), may hold values from 0 to 63, as said below
- targets: float32 [1024], P(('wide', 'narrow')), may hold values from -0.5 to 1
- w_qkv: bfloat16 [768, 2304], replicated, may hold values from -0.21875 to 0.21875
- b_qv: float32 [1536], replicated, may hold values from -3 to 3
- w_o: bfloat16 [768, 768], replicated, may hold values from -0.4375 to 0.4375
- b_o: float32 [768], replicated, may hold values from -3 to 3
- gain_one: float32 [768], replicated, may hold values from 0.1 to 1.9
- shift_one: float32 [768], replicated, may hold values from -2 to 2
- w_in: bfloat16 [768, 3072], replicated, may hold values from -0.21875 to 0.21875
- b_in: float32 [3072], replicated, may hold values from -3 to 3
- w_out: bfloat16 [3072, 768], replicated, may hold values from -0.109375 to 0.109375
- b_out: float32 [768], replicated, may hold values from -3 to 3
- gain_two: float32 [768], replicated, may hold values from 0.1 to 1.9
- shift_two: float32 [768], replicated, may hold values from -2 to 2
Outputs:
- encoded: bfloat16 [128, 128, 768], P(('wide', 'narrow'))
- similarity: float32 [1024], P(('wide', 'narrow'))
- grad_tokens: bfloat16 [256, 128, 768], P(('wide', 'narrow'))
- grad_w_qkv: float32 [768, 2304], P('narrow', 'wide')
- grad_b_qv: float32 [1536], replicated
- grad_w_o: float32 [768, 768], P('narrow', 'wide')
- grad_b_o: float32 [768], replicated
- grad_gain_one: float32 [768], replicated
- grad_shift_one: float32 [768], replicated
- grad_w_in: float32 [768, 3072], P('narrow', 'wide')
- grad_b_in: float32 [3072], replicated
- grad_w_out: float32 [3072, 768], P('narrow', 'wide')
- grad_b_out: float32 [768], replicated
- grad_gain_two: float32 [768], replicated
- grad_shift_two: float32 [768], replicated
Inputs may be any that keep to these rules, and one draw needn't show every extreme that they name: `destination`: -1 marks an empty row slot. Among the slots held by the devices of one narrow index, every wide index owns exactly 4 live slots; one device sends at most 1 slot to one owner, holds 0 to 8 live slots, and in every such group some device holds 8. `pair_index`: every sentence slot of a device is in exactly one pair; a pair joins two slots of live rows or two slots of empty rows. `segments`: within a row the numbers never fall and each of 0 to 7 covers 1 to 32 tokens.
All inputs are finite; a program needn't handle non-finite values.
Results may differ from a plain program's by a relative error of at most 0.017.
Values may be sent and summed in bfloat16 or wider, within the bound.
No kernel may reach another device: no remote copies, remote signals or barrier semaphores. Data moves between devices by JAX's collectives and lax.ppermute only.
A program may use at most 192 MiB of HBM per device.

v0:
```python
import math

import jax
import jax.numpy as jnp
from jax import lax
from jax.sharding import PartitionSpec as P

HEAD_DIM = 64
SEG_ROW = 8


NEG_FILL = -1e30
NORM_EPS = 1e-12


def layer_norm(values, gain, shift):
    middle = jnp.mean(values, axis=-1, keepdims=True)
    centered = values - middle
    spread = jnp.mean(centered * centered, axis=-1, keepdims=True)
    return centered * lax.rsqrt(spread + NORM_EPS) * gain + shift


def gelu_exact(values):
    return jax.nn.gelu(values, approximate=False)


def cosine_of(left_vec, right_vec):
    inner = jnp.mean(left_vec * right_vec, axis=-1)
    left_sq = jnp.mean(left_vec * left_vec, axis=-1)
    right_sq = jnp.mean(right_vec * right_vec, axis=-1)
    return inner * lax.rsqrt(left_sq + 1e-06) * lax.rsqrt(right_sq + 1e-06)


def slot_table(destination, wide_count, capacity):
    row_total = destination.shape[0]
    row_ids = jnp.arange(row_total, dtype=jnp.int32)
    earlier = (destination[:, None] == destination[None, :]) & (row_ids[None, :] < row_ids[:, None])
    rank_rows = jnp.sum(earlier.astype(jnp.int32), axis=1)
    slot_of = jnp.where(destination >= 0, destination * capacity + rank_rows, -1)
    wanted = jnp.arange(wide_count * capacity, dtype=jnp.int32)
    match_rows = slot_of[None, :] == wanted[:, None]
    filled = jnp.any(match_rows, axis=1)
    source_row = jnp.sum(jnp.where(match_rows, row_ids[None, :], 0), axis=1)
    return (source_row, filled, slot_of)


def compact_table(filled, rows_kept):
    running = jnp.cumsum(filled.astype(jnp.int32)) - 1
    slot_ids = jnp.arange(filled.shape[0], dtype=jnp.int32)
    targets_row = jnp.arange(rows_kept, dtype=jnp.int32)
    match_slots = filled[None, :] & (running[None, :] == targets_row[:, None])
    picked = jnp.sum(jnp.where(match_slots, slot_ids[None, :], 0), axis=1)
    return (picked, jnp.clip(running, 0, rows_kept - 1))


def keep_where(flags, values):
    shaped = flags.reshape(flags.shape + (1,) * (values.ndim - 1))
    return jnp.where(shaped, values, jnp.zeros((), values.dtype))


def block_scores(queries, key_rows, labels, score_scale):
    raw_scores = (
        jnp.einsum("rqhd,rkhd->rhqk", queries, key_rows, preferred_element_type=jnp.float32)
        * score_scale
    )
    same_segment = labels[:, :, None] == labels[:, None, :]
    return jnp.where(same_segment[:, None, :, :], raw_scores, NEG_FILL)


def on_device(
    tokens,
    segments,
    destination,
    pair_index,
    targets,
    w_qkv,
    b_qv,
    w_o,
    b_o,
    gain_one,
    shift_one,
    w_in,
    b_in,
    w_out,
    b_out,
    gain_two,
    shift_two,
):
    wide_count = lax.axis_size("wide")
    slot_dev, row_len, model_width = tokens.shape
    kept_rows = slot_dev // 2
    capacity = (slot_dev + wide_count - 1) // wide_count
    head_count = model_width // HEAD_DIM
    score_scale = 1.0 / math.sqrt(HEAD_DIM)
    live_rows = destination >= 0
    source_row, filled, slot_of = slot_table(destination, wide_count, capacity)
    send_tokens = keep_where(filled, tokens[source_row])
    send_labels = jnp.where(filled[:, None], segments[source_row], -1)
    got_tokens, got_labels = (
        lax.all_to_all(send_tokens, "wide", split_axis=0, concat_axis=0, tiled=True),
        lax.all_to_all(send_labels, "wide", split_axis=0, concat_axis=0, tiled=True),
    )
    got_filled = got_labels[:, 0] >= 0
    picked, back_rank = compact_table(got_filled, kept_rows)
    owner_tokens = got_tokens[picked]
    owner_labels = got_labels[picked]

    def to_slots(member):
        return keep_where(got_filled, member[back_rank])

    def to_home(member):
        return keep_where(live_rows, member[jnp.clip(slot_of, 0, member.shape[0] - 1)])

    tok_count = kept_rows * row_len
    flat_tokens = owner_tokens.reshape(tok_count, model_width)
    full_bias = jnp.concatenate(
        [b_qv[:model_width], jnp.zeros((model_width,), jnp.float32), b_qv[model_width:]]
    )
    projected = (
        jnp.dot(flat_tokens, w_qkv, preferred_element_type=jnp.float32) + full_bias
    ).astype(jnp.bfloat16)
    block_rows = min(kept_rows, max(1, 512 // row_len))
    block_count = kept_rows // block_rows
    head_shape = (block_count, block_rows, row_len, head_count, HEAD_DIM)
    queries = projected[:, :model_width].reshape(head_shape)
    key_rows = projected[:, model_width : 2 * model_width].reshape(head_shape)
    values = projected[:, 2 * model_width :].reshape(head_shape)
    block_tags = owner_labels.reshape(block_count, block_rows, row_len)

    def attend(member):
        query_blk, key_blk, value_blk, tag_blk = member
        scores = block_scores(query_blk, key_blk, tag_blk, score_scale)
        row_top = jnp.max(scores, axis=-1, keepdims=True)
        expo = jnp.exp(scores - row_top)
        row_total = jnp.sum(expo, axis=-1, keepdims=True)
        probability = (expo / row_total).astype(jnp.bfloat16)
        context_blk = jnp.einsum(
            "rhqk,rkhd->rqhd", probability, value_blk, preferred_element_type=jnp.float32
        )
        return (context_blk.astype(jnp.bfloat16), row_top[..., 0] + jnp.log(row_total[..., 0]))

    context, log_totals = lax.map(attend, (queries, key_rows, values, block_tags))
    context = context.reshape(tok_count, model_width)
    attn_out = jnp.dot(context, w_o, preferred_element_type=jnp.float32) + b_o
    hidden, norm_one_back = jax.vjp(
        layer_norm, flat_tokens.astype(jnp.float32) + attn_out, gain_one, shift_one
    )
    hidden_low = hidden.astype(jnp.bfloat16)
    up_proj = jnp.dot(hidden_low, w_in, preferred_element_type=jnp.float32) + b_in
    activated, gelu_back = jax.vjp(gelu_exact, up_proj)
    act_low = activated.astype(jnp.bfloat16)
    ffn_out = jnp.dot(act_low, w_out, preferred_element_type=jnp.float32) + b_out
    normed_out, norm_two_back = jax.vjp(layer_norm, hidden + ffn_out, gain_two, shift_two)
    encoded = normed_out.astype(jnp.bfloat16).reshape(kept_rows, row_len, model_width)
    onehot = (
        owner_labels[:, :, None] == jnp.arange(SEG_ROW, dtype=jnp.int32)[None, None, :]
    ).astype(jnp.float32)
    seg_count = jnp.sum(onehot, axis=1)
    pooled = (
        jnp.einsum(
            "rtd,rts->rsd",
            normed_out.reshape(kept_rows, row_len, model_width),
            onehot,
            precision=lax.Precision.HIGHEST,
        )
        / seg_count[:, :, None]
    )
    home_pooled = to_home(
        lax.all_to_all(
            to_slots(pooled.astype(jnp.bfloat16)), "wide", split_axis=0, concat_axis=0, tiled=True
        )
    )
    seg_slots = home_pooled.reshape(slot_dev * SEG_ROW, model_width).astype(jnp.float32)
    first = pair_index[:, 0]
    second = pair_index[:, 1]
    live_pair = live_rows[first // SEG_ROW]
    cosine, cosine_back = jax.vjp(cosine_of, seg_slots[first], seg_slots[second])
    similarity = jnp.where(live_pair, cosine, 0.0)
    err_weight = jnp.where(live_pair, 2.0 * (similarity - targets), 0.0)
    d_first, d_second = cosine_back(err_weight)
    d_slots = jnp.zeros_like(seg_slots).at[first].add(d_first).at[second].add(d_second)
    d_home = d_slots.reshape(slot_dev, SEG_ROW, model_width).astype(jnp.bfloat16)
    got_grads = lax.all_to_all(
        keep_where(filled, d_home[source_row]), "wide", split_axis=0, concat_axis=0, tiled=True
    )
    d_pooled = got_grads[picked].astype(jnp.float32)
    d_out = jnp.einsum(
        "rsd,rts->rtd", d_pooled / seg_count[:, :, None], onehot, precision=lax.Precision.HIGHEST
    ).reshape(tok_count, model_width)
    d_res_two, grad_gain_two, grad_shift_two = norm_two_back(d_out)
    d_ffn = d_res_two.astype(jnp.bfloat16)
    grad_b_out = jnp.sum(d_ffn.astype(jnp.float32), axis=0)
    grad_w_out = jnp.einsum("tf,td->fd", act_low, d_ffn, preferred_element_type=jnp.float32)
    d_act = jnp.einsum("td,fd->tf", d_ffn, w_out, preferred_element_type=jnp.float32)
    d_up = gelu_back(d_act)[0].astype(jnp.bfloat16)
    grad_b_in = jnp.sum(d_up.astype(jnp.float32), axis=0)
    grad_w_in = jnp.einsum("td,tf->df", hidden_low, d_up, preferred_element_type=jnp.float32)
    d_hidden = d_res_two + jnp.einsum("tf,df->td", d_up, w_in, preferred_element_type=jnp.float32)
    d_res_one, grad_gain_one, grad_shift_one = norm_one_back(d_hidden)
    d_attn = d_res_one.astype(jnp.bfloat16)
    grad_b_o = jnp.sum(d_attn.astype(jnp.float32), axis=0)
    grad_w_o = jnp.einsum("td,te->de", context, d_attn, preferred_element_type=jnp.float32)
    d_context = jnp.einsum("te,de->td", d_attn, w_o, preferred_element_type=jnp.float32).astype(
        jnp.bfloat16
    )
    d_context = d_context.reshape(head_shape)

    def attend_back(member):
        query_blk, key_blk, value_blk, tag_blk, total_blk, dctx_blk = member
        scores = block_scores(query_blk, key_blk, tag_blk, score_scale)
        probability = jnp.exp(scores - total_blk[..., None])
        d_prob = jnp.einsum(
            "rqhd,rkhd->rhqk", dctx_blk, value_blk, preferred_element_type=jnp.float32
        )
        inner = jnp.sum(probability * d_prob, axis=-1, keepdims=True)
        d_scores = (probability * (d_prob - inner)).astype(jnp.bfloat16)
        d_query = (
            jnp.einsum("rhqk,rkhd->rqhd", d_scores, key_blk, preferred_element_type=jnp.float32)
            * score_scale
        )
        d_key = (
            jnp.einsum("rhqk,rqhd->rkhd", d_scores, query_blk, preferred_element_type=jnp.float32)
            * score_scale
        )
        d_value = jnp.einsum(
            "rhqk,rqhd->rkhd",
            probability.astype(jnp.bfloat16),
            dctx_blk,
            preferred_element_type=jnp.float32,
        )
        return (
            d_query.astype(jnp.bfloat16),
            d_key.astype(jnp.bfloat16),
            d_value.astype(jnp.bfloat16),
        )

    d_query, d_key, d_value = lax.map(
        attend_back, (queries, key_rows, values, block_tags, log_totals, d_context)
    )
    d_query = d_query.reshape(tok_count, model_width)
    d_key = d_key.reshape(tok_count, model_width)
    d_value = d_value.reshape(tok_count, model_width)
    d_projected = jnp.concatenate([d_query, d_key, d_value], axis=1)
    grad_b_qv = jnp.concatenate(
        [jnp.sum(d_query.astype(jnp.float32), axis=0), jnp.sum(d_value.astype(jnp.float32), axis=0)]
    )
    grad_w_qkv = jnp.einsum(
        "td,te->de", flat_tokens, d_projected, preferred_element_type=jnp.float32
    )
    d_tokens = (
        d_res_one + jnp.einsum("te,de->td", d_projected, w_qkv, preferred_element_type=jnp.float32)
    ).astype(jnp.bfloat16)
    grad_tokens = to_home(
        lax.all_to_all(
            to_slots(d_tokens.reshape(kept_rows, row_len, model_width)),
            "wide",
            split_axis=0,
            concat_axis=0,
            tiled=True,
        )
    )
    matrix_terms = (grad_w_qkv, grad_w_o, grad_w_in, grad_w_out)
    partial_sums = (
        lax.psum_scatter(
            matrix_terms[0].astype(jnp.bfloat16), "wide", scatter_dimension=1, tiled=True
        ).astype(jnp.float32),
        lax.psum_scatter(
            matrix_terms[1].astype(jnp.bfloat16), "wide", scatter_dimension=1, tiled=True
        ).astype(jnp.float32),
        lax.psum_scatter(
            matrix_terms[2].astype(jnp.bfloat16), "wide", scatter_dimension=1, tiled=True
        ).astype(jnp.float32),
        lax.psum_scatter(
            matrix_terms[3].astype(jnp.bfloat16), "wide", scatter_dimension=1, tiled=True
        ).astype(jnp.float32),
    )
    matrix_sums = (
        lax.psum_scatter(
            partial_sums[0].astype(jnp.bfloat16), "narrow", scatter_dimension=0, tiled=True
        ).astype(jnp.float32),
        lax.psum_scatter(
            partial_sums[1].astype(jnp.bfloat16), "narrow", scatter_dimension=0, tiled=True
        ).astype(jnp.float32),
        lax.psum_scatter(
            partial_sums[2].astype(jnp.bfloat16), "narrow", scatter_dimension=0, tiled=True
        ).astype(jnp.float32),
        lax.psum_scatter(
            partial_sums[3].astype(jnp.bfloat16), "narrow", scatter_dimension=0, tiled=True
        ).astype(jnp.float32),
    )
    vector_sums = lax.psum(
        (
            grad_b_qv,
            grad_b_o,
            grad_gain_one,
            grad_shift_one,
            grad_b_in,
            grad_b_out,
            grad_gain_two,
            grad_shift_two,
        ),
        ("wide", "narrow"),
    )
    return (
        encoded,
        similarity,
        grad_tokens,
        matrix_sums[0],
        vector_sums[0],
        matrix_sums[1],
        vector_sums[1],
        vector_sums[2],
        vector_sums[3],
        matrix_sums[2],
        vector_sums[4],
        matrix_sums[3],
        vector_sums[5],
        vector_sums[6],
        vector_sums[7],
    )


def solution(mesh):
    in_specs = (
        P(("wide", "narrow"), None, None),
        P(("wide", "narrow"), None),
        P(("wide", "narrow")),
        P(("wide", "narrow"), None),
        P(("wide", "narrow")),
        P(),
        P(),
        P(),
        P(),
        P(),
        P(),
        P(),
        P(),
        P(),
        P(),
        P(),
        P(),
    )
    out_specs = (
        P(("wide", "narrow"), None, None),
        P(("wide", "narrow")),
        P(("wide", "narrow"), None, None),
        P("narrow", "wide"),
        P(),
        P("narrow", "wide"),
        P(),
        P(),
        P(),
        P("narrow", "wide"),
        P(),
        P("narrow", "wide"),
        P(),
        P(),
        P(),
    )
    return jax.shard_map(
        on_device, mesh=mesh, in_specs=in_specs, out_specs=out_specs, check_vma=False
    )
```

profile of v0, /device:TPU:0, one launch (start us, length us, event | category | flops | bytes accessed | tf_op | source)
XLA Modules:
  0.0 502.5 jit_solution(11176045441563611963)
XLA Ops:
  11.8 5.2 %all-to-all-start.1 = ((s32[8,1,128]{2,1,0:T(1,128)}), s32[8,1,128]{2,1,0:T(1,128)S(1)}, u32[]{:S(2)}, u32[]{:S(2)}) async-start(s32[8,1,128]{2,1,0:T(1,128)} %bitcast.2), calls=%async_computation.1 | async-start | bytes 8192 | tf_op jit(solution)/shard_map/all_to_all | solution.py:101
  19.1 3.3 gather_fusion
  22.4 2.7 broadcast_select_fusion.2
  25.2 4.3 all-to-all-start
  38.7 11.8 %all-to-all-done = bf16[8,128,768]{2,1,0:T(8,128)(2,1)} async-done(((bf16[8,128,768]{2,1,0:T(8,128)(2,1)}), bf16[8,128,768]{2,1,0:T(8,128)(2,1)}, u32[]{:S(2)}, u32[]{:S(2)}) %all-to-all-start) | async-done | bytes 1572896 | tf_op jit(solution)/shard_map/all_to_all | solution.py:100
  50.5 2.9 gather_fusion.2
  53.4 3.1 fusion.6
  58.0 2.3 copy.104
  60.3 2.5 squeeze.34
  62.8 2.3 copy.106
  65.1 2.4 squeeze.36
  67.5 2.3 copy.105
  69.8 2.4 squeeze.35
  72.2 2.2 fusion.78
  80.5 18.8 %multiply_convert_fusion = (bf16[512,3072]{1,0:T(8,128)(2,1)S(1)}, f32[512,3072]{1,0:T(8,128)}, f32[512,3072]{1,0:T(8,128)}) fusion(f32[3072]{0:T(1024)S(1)} %copy-done.48, bf16[768,3072]{1,0:T(8,128)(2,1)S(1)} %bitcast.126, f32[512,768]{1,0:T(8,128)S(1)} %get-tuple-element.178, f32[768]{0:T(1024)S(1)} %copy-done.52, f32[768]{0:T(1024)S(1)} %copy-done.44, ...), kind=kOutput, calls=%fused_computation.19 | convolution fusion | flops 2521694208 | bytes 22042624 | tf_op jit(solution)/shard_map/dot_general | solution.py:149
  99.4 2.8 fusion.80
  105.1 2.1 gather_fusion.5
  108.8 4.0 all-to-all-start.2
  115.4 2.6 all-to-all-done.2
  118.0 2.2 gather_fusion.6
  120.2 1.7 fusion.39
  121.9 2.3 gather_fusion.8
  124.2 2.3 gather_fusion.7
  129.4 1.9 scatter_custom_fusion
  131.3 2.8 scatter_custom_fusion.1
  135.7 2.2 gather_fusion.9
  139.5 4.0 all-to-all-start.3
  145.0 3.7 all-to-all-done.3
  148.7 2.2 gather_fusion.10
  150.9 2.4 fusion.81
  153.3 1.9 fusion.11
  156.9 9.5 %convert_reduce_fusion = (f32[3072]{0:T(1024)}, bf16[512,3072]{1,0:T(8,128)(2,1)S(1)}) fusion(f32[512,3072]{1,0:T(8,128)} %get-tuple-element.162, f32[512,3072]{1,0:T(8,128)} %get-tuple-element.179, f32[3072]{0:T(1024)S(1)} %copy-done.49, bf16[512,768]{1,0:T(8,128)(2,1)S(1)} %get-tuple-element.145, bf16[3072,768]{1,0:T(8,128)(2,1)} %param.30), kind=kOutput, calls=%fused_computation.17 | convolution fusion | flops 2442654720 | bytes 21258240 | tf_op jit(solution)/shard_map/td,fd->tf/dot_general | solution.py:194
  166.4 3.7 multiply_reduce_fusion.1
  173.7 1.9 convolution_convert_fusion.3
  175.5 3.2 convolution_convert_fusion.4
  178.7 2.3 copy.112
  181.0 2.4 squeeze.37
  183.5 4.3 convert_reduce_fusion.3
  187.8 3.2 multiply_reduce_fusion
  191.3 1.8 copy.123
  193.1 3.8 multiply_convert_fusion.1
  202.3 3.8 convolution_convert_fusion
  206.2 7.4 %convolution_convert_fusion.2 = bf16[768,3072]{1,0:T(8,128)(2,1)} fusion(bf16[512,3072]{1,0:T(8,128)(2,1)} %copy-done.53, f32[512,768]{1,0:T(8,128)} %copy-done.6, f32[768]{0:T(1024)} %param.27, f32[768]{0:T(1024)} %param.26, f32[512]{0:T(512)} %copy-done.34, f32[512]{0:T(512)S(1)} %copy-done.27), kind=kOutput, calls=%fused_computation.35 | convolution fusion | flops 2420244480 | bytes 9447424 | tf_op jit(solution)/shard_map/td,tf->df/dot_general | solution.py:197
  213.6 6.7 %copy.134 = bf16[768,3072]{0,1:T(8,128)(2,1)} copy(bf16[768,3072]{1,0:T(8,128)(2,1)} %convolution_convert_fusion.2) | data formatting | bytes 9437184
  220.3 6.9 %convolution_convert_fusion.1 = bf16[3072,768]{0,1:T(8,128)(2,1)} fusion(bf16[512,3072]{1,0:T(8,128)(2,1)} %copy-done.54, bf16[512,768]{1,0:T(8,128)(2,1)} %copy-done.17), kind=kOutput, calls=%fused_computation.34 | convolution fusion | flops 2418278400 | bytes 8650752 | tf_op jit(solution)/shard_map/tf,td->fd/dot_general | solution.py:193
  227.6 1.7 copy.132
  229.4 49.3 %reduce-scatter.15.cloned.1.call-done = bf16[768,288]{0,1:T(8,128)(2,1)} async-done(((bf16[768,2304]{0,1:T(8,128)(2,1)}), bf16[768,288]{0,1:T(8,128)(2,1)}) %reduce-scatter.15.cloned.1.call-update) | async-done | bytes 442384 | tf_op jit(solution)/shard_map/reduce_scatter | solution.py:264
  278.7 2.1 copy.130
  280.8 55.1 %reduce-scatter.29.cloned.1.call-done = bf16[384,768]{1,0:T(8,128)(2,1)} async-done(((bf16[3072,768]{1,0:T(8,128)(2,1)}), bf16[384,768]{1,0:T(8,128)(2,1)}) %reduce-scatter.29.cloned.1.call-update) | async-done | bytes 589840
  335.9 2.1 copy.135
  338.1 5.1 %add_convert_fusion.1 = bf16[512,768]{1,0:T(8,128)(2,1)} fusion(f32[512,768]{1,0:T(8,128)} %copy-done.8, bf16[512,2304]{0,1:T(8,128)(2,1)} %copy-done.20, bf16[768,2304]{1,0:T(8,128)(2,1)S(1)} %copy-done, f32[512]{0:T(512)S(1)} %copy-done.37), kind=kOutput, calls=%fused_computation.57 | convolution fusion | flops 1813118976 | bytes 8259584 | tf_op jit(solution)/shard_map/te,de->td/dot_general | solution.py:251
  343.1 3.0 gather_fusion.11
  346.2 2.9 broadcast_select_fusion
  349.1 4.4 all-to-all-start.4
  353.6 49.1 %reduce-scatter.21.cloned.1.call-done = bf16[3072,96]{0,1:T(8,128)(2,1)} async-done(((bf16[3072,768]{0,1:T(8,128)(2,1)}), bf16[3072,96]{0,1:T(8,128)(2,1)}) %reduce-scatter.21.cloned.1.call-update) | async-done | bytes 589840 | tf_op jit(solution)/shard_map/reduce_scatter | solution.py:273
  405.5 41.4 %all-reduce = (f32[1536]{0:T(1024)}, f32[768]{0:T(1024)}, f32[768]{0:T(1024)}, f32[768]{0:T(1024)}, f32[3072]{0:T(1024)}, /*index=5*/f32[768]{0:T(1024)}, f32[768]{0:T(1024)}, f32[768]{0:T(1024)}) all-reduce(f32[1536]{0:T(1024)S(1)} %pad_maximum_fusion.1, ...), channel_id=1, replica_groups=mesh['wide'=8,'narrow'=4] {'wide','narrow'}, use_global_device_ids=true, to_apply=%region_26.27 | all-reduce | flops 9216 | bytes 73728 | tf_op jit(solution)/shard_map/psum | solution.py:291
  446.8 3.3 gather_fusion.12
  450.2 2.7 broadcast_select_fusion.1
  456.0 1.7 copy.131
  457.6 1.7 copy.124
  459.4 11.4 %reduce-scatter.19.cloned.1.call-done = bf16[192,384]{1,0:T(8,128)(2,1)} async-done(((bf16[768,384]{1,0:T(8,128)(2,1)}), bf16[192,384]{1,0:T(8,128)(2,1)}) %reduce-scatter.19.cloned.1.call-update) | async-done | bytes 147472 | tf_op jit(solution)/shard_map/reduce_scatter | solution.py:284
  470.7 1.6 convert_element_type.181
  472.4 21.1 %reduce-scatter.23.cloned.1.call-done = bf16[768,96]{0,1:T(8,128)(2,1)} async-done(((bf16[3072,96]{0,1:T(8,128)(2,1)}), bf16[768,96]{0,1:T(8,128)(2,1)}) %reduce-scatter.23.cloned.1.call-update) | async-done | bytes 147472 | tf_op jit(solution)/shard_map/reduce_scatter | solution.py:287
  493.5 1.6 convert_element_type.184
  (216 shorter events, 55.0 us)
Async XLA Ops:
  7.2 46.2 %copy-start = (bf16[768,2304]{1,0:T(8,128)(2,1)S(1)}, bf16[768,2304]{1,0:T(8,128)(2,1)}, u32[]{:S(2)}) copy-start(bf16[768,2304]{1,0:T(8,128)(2,1)} %param.22) | copy-start | bytes 10616836
  9.6 7.5 %copy-start.40 = (pred[8]{0:T(512)(128)(4,1)}, pred[8]{0:T(512)(128)(4,1)S(1)}, u32[]{:S(2)}) copy-start(pred[8]{0:T(512)(128)(4,1)S(1)} %fusion.59) | copy-start | bytes 28
  9.9 1.9 copy-start.39
  11.8 13.3 %all-to-all-start.1 = ((s32[8,1,128]{2,1,0:T(1,128)}), s32[8,1,128]{2,1,0:T(1,128)S(1)}, u32[]{:S(2)}, u32[]{:S(2)}) async-start(s32[8,1,128]{2,1,0:T(1,128)} %bitcast.2), calls=%async_computation.1 | async-start | bytes 8192 | tf_op jit(solution)/shard_map/all_to_all | solution.py:101
  18.3 4.1 copy-start.41
  22.4 2.7 copy-start.46
  25.2 25.3 %all-to-all-start = ((bf16[8,128,768]{2,1,0:T(8,128)(2,1)}), bf16[8,128,768]{2,1,0:T(8,128)(2,1)}, u32[]{:S(2)}, u32[]{:S(2)}) async-start(bf16[8,128,768]{2,1,0:T(8,128)(2,1)} %broadcast_select_fusion.2), calls=%async_computation | async-start | bytes 3145728 | tf_op jit(solution)/shard_map/all_to_all | solution.py:100
  35.4 21.2 %copy-start.38 = (s32[1024]{0:T(1024)}, s32[1024]{0:T(1024)S(1)}, u32[]{:S(2)}) copy-start(s32[1024]{0:T(1024)S(1)} %pad_clamp_fusion.5) | copy-start | bytes 12292
  74.4 2.5 copy-start.1
  74.4 2.5 copy-start.21
  74.4 6.0 %slice-start.2 = ((s8[4718592]{0:T(1024)(128)(4,1)}), s8[4194304]{0:T(1024)(128)(4,1)S(1)}, s32[]{:S(2)}) async-start(s8[4718592]{0:T(1024)(128)(4,1)} %bitcast.125), calls=%async_computation.23 | async-start | bytes 8388608
  76.2 1.9 copy-start.13
  76.2 2.3 copy-start.47
  76.2 2.3 copy-start.50
  76.2 4.2 slice-start.3
  77.5 1.9 copy-start.15
  78.5 1.9 copy-start.44
  78.5 1.9 copy-start.48
  78.5 1.9 copy-start.52
  78.5 20.9 %slice-start = ((s8[4718592]{0:T(1024)(128)(4,1)}), s8[4194304]{0:T(1024)(128)(4,1)S(1)}, s32[]{:S(2)}) async-start(s8[4718592]{0:T(1024)(128)(4,1)} %bitcast.123), calls=%async_computation.21 | async-start | bytes 8388608
  79.5 19.9 %copy-start.6 = (f32[512,768]{1,0:T(8,128)}, f32[512,768]{1,0:T(8,128)S(1)}, u32[]{:S(2)}) copy-start(f32[512,768]{1,0:T(8,128)S(1)} %get-tuple-element.178) | copy-start | bytes 4718596
  79.5 19.8 %copy-start.26 = (f32[512]{0:T(512)}, f32[512]{0:T(512)S(1)}, u32[]{:S(2)}) copy-start(f32[512]{0:T(512)S(1)} %broadcast_multiply_fusion.1) | copy-start | bytes 6148
  80.4 18.9 %copy-start.34 = (f32[512]{0:T(512)}, f32[512]{0:T(512)S(1)}, u32[]{:S(2)}) copy-start(f32[512]{0:T(512)S(1)} %fusion.62) | copy-start | bytes 6148
  80.4 18.9 %slice-start.1 = ((s8[4718592]{0:T(1024)(128)(4,1)}), s8[524288]{0:T(1024)(128)(4,1)S(1)}, s32[]{:S(2)}) async-start(s8[4718592]{0:T(1024)(128)(4,1)} %bitcast.123), calls=%async_computation.22 | async-start | bytes 1048576
  80.5 18.9 %copy-start.51 = (f32[768]{0:T(1024)S(1)}, f32[768]{0:T(1024)}, u32[]{:S(2)}) copy-start(f32[768]{0:T(1024)} %param.31) | copy-start | bytes 9220
  99.3 2.9 copy-start.54
  99.4 3.2 copy-start.23
  99.4 3.2 copy-start.43
  102.5 2.6 copy-start.31
  102.6 2.5 copy-start.24
  108.8 9.2 %all-to-all-start.2 = ((bf16[8,8,768]{2,1,0:T(8,128)(2,1)}), bf16[8,8,768]{2,1,0:T(8,128)(2,1)}, u32[]{:S(2)}, u32[]{:S(2)}) async-start(bf16[8,8,768]{2,1,0:T(8,128)(2,1)} %broadcast_select_fusion.4), calls=%async_computation.2 | async-start | bytes 196608 | tf_op jit(solution)/shard_map/all_to_all | solution.py:169
  139.5 9.2 %all-to-all-start.3 = ((bf16[8,8,768]{2,1,0:T(8,128)(2,1)}), bf16[8,8,768]{2,1,0:T(8,128)(2,1)}, u32[]{:S(2)}, u32[]{:S(2)}) async-start(bf16[8,8,768]{2,1,0:T(8,128)(2,1)} %broadcast_select_fusion.3), calls=%async_computation.3 | async-start | bytes 196608 | tf_op jit(solution)/shard_map/all_to_all | solution.py:183
  143.5 84.1 %reduce-scatter.17.cloned.1.call-start = ((), (), s32[]{:S(2)}) async-start(), calls=%async_computation.14 | async-start | bytes 1327104 | tf_op jit(solution)/shard_map/reduce_scatter | solution.py:267
  150.9 2.4 copy-start.4
  150.9 4.3 copy-start.32
  150.9 4.3 copy-start.25
  155.2 11.2 %slice-start.4 = ((s8[4718592]{0:T(1024)(128)(4,1)}), s8[4194304]{0:T(1024)(128)(4,1)S(1)}, s32[]{:S(2)}) async-start(s8[4718592]{0:T(1024)(128)(4,1)} %bitcast.127), calls=%async_computation.25 | async-start | bytes 8388608
  156.6 9.7 %copy-start.17 = (bf16[512,768]{1,0:T(8,128)(2,1)}, bf16[512,768]{1,0:T(8,128)(2,1)S(1)}, u32[]{:S(2)}) copy-start(bf16[512,768]{1,0:T(8,128)(2,1)S(1)} %get-tuple-element.145) | copy-start | bytes 2359300
  156.9 9.5 %copy-start.7 = (f32[512,768]{1,0:T(8,128)S(1)}, f32[512,768]{1,0:T(8,128)}, u32[]{:S(2)}) copy-start(f32[512,768]{1,0:T(8,128)} %copy-done.6) | copy-start | bytes 4718596
  156.9 9.5 %copy-start.27 = (f32[512]{0:T(512)S(1)}, f32[512]{0:T(512)}, u32[]{:S(2)}) copy-start(f32[512]{0:T(512)} %copy-done.26) | copy-start | bytes 6148
  156.9 9.5 %copy-start.35 = (f32[512]{0:T(512)S(1)}, f32[512]{0:T(512)}, u32[]{:S(2)}) copy-start(f32[512]{0:T(512)} %copy-done.34) | copy-start | bytes 6148
  156.9 9.5 %copy-start.45 = (f32[768]{0:T(1024)S(1)}, f32[768]{0:T(1024)}, u32[]{:S(2)}) copy-start(f32[768]{0:T(1024)} %param.26) | copy-start | bytes 9220
  156.9 9.5 %slice-start.5 = ((s8[4718592]{0:T(1024)(128)(4,1)}), s8[524288]{0:T(1024)(128)(4,1)S(1)}, s32[]{:S(2)}) async-start(s8[4718592]{0:T(1024)(128)(4,1)} %bitcast.127), calls=%async_computation.26 | async-start | bytes 1048576
  166.4 3.8 copy-start.53
  166.4 3.7 copy-start.30
  170.8 2.8 copy-start.16
  170.8 1.9 copy-start.36
  183.5 4.3 copy-start.2
  183.5 4.3 copy-start.5
  183.5 4.3 copy-start.12
  183.5 4.3 copy-start.19
  191.0 87.7 %reduce-scatter.15.cloned.1.call-start = ((), (), s32[]{:S(2)}) async-start(), calls=%async_computation.13 | async-start | bytes 3981312 | tf_op jit(solution)/shard_map/reduce_scatter | solution.py:264
  193.0 3.8 copy-start.10
  196.8 1.8 copy-start.9
  206.1 129.8 %reduce-scatter.29.cloned.1.call-start = ((), (), s32[]{:S(2)}) async-start(), calls=%async_computation.20 | async-start | bytes 5308416
  220.3 182.4 %reduce-scatter.21.cloned.1.call-start = ((), (), s32[]{:S(2)}) async-start(), calls=%async_computation.16 | async-start | bytes 5308416 | tf_op jit(solution)/shard_map/reduce_scatter | solution.py:273
  227.2 110.8 %copy-start.37 = (f32[512]{0:T(512)S(1)}, f32[512]{0:T(512)}, u32[]{:S(2)}) copy-start(f32[512]{0:T(512)} %copy-done.36) | copy-start | bytes 6148
  227.2 225.6 %reduce-scatter.27.cloned.1.call-start = ((), (), s32[]{:S(2)}) async-start(), calls=%async_computation.19 | async-start | bytes 245760
  229.3 226.6 %reduce-scatter.25.cloned.1.call-start = ((), (), s32[]{:S(2)}) async-start(), calls=%async_computation.18 | async-start | bytes 737280
  280.8 190.0 %reduce-scatter.19.cloned.1.call-start = ((), (), s32[]{:S(2)}) async-start(), calls=%async_computation.15 | async-start | bytes 737280 | tf_op jit(solution)/shard_map/reduce_scatter | solution.py:284
  343.1 3.0 copy-start.42
  349.1 56.4 %copy-start.33 = (f32[768]{0:T(1024)S(1)}, f32[768]{0:T(1024)}, u32[]{:S(2)}) copy-start(f32[768]{0:T(1024)} %get-tuple-element.189) | copy-start | bytes 9220
  349.1 97.7 %all-to-all-start.4 = ((bf16[8,128,768]{2,1,0:T(8,128)(2,1)}), bf16[8,128,768]{2,1,0:T(8,128)(2,1)}, u32[]{:S(2)}, u32[]{:S(2)}) async-start(bf16[8,128,768]{2,1,0:T(8,128)(2,1)} %broadcast_select_fusion), calls=%async_computation.4 | async-start | bytes 3145728 | tf_op jit(solution)/shard_map/all_to_all | solution.py:254
  353.6 140.0 %reduce-scatter.23.cloned.1.call-start = ((), (), s32[]{:S(2)}) async-start(), calls=%async_computation.17 | async-start | bytes 737280 | tf_op jit(solution)/shard_map/reduce_scatter | solution.py:287
  (10 other events, 12.2 us)
Sparse Core Ops, SparseCore 0:
  191.1 36.0 reduce-scatter.16
  230.7 47.9 reduce-scatter.14
  282.1 53.7 reduce-scatter.28
  339.2 63.4 reduce-scatter.20
  405.4 19.6 reduce-scatter.26
  427.2 20.4 reduce-scatter.24
  450.0 20.6 reduce-scatter.18
  473.0 20.4 reduce-scatter.22
where the time goes:
time: 512 us; the launch traced here: 502 us
  waiting for transfers between devices  204 us (40%)
  local copies, waits for them, and re-layouts  83.7 us (16%)
  matrix products  83.5 us (16%)
  other arithmetic  51.5 us (10%)
  blocking collectives  41.4 us (8%)
  starting transfers between devices  22.7 us (4%)
  between operations  15.3 us (3%)
    unnamed x11, waiting for transfers between devices  55.3 us
    reduce_scatter x1, waiting for transfers between devices, on_device(): lax.psum_scatter(matrix_terms[0].astype(jnp.bfloat16), 'wide', scatter_di...  49.3 us
    reduce_scatter x1, waiting for transfers between devices, on_device(): lax.psum_scatter(matrix_terms[3].astype(jnp.bfloat16), 'wide', scatter_di...  49.1 us
    psum x1, blocking collectives, on_device(): lax.psum((grad_b_qv, grad_b_o, grad_gain_one, grad_shift_one, grad_b_in,...  41.4 us
    unnamed x132, local copies, waits for them, and re-layouts  25.6 us
    reduce_scatter x1, waiting for transfers between devices, on_device(): lax.psum_scatter(partial_sums[3].astype(jnp.bfloat16), 'narrow', scatter_...  21.1 us
    dot_general x1, matrix products, on_device(): jnp.dot(hidden_low, w_in, preferred_element_type=jnp.float32) + b_in  18.8 us
    all_to_all x1, waiting for transfers between devices, on_device(): lax.all_to_all(send_tokens, 'wide', split_axis=0, concat_axis=0, tiled=True)  11.8 us
  transfers between devices with their start and end apart: 13, of which 8 were waited for; matrix products, arithmetic and copies ran while one was open for 18% of the time, Pallas kernels for 0%

commit v1 on v0

v1 whole, which is shorter than its diff:
```python
import functools
import math

import jax
import jax.numpy as jnp
from jax import lax
from jax.experimental import pallas as pl
from jax.experimental.pallas import tpu as pltpu
from jax.sharding import PartitionSpec as P

HEAD_DIM = 64
SEG_ROW = 8
LANES = 128
META_ROWS = 16
NEG_FILL = -1e30
NORM_EPS = 1e-12
COS_EPS = 1e-06
F32 = jnp.float32
BF16 = jnp.bfloat16
VMEM_LIMIT = 60 * 1024 * 1024

NT = (((1,), (1,)), ((), ()))
TN = (((0,), (0,)), ((), ()))


def vmem_spec():
    return pl.BlockSpec(memory_space=pltpu.VMEM)


def params(steps=0):
    return pltpu.CompilerParams(
        dimension_semantics=("arbitrary",) * steps if steps else None,
        vmem_limit_bytes=VMEM_LIMIT,
    )


def split_three(values):
    high = values.astype(BF16)
    rest = values - high.astype(F32)
    middle = rest.astype(BF16)
    low = (rest - middle.astype(F32)).astype(BF16)
    return (high, middle, low)


def dot(left, right, dims=None):
    if dims is None:
        return jnp.dot(left, right, preferred_element_type=F32)
    return lax.dot_general(left, right, dims, preferred_element_type=F32)


def column_sum(values):
    return jnp.sum(values, axis=0, keepdims=True)


def row_mean(values):
    return jnp.mean(values, axis=-1, keepdims=True)


def prep_kernel(dest_ref, tok_ref, seg_ref, dest64_ref, pair_ref, targ_ref, out_ref):
    owner = pl.program_id(0)
    slot_dev = dest_ref.shape[0]
    filled = dest_ref[0] == owner
    for slot in range(1, slot_dev):
        filled = filled | (dest_ref[slot] == owner)
    row_len = tok_ref.shape[1]
    out_ref[0, :row_len, :] = tok_ref[0]
    slots = dest64_ref.shape[1]
    lane = lax.broadcasted_iota(jnp.int32, (pair_ref.shape[0], slots), 1)
    first = pair_ref[:, 0:1]
    second = pair_ref[:, 1:2]
    at_first = (lane == first).astype(F32)
    at_second = (lane == second).astype(F32)
    partner = column_sum(at_first * second.astype(F32) + at_second * first.astype(F32))
    target = column_sum((at_first + at_second) * targ_ref[...])
    high, middle, low = split_three(target)
    labels = seg_ref[0].astype(F32)
    labels = jnp.where(filled, labels, -1.0)
    rows = [
        labels,
        jnp.pad(dest64_ref[...].astype(F32), ((0, 0), (0, LANES - slots))),
        jnp.pad(partner, ((0, 0), (0, LANES - slots))),
        jnp.pad(high.astype(F32), ((0, 0), (0, LANES - slots))),
        jnp.pad(middle.astype(F32), ((0, 0), (0, LANES - slots))),
        jnp.pad(low.astype(F32), ((0, 0), (0, LANES - slots))),
    ]
    rows.append(jnp.zeros((META_ROWS - len(rows), LANES), F32))
    out_ref[0, row_len:, :LANES] = jnp.concatenate(rows, axis=0).astype(BF16)
    out_ref[0, row_len:, LANES:] = jnp.zeros((META_ROWS, out_ref.shape[2] - LANES), BF16)


def build_send(tokens, segments, destination, pair_index, targets, wide_count):
    slot_dev, row_len, width = tokens.shape

    def source(owner, dest_ref):
        found = jnp.int32(0)
        for slot in range(slot_dev):
            found = jnp.where(dest_ref[slot] == owner, slot, found)
        return found

    whole = lambda owner, dest_ref: (0, 0)
    slots = slot_dev * SEG_ROW
    pairs = pair_index.shape[0]
    return pl.pallas_call(
        prep_kernel,
        out_shape=jax.ShapeDtypeStruct((wide_count, row_len + META_ROWS, width), BF16),
        grid_spec=pltpu.PrefetchScalarGridSpec(
            num_scalar_prefetch=1,
            grid=(wide_count,),
            in_specs=[
                pl.BlockSpec((1, row_len, width), lambda o, d: (source(o, d), 0, 0)),
                pl.BlockSpec((1, 1, row_len), lambda o, d: (source(o, d), 0, 0)),
                pl.BlockSpec((1, slots), whole),
                pl.BlockSpec((pairs, 2), whole),
                pl.BlockSpec((pairs, 1), whole),
            ],
            out_specs=pl.BlockSpec((1, row_len + META_ROWS, width), lambda o, d: (o, 0, 0)),
        ),
        compiler_params=params(1),
        name="build_send",
    )(
        destination,
        tokens,
        segments.reshape(slot_dev, 1, row_len),
        jnp.repeat(destination, SEG_ROW).reshape(1, slots),
        pair_index,
        targets.reshape(pairs, 1),
    )


def attend_kernel(
    got_ref,
    wqkv_ref,
    bias_ref,
    wo_ref,
    bo_ref,
    gain_ref,
    shift_ref,
    x_ref,
    proj_ref,
    probs_ref,
    ctx_ref,
    hid_ref,
    low_ref,
    norm_ref,
    rstd_ref,
    lab_ref,
    labcol_ref,
):
    wide_count = got_ref.shape[0]
    tok_count, width = x_ref.shape
    row_len = got_ref.shape[1] - META_ROWS
    kept_rows = tok_count // row_len
    seen = jnp.int32(0)
    sources = [jnp.int32(0)] * kept_rows
    for slot in range(wide_count):
        top = jnp.max(got_ref[slot, row_len : row_len + 1, :LANES].astype(F32))
        live = top >= 0.0
        for row in range(kept_rows):
            sources[row] = jnp.where(live & (seen == row), slot, sources[row])
        seen = seen + live.astype(jnp.int32)
    for row in range(kept_rows):
        span = pl.ds(row * row_len, row_len)
        x_ref[span, :] = got_ref[sources[row], :row_len, :]
        tag = got_ref[sources[row], row_len : row_len + 1, :LANES].astype(F32)
        lab_ref[row : row + 1, :] = tag
        labcol_ref[span, :] = jnp.broadcast_to(tag, (LANES, LANES)).T
    total_cols = proj_ref.shape[1]
    tile = 256
    for start in range(0, total_cols, tile):
        cols = slice(start, start + tile)
        proj_ref[:, cols] = (dot(x_ref[...], wqkv_ref[:, cols]) + bias_ref[:, cols]).astype(BF16)

    scale = 1.0 / math.sqrt(HEAD_DIM)
    lane = lax.broadcasted_iota(jnp.int32, (row_len, LANES), 1)
    left = (lane < HEAD_DIM).astype(BF16)
    right = (lane >= HEAD_DIM).astype(BF16)

    def attend_row(row, carry):
        span = pl.ds(pl.multiple_of(row * row_len, row_len), row_len)
        same = labcol_ref[span, :] == lab_ref[pl.ds(row, 1), :]
        same = jnp.concatenate([same, same], axis=0)
        for pair in range(width // LANES):
            col = pair * LANES
            queries = proj_ref[span, col : col + LANES]
            key_rows = proj_ref[span, width + col : width + col + LANES]
            values = proj_ref[span, 2 * width + col : 2 * width + col + LANES]
            both = jnp.concatenate([queries * left, queries * right], axis=0)
            scores = jnp.where(same, dot(both, key_rows, NT) * scale, NEG_FILL)
            top = jnp.max(scores, axis=-1, keepdims=True)
            expo = jnp.exp(scores - top)
            total = jnp.sum(expo, axis=-1, keepdims=True)
            probs = (expo / total).astype(BF16)
            probs_ref[row, pair] = probs
            wide_probs = jnp.concatenate([probs[:row_len], probs[row_len:]], axis=1)
            split_values = jnp.concatenate([values * left, values * right], axis=0)
            ctx_ref[span, col : col + LANES] = dot(wide_probs, split_values).astype(BF16)
        return carry

    lax.fori_loop(0, kept_rows, attend_row, 0)
    for row in range(kept_rows):
        span = pl.ds(row * row_len, row_len)
        total = x_ref[span, :].astype(F32) + dot(ctx_ref[span, :], wo_ref[...]) + bo_ref[...]
        centered = total - row_mean(total)
        rstd = lax.rsqrt(row_mean(centered * centered) + NORM_EPS)
        normed = centered * rstd
        hidden = normed * gain_ref[...] + shift_ref[...]
        norm_ref[span, :] = normed
        rstd_ref[span, :] = rstd
        hid_ref[span, :] = hidden
        low_ref[span, :] = hidden.astype(BF16)


def attend_forward(got, w_qkv, bias, w_o, b_o, gain, shift, kept_rows):
    wide_count, slot_len, width = got.shape
    row_len = slot_len - META_ROWS
    tok_count = kept_rows * row_len
    shapes = (
        ((tok_count, width), BF16),
        ((tok_count, 3 * width), BF16),
        ((kept_rows, width // LANES, 2 * row_len, row_len), BF16),
        ((tok_count, width), BF16),
        ((tok_count, width), F32),
        ((tok_count, width), BF16),
        ((tok_count, width), F32),
        ((tok_count, 1), F32),
        ((8, LANES), F32),
        ((tok_count, LANES), F32),
    )
    return pl.pallas_call(
        attend_kernel,
        out_shape=[jax.ShapeDtypeStruct(*item) for item in shapes],
        in_specs=[vmem_spec()] * 7,
        out_specs=[vmem_spec()] * len(shapes),
        compiler_params=params(),
        name="attend_forward",
    )(got, w_qkv, bias, w_o, b_o, gain, shift)


def feed_kernel(
    low_ref,
    hid_ref,
    win_ref,
    bin_ref,
    wout_ref,
    bout_ref,
    gain_ref,
    shift_ref,
    lab_ref,
    act_ref,
    slope_ref,
    enc_ref,
    norm_ref,
    rstd_ref,
    pooled_ref,
    total_ref,
):
    step = pl.program_id(0)
    up = dot(low_ref[...], win_ref[...]) + bin_ref[...]
    phi = 0.5 * (1.0 + lax.erf(up * (1.0 / math.sqrt(2.0))))
    density = jnp.exp(-0.5 * up * up) * (1.0 / math.sqrt(2.0 * math.pi))
    act = (up * phi).astype(BF16)
    act_ref[...] = act
    slope_ref[...] = (phi + up * density).astype(BF16)
    part = dot(act, wout_ref[...])

    @pl.when(step == 0)
    def _():
        total_ref[...] = part + (hid_ref[...] + bout_ref[...])

    @pl.when(step > 0)
    def _():
        total_ref[...] += part

    @pl.when(step == pl.num_programs(0) - 1)
    def _():
        tok_count, width = total_ref.shape
        kept_rows = tok_count // LANES
        for row in range(kept_rows):
            span = slice(row * LANES, (row + 1) * LANES)
            total = total_ref[span, :]
            centered = total - row_mean(total)
            rstd = lax.rsqrt(row_mean(centered * centered) + NORM_EPS)
            normed = centered * rstd
            out = normed * gain_ref[...] + shift_ref[...]
            norm_ref[span, :] = normed
            rstd_ref[span, :] = rstd
            enc_ref[span, :] = out.astype(BF16)
            segment = lax.broadcasted_iota(jnp.int32, (SEG_ROW, LANES), 0).astype(F32)
            onehot = (lab_ref[row : row + 1, :] == segment).astype(F32)
            count = jnp.sum(onehot, axis=1, keepdims=True)
            high, middle, low = split_three(out)
            mask = onehot.astype(BF16)
            summed = dot(mask, high) + dot(mask, middle) + dot(mask, low)
            pooled_ref[row * SEG_ROW : (row + 1) * SEG_ROW, :] = (summed / count).astype(BF16)


def feed_forward(low, hidden, w_in, b_in, w_out, b_out, gain, shift, labels):
    tok_count, width = low.shape
    units = w_in.shape[1]
    tile = 512
    kept_rows = tok_count // LANES
    whole = lambda step: (0, 0)
    shapes = (
        ((tok_count, units), BF16),
        ((tok_count, units), BF16),
        ((tok_count, width), BF16),
        ((tok_count, width), F32),
        ((tok_count, 1), F32),
        ((kept_rows * SEG_ROW, width), BF16),
    )
    return pl.pallas_call(
        feed_kernel,
        out_shape=[jax.ShapeDtypeStruct(*item) for item in shapes],
        grid_spec=pltpu.PrefetchScalarGridSpec(
            num_scalar_prefetch=0,
            grid=(units // tile,),
            in_specs=[
                pl.BlockSpec((tok_count, width), whole),
                pl.BlockSpec((tok_count, width), whole),
                pl.BlockSpec((width, tile), lambda step: (0, step)),
                pl.BlockSpec((1, tile), lambda step: (0, step)),
                pl.BlockSpec((tile, width), lambda step: (step, 0)),
                pl.BlockSpec((1, width), whole),
                pl.BlockSpec((1, width), whole),
                pl.BlockSpec((1, width), whole),
                pl.BlockSpec((8, LANES), whole),
            ],
            out_specs=[
                pl.BlockSpec((tok_count, tile), lambda step: (0, step)),
                pl.BlockSpec((tok_count, tile), lambda step: (0, step)),
                pl.BlockSpec((tok_count, width), whole),
                pl.BlockSpec((tok_count, width), whole),
                pl.BlockSpec((tok_count, 1), whole),
                pl.BlockSpec((kept_rows * SEG_ROW, width), whole),
            ],
            scratch_shapes=[pltpu.VMEM((tok_count, width), F32)],
        ),
        compiler_params=params(1),
        name="feed_forward",
    )(low, hidden, w_in, b_in, w_out, b_out, gain, shift, labels)


def route_kernel(me_ref, meta_ref, pair_ref, place_ref, targ_ref, first_ref, second_ref, back_ref):
    wide_count = meta_ref.shape[0]
    me = me_ref[0]
    kept_rows = place_ref.shape[0] // SEG_ROW
    me_f = me.astype(F32)

    def table(row):
        return jnp.concatenate(
            [meta_ref[j, row : row + 1, :LANES].astype(F32) for j in range(wide_count)], axis=0
        )

    labels = table(0)
    dest = table(1)
    lane = lax.broadcasted_iota(jnp.int32, (wide_count, LANES), 1)
    slots = SEG_ROW * 2 * kept_rows
    dest = jnp.where(lane < slots, dest, -1.0)
    partner = table(2)
    target = table(3) + table(4) + table(5)
    sends = jnp.zeros((wide_count, LANES), F32)
    for owner in range(wide_count):
        to_owner = jnp.max((dest == float(owner)).astype(F32), axis=1, keepdims=True)
        sends = sends + jnp.where(lane == owner, to_owner, 0.0)
    row_id = lax.broadcasted_iota(jnp.int32, (wide_count, wide_count), 0)
    col_id = lax.broadcasted_iota(jnp.int32, (wide_count, wide_count), 1)
    below = (col_id < row_id).astype(BF16)
    earlier = dot(below, sends.astype(BF16))
    rank = jnp.zeros((wide_count, LANES), F32)
    for owner in range(wide_count):
        rank = rank + jnp.where(dest == float(owner), earlier[:, owner : owner + 1], 0.0)
    segment = (lane % SEG_ROW).astype(F32)
    per_owner = float(kept_rows * SEG_ROW)
    place = jnp.where(dest >= 0.0, dest * per_owner + rank * float(SEG_ROW) + segment, -1.0)
    live = (labels[:, 0:1] >= 0.0).astype(F32)
    my_rank = dot(below, jnp.broadcast_to(live, (wide_count, LANES)).astype(BF16))
    back = jnp.clip(my_rank, 0.0, float(kept_rows - 1))
    diagonal = lax.broadcasted_iota(jnp.int32, (wide_count, LANES), 0) == lane
    back_ref[...] = column_sum(jnp.where(diagonal, back, 0.0)).astype(jnp.int32)
    seg_lane = lax.broadcasted_iota(jnp.int32, (SEG_ROW, LANES), 1)
    seg_id = lax.broadcasted_iota(jnp.int32, (SEG_ROW, LANES), 0)
    for row in range(kept_rows):
        chosen = (live > 0.0) & (my_rank[:, 0:1] == float(row))
        pick = lambda values: column_sum(jnp.where(chosen, values, 0.0))
        own = (pick(dest) == me_f) & (seg_lane % SEG_ROW == seg_id)
        gather = lambda mask, values: jnp.sum(jnp.where(mask, values, 0.0), axis=1, keepdims=True)
        other = gather(own, pick(partner))
        at_other = seg_lane.astype(F32) == other
        out = slice(row * SEG_ROW, (row + 1) * SEG_ROW)
        place_ref[out, :] = gather(at_other, pick(place))
        targ_ref[out, :] = gather(own, pick(target))
    mine = lax.broadcasted_iota(jnp.int32, (wide_count, LANES), 0) == me
    my_place = column_sum(jnp.where(mine, place, 0.0))
    pair_lane = lax.broadcasted_iota(jnp.int32, (pair_ref.shape[0], LANES), 1)
    for column, out_ref in ((0, first_ref), (1, second_ref)):
        at_slot = pair_lane == pair_ref[:, column : column + 1]
        out_ref[...] = jnp.sum(jnp.where(at_slot, my_place, 0.0), axis=1, keepdims=True)


def route(me, meta, pair_index, kept_rows):
    wide_count = meta.shape[0]
    own = kept_rows * SEG_ROW
    pairs = pair_index.shape[0]
    shapes = (
        ((own, 1), F32),
        ((own, 1), F32),
        ((pairs, 1), F32),
        ((pairs, 1), F32),
        ((1, LANES), jnp.int32),
    )
    return pl.pallas_call(
        route_kernel,
        out_shape=[jax.ShapeDtypeStruct(*item) for item in shapes],
        in_specs=[pl.BlockSpec(memory_space=pltpu.SMEM), vmem_spec(), vmem_spec()],
        out_specs=[vmem_spec()] * len(shapes),
        compiler_params=params(),
        name="route",
    )(me, meta, pair_index)


def pick_rows(place_ref, all_ref):
    lane = lax.broadcasted_iota(jnp.int32, (place_ref.shape[0], all_ref.shape[0]), 1)
    return dot((lane.astype(F32) == place_ref[...]).astype(BF16), all_ref[...])


def cosine_parts(left, right):
    inner = row_mean(left * right)
    left_inv = lax.rsqrt(row_mean(left * left) + COS_EPS)
    right_inv = lax.rsqrt(row_mean(right * right) + COS_EPS)
    return (inner, left_inv, right_inv)


def cosine_kernel(first_ref, second_ref, all_ref, sim_ref):
    left = pick_rows(first_ref, all_ref)
    right = pick_rows(second_ref, all_ref)
    inner, left_inv, right_inv = cosine_parts(left, right)
    sim = inner * left_inv * right_inv
    sim_ref[...] = jnp.where(first_ref[...] >= 0.0, sim, 0.0)


def cosine_pairs(first, second, pooled_all):
    return pl.pallas_call(
        cosine_kernel,
        out_shape=jax.ShapeDtypeStruct(first.shape, F32),
        in_specs=[vmem_spec()] * 3,
        out_specs=vmem_spec(),
        compiler_params=params(),
        name="cosine_pairs",
    )(first, second, pooled_all)


def norm_back(grad, normed, rstd, gain):
    scaled = grad * gain
    return rstd * (scaled - row_mean(scaled) - normed * row_mean(scaled * normed))


def loss_back_kernel(
    own_ref,
    all_ref,
    place_ref,
    targ_ref,
    lab_ref,
    labcol_ref,
    norm_ref,
    rstd_ref,
    gain_ref,
    dres_ref,
    dffn_ref,
    dffn_t_ref,
    sums_ref,
):
    tok_count, width = norm_ref.shape
    kept_rows = tok_count // LANES
    left = own_ref[...].astype(F32)
    right = pick_rows(place_ref, all_ref)
    inner, left_inv, right_inv = cosine_parts(left, right)
    error = 2.0 * (inner * left_inv * right_inv - targ_ref[...])
    factor = error * left_inv * right_inv * (1.0 / width)
    d_pooled = (factor * (right - left * (inner * left_inv * left_inv))).astype(BF16).astype(F32)
    gain_sum = jnp.zeros((1, width), F32)
    shift_sum = jnp.zeros((1, width), F32)
    bias_sum = jnp.zeros((1, width), F32)
    lane = lax.broadcasted_iota(jnp.int32, (LANES, LANES), 1).astype(F32)
    for row in range(kept_rows):
        span = slice(row * LANES, (row + 1) * LANES)
        segment = lax.broadcasted_iota(jnp.int32, (SEG_ROW, LANES), 0).astype(F32)
        count = jnp.sum(
            (lab_ref[row : row + 1, :] == segment).astype(F32), axis=1, keepdims=True
        )
        per_token = d_pooled[row * SEG_ROW : (row + 1) * SEG_ROW, :] / count
        shift_sum = shift_sum + column_sum(per_token * count)
        padded = jnp.concatenate([per_token, jnp.zeros((LANES - SEG_ROW, width), F32)], axis=0)
        onehot = (labcol_ref[span, :] == lane).astype(BF16)
        high, middle, low = split_three(padded)
        d_out = dot(onehot, high) + dot(onehot, middle) + dot(onehot, low)
        normed = norm_ref[span, :]
        d_res = norm_back(d_out, normed, rstd_ref[span, :], gain_ref[...])
        d_low = d_res.astype(BF16)
        dres_ref[span, :] = d_res
        dffn_ref[span, :] = d_low
        dffn_t_ref[:, span] = d_low.T
        gain_sum = gain_sum + column_sum(d_out * normed)
        bias_sum = bias_sum + column_sum(d_low.astype(F32))
    sums_ref[0:1, :] = gain_sum
    sums_ref[1:2, :] = shift_sum
    sums_ref[2:3, :] = bias_sum
    sums_ref[3:8, :] = jnp.zeros((5, width), F32)


def loss_back(own, pooled_all, place, target, labels, label_cols, normed, rstd, gain):
    tok_count, width = normed.shape
    shapes = (
        ((tok_count, width), F32),
        ((tok_count, width), BF16),
        ((width, tok_count), BF16),
        ((8, width), F32),
    )
    return pl.pallas_call(
        loss_back_kernel,
        out_shape=[jax.ShapeDtypeStruct(*item) for item in shapes],
        in_specs=[vmem_spec()] * 9,
        out_specs=[vmem_spec()] * len(shapes),
        compiler_params=params(),
        name="loss_back",
    )(own, pooled_all, place, target, labels, label_cols, normed, rstd, gain)


def feed_back_kernel(
    dffn_ref,
    dres_ref,
    wout_ref,
    win_ref,
    slope_ref,
    norm_ref,
    rstd_ref,
    gain_ref,
    wo_ref,
    dup_t_ref,
    bsum_ref,
    done_ref,
    dattn_t_ref,
    dctx_ref,
    sums_ref,
    total_ref,
):
    step = pl.program_id(0)
    d_up = (dot(dffn_ref[...], wout_ref[...], NT) * slope_ref[...].astype(F32)).astype(BF16)
    dup_t_ref[...] = d_up.T
    bsum_ref[...] = column_sum(d_up.astype(F32))
    part = dot(d_up, win_ref[...], NT)

    @pl.when(step == 0)
    def _():
        total_ref[...] = part + dres_ref[...]

    @pl.when(step > 0)
    def _():
        total_ref[...] += part

    @pl.when(step == pl.num_programs(0) - 1)
    def _():
        tok_count, width = total_ref.shape
        kept_rows = tok_count // LANES
        gain_sum = jnp.zeros((1, width), F32)
        shift_sum = jnp.zeros((1, width), F32)
        bias_sum = jnp.zeros((1, width), F32)
        for row in range(kept_rows):
            span = slice(row * LANES, (row + 1) * LANES)
            d_hidden = total_ref[span, :]
            normed = norm_ref[span, :]
            d_res = norm_back(d_hidden, normed, rstd_ref[span, :], gain_ref[...])
            d_low = d_res.astype(BF16)
            done_ref[span, :] = d_res
            dattn_t_ref[:, span] = d_low.T
            dctx_ref[span, :] = dot(d_low, wo_ref[...], NT).astype(BF16)
            gain_sum = gain_sum + column_sum(d_hidden * normed)
            shift_sum = shift_sum + column_sum(d_hidden)
            bias_sum = bias_sum + column_sum(d_low.astype(F32))
        sums_ref[0:1, :] = gain_sum
        sums_ref[1:2, :] = shift_sum
        sums_ref[2:3, :] = bias_sum
        sums_ref[3:8, :] = jnp.zeros((5, width), F32)


def feed_back(d_ffn, d_res, w_out, w_in, slope, normed, rstd, gain, w_o):
    tok_count, width = d_ffn.shape
    units = w_in.shape[1]
    tile = 512
    whole = lambda step: (0, 0)
    shapes = (
        ((units, tok_count), BF16),
        ((1, units), F32),
        ((tok_count, width), F32),
        ((width, tok_count), BF16),
        ((tok_count, width), BF16),
        ((8, width), F32),
    )
    return pl.pallas_call(
        feed_back_kernel,
        out_shape=[jax.ShapeDtypeStruct(*item) for item in shapes],
        grid_spec=pltpu.PrefetchScalarGridSpec(
            num_scalar_prefetch=0,
            grid=(units // tile,),
            in_specs=[
                pl.BlockSpec((tok_count, width), whole),
                pl.BlockSpec((tok_count, width), whole),
                pl.BlockSpec((tile, width), lambda step: (step, 0)),
                pl.BlockSpec((width, tile), lambda step: (0, step)),
                pl.BlockSpec((tok_count, tile), lambda step: (0, step)),
                pl.BlockSpec((tok_count, width), whole),
                pl.BlockSpec((tok_count, 1), whole),
                pl.BlockSpec((1, width), whole),
                pl.BlockSpec((width, width), whole),
            ],
            out_specs=[
                pl.BlockSpec((tile, tok_count), lambda step: (step, 0)),
                pl.BlockSpec((1, tile), lambda step: (0, step)),
                pl.BlockSpec((tok_count, width), whole),
                pl.BlockSpec((width, tok_count), whole),
                pl.BlockSpec((tok_count, width), whole),
                pl.BlockSpec((8, width), whole),
            ],
            scratch_shapes=[pltpu.VMEM((tok_count, width), F32)],
        ),
        compiler_params=params(1),
        name="feed_back",
    )(d_ffn, d_res, w_out, w_in, slope, normed, rstd, gain, w_o)


def attend_back_kernel(
    proj_ref, probs_ref, dctx_ref, done_ref, wqkv_ref, dproj_t_ref, dtok_ref, sums_ref, dproj_ref
):
    row = pl.program_id(0)
    row_len, width = dctx_ref.shape
    scale = 1.0 / math.sqrt(HEAD_DIM)
    lane = lax.broadcasted_iota(jnp.int32, (row_len, LANES), 1)
    left = (lane < HEAD_DIM).astype(BF16)
    right = (lane >= HEAD_DIM).astype(BF16)

    def twice(values):
        return jnp.concatenate([values * left, values * right], axis=0)

    for pair in range(width // LANES):
        col = pair * LANES
        queries = proj_ref[:, col : col + LANES]
        key_rows = proj_ref[:, width + col : width + col + LANES]
        values = proj_ref[:, 2 * width + col : 2 * width + col + LANES]
        probs = probs_ref[0, pair]
        d_ctx = twice(dctx_ref[:, col : col + LANES])
        d_probs = dot(d_ctx, values, NT)
        probs_f = probs.astype(F32)
        inner = jnp.sum(probs_f * d_probs, axis=-1, keepdims=True)
        d_scores = (probs_f * (d_probs - inner)).astype(BF16)
        wide_scores = jnp.concatenate([d_scores[:row_len], d_scores[row_len:]], axis=1)
        d_query = dot(wide_scores, twice(key_rows)) * scale
        d_key = dot(d_scores, twice(queries), TN) * scale
        d_value = dot(probs, d_ctx, TN)
        for part, grad in ((0, d_query), (1, d_key), (2, d_value)):
            low = grad.astype(BF16)
            place = part * width + col
            dproj_ref[:, place : place + LANES] = low
            dproj_t_ref[place : place + LANES, :] = low.T
            summed = column_sum(low.astype(F32))

            @pl.when(row == 0)
            def _():
                sums_ref[:, place : place + LANES] = summed

            @pl.when(row > 0)
            def _():
                sums_ref[:, place : place + LANES] += summed

    grad = done_ref[...] + dot(dproj_ref[...], wqkv_ref[...], NT)
    dtok_ref[...] = grad.astype(BF16)


def attend_back(proj, probs, d_ctx, d_one, w_qkv):
    tok_count, width = d_ctx.shape
    kept_rows = tok_count // LANES
    shapes = (
        ((3 * width, tok_count), BF16),
        ((tok_count, width), BF16),
        ((1, 3 * width), F32),
    )
    return pl.pallas_call(
        attend_back_kernel,
        out_shape=[jax.ShapeDtypeStruct(*item) for item in shapes],
        grid_spec=pltpu.PrefetchScalarGridSpec(
            num_scalar_prefetch=0,
            grid=(kept_rows,),
            in_specs=[
                pl.BlockSpec((LANES, 3 * width), lambda row: (row, 0)),
                pl.BlockSpec((1,) + probs.shape[1:], lambda row: (row, 0, 0, 0)),
                pl.BlockSpec((LANES, width), lambda row: (row, 0)),
                pl.BlockSpec((LANES, width), lambda row: (row, 0)),
                pl.BlockSpec((width, 3 * width), lambda row: (0, 0)),
            ],
            out_specs=[
                pl.BlockSpec((3 * width, LANES), lambda row: (0, row)),
                pl.BlockSpec((LANES, width), lambda row: (row, 0)),
                pl.BlockSpec((1, 3 * width), lambda row: (0, 0)),
            ],
            scratch_shapes=[pltpu.VMEM((LANES, 3 * width), BF16)],
        ),
        compiler_params=params(1),
        name="attend_back",
    )(proj, probs, d_ctx, d_one, w_qkv)


def spread_kernel(index_ref, rows_ref, out_ref):
    out_ref[...] = rows_ref[...]


def spread_rows(index, rows, count):
    block = (1,) + rows.shape[1:]
    return pl.pallas_call(
        spread_kernel,
        out_shape=jax.ShapeDtypeStruct((count,) + rows.shape[1:], rows.dtype),
        grid_spec=pltpu.PrefetchScalarGridSpec(
            num_scalar_prefetch=1,
            grid=(count,),
            in_specs=[pl.BlockSpec(block, lambda slot, idx: (idx[slot], 0, 0))],
            out_specs=pl.BlockSpec(block, lambda slot, idx: (slot, 0, 0)),
        ),
        compiler_params=params(1),
        name="spread_rows",
    )(index, rows)


def home_kernel(dest_ref, rows_ref, out_ref):
    live = dest_ref[pl.program_id(0)] >= 0

    @pl.when(live)
    def _():
        out_ref[...] = rows_ref[...]

    @pl.when(jnp.logical_not(live))
    def _():
        out_ref[...] = jnp.zeros_like(out_ref)


def home_rows(destination, rows):
    block = (1,) + rows.shape[1:]
    count = destination.shape[0]
    return pl.pallas_call(
        home_kernel,
        out_shape=jax.ShapeDtypeStruct((count,) + rows.shape[1:], rows.dtype),
        grid_spec=pltpu.PrefetchScalarGridSpec(
            num_scalar_prefetch=1,
            grid=(count,),
            in_specs=[
                pl.BlockSpec(block, lambda slot, dest: (jnp.maximum(dest[slot], 0), 0, 0))
            ],
            out_specs=pl.BlockSpec(block, lambda slot, dest: (slot, 0, 0)),
        ),
        compiler_params=params(1),
        name="home_rows",
    )(destination, rows)


def swap(values, axis, bit):
    count = lax.axis_size(axis)
    return lax.ppermute(values, axis, [(i, i ^ (1 << bit)) for i in range(count)])


def pick(values, dim, index):
    return lax.dynamic_index_in_dim(values, index, dim, keepdims=False)


def add_low(kept, received):
    return (kept.astype(F32) + received.astype(F32)).astype(BF16)


def half_terms(lefts, rights, side):
    wide_count = lax.axis_size("wide")
    parts = []
    for left, right in zip(lefts, rights):
        rows = left.shape[0] // wide_count
        chosen = pick(left.reshape(wide_count // 2, 2, rows, left.shape[1]), 1, side)
        parts.append(
            jnp.einsum("prt,tk->prk", chosen, right, preferred_element_type=F32)
        )
    return parts[0] if len(parts) == 1 else jnp.concatenate(parts, axis=1)


def reduce_wide(lefts, rights, order):
    place = lax.axis_index("wide")
    wide_count = lax.axis_size("wide")
    bits = wide_count.bit_length() - 1
    mine = place & 1
    sent = half_terms(lefts, rights, 1 - mine).astype(BF16)
    received = swap(sent, "wide", 0)
    held = (half_terms(lefts, rights, mine) + received.astype(F32)).astype(BF16)
    held = held.reshape((2,) * (bits - 1) + held.shape[1:])
    left_bits = list(range(bits - 1, 0, -1))
    for bit in order:
        dim = left_bits.index(bit)
        side = (place >> bit) & 1
        received = swap(pick(held, dim, 1 - side), "wide", bit)
        held = add_low(pick(held, dim, side), received)
        left_bits.remove(bit)
    return held


def sum_pieces(pieces):
    received = lax.all_to_all(pieces, "narrow", split_axis=0, concat_axis=0, tiled=True)
    return jnp.sum(received.astype(F32), axis=0)


def sum_vectors(values):
    for axis in ("wide", "narrow"):
        count = lax.axis_size(axis)
        for bit in range(count.bit_length() - 1):
            values = values + swap(values, axis, bit)
    return values


def on_device(
    tokens,
    segments,
    destination,
    pair_index,
    targets,
    w_qkv,
    b_qv,
    w_o,
    b_o,
    gain_one,
    shift_one,
    w_in,
    b_in,
    w_out,
    b_out,
    gain_two,
    shift_two,
):
    wide_count = lax.axis_size("wide")
    narrow_count = lax.axis_size("narrow")
    slot_dev, row_len, width = tokens.shape
    kept_rows = slot_dev // 2
    units = w_in.shape[1]
    me = lax.axis_index("wide")
    line = lambda vector: vector.reshape(1, -1)

    sent = build_send(tokens, segments, destination, pair_index, targets, wide_count)
    got = lax.all_to_all(sent, "wide", split_axis=0, concat_axis=0, tiled=True)
    full_bias = jnp.concatenate(
        [b_qv[:width], jnp.zeros((width,), F32), b_qv[width:]]
    ).reshape(1, 3 * width)
    x, proj, probs, context, hidden, hidden_low, norm_one, rstd_one, labels, label_cols = (
        attend_forward(
            got, w_qkv, full_bias, w_o, line(b_o), line(gain_one), line(shift_one), kept_rows
        )
    )
    act, slope, encoded, norm_two, rstd_two, pooled = feed_forward(
        hidden_low,
        hidden,
        w_in,
        line(b_in),
        w_out,
        line(b_out),
        line(gain_two),
        line(shift_two),
        labels,
    )
    place, target, first, second, back = route(
        me.astype(jnp.int32).reshape(1), got[:, row_len:, :], pair_index, kept_rows
    )
    pooled_all = lax.all_to_all(
        jnp.broadcast_to(pooled[None], (wide_count,) + pooled.shape),
        "wide",
        split_axis=0,
        concat_axis=0,
        tiled=True,
    ).reshape(wide_count * kept_rows * SEG_ROW, width)
    similarity = cosine_pairs(first, second, pooled_all).reshape(-1)
    d_res_two, d_ffn, d_ffn_t, sums_two = loss_back(
        pooled, pooled_all, place, target, labels, label_cols, norm_two, rstd_two, line(gain_two)
    )

    bits = wide_count.bit_length() - 1
    half = 1 + (bits - 1) // 2
    low_first = list(range(1, bits))
    high_first = list(range(half, bits)) + list(range(1, half))

    sum_out = reduce_wide([d_ffn_t], [act], low_first)
    d_up_t, sum_b_in, d_one, d_attn_t, d_ctx, sums_one = feed_back(
        d_ffn, d_res_two, w_out, w_in, slope, norm_one, rstd_one, line(gain_one), w_o
    )
    sum_in = reduce_wide([d_up_t], [hidden_low], high_first)
    d_proj_t, d_rows, sums_qkv = attend_back(proj, probs, d_ctx, d_one, w_qkv)
    sum_mix = reduce_wide([d_proj_t, d_attn_t], [x, context], low_first)

    home = lax.all_to_all(
        spread_rows(back[0, :wide_count], d_rows.reshape(kept_rows, row_len, width), wide_count),
        "wide",
        split_axis=0,
        concat_axis=0,
        tiled=True,
    )
    grad_tokens = home_rows(destination, home)

    rows_out = sum_out.shape[0]
    cols_out = units // narrow_count
    pieces_out = sum_out.reshape(rows_out, narrow_count, cols_out).transpose(1, 0, 2)
    grad_w_out = sum_pieces(pieces_out).T
    rows_in = width // narrow_count
    grad_w_in = sum_pieces(sum_in.T.reshape(narrow_count, rows_in, sum_in.shape[0]))
    grad_mix = sum_pieces(sum_mix.T.reshape(narrow_count, rows_in, sum_mix.shape[0]))
    cols_qkv = 3 * width // wide_count
    grad_w_qkv = grad_mix[:, :cols_qkv]
    grad_w_o = grad_mix[:, cols_qkv:]

    vectors = jnp.concatenate(
        [
            sums_qkv[0, :width],
            sums_qkv[0, 2 * width :],
            sums_one[2],
            sums_one[0],
            sums_one[1],
            sum_b_in[0],
            sums_two[2],
            sums_two[0],
            sums_two[1],
        ]
    )
    vectors = sum_vectors(vectors.reshape(-1, LANES)).reshape(-1)
    cuts = (2 * width, width, width, width, units, width, width, width)
    outs = []
    start = 0
    for size in cuts:
        outs.append(vectors[start : start + size])
        start += size
    grad_b_qv, grad_b_o, grad_gain_one, grad_shift_one = outs[:4]
    grad_b_in, grad_b_out, grad_gain_two, grad_shift_two = outs[4:]
    return (
        encoded.reshape(kept_rows, row_len, width),
        similarity,
        grad_tokens,
        grad_w_qkv,
        grad_b_qv,
        grad_w_o,
        grad_b_o,
        grad_gain_one,
        grad_shift_one,
        grad_w_in,
        grad_b_in,
        grad_w_out,
        grad_b_out,
        grad_gain_two,
        grad_shift_two,
    )


def solution(mesh):
    rows = ("wide", "narrow")
    in_specs = (P(rows, None, None), P(rows, None), P(rows), P(rows, None), P(rows)) + (P(),) * 12
    matrix = P("narrow", "wide")
    out_specs = (
        P(rows, None, None),
        P(rows),
        P(rows, None, None),
        matrix,
        P(),
        matrix,
        P(),
        P(),
        P(),
        matrix,
        P(),
        matrix,
        P(),
        P(),
        P(),
    )
    return jax.shard_map(
        on_device, mesh=mesh, in_specs=in_specs, out_specs=out_specs, check_vma=False
    )
```

time: 512 us -> 305 us (0.60); the launches traced: 502 us -> 302 us
  waiting for transfers between devices: 204 us -> 91.9 us
  Pallas kernels: 0 us -> 94.4 us
  matrix products: 83.5 us -> 21.9 us
  local copies, waits for them, and re-layouts: 83.7 us -> 34.8 us
  blocking collectives: 41.4 us -> 0 us
  other arithmetic: 51.5 us -> 18.4 us
  starting transfers between devices: 22.7 us -> 39.6 us
  between operations: 15.3 us -> 1.16 us
    reduce_scatter x5 -> x0, waiting for transfers between devices: 131 us -> none  [the longest x1 49.3 us: on_device(): lax.psum_scatter(matrix_terms[0].astype(jnp.bfloat16), 'wide', scatter_di...]
    pallas_call x0 -> x10, Pallas kernels: none -> 94.4 us  [the longest x1 23.7 us: attend_back(): pl.pallas_call(attend_back_kernel, out_shape=[jax.ShapeDtypeStruct(*item)...]
    ppermute x0 -> x14, waiting for transfers between devices: none -> 68.3 us  [swap(): return lax.ppermute(values, axis, [(i, i ^ 1 << bit) for i in range(count)])]
    dot_general x20 -> x8, matrix products: 83.5 us -> 21.9 us  [half_terms(): jnp.einsum('prt,tk->prk', chosen, right, preferred_element_type=F32)]
    unnamed x11 -> x0, waiting for transfers between devices: 55.3 us -> none
    psum x1 -> x0, blocking collectives: 41.4 us -> none  [on_device(): lax.psum((grad_b_qv, grad_b_o, grad_gain_one, grad_shift_one, grad_b_in,...]
    gather x13 -> x0, local copies, waits for them, and re-layouts: 29.1 us -> none  [the longest x2 5.53 us: to_home(): member[jnp.clip(slot_of, 0, member.shape[0] - 1)]]
    unnamed x132 -> x67, local copies, waits for them, and re-layouts: 25.6 us -> 8.29 us
  transfers between devices with their start and end apart: 13 -> 20, of which waited for: 8 -> 10; matrix products, arithmetic and copies ran while one was open for 18% -> 20% of each run, Pallas kernels for 0% -> 18%
where the time goes in v1:
time: 305 us; the launch traced here: 302 us
  Pallas kernels  94.4 us (31%)
  waiting for transfers between devices  91.9 us (30%)
  starting transfers between devices  39.6 us (13%)
  local copies, waits for them, and re-layouts  34.8 us (11%)
  matrix products  21.9 us (7%)
  other arithmetic  18.4 us (6%)
    ppermute x14, waiting for transfers between devices, swap(): return lax.ppermute(values, axis, [(i, i ^ 1 << bit) for i in range(count)])  68.3 us
    pallas_call x1, Pallas kernels, attend_back(): pl.pallas_call(attend_back_kernel, out_shape=[jax.ShapeDtypeStruct(*item)...  23.7 us
    dot_general x8, matrix products, half_terms(): jnp.einsum('prt,tk->prk', chosen, right, preferred_element_type=F32)  21.9 us
    all_to_all x1, waiting for transfers between devices, on_device(): got = lax.all_to_all(sent, 'wide', split_axis=0, concat_axis=0, tiled=True)  19 us
    pallas_call x1, Pallas kernels, feed_back(): pl.pallas_call(feed_back_kernel, out_shape=[jax.ShapeDtypeStruct(*item) f...  16 us
    ppermute x14, starting transfers between devices, swap(): return lax.ppermute(values, axis, [(i, i ^ 1 << bit) for i in range(count)])  14.7 us
    pallas_call x1, Pallas kernels, feed_forward(): pl.pallas_call(feed_kernel, out_shape=[jax.ShapeDtypeStruct(*item) for it...  14.5 us
    all_to_all x3, starting transfers between devices, sum_pieces(): lax.all_to_all(pieces, 'narrow', split_axis=0, concat_axis=0, tiled=True)  12.6 us
  transfers between devices with their start and end apart: 20, of which 10 were waited for; matrix products, arithmetic and copies ran while one was open for 20% of the time, Pallas kernels for 18%

profile of v1, /device:TPU:0, one launch (start us, length us, event | category | flops | bytes accessed | tf_op | source)
XLA Modules:
  0.0 302.3 jit_solution(12477000710556885525)
XLA Ops:
  0.6 1.4 copy.49.pair_ref
  2.0 1.3 copy.50.targ_ref
  4.7 6.5 %build_send.1 = bf16[8,144,768]{2,1,0:T(8,128)(2,1)} custom-call(s32[8]{0:T(128)} %dest_ref.3, bf16[8,128,768]{2,1,0:T(8,128)(2,1)} %tok_ref.1, s32[8,1,128]{2,1,0:T(1,128)} %bitcast.144, s32[1,64]{1,0:T(1,128)} %reshape_reshape.3.dest64_ref, s32[32,2]{1,0:T(8,128)} %copy.49.pair_ref, f32[32,1]{1,0:T(8,128)} %copy.50.targ_ref), custom_call_target="tpu_custom_call" | custom-call | tf_op jit(solution)/shard_map/build_send/pallas_call | solution.py:103
  11.2 5.0 %all-to-all-start = ((bf16[8,144,768]{2,1,0:T(8,128)(2,1)}), bf16[8,144,768]{2,1,0:T(8,128)(2,1)S(1)}, u32[]{:S(2)}, u32[]{:S(2)}) async-start(bf16[8,144,768]{2,1,0:T(8,128)(2,1)} %build_send.1), calls=%async_computation | async-start | bytes 3538944 | tf_op jit(solution)/shard_map/all_to_all | solution.py:846
  20.4 19.0 %all-to-all-done.got_ref = bf16[8,144,768]{2,1,0:T(8,128)(2,1)S(1)} async-done(((bf16[8,144,768]{2,1,0:T(8,128)(2,1)}), bf16[8,144,768]{2,1,0:T(8,128)(2,1)S(1)}, u32[]{:S(2)}, u32[]{:S(2)}) %all-to-all-start) | async-done | bytes 1769504 | tf_op jit(solution)/shard_map/all_to_all | solution.py:846
  39.3 1.2 copy-done
  40.5 12.5 %attend_forward.1 = (bf16[512,768]{1,0:T(8,128)(2,1)}, bf16[512,2304]{1,0:T(8,128)(2,1)}, bf16[4,6,256,128]{3,2,1,0:T(8,128)(2,1)}, bf16[512,768]{1,0:T(8,128)(2...) custom-call(bf16[8,144,768]{2,1,0:T(8,128)(2,1)} %copy-done, ...), custom_call_target="tpu_custom_call" | custom-call | tf_op jit(solution)/shard_map/attend_forward/pallas_call | solution.py:229
  53.1 14.5 %feed_forward.1 = (bf16[512,3072]{1,0:T(8,128)(2,1)}, bf16[512,3072]{1,0:T(8,128)(2,1)}, bf16[512,768]{1,0:T(8,128)(2,1)}, f32[512,768]{1,0:T(8,128)}, f32[512,1]{1,0:T(8,128)}, /*index=5*/bf16[32,768]{1,0:T(8,128)(2,1)}) custom-call(bf16[512,768]{1,0:T(8,128)(2,1)} %get-tuple-element.49.low_ref, f32[512,768]{1,0:T(8,128)} %get-tuple-element.50.hid_ref, ...), custom_call_target="tpu_custom_call" | custom-call | tf_op jit(solution)/shard_map/feed_forward/pallas_call | solution.py:311
  67.5 1.6 broadcast_in_dim.14
  69.1 3.6 %all-to-all-start.1 = ((bf16[8,32,768]{2,1,0:T(8,128)(2,1)}), bf16[8,32,768]{2,1,0:T(8,128)(2,1)S(1)}, u32[]{:S(2)}, u32[]{:S(2)}) async-start(bf16[8,32,768]{2,1,0:T(8,128)(2,1)} %broadcast_in_dim.14), calls=%async_computation.1 | async-start | bytes 786432 | tf_op jit(solution)/shard_map/all_to_all | solution.py:869
  72.8 1.6 slice.120.meta_ref
  74.4 2.0 route.1
  76.4 1.2 slice_bitcast_fusion.8.index_ref
  77.6 3.3 %all-to-all-done.1 = bf16[8,32,768]{2,1,0:T(8,128)(2,1)S(1)} async-done(((bf16[8,32,768]{2,1,0:T(8,128)(2,1)}), bf16[8,32,768]{2,1,0:T(8,128)(2,1)S(1)}, u32[]{:S(2)}, u32[]{:S(2)}) %all-to-all-start.1) | async-done | bytes 393248 | tf_op jit(solution)/shard_map/all_to_all | solution.py:869
  81.6 5.2 %loss_back.1 = (f32[512,768]{1,0:T(8,128)}, bf16[512,768]{1,0:T(8,128)(2,1)}, bf16[768,512]{1,0:T(8,128)(2,1)}, f32[8,768]{1,0:T(8,128)}) custom-call(bf16[32,768]{1,0:T(8,128)(2,1)} %get-tuple-element.55.own_ref, bf16[256,768]{1,0:T(8,128)(2,1)} %bitcast.125, f32[32,1]{1,0:T(8,128)} %get-tuple-element.59.place_ref, f32[32,1]{1,0:T(8,128)} %get-tuple-element.60.targ_ref, ...), custom_call_target="tpu_custom_call" | custom-call | tf_op jit(solution)/shard_map/loss_back/pallas_call | solution.py:518
  86.7 4.9 %convolution_convert_fusion = bf16[4,96,3072]{2,1,0:T(8,128)(2,1)} fusion(bf16[512,3072]{1,0:T(8,128)(2,1)} %get-tuple-element.82, bf16[4,2,96,512]{3,2,1,0:T(8,128)(2,1)} %bitcast.149, s32[]{:T(128)S(6)} %select_n.41), kind=kOutput, calls=%fused_computation.4 | convolution fusion | flops 1209139200 | bytes 5898244 | tf_op jit(solution)/shard_map/prt,tk->prk/dot_general | solution.py:781
  91.6 16.0 %feed_back.1 = (bf16[3072,512]{1,0:T(8,128)(2,1)}, f32[1,3072]{1,0:T(1,128)}, f32[512,768]{1,0:T(8,128)}, bf16[768,512]{1,0:T(8,128)(2,1)}, bf16[512,768]{1,0:T(8,128)(2,1)}, /*index=5*/f32[8,768]{1,0:T(8,128)}) custom-call(bf16[512,768]{1,0:T(8,128)(2,1)} %get-tuple-element.64.dffn_ref, f32[512,768]{1,0:T(8,128)} %get-tuple-element.65.dres_ref, ...), custom_call_target="tpu_custom_call" | custom-call | tf_op jit(solution)/shard_map/feed_back/pallas_call | solution.py:598
  107.7 4.2 %convolution_convert_fusion.1 = bf16[4,384,768]{2,1,0:T(8,128)(2,1)} fusion(bf16[4,2,384,512]{3,2,1,0:T(8,128)(2,1)} %bitcast.146, s32[]{:T(128)S(6)} %select_n.41, bf16[512,768]{1,0:T(8,128)(2,1)S(1)} %copy-done.12), kind=kOutput, calls=%fused_computation.15 | convolution fusion | flops 1209139200 | bytes 4718596 | tf_op jit(solution)/shard_map/prt,tk->prk/dot_general | solution.py:781
  112.4 23.7 %attend_back.1 = (bf16[2304,512]{1,0:T(8,128)(2,1)}, bf16[512,768]{1,0:T(8,128)(2,1)}, f32[1,2304]{1,0:T(1,128)}) custom-call(bf16[512,2304]{1,0:T(8,128)(2,1)} %get-tuple-element.57.proj_ref, bf16[4,6,256,128]{3,2,1,0:T(8,128)(2,1)} %get-tuple-element.58.probs_ref, bf16[512,768]{1,0:T(8,128)(2,1)} %get-tuple-element.69.dctx_ref, ...), custom_call_target="tpu_custom_call" | custom-call | tf_op jit(solution)/shard_map/attend_back/pallas_call | solution.py:685
  136.6 2.4 convolution_convert_fusion.2
  139.0 1.6 pad_maximum_fusion
  140.6 5.9 %spread_rows.1 = bf16[8,128,768]{2,1,0:T(8,128)(2,1)} custom-call(s32[8]{0:T(128)} %slice_bitcast_fusion.8.index_ref, bf16[4,128,768]{2,1,0:T(8,128)(2,1)} %bitcast.134), custom_call_target="tpu_custom_call" | custom-call | tf_op jit(solution)/shard_map/spread_rows/pallas_call | solution.py:716
  146.5 3.8 %all-to-all-start.2 = ((bf16[8,128,768]{2,1,0:T(8,128)(2,1)}), bf16[8,128,768]{2,1,0:T(8,128)(2,1)S(1)}, u32[]{:S(2)}, u32[]{:S(2)}) async-start(bf16[8,128,768]{2,1,0:T(8,128)(2,1)} %spread_rows.1), calls=%async_computation.2 | async-start | bytes 3145728 | tf_op jit(solution)/shard_map/all_to_all | solution.py:894
  152.2 2.7 fusion.20
  155.0 3.1 %add_convert_fusion = bf16[4,96,3072]{2,1,0:T(8,128)(2,1)S(1)} fusion(bf16[4,96,3072]{2,1,0:T(8,128)(2,1)} %collective-permute-done.11, bf16[512,3072]{1,0:T(8,128)(2,1)S(1)} %copy-done.26, bf16[4,2,96,512]{3,2,1,0:T(8,128)(2,1)S(1)} %bitcast.150, s32[]{:T(128)S(6)} %select_n.40), kind=kOutput, calls=%fused_computation.2 | convolution fusion | flops 1211498496 | bytes 8257540 | tf_op jit(solution)/shard_map/prt,tk->prk/dot_general | solution.py:781
  158.1 1.2 dynamic-slice_bitcast_fusion
  159.3 1.7 collective-permute-start.12
  161.5 2.2 fusion
  163.7 1.2 constant_dynamic-slice_fusion.3
  164.9 1.4 copy.53
  166.6 3.7 %add_convert_fusion.1 = bf16[4,384,768]{2,1,0:T(8,128)(2,1)S(1)} fusion(bf16[4,384,768]{2,1,0:T(8,128)(2,1)} %collective-permute-done.8, bf16[4,2,384,512]{3,2,1,0:T(8,128)(2,1)} %bitcast.147, s32[]{:T(128)S(6)} %select_n.40, bf16[512,768]{1,0:T(8,128)(2,1)S(1)} %copy-done.13), kind=kOutput, calls=%fused_computation.3 | convolution fusion | flops 1211498496 | bytes 7077892 | tf_op jit(solution)/shard_map/prt,tk->prk/dot_general | solution.py:781
  170.3 25.7 %collective-permute-done.12 = bf16[2,96,3072]{2,1,0:T(8,128)(2,1)} collective-permute-done((bf16[2,96,3072]{2,1,0:T(8,128)(2,1)}, bf16[2,96,3072]{2,1,0:T(8,128)(2,1)}, u32[]{:S(2)}, u32[]{:S(2)}) %collective-permute-start.12) | collective-permute-done | bytes 1179680 | tf_op jit(solution)/shard_map/ppermute | solution.py:763
  196.0 1.7 fusion.6
  197.8 1.6 collective-permute-start.13
  199.3 1.2 constant_dynamic-slice_fusion.1
  200.5 2.4 copy.55
  203.8 2.4 copy.58
  206.1 14.6 %collective-permute-done.1 = bf16[2,384,768]{1,2,0:T(8,128)(2,1)} collective-permute-done((bf16[2,384,768]{1,2,0:T(8,128)(2,1)}, bf16[2,384,768]{1,2,0:T(8,128)(2,1)}, u32[]{:S(2)}, u32[]{:S(2)}) %collective-permute-start.1) | collective-permute-done | bytes 1179680 | tf_op jit(solution)/shard_map/ppermute | solution.py:763
  220.7 1.9 fusion.8
  222.7 1.0 copy-done.2
  224.6 1.5 collective-permute-start.2
  226.1 2.0 fusion.16
  228.2 1.8 reshape.161
  230.9 4.2 %all-to-all-start.5 = ((bf16[4,96,768]{2,1,0:T(8,128)(2,1)}), bf16[4,96,768]{2,1,0:T(8,128)(2,1)S(1)}, u32[]{:S(2)}, u32[]{:S(2)}) async-start(bf16[4,96,768]{2,1,0:T(8,128)(2,1)} %copy.57), calls=%async_computation.5 | async-start | bytes 1179648 | tf_op jit(solution)/shard_map/all_to_all | solution.py:806
  235.2 1.4 copy.59
  236.6 2.8 collective-permute-done.9
  239.4 1.9 fusion.7
  241.4 8.7 %collective-permute-done.2 = bf16[384,768]{0,1:T(8,128)(2,1)} collective-permute-done((bf16[384,768]{0,1:T(8,128)(2,1)}, bf16[384,768]{0,1:T(8,128)(2,1)}, u32[]{:S(2)}, u32[]{:S(2)}) %collective-permute-start.2) | collective-permute-done | bytes 589856 | tf_op jit(solution)/shard_map/ppermute | solution.py:763
  250.1 2.0 fusion.18
  252.1 4.2 %all-to-all-start.3 = ((bf16[4,192,384]{2,1,0:T(8,128)(2,1)}), bf16[4,192,384]{2,1,0:T(8,128)(2,1)S(1)}, u32[]{:S(2)}, u32[]{:S(2)}) async-start(bf16[4,192,384]{2,1,0:T(8,128)(2,1)} %bitcast.22), calls=%async_computation.3 | async-start | bytes 1179648 | tf_op jit(solution)/shard_map/all_to_all | solution.py:806
  256.4 1.0 collective-permute-start.10
  257.4 1.2 collective-permute-start.4
  258.6 11.8 %collective-permute-done.4 = f32[72,128]{1,0:T(8,128)S(1)} collective-permute-done((f32[72,128]{1,0:T(8,128)S(1)}, f32[72,128]{1,0:T(8,128)S(1)}, u32[]{:S(2)}, u32[]{:S(2)}) %collective-permute-start.4) | collective-permute-done | bytes 36896 | tf_op jit(solution)/shard_map/ppermute | solution.py:763
  270.4 1.6 collective-permute-start.5
  271.9 2.5 collective-permute-done.5
  274.4 1.7 collective-permute-start.6
  276.1 2.2 collective-permute-done.6
  278.4 2.6 collective-permute-start.7
  281.0 2.0 cosine_pairs.1
  283.0 1.3 reduce
  284.4 2.0 fusion.17
  286.4 4.1 %all-to-all-start.4 = ((bf16[4,192,384]{2,1,0:T(8,128)(2,1)}), bf16[4,192,384]{2,1,0:T(8,128)(2,1)S(1)}, u32[]{:S(2)}, u32[]{:S(2)}) async-start(bf16[4,192,384]{2,1,0:T(8,128)(2,1)} %bitcast.131), calls=%async_computation.4 | async-start | bytes 1179648 | tf_op jit(solution)/shard_map/all_to_all | solution.py:806
  292.3 6.1 %home_rows.1 = bf16[8,128,768]{2,1,0:T(8,128)(2,1)} custom-call(s32[8]{0:T(128)} %dest_ref.3, bf16[8,128,768]{2,1,0:T(8,128)(2,1)} %copy-done.1), custom_call_target="tpu_custom_call" | custom-call | tf_op jit(solution)/shard_map/home_rows/pallas_call | solution.py:745
  300.1 1.4 all-to-all-done.4
  (113 shorter events, 17.1 us)
Async XLA Ops:
  11.2 5.1 %copy-start.18 = (f32[1536]{0:T(1024)S(1)}, f32[1536]{0:T(1024)}, u32[]{:S(2)}) copy-start(f32[1536]{0:T(1024)} %param.23) | copy-start | bytes 18436
  11.2 5.7 %copy-start.20 = (f32[768]{0:T(1024)S(1)}, f32[768]{0:T(1024)}, u32[]{:S(2)}) copy-start(f32[768]{0:T(1024)} %param.26) | copy-start | bytes 9220
  11.2 6.3 %copy-start.21 = (f32[768]{0:T(1024)S(1)}, f32[768]{0:T(1024)}, u32[]{:S(2)}) copy-start(f32[768]{0:T(1024)} %param.25) | copy-start | bytes 9220
  11.2 6.9 %copy-start.22 = (f32[768]{0:T(1024)S(1)}, f32[768]{0:T(1024)}, u32[]{:S(2)}) copy-start(f32[768]{0:T(1024)} %param.27) | copy-start | bytes 9220
  11.2 7.4 %copy-start.23 = (f32[768]{0:T(1024)S(1)}, f32[768]{0:T(1024)}, u32[]{:S(2)}) copy-start(f32[768]{0:T(1024)} %param.32) | copy-start | bytes 9220
  11.2 8.0 %copy-start.24 = (f32[768]{0:T(1024)S(1)}, f32[768]{0:T(1024)}, u32[]{:S(2)}) copy-start(f32[768]{0:T(1024)} %param.31) | copy-start | bytes 9220
  11.2 8.6 %copy-start.25 = (f32[768]{0:T(1024)S(1)}, f32[768]{0:T(1024)}, u32[]{:S(2)}) copy-start(f32[768]{0:T(1024)} %param.33) | copy-start | bytes 9220
  11.2 28.1 %all-to-all-start = ((bf16[8,144,768]{2,1,0:T(8,128)(2,1)}), bf16[8,144,768]{2,1,0:T(8,128)(2,1)S(1)}, u32[]{:S(2)}, u32[]{:S(2)}) async-start(bf16[8,144,768]{2,1,0:T(8,128)(2,1)} %build_send.1), calls=%async_computation | async-start | bytes 3538944 | tf_op jit(solution)/shard_map/all_to_all | solution.py:846
  39.3 1.2 copy-start
  69.1 11.7 %all-to-all-start.1 = ((bf16[8,32,768]{2,1,0:T(8,128)(2,1)}), bf16[8,32,768]{2,1,0:T(8,128)(2,1)S(1)}, u32[]{:S(2)}, u32[]{:S(2)}) async-start(bf16[8,32,768]{2,1,0:T(8,128)(2,1)} %broadcast_in_dim.14), calls=%async_computation.1 | async-start | bytes 786432 | tf_op jit(solution)/shard_map/all_to_all | solution.py:869
  80.8 0.7 copy-start.6
  91.6 63.3 %collective-permute-start.11 = (bf16[4,96,3072]{2,1,0:T(8,128)(2,1)}, bf16[4,96,3072]{2,1,0:T(8,128)(2,1)}, u32[]{:S(2)}, u32[]{:S(2)}) collective-permute-start(bf16[4,96,3072]{2,1,0:T(8,128)(2,1)} %convolution_convert_fusion), channel_id=1, source_target_pairs={{0,4},{4,0},{8,12},{12,8},{16,20},{20,16},{24,28},{28,24},{1,5},{5... | collective-permute-start | bytes 7077896 | tf_op jit(solution)/shard_map/ppermute | solution.py:763
  91.6 16.0 %copy-start.12 = (bf16[512,768]{1,0:T(8,128)(2,1)S(1)}, bf16[512,768]{1,0:T(8,128)(2,1)}, u32[]{:S(2)}) copy-start(bf16[512,768]{1,0:T(8,128)(2,1)} %get-tuple-element.49.low_ref) | copy-start | bytes 2359300
  111.9 54.7 %collective-permute-start.8 = (bf16[4,384,768]{2,1,0:T(8,128)(2,1)}, bf16[4,384,768]{2,1,0:T(8,128)(2,1)}, u32[]{:S(2)}, u32[]{:S(2)}) collective-permute-start(bf16[4,384,768]{2,1,0:T(8,128)(2,1)} %convolution_convert_fusion.1), channel_id=1, source_target_pairs={{0,4},{4,0},{8,12},{12,8},{16,20},{20,16},{24,28},{28,24},{1,5},{5... | collective-permute-start | bytes 7077896 | tf_op jit(solution)/shard_map/ppermute | solution.py:763
  112.4 23.7 %copy-start.7 = (bf16[512,768]{1,0:T(8,128)(2,1)S(1)}, bf16[512,768]{1,0:T(8,128)(2,1)}, u32[]{:S(2)}) copy-start(bf16[512,768]{1,0:T(8,128)(2,1)} %get-tuple-element.75) | copy-start | bytes 2359300
  112.4 23.7 %copy-start.10 = (bf16[768,512]{1,0:T(8,128)(2,1)S(1)}, bf16[768,512]{1,0:T(8,128)(2,1)}, u32[]{:S(2)}) copy-start(bf16[768,512]{1,0:T(8,128)(2,1)} %get-tuple-element.74) | copy-start | bytes 2359300
  112.4 24.2 %copy-start.11 = (bf16[512,768]{1,0:T(8,128)(2,1)S(1)}, bf16[512,768]{1,0:T(8,128)(2,1)}, u32[]{:S(2)}) copy-start(bf16[512,768]{1,0:T(8,128)(2,1)} %get-tuple-element.73) | copy-start | bytes 2359300
  139.0 1.6 copy-start.19
  140.5 20.9 %collective-permute-start = (bf16[4,384,768]{2,1,0:T(8,128)(2,1)}, bf16[4,384,768]{2,1,0:T(8,128)(2,1)}, u32[]{:S(2)}, u32[]{:S(2)}) collective-permute-start(bf16[4,384,768]{2,1,0:T(8,128)(2,1)} %pad_maximum_fusion), channel_id=1, source_target_pairs={{0,4},{4,0},{8,12},{12,8},{16,20},{20,16},{24,28},{28,24},{1,5},{5... | collective-permute-start | bytes 7077896 | tf_op jit(solution)/shard_map/ppermute | solution.py:763
  140.6 10.7 %copy-start.17 = (f32[1,3072]{1,0:T(1,128)S(1)}, f32[1,3072]{1,0:T(1,128)}, u32[]{:S(2)}) copy-start(f32[1,3072]{1,0:T(1,128)} %get-tuple-element.78) | copy-start | bytes 36868
  146.5 84.4 %all-to-all-start.2 = ((bf16[8,128,768]{2,1,0:T(8,128)(2,1)}), bf16[8,128,768]{2,1,0:T(8,128)(2,1)S(1)}, u32[]{:S(2)}, u32[]{:S(2)}) async-start(bf16[8,128,768]{2,1,0:T(8,128)(2,1)} %spread_rows.1), calls=%async_computation.2 | async-start | bytes 3145728 | tf_op jit(solution)/shard_map/all_to_all | solution.py:894
  151.3 3.6 %copy-start.15 = (f32[9216]{0:T(1024)}, f32[9216]{0:T(1024)S(1)}, u32[]{:S(2)}) copy-start(f32[9216]{0:T(1024)S(1)} %constant_dynamic-update-slice_fusion.3) | copy-start | bytes 110596
  152.2 2.8 copy-start.26
  152.2 2.8 copy-start.27
  158.1 3.4 %copy-start.8 = (bf16[4,96,3072]{2,1,0:T(8,128)(2,1)}, bf16[4,96,3072]{2,1,0:T(8,128)(2,1)S(1)}, u32[]{:S(2)}) copy-start(bf16[4,96,3072]{2,1,0:T(8,128)(2,1)S(1)} %add_convert_fusion) | copy-start | bytes 7077892
  159.3 36.8 %collective-permute-start.12 = (bf16[2,96,3072]{2,1,0:T(8,128)(2,1)}, bf16[2,96,3072]{2,1,0:T(8,128)(2,1)}, u32[]{:S(2)}, u32[]{:S(2)}) collective-permute-start(bf16[2,96,3072]{2,1,0:T(8,128)(2,1)} %dynamic-slice_bitcast_fusion), channel_id=1, source_target_pairs={{0,8},{4,12},{8,0},{12,4},{16,24},{20,28},{24,16},{28,20},{1,9},{5... | collective-permute-start | bytes 3538952 | tf_op jit(solution)/shard_map/ppermute | solution.py:763
  164.9 1.7 copy-start.13
  166.3 29.8 %copy-start.9 = (bf16[4,96,3072]{2,1,0:T(8,128)(2,1)S(1)}, bf16[4,96,3072]{2,1,0:T(8,128)(2,1)}, u32[]{:S(2)}) copy-start(bf16[4,96,3072]{2,1,0:T(8,128)(2,1)} %copy-done.8) | copy-start | bytes 7077892
  166.3 54.5 %collective-permute-start.1 = (bf16[2,384,768]{1,2,0:T(8,128)(2,1)}, bf16[2,384,768]{1,2,0:T(8,128)(2,1)}, u32[]{:S(2)}, u32[]{:S(2)}) collective-permute-start(bf16[2,384,768]{1,2,0:T(8,128)(2,1)} %bitcast.133), channel_id=1, source_target_pairs={{0,8},{4,12},{8,0},{12,4},{16,24},{20,28},{24,16},{28,20},{1,9},{5... | collective-permute-start | bytes 3538952 | tf_op jit(solution)/shard_map/ppermute | solution.py:763
  197.7 1.6 copy-start.4
  197.8 28.4 %collective-permute-start.13 = (bf16[96,3072]{1,0:T(8,128)(2,1)S(1)}, bf16[96,3072]{1,0:T(8,128)(2,1)}, u32[]{:S(2)}, u32[]{:S(2)}) collective-permute-start(bf16[96,3072]{1,0:T(8,128)(2,1)S(1)} %dynamic-slice_bitcast_fusion.1), channel_id=1, source_target_pairs={{0,16},{4,20},{8,24},{12,28},{16,0},{20,4},{24,8},{28,12},{1,17},{... | collective-permute-start | bytes 1769480 | tf_op jit(solution)/shard_map/ppermute | solution.py:763
  202.9 36.6 %collective-permute-start.9 = (bf16[2,384,768]{1,2,0:T(8,128)(2,1)}, bf16[2,384,768]{1,2,0:T(8,128)(2,1)}, u32[]{:S(2)}, u32[]{:S(2)}) collective-permute-start(bf16[2,384,768]{1,2,0:T(8,128)(2,1)} %bitcast.132), channel_id=1, source_target_pairs={{0,16},{4,20},{8,24},{12,28},{16,0},{20,4},{24,8},{28,12},{1,17},{... | collective-permute-start | bytes 3538952 | tf_op jit(solution)/shard_map/ppermute | solution.py:763
  206.1 20.0 %copy-start.5 = (bf16[2,96,3072]{2,1,0:T(8,128)(2,1)S(1)}, bf16[2,96,3072]{2,1,0:T(8,128)(2,1)}, u32[]{:S(2)}) copy-start(bf16[2,96,3072]{2,1,0:T(8,128)(2,1)} %copy-done.4) | copy-start | bytes 3538948
  222.7 1.0 copy-start.2
  224.6 10.5 %copy-start.16 = (f32[9216]{0:T(1024)S(1)}, f32[9216]{0:T(1024)}, u32[]{:S(2)}) copy-start(f32[9216]{0:T(1024)} %copy-done.15) | copy-start | bytes 110596
  224.6 25.4 %collective-permute-start.2 = (bf16[384,768]{0,1:T(8,128)(2,1)}, bf16[384,768]{0,1:T(8,128)(2,1)}, u32[]{:S(2)}, u32[]{:S(2)}) collective-permute-start(bf16[384,768]{0,1:T(8,128)(2,1)} %dynamic-slice_bitcast_fusion.3), channel_id=1, source_target_pairs={{0,16},{4,20},{8,24},{12,28},{16,0},{20,4},{24,8},{28,12},{1,17},{... | collective-permute-start | bytes 1769480 | tf_op jit(solution)/shard_map/ppermute | solution.py:763
  230.9 10.5 %copy-start.1 = (bf16[8,128,768]{2,1,0:T(8,128)(2,1)}, bf16[8,128,768]{2,1,0:T(8,128)(2,1)S(1)}, u32[]{:S(2)}) copy-start(bf16[8,128,768]{2,1,0:T(8,128)(2,1)S(1)} %all-to-all-done.2.rows_ref) | copy-start | bytes 4718596
  230.9 21.3 %all-to-all-start.5 = ((bf16[4,96,768]{2,1,0:T(8,128)(2,1)}), bf16[4,96,768]{2,1,0:T(8,128)(2,1)S(1)}, u32[]{:S(2)}, u32[]{:S(2)}) async-start(bf16[4,96,768]{2,1,0:T(8,128)(2,1)} %copy.57), calls=%async_computation.5 | async-start | bytes 1179648 | tf_op jit(solution)/shard_map/all_to_all | solution.py:806
  235.1 22.3 %collective-permute-start.3 = (f32[72,128]{1,0:T(8,128)S(1)}, f32[72,128]{1,0:T(8,128)S(1)}, u32[]{:S(2)}, u32[]{:S(2)}) collective-permute-start(f32[72,128]{1,0:T(8,128)S(1)} %bitcast.141), channel_id=1, source_target_pairs={{0,4},{4,0},{8,12},{12,8},{16,20},{20,16},{24,28},{28,24},{1,5},{5... | collective-permute-start | bytes 110600 | tf_op jit(solution)/shard_map/ppermute | solution.py:763
  236.6 13.5 %copy-start.3 = (bf16[2,384,768]{1,2,0:T(8,128)(2,1)S(1)}, bf16[2,384,768]{1,2,0:T(8,128)(2,1)}, u32[]{:S(2)}) copy-start(bf16[2,384,768]{1,2,0:T(8,128)(2,1)} %copy-done.2) | copy-start | bytes 3538948
  252.1 34.3 %all-to-all-start.3 = ((bf16[4,192,384]{2,1,0:T(8,128)(2,1)}), bf16[4,192,384]{2,1,0:T(8,128)(2,1)S(1)}, u32[]{:S(2)}, u32[]{:S(2)}) async-start(bf16[4,192,384]{2,1,0:T(8,128)(2,1)} %bitcast.22), calls=%async_computation.3 | async-start | bytes 1179648 | tf_op jit(solution)/shard_map/all_to_all | solution.py:806
  256.4 27.9 %collective-permute-start.10 = (bf16[384,768]{0,1:T(8,128)(2,1)S(1)}, bf16[384,768]{0,1:T(8,128)(2,1)}, u32[]{:S(2)}, u32[]{:S(2)}) collective-permute-start(bf16[384,768]{0,1:T(8,128)(2,1)S(1)} %dynamic-slice_bitcast_fusion.2), channel_id=1, source_target_pairs={{0,8},{4,12},{8,0},{12,4},{16,24},{20,28},{24,16},{28,20},{1,9},{5... | collective-permute-start | bytes 1769480 | tf_op jit(solution)/shard_map/ppermute | solution.py:763
  257.4 13.0 %collective-permute-start.4 = (f32[72,128]{1,0:T(8,128)S(1)}, f32[72,128]{1,0:T(8,128)S(1)}, u32[]{:S(2)}, u32[]{:S(2)}) collective-permute-start(f32[72,128]{1,0:T(8,128)S(1)} %bitcast_add_fusion), channel_id=1, source_target_pairs={{0,8},{4,12},{8,0},{12,4},{16,24},{20,28},{24,16},{28,20},{1,9},{5... | collective-permute-start | bytes 110600 | tf_op jit(solution)/shard_map/ppermute | solution.py:763
  270.4 4.0 %collective-permute-start.5 = (f32[72,128]{1,0:T(8,128)S(1)}, f32[72,128]{1,0:T(8,128)S(1)}, u32[]{:S(2)}, u32[]{:S(2)}) collective-permute-start(f32[72,128]{1,0:T(8,128)S(1)} %fusion.48), channel_id=1, source_target_pairs={{0,16},{4,20},{8,24},{12,28},{16,0},{20,4},{24,8},{28,12},{1,17},{... | collective-permute-start | bytes 110600 | tf_op jit(solution)/shard_map/ppermute | solution.py:763
  274.4 4.0 %collective-permute-start.6 = (f32[72,128]{1,0:T(8,128)S(1)}, f32[72,128]{1,0:T(8,128)S(1)}, u32[]{:S(2)}, u32[]{:S(2)}) collective-permute-start(f32[72,128]{1,0:T(8,128)S(1)} %add.96), channel_id=1, source_target_pairs={{0,1},{1,0},{2,3},{3,2},{4,5},{5,4},{6,7},{7,6},{8,9},{9,8},{10,11... | collective-permute-start | bytes 110600 | tf_op jit(solution)/shard_map/ppermute | solution.py:763
  278.4 6.0 %collective-permute-start.7 = (f32[72,128]{1,0:T(8,128)S(1)}, f32[72,128]{1,0:T(8,128)S(1)}, u32[]{:S(2)}, u32[]{:S(2)}) collective-permute-start(f32[72,128]{1,0:T(8,128)S(1)} %add.97), channel_id=1, source_target_pairs={{0,2},{1,3},{2,0},{3,1},{4,6},{5,7},{6,4},{7,5},{8,10},{9,11},{10,... | collective-permute-start | bytes 110600 | tf_op jit(solution)/shard_map/ppermute | solution.py:763
  286.4 15.1 %all-to-all-start.4 = ((bf16[4,192,384]{2,1,0:T(8,128)(2,1)}), bf16[4,192,384]{2,1,0:T(8,128)(2,1)S(1)}, u32[]{:S(2)}, u32[]{:S(2)}) async-start(bf16[4,192,384]{2,1,0:T(8,128)(2,1)} %bitcast.131), calls=%async_computation.4 | async-start | bytes 1179648 | tf_op jit(solution)/shard_map/all_to_all | solution.py:806
  298.5 3.8 %copy-start.14 = (f32[192,384]{1,0:T(8,128)}, f32[192,384]{1,0:T(8,128)S(1)}, u32[]{:S(2)}) copy-start(f32[192,384]{1,0:T(8,128)S(1)} %convert_reduce_fusion.2) | copy-start | bytes 884740

commit v2 on v1

--- a/solution.py
+++ b/solution.py
@@ -17,7 +17,12 @@
 COS_EPS = 1e-06
 F32 = jnp.float32
 BF16 = jnp.bfloat16
-VMEM_LIMIT = 60 * 1024 * 1024
+VMEM_LIMIT = 24 * 1024 * 1024
+
+
+def cost(micros):
+    return pl.CostEstimate(flops=0, bytes_accessed=int(micros * 3.0e6), transcendentals=0)
+
 
 NT = (((1,), (1,)), ((), ()))
 TN = (((0,), (0,)), ((), ()))
@@ -56,75 +61,70 @@
     return jnp.mean(values, axis=-1, keepdims=True)
 
 
-def prep_kernel(dest_ref, tok_ref, seg_ref, dest64_ref, pair_ref, targ_ref, out_ref):
-    owner = pl.program_id(0)
+def prep_kernel(dest_ref, pair_ref, targ_ref, tok_ref, seg_ref, out_ref, sems):
     slot_dev = dest_ref.shape[0]
-    filled = dest_ref[0] == owner
-    for slot in range(1, slot_dev):
-        filled = filled | (dest_ref[slot] == owner)
+    wide_count, _, width = out_ref.shape
     row_len = tok_ref.shape[1]
-    out_ref[0, :row_len, :] = tok_ref[0]
-    slots = dest64_ref.shape[1]
-    lane = lax.broadcasted_iota(jnp.int32, (pair_ref.shape[0], slots), 1)
-    first = pair_ref[:, 0:1]
-    second = pair_ref[:, 1:2]
-    at_first = (lane == first).astype(F32)
-    at_second = (lane == second).astype(F32)
-    partner = column_sum(at_first * second.astype(F32) + at_second * first.astype(F32))
-    target = column_sum((at_first + at_second) * targ_ref[...])
+    sources = []
+    lives = []
+    copies = []
+    for owner in range(wide_count):
+        found = jnp.int32(0)
+        live = dest_ref[0] == owner
+        for slot in range(1, slot_dev):
+            match = dest_ref[slot] == owner
+            found = jnp.where(match, slot, found)
+            live = live | match
+        sources.append(found)
+        lives.append(live)
+        copy = pltpu.make_async_copy(
+            tok_ref.at[found], out_ref.at[owner, pl.ds(0, row_len), :], sems.at[owner]
+        )
+        copy.start()
+        copies.append(copy)
+    lane = lax.broadcasted_iota(jnp.int32, (1, LANES), 1)
+    dest = jnp.full((1, LANES), -1, jnp.int32)
+    for slot in range(slot_dev):
+        dest = jnp.where(lane // SEG_ROW == slot, dest_ref[slot], dest)
+    partner = jnp.zeros((1, LANES), jnp.int32)
+    target = jnp.zeros((1, LANES), F32)
+    for pair in range(pair_ref.shape[1]):
+        first = pair_ref[0, pair]
+        second = pair_ref[1, pair]
+        at_first = lane == first
+        at_second = lane == second
+        partner = jnp.where(at_first, second, jnp.where(at_second, first, partner))
+        target = jnp.where(at_first | at_second, targ_ref[0, pair], target)
     high, middle, low = split_three(target)
-    labels = seg_ref[0].astype(F32)
-    labels = jnp.where(filled, labels, -1.0)
-    rows = [
-        labels,
-        jnp.pad(dest64_ref[...].astype(F32), ((0, 0), (0, LANES - slots))),
-        jnp.pad(partner, ((0, 0), (0, LANES - slots))),
-        jnp.pad(high.astype(F32), ((0, 0), (0, LANES - slots))),
-        jnp.pad(middle.astype(F32), ((0, 0), (0, LANES - slots))),
-        jnp.pad(low.astype(F32), ((0, 0), (0, LANES - slots))),
-    ]
-    rows.append(jnp.zeros((META_ROWS - len(rows), LANES), F32))
-    out_ref[0, row_len:, :LANES] = jnp.concatenate(rows, axis=0).astype(BF16)
-    out_ref[0, row_len:, LANES:] = jnp.zeros((META_ROWS, out_ref.shape[2] - LANES), BF16)
+    fixed = [dest.astype(F32), partner.astype(F32)]
+    fixed += [high.astype(F32), middle.astype(F32), low.astype(F32)]
+    fixed.append(jnp.zeros((META_ROWS - 1 - len(fixed), LANES), F32))
+    for owner in range(wide_count):
+        labels = seg_ref[pl.ds(sources[owner], 1), :].astype(F32)
+        labels = jnp.where(lives[owner], labels, -1.0)
+        table = jnp.concatenate([labels] + fixed, axis=0)
+        out_ref[owner, row_len:, :LANES] = table.astype(BF16)
+        out_ref[owner, row_len:, LANES:] = jnp.zeros((META_ROWS, width - LANES), BF16)
+    for copy in copies:
+        copy.wait()
+
+
+def smem_spec():
+    return pl.BlockSpec(memory_space=pltpu.SMEM)
 
 
 def build_send(tokens, segments, destination, pair_index, targets, wide_count):
     slot_dev, row_len, width = tokens.shape
-
-    def source(owner, dest_ref):
-        found = jnp.int32(0)
-        for slot in range(slot_dev):
-            found = jnp.where(dest_ref[slot] == owner, slot, found)
-        return found
-
-    whole = lambda owner, dest_ref: (0, 0)
-    slots = slot_dev * SEG_ROW
-    pairs = pair_index.shape[0]
     return pl.pallas_call(
         prep_kernel,
         out_shape=jax.ShapeDtypeStruct((wide_count, row_len + META_ROWS, width), BF16),
-        grid_spec=pltpu.PrefetchScalarGridSpec(
-            num_scalar_prefetch=1,
-            grid=(wide_count,),
-            in_specs=[
-                pl.BlockSpec((1, row_len, width), lambda o, d: (source(o, d), 0, 0)),
-                pl.BlockSpec((1, 1, row_len), lambda o, d: (source(o, d), 0, 0)),
-                pl.BlockSpec((1, slots), whole),
-                pl.BlockSpec((pairs, 2), whole),
-                pl.BlockSpec((pairs, 1), whole),
-            ],
-            out_specs=pl.BlockSpec((1, row_len + META_ROWS, width), lambda o, d: (o, 0, 0)),
-        ),
-        compiler_params=params(1),
+        in_specs=[smem_spec()] * 3 + [pl.BlockSpec(memory_space=pl.ANY), vmem_spec()],
+        out_specs=vmem_spec(),
+        scratch_shapes=[pltpu.SemaphoreType.DMA((wide_count,))],
+        cost_estimate=cost(3),
+        compiler_params=params(),
         name="build_send",
-    )(
-        destination,
-        tokens,
-        segments.reshape(slot_dev, 1, row_len),
-        jnp.repeat(destination, SEG_ROW).reshape(1, slots),
-        pair_index,
-        targets.reshape(pairs, 1),
-    )
+    )(destination, pair_index.T, targets.reshape(1, -1), tokens, segments)
 
 
 def attend_kernel(
@@ -135,19 +135,20 @@
     bo_ref,
     gain_ref,
     shift_ref,
-    x_ref,
+    stack_ref,
     proj_ref,
     probs_ref,
-    ctx_ref,
     hid_ref,
-    low_ref,
     norm_ref,
     rstd_ref,
     lab_ref,
     labcol_ref,
+    meta_ref,
+    source_ref,
 ):
+    x_ref, ctx_ref, low_ref = stack_ref.at[0], stack_ref.at[1], stack_ref.at[2]
     wide_count = got_ref.shape[0]
-    tok_count, width = x_ref.shape
+    tok_count, width = hid_ref.shape
     row_len = got_ref.shape[1] - META_ROWS
     kept_rows = tok_count // row_len
     seen = jnp.int32(0)
@@ -158,7 +159,9 @@
         for row in range(kept_rows):
             sources[row] = jnp.where(live & (seen == row), slot, sources[row])
         seen = seen + live.astype(jnp.int32)
+    meta_ref[...] = got_ref[:, row_len:, :LANES]
     for row in range(kept_rows):
+        source_ref[row] = sources[row]
         span = pl.ds(row * row_len, row_len)
         x_ref[span, :] = got_ref[sources[row], :row_len, :]
         tag = got_ref[sources[row], row_len : row_len + 1, :LANES].astype(F32)
@@ -215,22 +218,23 @@
     row_len = slot_len - META_ROWS
     tok_count = kept_rows * row_len
     shapes = (
-        ((tok_count, width), BF16),
+        ((3, tok_count, width), BF16),
         ((tok_count, 3 * width), BF16),
         ((kept_rows, width // LANES, 2 * row_len, row_len), BF16),
-        ((tok_count, width), BF16),
         ((tok_count, width), F32),
-        ((tok_count, width), BF16),
         ((tok_count, width), F32),
         ((tok_count, 1), F32),
         ((8, LANES), F32),
         ((tok_count, LANES), F32),
+        ((wide_count, META_ROWS, LANES), BF16),
+        ((kept_rows,), jnp.int32),
     )
     return pl.pallas_call(
         attend_kernel,
         out_shape=[jax.ShapeDtypeStruct(*item) for item in shapes],
         in_specs=[vmem_spec()] * 7,
-        out_specs=[vmem_spec()] * len(shapes),
+        out_specs=[vmem_spec()] * (len(shapes) - 1) + [smem_spec()],
+        cost_estimate=cost(8),
         compiler_params=params(),
         name="attend_forward",
     )(got, w_qkv, bias, w_o, b_o, gain, shift)
@@ -252,6 +256,7 @@
     norm_ref,
     rstd_ref,
     pooled_ref,
+    copies_ref,
     total_ref,
 ):
     step = pl.program_id(0)
@@ -292,10 +297,12 @@
             mask = onehot.astype(BF16)
             summed = dot(mask, high) + dot(mask, middle) + dot(mask, low)
             pooled_ref[row * SEG_ROW : (row + 1) * SEG_ROW, :] = (summed / count).astype(BF16)
-
-
-def feed_forward(low, hidden, w_in, b_in, w_out, b_out, gain, shift, labels):
-    tok_count, width = low.shape
+        for owner in range(copies_ref.shape[0]):
+            copies_ref[owner] = pooled_ref[...]
+
+
+def feed_forward(stack, hidden, w_in, b_in, w_out, b_out, gain, shift, labels, wide_count):
+    _, tok_count, width = stack.shape
     units = w_in.shape[1]
     tile = 512
     kept_rows = tok_count // LANES
@@ -307,6 +314,7 @@
         ((tok_count, width), F32),
         ((tok_count, 1), F32),
         ((kept_rows * SEG_ROW, width), BF16),
+        ((wide_count, kept_rows * SEG_ROW, width), BF16),
     )
     return pl.pallas_call(
         feed_kernel,
@@ -315,7 +323,7 @@
             num_scalar_prefetch=0,
             grid=(units // tile,),
             in_specs=[
-                pl.BlockSpec((tok_count, width), whole),
+                pl.BlockSpec((pl.Squeezed(), tok_count, width), lambda step: (2, 0, 0)),
                 pl.BlockSpec((tok_count, width), whole),
                 pl.BlockSpec((width, tile), lambda step: (0, step)),
                 pl.BlockSpec((1, tile), lambda step: (0, step)),
@@ -332,15 +340,17 @@
                 pl.BlockSpec((tok_count, width), whole),
                 pl.BlockSpec((tok_count, 1), whole),
                 pl.BlockSpec((kept_rows * SEG_ROW, width), whole),
+                pl.BlockSpec((wide_count, kept_rows * SEG_ROW, width), lambda step: (0, 0, 0)),
             ],
             scratch_shapes=[pltpu.VMEM((tok_count, width), F32)],
         ),
+        cost_estimate=cost(10),
         compiler_params=params(1),
         name="feed_forward",
-    )(low, hidden, w_in, b_in, w_out, b_out, gain, shift, labels)
-
-
-def route_kernel(me_ref, meta_ref, pair_ref, place_ref, targ_ref, first_ref, second_ref, back_ref):
+    )(stack, hidden, w_in, b_in, w_out, b_out, gain, shift, labels)
+
+
+def route_kernel(me_ref, meta_ref, pair_ref, place_ref, targ_ref, first_ref, second_ref):
     wide_count = meta_ref.shape[0]
     me = me_ref[0]
     kept_rows = place_ref.shape[0] // SEG_ROW
@@ -374,9 +384,6 @@
     place = jnp.where(dest >= 0.0, dest * per_owner + rank * float(SEG_ROW) + segment, -1.0)
     live = (labels[:, 0:1] >= 0.0).astype(F32)
     my_rank = dot(below, jnp.broadcast_to(live, (wide_count, LANES)).astype(BF16))
-    back = jnp.clip(my_rank, 0.0, float(kept_rows - 1))
-    diagonal = lax.broadcasted_iota(jnp.int32, (wide_count, LANES), 0) == lane
-    back_ref[...] = column_sum(jnp.where(diagonal, back, 0.0)).astype(jnp.int32)
     seg_lane = lax.broadcasted_iota(jnp.int32, (SEG_ROW, LANES), 1)
     seg_id = lax.broadcasted_iota(jnp.int32, (SEG_ROW, LANES), 0)
     for row in range(kept_rows):
@@ -406,13 +413,13 @@
         ((own, 1), F32),
         ((pairs, 1), F32),
         ((pairs, 1), F32),
-        ((1, LANES), jnp.int32),
     )
     return pl.pallas_call(
         route_kernel,
         out_shape=[jax.ShapeDtypeStruct(*item) for item in shapes],
-        in_specs=[pl.BlockSpec(memory_space=pltpu.SMEM), vmem_spec(), vmem_spec()],
+        in_specs=[smem_spec(), vmem_spec(), vmem_spec()],
         out_specs=[vmem_spec()] * len(shapes),
+        cost_estimate=cost(1),
         compiler_params=params(),
         name="route",
     )(me, meta, pair_index)
@@ -444,6 +451,7 @@
         out_shape=jax.ShapeDtypeStruct(first.shape, F32),
         in_specs=[vmem_spec()] * 3,
         out_specs=vmem_spec(),
+        cost_estimate=cost(1),
         compiler_params=params(),
         name="cosine_pairs",
     )(first, second, pooled_all)
@@ -520,6 +528,7 @@
         out_shape=[jax.ShapeDtypeStruct(*item) for item in shapes],
         in_specs=[vmem_spec()] * 9,
         out_specs=[vmem_spec()] * len(shapes),
+        cost_estimate=cost(3),
         compiler_params=params(),
         name="loss_back",
     )(own, pooled_all, place, target, labels, label_cols, normed, rstd, gain)
@@ -622,16 +631,29 @@
             ],
             scratch_shapes=[pltpu.VMEM((tok_count, width), F32)],
         ),
+        cost_estimate=cost(10),
         compiler_params=params(1),
         name="feed_back",
     )(d_ffn, d_res, w_out, w_in, slope, normed, rstd, gain, w_o)
 
 
 def attend_back_kernel(
-    proj_ref, probs_ref, dctx_ref, done_ref, wqkv_ref, dproj_t_ref, dtok_ref, sums_ref, dproj_ref
+    source_ref,
+    proj_ref,
+    probs_ref,
+    dctx_ref,
+    done_ref,
+    wqkv_ref,
+    dattn_t_ref,
+    dmix_t_ref,
+    dtok_ref,
+    sums_ref,
+    dproj_ref,
 ):
     row = pl.program_id(0)
     row_len, width = dctx_ref.shape
+    blocks = dmix_t_ref.shape[0]
+    main = 3 * width // blocks
     scale = 1.0 / math.sqrt(HEAD_DIM)
     lane = lax.broadcasted_iota(jnp.int32, (row_len, LANES), 1)
     left = (lane < HEAD_DIM).astype(BF16)
@@ -659,7 +681,15 @@
             low = grad.astype(BF16)
             place = part * width + col
             dproj_ref[:, place : place + LANES] = low
-            dproj_t_ref[place : place + LANES, :] = low.T
+            turned = low.T
+            start = place
+            while start < place + LANES:
+                block, offset = divmod(start, main)
+                stop = min(place + LANES, (block + 1) * main)
+                dmix_t_ref[block, offset : offset + stop - start, :] = turned[
+                    start - place : stop - place, :
+                ]
+                start = stop
             summed = column_sum(low.astype(F32))
 
             @pl.when(row == 0)
@@ -670,92 +700,221 @@
             def _():
                 sums_ref[:, place : place + LANES] += summed
 
+    rest = width // blocks
+    for block in range(blocks):
+        dmix_t_ref[block, main:, :] = dattn_t_ref[block * rest : (block + 1) * rest, :]
     grad = done_ref[...] + dot(dproj_ref[...], wqkv_ref[...], NT)
-    dtok_ref[...] = grad.astype(BF16)
-
-
-def attend_back(proj, probs, d_ctx, d_one, w_qkv):
+    dtok_ref[0] = grad.astype(BF16)
+
+
+def attend_back(sources, proj, probs, d_ctx, d_one, w_qkv, d_attn_t, blocks, wide_count):
     tok_count, width = d_ctx.shape
     kept_rows = tok_count // LANES
     shapes = (
-        ((3 * width, tok_count), BF16),
-        ((tok_count, width), BF16),
+        ((blocks, 4 * width // blocks, tok_count), BF16),
+        ((wide_count, LANES, width), BF16),
         ((1, 3 * width), F32),
     )
     return pl.pallas_call(
         attend_back_kernel,
         out_shape=[jax.ShapeDtypeStruct(*item) for item in shapes],
         grid_spec=pltpu.PrefetchScalarGridSpec(
-            num_scalar_prefetch=0,
+            num_scalar_prefetch=1,
             grid=(kept_rows,),
             in_specs=[
-                pl.BlockSpec((LANES, 3 * width), lambda row: (row, 0)),
-                pl.BlockSpec((1,) + probs.shape[1:], lambda row: (row, 0, 0, 0)),
-                pl.BlockSpec((LANES, width), lambda row: (row, 0)),
-                pl.BlockSpec((LANES, width), lambda row: (row, 0)),
-                pl.BlockSpec((width, 3 * width), lambda row: (0, 0)),
+                pl.BlockSpec((LANES, 3 * width), lambda row, src: (row, 0)),
+                pl.BlockSpec((1,) + probs.shape[1:], lambda row, src: (row, 0, 0, 0)),
+                pl.BlockSpec((LANES, width), lambda row, src: (row, 0)),
+                pl.BlockSpec((LANES, width), lambda row, src: (row, 0)),
+                pl.BlockSpec((width, 3 * width), lambda row, src: (0, 0)),
+                pl.BlockSpec((width, LANES), lambda row, src: (0, row)),
             ],
             out_specs=[
-                pl.BlockSpec((3 * width, LANES), lambda row: (0, row)),
-                pl.BlockSpec((LANES, width), lambda row: (row, 0)),
-                pl.BlockSpec((1, 3 * width), lambda row: (0, 0)),
+                pl.BlockSpec((blocks, 4 * width // blocks, LANES), lambda row, src: (0, 0, row)),
+                pl.BlockSpec((1, LANES, width), lambda row, src: (src[row], 0, 0)),
+                pl.BlockSpec((1, 3 * width), lambda row, src: (0, 0)),
             ],
             scratch_shapes=[pltpu.VMEM((LANES, 3 * width), BF16)],
         ),
+        cost_estimate=cost(20),
         compiler_params=params(1),
         name="attend_back",
-    )(proj, probs, d_ctx, d_one, w_qkv)
-
-
-def spread_kernel(index_ref, rows_ref, out_ref):
-    out_ref[...] = rows_ref[...]
-
-
-def spread_rows(index, rows, count):
-    block = (1,) + rows.shape[1:]
-    return pl.pallas_call(
-        spread_kernel,
-        out_shape=jax.ShapeDtypeStruct((count,) + rows.shape[1:], rows.dtype),
-        grid_spec=pltpu.PrefetchScalarGridSpec(
-            num_scalar_prefetch=1,
-            grid=(count,),
-            in_specs=[pl.BlockSpec(block, lambda slot, idx: (idx[slot], 0, 0))],
-            out_specs=pl.BlockSpec(block, lambda slot, idx: (slot, 0, 0)),
-        ),
-        compiler_params=params(1),
-        name="spread_rows",
-    )(index, rows)
-
-
-def home_kernel(dest_ref, rows_ref, out_ref):
-    live = dest_ref[pl.program_id(0)] >= 0
-
-    @pl.when(live)
-    def _():
-        out_ref[...] = rows_ref[...]
-
-    @pl.when(jnp.logical_not(live))
-    def _():
-        out_ref[...] = jnp.zeros_like(out_ref)
+    )(sources, proj, probs, d_ctx, d_one, w_qkv, d_attn_t)
+
+
+def home_kernel(dest_ref, rows_ref, out_ref, sems):
+    slot_dev = out_ref.shape[0]
+
+    def copy(slot):
+        return pltpu.make_async_copy(
+            rows_ref.at[jnp.maximum(dest_ref[slot], 0)], out_ref.at[slot], sems.at[slot]
+        )
+
+    for slot in range(slot_dev):
+        copy(slot).start()
+    for slot in range(slot_dev):
+        copy(slot).wait()
+
+        @pl.when(dest_ref[slot] < 0)
+        def _():
+            out_ref[slot] = jnp.zeros(out_ref.shape[1:], out_ref.dtype)
 
 
 def home_rows(destination, rows):
-    block = (1,) + rows.shape[1:]
     count = destination.shape[0]
     return pl.pallas_call(
         home_kernel,
         out_shape=jax.ShapeDtypeStruct((count,) + rows.shape[1:], rows.dtype),
-        grid_spec=pltpu.PrefetchScalarGridSpec(
-            num_scalar_prefetch=1,
-            grid=(count,),
-            in_specs=[
-                pl.BlockSpec(block, lambda slot, dest: (jnp.maximum(dest[slot], 0), 0, 0))
-            ],
-            out_specs=pl.BlockSpec(block, lambda slot, dest: (slot, 0, 0)),
-        ),
-        compiler_params=params(1),
+        in_specs=[smem_spec(), pl.BlockSpec(memory_space=pl.ANY)],
+        out_specs=vmem_spec(),
+        scratch_shapes=[pltpu.SemaphoreType.DMA((count,))],
+        cost_estimate=cost(3),
+        compiler_params=params(),
         name="home_rows",
     )(destination, rows)
+
+
+def block_at(index, bit, value):
+    low = index & ((1 << bit) - 1)
+    return ((index >> bit) << (bit + 1)) | (value << bit) | low
+
+
+def grad_kernel(first_bit, second_bit, spans, blocks, me_ref, own_ref, *refs):
+    recv_refs, refs = refs[:blocks], refs[blocks:]
+    step = pl.program_id(0)
+    half_steps = pl.num_programs(0) // 2
+    terms = len(spans)
+    own_xs, recv_xs = refs[:terms], refs[terms : 2 * terms]
+    outs = refs[2 * terms : 2 * terms + 4]
+    own_lefts = refs[2 * terms + 4 : 3 * terms + 4]
+    recv_lefts = refs[3 * terms + 4 :]
+    me = me_ref[0]
+    for half, bit in ((0, first_bit), (1, second_bit)):
+
+        @pl.when(step == half * half_steps)
+        def _():
+            side = (me >> bit) & 1
+            for block in range(blocks):
+                low = block & ((1 << (bit - 1)) - 1)
+                rest = ((block >> bit) << (bit - 1)) | low
+                kept = ((block >> (bit - 1)) & 1) == side
+                index = jnp.where(kept, rest, rest + blocks // 2)
+                for (start, stop), own_left, recv_left in zip(spans, own_lefts, recv_lefts):
+                    own_left[index] = own_ref[2 * block + (me & 1), start:stop, :]
+                    recv_left[index] = recv_refs[block][start:stop, :]
+
+    for term, (start, stop) in enumerate(spans):
+        rows = stop - start
+        chunk = blocks if blocks * rows <= 384 else blocks // 2
+        for base in range(0, blocks, chunk):
+            span = slice(base, base + chunk)
+            flat = lambda left: left[span].reshape(chunk * rows, left.shape[2])
+            part = dot(flat(own_lefts[term]), own_xs[term][...])
+            part = part + dot(flat(recv_lefts[term]), recv_xs[term][...])
+            part = part.astype(BF16).reshape(chunk, rows, part.shape[1])
+            for index in range(chunk):
+                block = base + index
+                role, place = divmod(block, blocks // 2)
+                for half in range(2):
+
+                    @pl.when((step < half_steps) == (half == 0))
+                    def _():
+                        outs[2 * half + role][place, start:stop, :] = part[index]
+
+
+def grad_terms(me, own, received, own_xs, recv_xs, spans, first_bit, second_bit, tile):
+    blocks = len(received)
+    rows, tok_count = received[0].shape
+    columns = own_xs[0][0].shape[-1]
+    steps = columns // tile
+    half = steps // 2
+
+    def x_spec(item):
+        array, lead = item
+        if lead is None:
+            return pl.BlockSpec((tok_count, tile), lambda step: (0, step))
+        return pl.BlockSpec((pl.Squeezed(), tok_count, tile), lambda step: (lead, 0, step))
+
+    out_block = (blocks // 2, rows, tile)
+    first_spec = pl.BlockSpec(out_block, lambda step: (0, 0, jnp.minimum(step, half - 1)))
+    second_spec = pl.BlockSpec(out_block, lambda step: (0, 0, jnp.maximum(step - half, 0)))
+    shape = jax.ShapeDtypeStruct((blocks // 2, rows, columns // 2), BF16)
+    whole = lambda step: (0, 0, 0)
+    lefts = [pltpu.VMEM((blocks, stop - start, tok_count), BF16) for start, stop in spans]
+    return pl.pallas_call(
+        functools.partial(grad_kernel, first_bit, second_bit, spans, blocks),
+        out_shape=[shape] * 4,
+        grid_spec=pltpu.PrefetchScalarGridSpec(
+            num_scalar_prefetch=0,
+            grid=(steps,),
+            in_specs=[
+                smem_spec(),
+                pl.BlockSpec(own.shape, whole),
+            ]
+            + [pl.BlockSpec((rows, tok_count), lambda step: (0, 0))] * blocks
+            + [x_spec(item) for item in own_xs + recv_xs],
+            out_specs=[first_spec, first_spec, second_spec, second_spec],
+            scratch_shapes=lefts + lefts,
+        ),
+        cost_estimate=cost(7),
+        compiler_params=params(1),
+        name="grad_terms",
+    )(me, own, *received, *[item[0] for item in own_xs + recv_xs])
+
+
+def fold_kernel(bits, places, me_ref, *refs):
+    me = me_ref[0]
+    for half in range(2):
+        kept_ref, recv_ref = refs[2 * half], refs[2 * half + 1]
+        keep_out, send_out = refs[4 + 2 * half], refs[5 + 2 * half]
+        side = (me >> bits[half]) & 1
+        for index in range(keep_out.shape[0]):
+            for value, out_ref in ((1 - side, send_out), (side, keep_out)):
+                block = block_at(index, places[half], value)
+                out_ref[index] = add_low(kept_ref[block], recv_ref[block])
+
+
+def fold(me, halves, bits, places):
+    shapes = []
+    for kept, _ in halves:
+        shapes += [jax.ShapeDtypeStruct((kept.shape[0] // 2,) + kept.shape[1:], BF16)] * 2
+    return pl.pallas_call(
+        functools.partial(fold_kernel, bits, places),
+        out_shape=shapes,
+        in_specs=[smem_spec()] + [vmem_spec()] * 4,
+        out_specs=[vmem_spec()] * 4,
+        cost_estimate=cost(0.5),
+        compiler_params=params(),
+        name="fold",
+    )(me, *halves[0], *halves[1])
+
+
+def piece_kernel(turned, *refs):
+    out_ref = refs[4]
+    count = out_ref.shape[0]
+    depth = out_ref.shape[1] if turned else out_ref.shape[2]
+    for half in range(2):
+        total = add_low(refs[2 * half][0], refs[2 * half + 1][0])
+        if turned:
+            total = total.T
+        for index in range(count // 2):
+            span = slice(index * depth, (index + 1) * depth)
+            out_ref[half * (count // 2) + index] = total[span, :] if turned else total[:, span]
+
+
+def narrow_pieces(halves, narrow_count, turned):
+    _, rows, columns = halves[0][0].shape
+    depth = 2 * columns // narrow_count
+    shape = (narrow_count,) + ((depth, rows) if turned else (rows, depth))
+    return pl.pallas_call(
+        functools.partial(piece_kernel, turned),
+        out_shape=jax.ShapeDtypeStruct(shape, BF16),
+        in_specs=[vmem_spec()] * 4,
+        out_specs=vmem_spec(),
+        cost_estimate=cost(1),
+        compiler_params=params(),
+        name="narrow_pieces",
+    )(*halves[0], *halves[1])
 
 
 def swap(values, axis, bit):
@@ -771,35 +930,49 @@
     return (kept.astype(F32) + received.astype(F32)).astype(BF16)
 
 
-def half_terms(lefts, rights, side):
-    wide_count = lax.axis_size("wide")
-    parts = []
-    for left, right in zip(lefts, rights):
-        rows = left.shape[0] // wide_count
-        chosen = pick(left.reshape(wide_count // 2, 2, rows, left.shape[1]), 1, side)
-        parts.append(
-            jnp.einsum("prt,tk->prk", chosen, right, preferred_element_type=F32)
-        )
-    return parts[0] if len(parts) == 1 else jnp.concatenate(parts, axis=1)
-
-
-def reduce_wide(lefts, rights, order):
-    place = lax.axis_index("wide")
-    wide_count = lax.axis_size("wide")
-    bits = wide_count.bit_length() - 1
-    mine = place & 1
-    sent = half_terms(lefts, rights, 1 - mine).astype(BF16)
-    received = swap(sent, "wide", 0)
-    held = (half_terms(lefts, rights, mine) + received.astype(F32)).astype(BF16)
-    held = held.reshape((2,) * (bits - 1) + held.shape[1:])
-    left_bits = list(range(bits - 1, 0, -1))
-    for bit in order:
-        dim = left_bits.index(bit)
-        side = (place >> bit) & 1
-        received = swap(pick(held, dim, 1 - side), "wide", bit)
-        held = add_low(pick(held, dim, side), received)
-        left_bits.remove(bit)
-    return held
+def after(value, *others):
+    return lax.optimization_barrier((value,) + others)[0]
+
+
+def partner_half(turned, me):
+    blocks, rows, tok_count = turned.shape
+    pairs = turned.reshape(blocks // 2, 2, rows, tok_count)
+    return [swap(pick(pairs[block], 0, 1 - (me & 1)), "wide", 0) for block in range(blocks // 2)]
+
+
+class Folding:
+    def __init__(self, me, outs, orders):
+        self.me = me
+        self.orders = orders
+        self.left = [sorted(order) for order in orders]
+        self.kept = [outs[0], outs[2]]
+        self.sent = [outs[1], outs[3]]
+        self.level = 0
+        self.exchange()
+
+    def exchange(self):
+        self.received = [
+            swap(self.sent[half], "wide", self.orders[half][self.level]) for half in range(2)
+        ]
+        for half in range(2):
+            self.left[half].remove(self.orders[half][self.level])
+        self.level += 1
+
+    def halves(self):
+        return [(self.kept[half], self.received[half]) for half in range(2)]
+
+    def step(self):
+        bits = [order[self.level] for order in self.orders]
+        places = [left.index(bit) for left, bit in zip(self.left, bits)]
+        outs = fold(self.me, self.halves(), bits, places)
+        self.kept = [outs[0], outs[2]]
+        self.sent = [outs[1], outs[3]]
+        self.exchange()
+
+    def finish(self, narrow_count, turned):
+        while self.level < len(self.orders[0]):
+            self.step()
+        return narrow_pieces(self.halves(), narrow_count, turned)
 
 
 def sum_pieces(pieces):
@@ -808,10 +981,13 @@
 
 
 def sum_vectors(values):
-    for axis in ("wide", "narrow"):
-        count = lax.axis_size(axis)
-        for bit in range(count.bit_length() - 1):
-            values = values + swap(values, axis, bit)
+    wide_bits = lax.axis_size("wide").bit_length() - 1
+    narrow_bits = lax.axis_size("narrow").bit_length() - 1
+    steps = [("wide", 0)]
+    steps += [("narrow", bit) for bit in range(narrow_bits)]
+    steps += [("wide", bit) for bit in range(1, wide_bits)]
+    for axis, bit in steps:
+        values = values + swap(values, axis, bit)
     return values
 
 
@@ -840,6 +1016,7 @@
     kept_rows = slot_dev // 2
     units = w_in.shape[1]
     me = lax.axis_index("wide")
+    me_line = me.astype(jnp.int32).reshape(1)
     line = lambda vector: vector.reshape(1, -1)
 
     sent = build_send(tokens, segments, destination, pair_index, targets, wide_count)
@@ -847,13 +1024,14 @@
     full_bias = jnp.concatenate(
         [b_qv[:width], jnp.zeros((width,), F32), b_qv[width:]]
     ).reshape(1, 3 * width)
-    x, proj, probs, context, hidden, hidden_low, norm_one, rstd_one, labels, label_cols = (
+    stack, proj, probs, hidden, norm_one, rstd_one, labels, label_cols, meta, sources = (
         attend_forward(
             got, w_qkv, full_bias, w_o, line(b_o), line(gain_one), line(shift_one), kept_rows
         )
     )
-    act, slope, encoded, norm_two, rstd_two, pooled = feed_forward(
-        hidden_low,
+    stack_recv = swap(stack, "wide", 0)
+    act, slope, encoded, norm_two, rstd_two, pooled, pooled_copies = feed_forward(
+        stack,
         hidden,
         w_in,
         line(b_in),
@@ -862,16 +1040,12 @@
         line(gain_two),
         line(shift_two),
         labels,
-    )
-    place, target, first, second, back = route(
-        me.astype(jnp.int32).reshape(1), got[:, row_len:, :], pair_index, kept_rows
-    )
+        wide_count,
+    )
+    act_recv = swap(act, "wide", 0)
+    place, target, first, second = route(me_line, meta, pair_index, kept_rows)
     pooled_all = lax.all_to_all(
-        jnp.broadcast_to(pooled[None], (wide_count,) + pooled.shape),
-        "wide",
-        split_axis=0,
-        concat_axis=0,
-        tiled=True,
+        pooled_copies, "wide", split_axis=0, concat_axis=0, tiled=True
     ).reshape(wide_count * kept_rows * SEG_ROW, width)
     similarity = cosine_pairs(first, second, pooled_all).reshape(-1)
     d_res_two, d_ffn, d_ffn_t, sums_two = loss_back(
@@ -879,35 +1053,98 @@
     )
 
     bits = wide_count.bit_length() - 1
-    half = 1 + (bits - 1) // 2
+    middle = 1 + (bits - 1) // 2
     low_first = list(range(1, bits))
-    high_first = list(range(half, bits)) + list(range(1, half))
-
-    sum_out = reduce_wide([d_ffn_t], [act], low_first)
+    high_first = list(range(middle, bits)) + list(range(1, middle))
+    orders = (low_first, high_first)
+    first_bits = (low_first[0], high_first[0])
+    tok_count = kept_rows * row_len
+    blocks = lambda turned: turned.reshape(wide_count, -1, tok_count)
+
+    turned_out = blocks(d_ffn_t)
+    rows_out = turned_out.shape[1]
+    fold_out = Folding(
+        me_line,
+        grad_terms(
+            me_line,
+            turned_out,
+            partner_half(turned_out, me),
+            [(act, None)],
+            [(act_recv, None)],
+            ((0, rows_out),),
+            *first_bits,
+            512,
+        ),
+        orders,
+    )
     d_up_t, sum_b_in, d_one, d_attn_t, d_ctx, sums_one = feed_back(
-        d_ffn, d_res_two, w_out, w_in, slope, norm_one, rstd_one, line(gain_one), w_o
-    )
-    sum_in = reduce_wide([d_up_t], [hidden_low], high_first)
-    d_proj_t, d_rows, sums_qkv = attend_back(proj, probs, d_ctx, d_one, w_qkv)
-    sum_mix = reduce_wide([d_proj_t, d_attn_t], [x, context], low_first)
-
+        after(d_ffn, *fold_out.sent),
+        d_res_two,
+        w_out,
+        w_in,
+        slope,
+        norm_one,
+        rstd_one,
+        line(gain_one),
+        w_o,
+    )
+    turned_in = blocks(d_up_t)
+    rows_in = turned_in.shape[1]
+    recv_in = partner_half(turned_in, me)
+    fold_out.step()
+    fold_in = Folding(
+        me_line,
+        grad_terms(
+            me_line,
+            turned_in,
+            after(tuple(recv_in), *fold_out.sent),
+            [(stack, 2)],
+            [(stack_recv, 2)],
+            ((0, rows_in),),
+            *first_bits,
+            width // 2,
+        ),
+        orders,
+    )
+    turned_mix, d_rows, sums_qkv = attend_back(
+        sources,
+        proj,
+        probs,
+        after(d_ctx, *fold_in.sent),
+        d_one,
+        w_qkv,
+        d_attn_t,
+        wide_count,
+        wide_count,
+    )
+    recv_mix = partner_half(turned_mix, me)
+    fold_in.step()
+    pieces_out = fold_out.finish(narrow_count, False)
+    cols_qkv = 3 * width // wide_count
+    rows_mix = turned_mix.shape[1]
+    fold_mix = Folding(
+        me_line,
+        grad_terms(
+            me_line,
+            turned_mix,
+            after(tuple(recv_mix), pieces_out, *fold_in.sent),
+            [(stack, 0), (stack, 1)],
+            [(stack_recv, 0), (stack_recv, 1)],
+            ((0, cols_qkv), (cols_qkv, rows_mix)),
+            *first_bits,
+            width // 2,
+        ),
+        orders,
+    )
+    grad_w_out = sum_pieces(pieces_out).T
+    pieces_in = fold_in.finish(narrow_count, True)
+    grad_w_in = sum_pieces(after(pieces_in, *fold_mix.sent))
+    fold_mix.step()
     home = lax.all_to_all(
-        spread_rows(back[0, :wide_count], d_rows.reshape(kept_rows, row_len, width), wide_count),
-        "wide",
-        split_axis=0,
-        concat_axis=0,
-        tiled=True,
+        after(d_rows, *fold_mix.sent), "wide", split_axis=0, concat_axis=0, tiled=True
     )
     grad_tokens = home_rows(destination, home)
-
-    rows_out = sum_out.shape[0]
-    cols_out = units // narrow_count
-    pieces_out = sum_out.reshape(rows_out, narrow_count, cols_out).transpose(1, 0, 2)
-    grad_w_out = sum_pieces(pieces_out).T
-    rows_in = width // narrow_count
-    grad_w_in = sum_pieces(sum_in.T.reshape(narrow_count, rows_in, sum_in.shape[0]))
-    grad_mix = sum_pieces(sum_mix.T.reshape(narrow_count, rows_in, sum_mix.shape[0]))
-    cols_qkv = 3 * width // wide_count
+    grad_mix = sum_pieces(fold_mix.finish(narrow_count, True))
     grad_w_qkv = grad_mix[:, :cols_qkv]
     grad_w_o = grad_mix[:, cols_qkv:]
 

time: 305 us -> 268 us (0.88)
  waiting for transfers between devices: 91.9 us -> 62.8 us
  local copies, waits for them, and re-layouts: 34.8 us -> 57.4 us
  matrix products: 21.9 us -> 0 us
  other arithmetic: 18.4 us -> 4.52 us
  starting transfers between devices: 39.6 us -> 49.8 us
  Pallas kernels: 94.4 us -> 90.1 us
    ppermute x14 -> x31, waiting for transfers between devices: 68.3 us -> 29.1 us  [swap(): return lax.ppermute(values, axis, [(i, i ^ 1 << bit) for i in range(count)])]
    unnamed x67 -> x165, local copies, waits for them, and re-layouts: 8.29 us -> 44.3 us
    dot_general x8 -> x0, matrix products: 21.9 us -> none  [half_terms(): jnp.einsum('prt,tk->prk', chosen, right, preferred_element_type=F32)]
    pallas_call x1 -> x9, Pallas kernels: 5.9 us -> 26.5 us  [the longest x3 21.2 us: grad_terms(): pl.pallas_call(functools.partial(grad_kernel, first_bit, second_bit, span...]
    convert_element_type x7 -> x0, other arithmetic: 13.8 us -> none  [the longest x6 11.6 us: add_low(): return (kept.astype(F32) + received.astype(F32)).astype(BF16)]
    all_to_all x3, waiting for transfers between devices: 1.42 us -> 9.87 us  [sum_pieces(): lax.all_to_all(pieces, 'narrow', split_axis=0, concat_axis=0, tiled=True)]
    ppermute x14 -> x31, starting transfers between devices: 14.7 us -> 21.5 us  [swap(): return lax.ppermute(values, axis, [(i, i ^ 1 << bit) for i in range(count)])]
    dynamic_slice x4 -> x0, local copies, waits for them, and re-layouts: 6.16 us -> none  [pick(): return lax.dynamic_index_in_dim(values, index, dim, keepdims=False)]
  transfers between devices with their start and end apart: 20 -> 37, of which waited for: 10 -> 16; matrix products, arithmetic and copies ran while one was open for 20% -> 8% of each run, Pallas kernels for 18% -> 24%
where the time goes in v2:
time: 268 us; the launch traced here: 266 us
  Pallas kernels  90.1 us (34%)
  waiting for transfers between devices  62.8 us (23%)
  local copies, waits for them, and re-layouts  57.4 us (21%)
  starting transfers between devices  49.8 us (19%)
  other arithmetic  4.52 us (2%)
    unnamed x165, local copies, waits for them, and re-layouts  44.3 us
    ppermute x31, waiting for transfers between devices, swap(): return lax.ppermute(values, axis, [(i, i ^ 1 << bit) for i in range(count)])  29.1 us
    pallas_call x1, Pallas kernels, attend_back(): pl.pallas_call(attend_back_kernel, out_shape=[jax.ShapeDtypeStruct(*item)...  22.2 us
    ppermute x31, starting transfers between devices, swap(): return lax.ppermute(values, axis, [(i, i ^ 1 << bit) for i in range(count)])  21.5 us
    pallas_call x3, Pallas kernels, grad_terms(): pl.pallas_call(functools.partial(grad_kernel, first_bit, second_bit, span...  21.2 us
    all_to_all x1, waiting for transfers between devices, on_device(): got = lax.all_to_all(sent, 'wide', split_axis=0, concat_axis=0, tiled=True)  20.1 us
    all_to_all x3, starting transfers between devices, sum_pieces(): lax.all_to_all(pieces, 'narrow', split_axis=0, concat_axis=0, tiled=True)  15 us
    pallas_call x1, Pallas kernels, feed_forward(): pl.pallas_call(feed_kernel, out_shape=[jax.ShapeDtypeStruct(*item) for it...  11.2 us
  transfers between devices with their start and end apart: 37, of which 16 were waited for; matrix products, arithmetic and copies ran while one was open for 8% of the time, Pallas kernels for 24%

profile of v2, /device:TPU:0, one launch (start us, length us, event | category | flops | bytes accessed | tf_op | source)
XLA Modules:
  0.0 266.1 jit_solution(15234548369349403157)
XLA Ops:
  0.7 1.4 copy-done.17
  4.7 4.0 %build_send.1 = bf16[8,144,768]{2,1,0:T(8,128)(2,1)} custom-call(s32[8]{0:T(128)S(1)} %copy-done.58, s32[2,32]{1,0:T(2,128)S(1)} %bitcast.67, f32[1,32]{1,0:T(1,128)S(1)} %bitcast.68, bf16[8,128,768]{2,1,0:T(8,128)(2,1)S(1)} %copy-done.17, s32[8,128]{1,0:T(8,128)S(1)} %copy-done.52), custom_call_target="tpu_custom_call" | custom-call | bytes 9000000 | tf_op jit(solution)/shard_map/build_send/pallas_call | solution.py:118
  8.8 5.3 %all-to-all-start = ((bf16[8,144,768]{2,1,0:T(8,128)(2,1)}), bf16[8,144,768]{2,1,0:T(8,128)(2,1)S(1)}, u32[]{:S(2)}, u32[]{:S(2)}) async-start(bf16[8,144,768]{2,1,0:T(8,128)(2,1)} %build_send.1), calls=%async_computation | async-start | bytes 3538944 | tf_op jit(solution)/shard_map/all_to_all | solution.py:1023
  17.2 20.1 %all-to-all-done.got_ref = bf16[8,144,768]{2,1,0:T(8,128)(2,1)S(1)} async-done(((bf16[8,144,768]{2,1,0:T(8,128)(2,1)}), bf16[8,144,768]{2,1,0:T(8,128)(2,1)S(1)}, u32[]{:S(2)}, u32[]{:S(2)}) %all-to-all-start) | async-done | bytes 1769504 | tf_op jit(solution)/shard_map/all_to_all | solution.py:1023
  37.3 1.2 copy-done.8
  38.5 2.0 copy-done.4
  40.5 1.5 copy-done.9
  44.0 7.6 %attend_forward.1 = (bf16[3,512,768]{2,1,0:T(8,128)(2,1)S(1)}, bf16[512,2304]{1,0:T(8,128)(2,1)S(1)}, bf16[4,6,256,128]{3,2,1,0:T(8,128)(2,1)S(1)}, f32[512,768]...) custom-call(bf16[8,144,768]{2,1,0:T(8,128)(2,1)S(1)} %copy-done.9, ...), custom_call_target="tpu_custom_call" | custom-call | bytes 24000000 | tf_op jit(solution)/shard_map/attend_forward/pallas_call | solution.py:232
  51.6 1.4 copy-done.13
  53.0 1.1 copy-done.15
  56.7 2.9 %copy-done.2 = bf16[3072,768]{1,0:T(8,128)(2,1)S(1)} copy-done((bf16[3072,768]{1,0:T(8,128)(2,1)S(1)}, bf16[3072,768]{1,0:T(8,128)(2,1)}, u32[]{:S(2)}) %copy-start.2) | copy-done | bytes 4718616
  59.6 11.2 %feed_forward.1 = (bf16[512,3072]{1,0:T(8,128)(2,1)}, bf16[512,3072]{1,0:T(8,128)(2,1)S(1)}, bf16[512,768]{1,0:T(8,128)(2,1)}, f32[512,768]{1,0:T(8,128)S(1)}, f...) custom-call(bf16[3,512,768]{2,1,0:T(8,128)(2,1)S(1)} %get-tuple-element.85.low_ref.refs_4_.refs_5_,, ...), custom_call_target="tpu_custom_call" | custom-call | bytes 30000000 | tf_op jit(solution)/shard_map/feed_forward/pallas_call | solution.py:319
  70.9 1.6 copy-done.11
  72.5 1.2 copy-done.18
  76.3 4.3 %all-to-all-start.1 = ((bf16[8,32,768]{2,1,0:T(8,128)(2,1)}), bf16[8,32,768]{2,1,0:T(8,128)(2,1)}, u32[]{:S(2)}, u32[]{:S(2)}) async-start(bf16[8,32,768]{2,1,0:T(8,128)(2,1)} %copy-done.22), calls=%async_computation.1 | async-start | bytes 786432 | tf_op jit(solution)/shard_map/all_to_all | solution.py:1047
  84.9 3.8 %all-to-all-done.1 = bf16[8,32,768]{2,1,0:T(8,128)(2,1)} async-done(((bf16[8,32,768]{2,1,0:T(8,128)(2,1)}), bf16[8,32,768]{2,1,0:T(8,128)(2,1)}, u32[]{:S(2)}, u32[]{:S(2)}) %all-to-all-start.1) | async-done | bytes 393248 | tf_op jit(solution)/shard_map/all_to_all | solution.py:1047
  88.7 1.4 copy-done.19
  90.1 0.9 copy-done.26
  91.1 0.9 copy-done.28
  95.6 2.7 %loss_back.1 = (f32[512,768]{1,0:T(8,128)S(1)}, bf16[512,768]{1,0:T(8,128)(2,1)S(1)}, bf16[768,512]{1,0:T(8,128)(2,1)S(1)}, f32[8,768]{1,0:T(8,128)S(1)}) custom-call(bf16[32,768]{1,0:T(8,128)(2,1)S(1)} %copy-done.30, bf16[256,768]{1,0:T(8,128)(2,1)} %bitcast.5.all_ref, f32[32,1]{1,0:T(8,128)S(1)} %copy-done.38, f32[32,1]{1,0:T(8,128)S(1)} %copy-done.40, ...), custom_call_target="tpu_custom_call" | custom-call | bytes 9000000 | tf_op jit(solution)/shard_map/loss_back/pallas_call | solution.py:526
  101.1 6.9 %grad_terms.3 = (bf16[2,96,1536]{2,1,0:T(8,128)(2,1)S(1)}, bf16[2,96,1536]{2,1,0:T(8,128)(2,1)S(1)}, bf16[2,96,1536]{2,1,0:T(8,128)(2,1)S(1)}, bf16[2,96,1536]{2,1,0:T(8,128)(2,1)S(1)}) custom-call(s32[1]{0:T(128)} %bitcast.4.me_ref, bf16[8,96,512]{2,1,0:T(8,128)(2,1)S(1)} %bitcast.64, bf16[96,512]{1,0:T(8,128)(2,1)S(1)} %collective-permute-done.refs_0_, ...), custom_call_target="tpu_custom_call" | custom-call | bytes 21000000 | tf_op jit(solution)/shard_map/grad_terms/pallas_call | solution.py:844
  109.2 2.3 copy-done.1
  111.5 2.3 copy-done.3
  113.9 10.2 %feed_back.1 = (bf16[3072,512]{1,0:T(8,128)(2,1)S(1)}, f32[1,3072]{1,0:T(1,128)S(1)}, f32[512,768]{1,0:T(8,128)S(1)}, bf16[768,512]{1,0:T(8,128)(2,1)S(1)}, bf16...) custom-call(bf16[512,768]{1,0:T(8,128)(2,1)S(1)} %get-tuple-element.107.dffn_ref, ...), custom_call_target="tpu_custom_call" | custom-call | bytes 30000000 | tf_op jit(solution)/shard_map/feed_back/pallas_call | solution.py:607
  126.5 1.5 collective-permute-start.16
  127.9 1.5 collective-permute-start.17
  129.5 7.0 %grad_terms.4 = (bf16[2,384,384]{2,1,0:T(8,128)(2,1)S(1)}, bf16[2,384,384]{2,1,0:T(8,128)(2,1)}, bf16[2,384,384]{2,1,0:T(8,128)(2,1)S(1)}, bf16[2,384,384]{2,1,0:T(8,128)(2,1)}) custom-call(s32[1]{0:T(128)} %bitcast.4.me_ref, bf16[8,384,512]{2,1,0:T(8,128)(2,1)S(1)} %bitcast.63, bf16[384,512]{1,0:T(8,128)(2,1)S(1)} %collective-permute-done.5.refs_0_, ...), custom_call_target="tpu_custom_call" | custom-call | bytes 21000000 | tf_op jit(solution)/shard_map/grad_terms/pallas_call | solution.py:844
  137.0 1.1 collective-permute-start.19
  138.1 22.2 %attend_back.1 = (bf16[8,384,512]{2,1,0:T(8,128)(2,1)S(1)}, bf16[8,128,768]{2,1,0:T(8,128)(2,1)}, f32[1,2304]{1,0:T(1,128)S(1)}) custom-call(s32[4]{0:T(128)S(1)} %copy-done.62, bf16[512,2304]{1,0:T(8,128)(2,1)S(1)} %copy-done.14, bf16[4,6,256,128]{3,2,1,0:T(8,128)(2,1)S(1)} %copy-done.21, bf16[512,768]{1,0:T(8,128)(2,1)S(1)} %get-tuple-element.124.dctx_ref, ...), custom_call_target="tpu_custom_call" | custom-call | bytes 60000000 | tf_op jit(solution)/shard_map/attend_back/pallas_call | solution.py:718
  160.3 2.0 fusion
  162.9 0.9 narrow_pieces.3
  163.9 4.9 %all-to-all-start.5 = ((bf16[4,96,768]{2,1,0:T(8,128)(2,1)}), bf16[4,96,768]{2,1,0:T(8,128)(2,1)}, u32[]{:S(2)}, u32[]{:S(2)}) async-start(bf16[4,96,768]{2,1,0:T(8,128)(2,1)} %narrow_pieces.3), calls=%async_computation.5 | async-start | bytes 1179648 | tf_op jit(solution)/shard_map/all_to_all | solution.py:979
  168.7 1.1 dynamic-slice_bitcast_fusion.3
  169.9 1.0 dynamic-slice_bitcast_fusion.2
  172.3 1.8 fold.4
  174.0 1.0 collective-permute-start.29
  175.0 1.5 collective-permute-start.30
  176.5 7.3 %grad_terms.5 = (bf16[2,384,384]{2,1,0:T(8,128)(2,1)S(1)}, bf16[2,384,384]{2,1,0:T(8,128)(2,1)}, bf16[2,384,384]{2,1,0:T(8,128)(2,1)S(1)}, bf16[2,384,384]{2,1,0:T(8,128)(2,1)}) custom-call(s32[1]{0:T(128)} %bitcast.4.me_ref, bf16[8,384,512]{2,1,0:T(8,128)(2,1)S(1)} %copy-done.7, bf16[384,512]{1,0:T(8,128)(2,1)S(1)} %collective-permute-done.12.refs_0_, ...), custom_call_target="tpu_custom_call" | custom-call | bytes 21000000 | tf_op jit(solution)/shard_map/grad_terms/pallas_call | solution.py:844
  184.4 1.1 collective-permute-start.21
  185.5 1.0 narrow_pieces.5
  186.6 5.1 %all-to-all-start.4 = ((bf16[4,192,384]{2,1,0:T(8,128)(2,1)}), bf16[4,192,384]{2,1,0:T(8,128)(2,1)}, u32[]{:S(2)}, u32[]{:S(2)}) async-start(bf16[4,192,384]{2,1,0:T(8,128)(2,1)} %narrow_pieces.5), calls=%async_computation.4 | async-start | bytes 1179648 | tf_op jit(solution)/shard_map/all_to_all | solution.py:979
  191.6 1.5 slice_reduce_fusion
  193.1 1.5 slice_reduce_fusion.3
  194.6 4.2 %collective-permute-done.20.refs_1_ = bf16[2,384,384]{2,1,0:T(8,128)(2,1)S(1)} collective-permute-done((bf16[2,384,384]{2,1,0:T(8,128)(2,1)}, bf16[2,384,384]{2,1,0:T(8,128)(2,1)S(1)}, u32[]{:S(2)}, u32[]{:S(2)}) %collective-permute-start.20) | collective-permute-done | bytes 589856 | tf_op jit(solution)/shard_map/ppermute | solution.py:922
  199.4 1.2 collective-permute-start.22
  200.6 0.9 collective-permute-start.23
  201.5 1.3 constant_dynamic-update-slice_fusion.8
  202.8 1.3 constant_dynamic-update-slice_fusion.7
  204.1 1.3 constant_dynamic-update-slice_fusion.6
  205.4 1.4 collective-permute-done.22.refs_1_
  207.6 1.1 narrow_pieces.4
  208.7 5.1 %all-to-all-start.3 = ((bf16[4,192,384]{2,1,0:T(8,128)(2,1)}), bf16[4,192,384]{2,1,0:T(8,128)(2,1)S(1)}, u32[]{:S(2)}, u32[]{:S(2)}) async-start(bf16[4,192,384]{2,1,0:T(8,128)(2,1)} %narrow_pieces.4), calls=%async_computation.3 | async-start | bytes 1179648 | tf_op jit(solution)/shard_map/all_to_all | solution.py:979
  214.0 1.2 collective-permute-done.24
  215.2 2.1 collective-permute-start.25
  217.3 9.9 %all-to-all-done.3 = bf16[4,192,384]{2,1,0:T(8,128)(2,1)S(1)} async-done(((bf16[4,192,384]{2,1,0:T(8,128)(2,1)}), bf16[4,192,384]{2,1,0:T(8,128)(2,1)S(1)}, u32[]{:S(2)}, u32[]{:S(2)}) %all-to-all-start.3) | async-done | bytes 589856 | tf_op jit(solution)/shard_map/all_to_all | solution.py:979
  227.2 3.6 %all-to-all-start.2 = ((bf16[8,128,768]{2,1,0:T(8,128)(2,1)}), bf16[8,128,768]{2,1,0:T(8,128)(2,1)S(1)}, u32[]{:S(2)}, u32[]{:S(2)}) async-start(bf16[8,128,768]{2,1,0:T(8,128)(2,1)} %get-tuple-element.145), calls=%async_computation.2 | async-start | bytes 3145728 | tf_op jit(solution)/shard_map/all_to_all | solution.py:1143
  230.9 4.8 %collective-permute-done.26 = f32[72,128]{1,0:T(8,128)S(1)} collective-permute-done((f32[72,128]{1,0:T(8,128)S(1)}, f32[72,128]{1,0:T(8,128)S(1)}, u32[]{:S(2)}, u32[]{:S(2)}) %collective-permute-start.26) | collective-permute-done | bytes 36896 | tf_op jit(solution)/shard_map/ppermute | solution.py:922
  235.7 1.9 collective-permute-start.27
  237.6 13.9 %collective-permute-done.27 = f32[72,128]{1,0:T(8,128)S(1)} collective-permute-done((f32[72,128]{1,0:T(8,128)S(1)}, f32[72,128]{1,0:T(8,128)S(1)}, u32[]{:S(2)}, u32[]{:S(2)}) %collective-permute-start.27) | collective-permute-done | bytes 36896 | tf_op jit(solution)/shard_map/ppermute | solution.py:922
  251.6 1.6 collective-permute-start.28
  253.1 1.4 cosine_pairs.1
  257.4 1.9 convert_reduce_fusion
  259.3 1.9 convert_reduce_fusion.1
  262.1 3.9 %home_rows.1 = bf16[8,128,768]{2,1,0:T(8,128)(2,1)} custom-call(s32[8]{0:T(128)S(1)} %copy-done.59, bf16[8,128,768]{2,1,0:T(8,128)(2,1)S(1)} %all-to-all-done.2.rows_ref), custom_call_target="tpu_custom_call" | custom-call | bytes 9000000 | tf_op jit(solution)/shard_map/home_rows/pallas_call | solution.py:765
  (236 shorter events, 35.7 us)
Async XLA Ops:
  8.8 7.8 %copy-start.76 = (f32[768]{0:T(1024)S(1)}, f32[768]{0:T(1024)}, u32[]{:S(2)}) copy-start(f32[768]{0:T(1024)} %param.32) | copy-start | bytes 9220
  8.8 29.7 %copy-start.10 = (bf16[768,768]{1,0:T(8,128)(2,1)S(1)}, bf16[768,768]{1,0:T(8,128)(2,1)}, u32[]{:S(2)}) copy-start(bf16[768,768]{1,0:T(8,128)(2,1)} %wo_ref.3) | copy-start | bytes 3538948
  8.8 28.4 %all-to-all-start = ((bf16[8,144,768]{2,1,0:T(8,128)(2,1)}), bf16[8,144,768]{2,1,0:T(8,128)(2,1)S(1)}, u32[]{:S(2)}, u32[]{:S(2)}) async-start(bf16[8,144,768]{2,1,0:T(8,128)(2,1)} %build_send.1), calls=%async_computation | async-start | bytes 3538944 | tf_op jit(solution)/shard_map/all_to_all | solution.py:1023
  16.6 40.1 %copy-start.33 = (f32[1,768]{1,0:T(1,128)}, f32[1,768]{1,0:T(1,128)S(1)}, u32[]{:S(2)}) copy-start(f32[1,768]{1,0:T(1,128)S(1)} %reshape.129.gain_ref) | copy-start | bytes 9220
  44.0 12.7 %copy-start = (bf16[768,3072]{1,0:T(8,128)(2,1)S(1)}, bf16[768,3072]{1,0:T(8,128)(2,1)}, u32[]{:S(2)}) copy-start(bf16[768,3072]{1,0:T(8,128)(2,1)} %win_ref.3) | copy-start | bytes 14155780
  44.0 12.7 %copy-start.47 = (f32[1,768]{1,0:T(1,128)S(1)}, f32[1,768]{1,0:T(1,128)}, u32[]{:S(2)}) copy-start(f32[1,768]{1,0:T(1,128)} %reshape.128.bout_ref) | copy-start | bytes 9220
  44.0 12.7 %copy-start.48 = (f32[1,768]{1,0:T(1,128)S(1)}, f32[1,768]{1,0:T(1,128)}, u32[]{:S(2)}) copy-start(f32[1,768]{1,0:T(1,128)} %reshape.130.shift_ref) | copy-start | bytes 9220
  44.0 12.7 %copy-start.49 = (f32[3072]{0:T(1024)S(1)}, f32[3072]{0:T(1024)}, u32[]{:S(2)}) copy-start(f32[3072]{0:T(1024)} %param.29) | copy-start | bytes 36868
  56.7 14.2 %copy-start.20 = (bf16[4,6,256,128]{3,2,1,0:T(8,128)(2,1)}, bf16[4,6,256,128]{3,2,1,0:T(8,128)(2,1)S(1)}, u32[]{:S(2)}) copy-start(bf16[4,6,256,128]{3,2,1,0:T(8,128)(2,1)S(1)} %get-tuple-element.95.probs_ref) | copy-start | bytes 4718596
  56.7 14.2 %copy-start.41 = (f32[8,128]{1,0:T(8,128)}, f32[8,128]{1,0:T(8,128)S(1)}, u32[]{:S(2)}) copy-start(f32[8,128]{1,0:T(8,128)S(1)} %get-tuple-element.87.lab_ref) | copy-start | bytes 12292
  75.8 25.3 %collective-permute-start.4 = (bf16[512,3072]{1,0:T(8,128)(2,1)}, bf16[512,3072]{1,0:T(8,128)(2,1)}, u32[]{:S(2)}, u32[]{:S(2)}) collective-permute-start(bf16[512,3072]{1,0:T(8,128)(2,1)} %get-tuple-element.104.refs_4_), channel_id=1, source_target_pairs={{0,4},{4,0},{8,12},{12,8},{16,20},{20,16},{24,28},{28,24},{1,5},{5... | collective-permute-start | bytes 9437192 | tf_op jit(solution)/shard_map/ppermute | solution.py:922
  75.8 53.7 %collective-permute-start.11 = (bf16[3,512,768]{2,1,0:T(8,128)(2,1)S(1)}, bf16[3,512,768]{2,1,0:T(8,128)(2,1)}, u32[]{:S(2)}, u32[]{:S(2)}) collective-permute-start(bf16[3,512,768]{2,1,0:T(8,128)(2,1)S(1)} %get-tuple-element.85.low_ref.refs_4_.refs_5_), channel_id=1, source_target_pairs={{0,4},{4,0},{8,12},{12,8},{16,20},{20,16},{24,28},{28,24},{1,5},{5... | collective-permute-start | bytes 7077896 | tf_op jit(solution)/shard_map/ppermute | solution.py:922
  76.3 12.4 %all-to-all-start.1 = ((bf16[8,32,768]{2,1,0:T(8,128)(2,1)}), bf16[8,32,768]{2,1,0:T(8,128)(2,1)}, u32[]{:S(2)}, u32[]{:S(2)}) async-start(bf16[8,32,768]{2,1,0:T(8,128)(2,1)} %copy-done.22), calls=%async_computation.1 | async-start | bytes 786432 | tf_op jit(solution)/shard_map/all_to_all | solution.py:1047
  98.3 9.7 %copy-start.56 = (f32[8,768]{1,0:T(8,128)}, f32[8,768]{1,0:T(8,128)S(1)}, u32[]{:S(2)}) copy-start(f32[8,768]{1,0:T(8,128)S(1)} %get-tuple-element.151) | copy-start | bytes 73732
  98.4 1.4 collective-permute-start
  98.5 1.5 collective-permute-start.1
  99.1 1.4 collective-permute-start.2
  99.8 1.3 collective-permute-start.3
  101.1 8.1 %copy-start.12 = (bf16[512,3072]{1,0:T(8,128)(2,1)S(1)}, bf16[512,3072]{1,0:T(8,128)(2,1)}, u32[]{:S(2)}) copy-start(bf16[512,3072]{1,0:T(8,128)(2,1)} %copy-done.11) | copy-start | bytes 9437188
  101.1 8.1 %copy-start.16 = (f32[512,768]{1,0:T(8,128)S(1)}, f32[512,768]{1,0:T(8,128)}, u32[]{:S(2)}) copy-start(f32[512,768]{1,0:T(8,128)} %copy-done.15) | copy-start | bytes 4718596
  101.1 8.1 %copy-start.24 = (f32[512,1]{1,0:T(8,128)S(1)}, f32[512,1]{1,0:T(8,128)}, u32[]{:S(2)}) copy-start(f32[512,1]{1,0:T(8,128)} %copy-done.23) | copy-start | bytes 6148
  101.1 8.1 %copy-start.36 = (f32[1,768]{1,0:T(1,128)S(1)}, f32[1,768]{1,0:T(1,128)}, u32[]{:S(2)}) copy-start(f32[1,768]{1,0:T(1,128)} %reshape.125.gain_ref) | copy-start | bytes 9220
  108.0 17.4 %collective-permute-start.9 = (bf16[2,96,1536]{2,1,0:T(8,128)(2,1)S(1)}, bf16[2,96,1536]{2,1,0:T(8,128)(2,1)S(1)}, u32[]{:S(2)}, u32[]{:S(2)}) collective-permute-start(bf16[2,96,1536]{2,1,0:T(8,128)(2,1)S(1)} %get-tuple-element.105), channel_id=1, source_target_pairs={{0,8},{4,12},{8,0},{12,4},{16,24},{20,28},{24,16},{28,20},{1,9},{5... | collective-permute-start | bytes 1769480 | tf_op jit(solution)/shard_map/ppermute | solution.py:922
  108.6 16.9 %collective-permute-start.10 = (bf16[2,96,1536]{2,1,0:T(8,128)(2,1)S(1)}, bf16[2,96,1536]{2,1,0:T(8,128)(2,1)S(1)}, u32[]{:S(2)}, u32[]{:S(2)}) collective-permute-start(bf16[2,96,1536]{2,1,0:T(8,128)(2,1)S(1)} %get-tuple-element.106), channel_id=1, source_target_pairs={{0,16},{4,20},{8,24},{12,28},{16,0},{20,4},{24,8},{28,12},{1,17},{... | collective-permute-start | bytes 1769480 | tf_op jit(solution)/shard_map/ppermute | solution.py:922
  124.7 1.8 collective-permute-start.5
  124.8 3.1 %collective-permute-start.6 = (bf16[384,512]{1,0:T(8,128)(2,1)S(1)}, bf16[384,512]{1,0:T(8,128)(2,1)S(1)}, u32[]{:S(2)}, u32[]{:S(2)}) collective-permute-start(bf16[384,512]{1,0:T(8,128)(2,1)S(1)} %dynamic-slice_bitcast_fusion.6), channel_id=1, source_target_pairs={{0,4},{4,0},{8,12},{12,8},{16,20},{20,16},{24,28},{28,24},{1,5},{5... | collective-permute-start | bytes 1179656 | tf_op jit(solution)/shard_map/ppermute | solution.py:922
  125.4 4.0 %collective-permute-start.7 = (bf16[384,512]{1,0:T(8,128)(2,1)S(1)}, bf16[384,512]{1,0:T(8,128)(2,1)S(1)}, u32[]{:S(2)}, u32[]{:S(2)}) collective-permute-start(bf16[384,512]{1,0:T(8,128)(2,1)S(1)} %dynamic-slice_bitcast_fusion.5), channel_id=1, source_target_pairs={{0,4},{4,0},{8,12},{12,8},{16,20},{20,16},{24,28},{28,24},{1,5},{5... | collective-permute-start | bytes 1179656 | tf_op jit(solution)/shard_map/ppermute | solution.py:922
  125.5 3.9 %collective-permute-start.8 = (bf16[384,512]{1,0:T(8,128)(2,1)S(1)}, bf16[384,512]{1,0:T(8,128)(2,1)S(1)}, u32[]{:S(2)}, u32[]{:S(2)}) collective-permute-start(bf16[384,512]{1,0:T(8,128)(2,1)S(1)} %dynamic-slice_bitcast_fusion.4), channel_id=1, source_target_pairs={{0,4},{4,0},{8,12},{12,8},{16,20},{20,16},{24,28},{28,24},{1,5},{5... | collective-permute-start | bytes 1179656 | tf_op jit(solution)/shard_map/ppermute | solution.py:922
  126.5 36.4 %collective-permute-start.16 = (bf16[1,96,1536]{2,1,0:T(8,128)(2,1)S(1)}, bf16[1,96,1536]{2,1,0:T(8,128)(2,1)S(1)}, u32[]{:S(2)}, u32[]{:S(2)}) collective-permute-start(bf16[1,96,1536]{2,1,0:T(8,128)(2,1)S(1)} %get-tuple-element.116), channel_id=1, source_target_pairs={{0,16},{4,20},{8,24},{12,28},{16,0},{20,4},{24,8},{28,12},{1,17},{... | collective-permute-start | bytes 884744 | tf_op jit(solution)/shard_map/ppermute | solution.py:922
  127.9 35.0 %collective-permute-start.17 = (bf16[1,96,1536]{2,1,0:T(8,128)(2,1)S(1)}, bf16[1,96,1536]{2,1,0:T(8,128)(2,1)S(1)}, u32[]{:S(2)}, u32[]{:S(2)}) collective-permute-start(bf16[1,96,1536]{2,1,0:T(8,128)(2,1)S(1)} %get-tuple-element.117), channel_id=1, source_target_pairs={{0,8},{4,12},{8,0},{12,4},{16,24},{20,28},{24,16},{28,20},{1,9},{5... | collective-permute-start | bytes 884744 | tf_op jit(solution)/shard_map/ppermute | solution.py:922
  129.4 8.7 %copy-start.5 = (bf16[768,2304]{1,0:T(8,128)(2,1)S(1)}, bf16[768,2304]{1,0:T(8,128)(2,1)}, u32[]{:S(2)}) copy-start(bf16[768,2304]{1,0:T(8,128)(2,1)} %wqkv_ref.3) | copy-start | bytes 10616836
  129.4 8.7 %copy-start.14 = (bf16[512,2304]{1,0:T(8,128)(2,1)S(1)}, bf16[512,2304]{1,0:T(8,128)(2,1)}, u32[]{:S(2)}) copy-start(bf16[512,2304]{1,0:T(8,128)(2,1)} %copy-done.13) | copy-start | bytes 7077892
  129.4 8.6 %copy-start.21 = (bf16[4,6,256,128]{3,2,1,0:T(8,128)(2,1)S(1)}, bf16[4,6,256,128]{3,2,1,0:T(8,128)(2,1)}, u32[]{:S(2)}) copy-start(bf16[4,6,256,128]{3,2,1,0:T(8,128)(2,1)} %copy-done.20) | copy-start | bytes 4718596
  129.5 8.6 %copy-start.62 = (s32[4]{0:T(128)S(1)}, s32[4]{0:T(128)}, u32[]{:S(2)}) copy-start(s32[4]{0:T(128)} %copy-done.61) | copy-start | bytes 52
  136.4 35.3 %collective-permute-start.18 = (bf16[2,384,384]{2,1,0:T(8,128)(2,1)}, bf16[2,384,384]{2,1,0:T(8,128)(2,1)}, u32[]{:S(2)}, u32[]{:S(2)}) collective-permute-start(bf16[2,384,384]{2,1,0:T(8,128)(2,1)} %get-tuple-element.122), channel_id=1, source_target_pairs={{0,8},{4,12},{8,0},{12,4},{16,24},{20,28},{24,16},{28,20},{1,9},{5... | collective-permute-start | bytes 1769480 | tf_op jit(solution)/shard_map/ppermute | solution.py:922
  137.0 35.3 %collective-permute-start.19 = (bf16[2,384,384]{2,1,0:T(8,128)(2,1)}, bf16[2,384,384]{2,1,0:T(8,128)(2,1)}, u32[]{:S(2)}, u32[]{:S(2)}) collective-permute-start(bf16[2,384,384]{2,1,0:T(8,128)(2,1)} %get-tuple-element.123), channel_id=1, source_target_pairs={{0,16},{4,20},{8,24},{12,28},{16,0},{20,4},{24,8},{28,12},{1,17},{... | collective-permute-start | bytes 1769480 | tf_op jit(solution)/shard_map/ppermute | solution.py:922
  163.9 22.7 %all-to-all-start.5 = ((bf16[4,96,768]{2,1,0:T(8,128)(2,1)}), bf16[4,96,768]{2,1,0:T(8,128)(2,1)}, u32[]{:S(2)}, u32[]{:S(2)}) async-start(bf16[4,96,768]{2,1,0:T(8,128)(2,1)} %narrow_pieces.3), calls=%async_computation.5 | async-start | bytes 1179648 | tf_op jit(solution)/shard_map/all_to_all | solution.py:979
  169.9 5.2 %collective-permute-start.12 = (bf16[384,512]{1,0:T(8,128)(2,1)S(1)}, bf16[384,512]{1,0:T(8,128)(2,1)S(1)}, u32[]{:S(2)}, u32[]{:S(2)}) collective-permute-start(bf16[384,512]{1,0:T(8,128)(2,1)S(1)} %dynamic-slice_bitcast_fusion.3), channel_id=1, source_target_pairs={{0,4},{4,0},{8,12},{12,8},{16,20},{20,16},{24,28},{28,24},{1,5},{5... | collective-permute-start | bytes 1179656 | tf_op jit(solution)/shard_map/ppermute | solution.py:922
  171.0 5.5 %collective-permute-start.13 = (bf16[384,512]{1,0:T(8,128)(2,1)S(1)}, bf16[384,512]{1,0:T(8,128)(2,1)S(1)}, u32[]{:S(2)}, u32[]{:S(2)}) collective-permute-start(bf16[384,512]{1,0:T(8,128)(2,1)S(1)} %dynamic-slice_bitcast_fusion.2), channel_id=1, source_target_pairs={{0,4},{4,0},{8,12},{12,8},{16,20},{20,16},{24,28},{28,24},{1,5},{5... | collective-permute-start | bytes 1179656 | tf_op jit(solution)/shard_map/ppermute | solution.py:922
  171.6 4.9 %collective-permute-start.14 = (bf16[384,512]{1,0:T(8,128)(2,1)S(1)}, bf16[384,512]{1,0:T(8,128)(2,1)S(1)}, u32[]{:S(2)}, u32[]{:S(2)}) collective-permute-start(bf16[384,512]{1,0:T(8,128)(2,1)S(1)} %dynamic-slice_bitcast_fusion.1), channel_id=1, source_target_pairs={{0,4},{4,0},{8,12},{12,8},{16,20},{20,16},{24,28},{28,24},{1,5},{5... | collective-permute-start | bytes 1179656 | tf_op jit(solution)/shard_map/ppermute | solution.py:922
  171.7 4.8 %collective-permute-start.15 = (bf16[384,512]{1,0:T(8,128)(2,1)S(1)}, bf16[384,512]{1,0:T(8,128)(2,1)S(1)}, u32[]{:S(2)}, u32[]{:S(2)}) collective-permute-start(bf16[384,512]{1,0:T(8,128)(2,1)S(1)} %dynamic-slice_bitcast_fusion), channel_id=1, source_target_pairs={{0,4},{4,0},{8,12},{12,8},{16,20},{20,16},{24,28},{28,24},{1,5},{5... | collective-permute-start | bytes 1179656 | tf_op jit(solution)/shard_map/ppermute | solution.py:922
  174.0 11.5 %collective-permute-start.29 = (bf16[1,384,384]{2,1,0:T(8,128)(2,1)S(1)}, bf16[1,384,384]{2,1,0:T(8,128)(2,1)S(1)}, u32[]{:S(2)}, u32[]{:S(2)}) collective-permute-start(bf16[1,384,384]{2,1,0:T(8,128)(2,1)S(1)} %get-tuple-element.133), channel_id=1, source_target_pairs={{0,16},{4,20},{8,24},{12,28},{16,0},{20,4},{24,8},{28,12},{1,17},{... | collective-permute-start | bytes 884744 | tf_op jit(solution)/shard_map/ppermute | solution.py:922
  175.0 10.5 %collective-permute-start.30 = (bf16[1,384,384]{2,1,0:T(8,128)(2,1)S(1)}, bf16[1,384,384]{2,1,0:T(8,128)(2,1)S(1)}, u32[]{:S(2)}, u32[]{:S(2)}) collective-permute-start(bf16[1,384,384]{2,1,0:T(8,128)(2,1)S(1)} %get-tuple-element.134), channel_id=1, source_target_pairs={{0,8},{4,12},{8,0},{12,4},{16,24},{20,28},{24,16},{28,20},{1,9},{5... | collective-permute-start | bytes 884744 | tf_op jit(solution)/shard_map/ppermute | solution.py:922
  183.9 10.7 %copy-start.55 = (f32[1,2304]{1,0:T(1,128)S(1)}, f32[1,2304]{1,0:T(1,128)}, u32[]{:S(2)}) copy-start(f32[1,2304]{1,0:T(1,128)} %copy-done.54) | copy-start | bytes 27652
  183.9 14.9 %collective-permute-start.20 = (bf16[2,384,384]{2,1,0:T(8,128)(2,1)}, bf16[2,384,384]{2,1,0:T(8,128)(2,1)S(1)}, u32[]{:S(2)}, u32[]{:S(2)}) collective-permute-start(bf16[2,384,384]{2,1,0:T(8,128)(2,1)} %get-tuple-element.140), channel_id=1, source_target_pairs={{0,8},{4,12},{8,0},{12,4},{16,24},{20,28},{24,16},{28,20},{1,9},{5... | collective-permute-start | bytes 1769480 | tf_op jit(solution)/shard_map/ppermute | solution.py:922
  184.4 14.6 %collective-permute-start.21 = (bf16[2,384,384]{2,1,0:T(8,128)(2,1)}, bf16[2,384,384]{2,1,0:T(8,128)(2,1)S(1)}, u32[]{:S(2)}, u32[]{:S(2)}) collective-permute-start(bf16[2,384,384]{2,1,0:T(8,128)(2,1)} %get-tuple-element.142), channel_id=1, source_target_pairs={{0,16},{4,20},{8,24},{12,28},{16,0},{20,4},{24,8},{28,12},{1,17},{... | collective-permute-start | bytes 1769480 | tf_op jit(solution)/shard_map/ppermute | solution.py:922
  186.6 22.2 %all-to-all-start.4 = ((bf16[4,192,384]{2,1,0:T(8,128)(2,1)}), bf16[4,192,384]{2,1,0:T(8,128)(2,1)}, u32[]{:S(2)}, u32[]{:S(2)}) async-start(bf16[4,192,384]{2,1,0:T(8,128)(2,1)} %narrow_pieces.5), calls=%async_computation.4 | async-start | bytes 1179648 | tf_op jit(solution)/shard_map/all_to_all | solution.py:979
  199.3 14.5 %copy-start.70 = (f32[768]{0:T(1024)S(1)}, f32[768]{0:T(1024)}, u32[]{:S(2)}) copy-start(f32[768]{0:T(1024)} %get-tuple-element.159) | copy-start | bytes 9220
  199.3 14.5 %copy-start.69 = (f32[768]{0:T(1024)S(1)}, f32[768]{0:T(1024)}, u32[]{:S(2)}) copy-start(f32[768]{0:T(1024)} %get-tuple-element.158) | copy-start | bytes 9220
  199.4 14.5 %copy-start.68 = (f32[768]{0:T(1024)S(1)}, f32[768]{0:T(1024)}, u32[]{:S(2)}) copy-start(f32[768]{0:T(1024)} %get-tuple-element.157) | copy-start | bytes 9220
  199.4 14.5 %copy-start.67 = (f32[768]{0:T(1024)S(1)}, f32[768]{0:T(1024)}, u32[]{:S(2)}) copy-start(f32[768]{0:T(1024)} %get-tuple-element.156) | copy-start | bytes 9220
  199.4 7.4 %collective-permute-start.22 = (bf16[1,384,384]{2,1,0:T(8,128)(2,1)S(1)}, bf16[1,384,384]{2,1,0:T(8,128)(2,1)S(1)}, u32[]{:S(2)}, u32[]{:S(2)}) collective-permute-start(bf16[1,384,384]{2,1,0:T(8,128)(2,1)S(1)} %get-tuple-element.143), channel_id=1, source_target_pairs={{0,16},{4,20},{8,24},{12,28},{16,0},{20,4},{24,8},{28,12},{1,17},{... | collective-permute-start | bytes 884744 | tf_op jit(solution)/shard_map/ppermute | solution.py:922
  200.6 7.1 %collective-permute-start.23 = (bf16[1,384,384]{2,1,0:T(8,128)(2,1)S(1)}, bf16[1,384,384]{2,1,0:T(8,128)(2,1)S(1)}, u32[]{:S(2)}, u32[]{:S(2)}) collective-permute-start(bf16[1,384,384]{2,1,0:T(8,128)(2,1)S(1)} %get-tuple-element.144), channel_id=1, source_target_pairs={{0,8},{4,12},{8,0},{12,4},{16,24},{20,28},{24,16},{28,20},{1,9},{5... | collective-permute-start | bytes 884744 | tf_op jit(solution)/shard_map/ppermute | solution.py:922
  205.4 8.4 %copy-start.66 = (f32[9216]{0:T(1024)S(1)}, f32[9216]{0:T(1024)}, u32[]{:S(2)}) copy-start(f32[9216]{0:T(1024)} %constant_dynamic-update-slice_fusion.6) | copy-start | bytes 110596
  208.7 18.5 %all-to-all-start.3 = ((bf16[4,192,384]{2,1,0:T(8,128)(2,1)}), bf16[4,192,384]{2,1,0:T(8,128)(2,1)S(1)}, u32[]{:S(2)}, u32[]{:S(2)}) async-start(bf16[4,192,384]{2,1,0:T(8,128)(2,1)} %narrow_pieces.4), calls=%async_computation.3 | async-start | bytes 1179648 | tf_op jit(solution)/shard_map/all_to_all | solution.py:979
  213.9 1.3 collective-permute-start.24
  215.2 37.9 %copy-start.44 = (f32[32,1]{1,0:T(8,128)S(1)}, f32[32,1]{1,0:T(8,128)}, u32[]{:S(2)}) copy-start(f32[32,1]{1,0:T(8,128)} %copy-done.43) | copy-start | bytes 388
  215.2 37.9 %copy-start.46 = (f32[32,1]{1,0:T(8,128)S(1)}, f32[32,1]{1,0:T(8,128)}, u32[]{:S(2)}) copy-start(f32[32,1]{1,0:T(8,128)} %copy-done.45) | copy-start | bytes 388
  215.2 15.5 %collective-permute-start.25 = (f32[72,128]{1,0:T(8,128)S(1)}, f32[72,128]{1,0:T(8,128)S(1)}, u32[]{:S(2)}, u32[]{:S(2)}) collective-permute-start(f32[72,128]{1,0:T(8,128)S(1)} %bitcast_add_fusion), channel_id=1, source_target_pairs={{0,1},{1,0},{2,3},{3,2},{4,5},{5,4},{6,7},{7,6},{8,9},{9,8},{10,11... | collective-permute-start | bytes 110600 | tf_op jit(solution)/shard_map/ppermute | solution.py:922
  227.2 34.9 %all-to-all-start.2 = ((bf16[8,128,768]{2,1,0:T(8,128)(2,1)}), bf16[8,128,768]{2,1,0:T(8,128)(2,1)S(1)}, u32[]{:S(2)}, u32[]{:S(2)}) async-start(bf16[8,128,768]{2,1,0:T(8,128)(2,1)} %get-tuple-element.145), calls=%async_computation.2 | async-start | bytes 3145728 | tf_op jit(solution)/shard_map/all_to_all | solution.py:1143
  230.8 4.9 %collective-permute-start.26 = (f32[72,128]{1,0:T(8,128)S(1)}, f32[72,128]{1,0:T(8,128)S(1)}, u32[]{:S(2)}, u32[]{:S(2)}) collective-permute-start(f32[72,128]{1,0:T(8,128)S(1)} %fusion.4), channel_id=1, source_target_pairs={{0,2},{1,3},{2,0},{3,1},{4,6},{5,7},{6,4},{7,5},{8,10},{9,11},{10,... | collective-permute-start | bytes 110600 | tf_op jit(solution)/shard_map/ppermute | solution.py:922
  235.7 15.8 %collective-permute-start.27 = (f32[72,128]{1,0:T(8,128)S(1)}, f32[72,128]{1,0:T(8,128)S(1)}, u32[]{:S(2)}, u32[]{:S(2)}) collective-permute-start(f32[72,128]{1,0:T(8,128)S(1)} %add.35), channel_id=1, source_target_pairs={{0,8},{4,12},{8,0},{12,4},{16,24},{20,28},{24,16},{28,20},{1,9},{5... | collective-permute-start | bytes 110600 | tf_op jit(solution)/shard_map/ppermute | solution.py:922
  251.6 10.5 %copy-start.59 = (s32[8]{0:T(128)S(1)}, s32[8]{0:T(128)}, u32[]{:S(2)}) copy-start(s32[8]{0:T(128)} %dest_ref.3) | copy-start | bytes 100
  251.6 4.0 %collective-permute-start.28 = (f32[72,128]{1,0:T(8,128)S(1)}, f32[72,128]{1,0:T(8,128)S(1)}, u32[]{:S(2)}, u32[]{:S(2)}) collective-permute-start(f32[72,128]{1,0:T(8,128)S(1)} %add.36), channel_id=1, source_target_pairs={{0,16},{4,20},{8,24},{12,28},{16,0},{20,4},{24,8},{28,12},{1,17},{... | collective-permute-start | bytes 110600 | tf_op jit(solution)/shard_map/ppermute | solution.py:922
  (51 other events, 98.3 us)

commit v3 on v2

--- a/solution.py
+++ b/solution.py
@@ -17,7 +17,7 @@
 COS_EPS = 1e-06
 F32 = jnp.float32
 BF16 = jnp.bfloat16
-VMEM_LIMIT = 24 * 1024 * 1024
+VMEM_LIMIT = 67043328
 
 
 def cost(micros):
@@ -30,6 +30,14 @@
 
 def vmem_spec():
     return pl.BlockSpec(memory_space=pltpu.VMEM)
+
+
+def hbm_shape(shape, dtype):
+    return pltpu.HBM(shape, dtype)
+
+
+def make_shape(shape, dtype, make=jax.ShapeDtypeStruct):
+    return make(shape, dtype)
 
 
 def params(steps=0):
@@ -231,7 +239,7 @@
     )
     return pl.pallas_call(
         attend_kernel,
-        out_shape=[jax.ShapeDtypeStruct(*item) for item in shapes],
+        out_shape=[make_shape(*item) for item in shapes],
         in_specs=[vmem_spec()] * 7,
         out_specs=[vmem_spec()] * (len(shapes) - 1) + [smem_spec()],
         cost_estimate=cost(8),
@@ -318,7 +326,7 @@
     )
     return pl.pallas_call(
         feed_kernel,
-        out_shape=[jax.ShapeDtypeStruct(*item) for item in shapes],
+        out_shape=[make_shape(*item) for item in shapes],
         grid_spec=pltpu.PrefetchScalarGridSpec(
             num_scalar_prefetch=0,
             grid=(units // tile,),
@@ -416,7 +424,7 @@
     )
     return pl.pallas_call(
         route_kernel,
-        out_shape=[jax.ShapeDtypeStruct(*item) for item in shapes],
+        out_shape=[make_shape(*item) for item in shapes],
         in_specs=[smem_spec(), vmem_spec(), vmem_spec()],
         out_specs=[vmem_spec()] * len(shapes),
         cost_estimate=cost(1),
@@ -457,12 +465,19 @@
     )(first, second, pooled_all)
 
 
+def part_blocks(parity, held, own_ref, send_refs, first=0):
+    for index in range(held.shape[0] // 2):
+        own_ref[index] = held[2 * index + parity]
+        send_refs[first + index][...] = held[2 * index + 1 - parity]
+
+
 def norm_back(grad, normed, rstd, gain):
     scaled = grad * gain
     return rstd * (scaled - row_mean(scaled) - normed * row_mean(scaled * normed))
 
 
 def loss_back_kernel(
+    me_ref,
     own_ref,
     all_ref,
     place_ref,
@@ -474,9 +489,12 @@
     gain_ref,
     dres_ref,
     dffn_ref,
-    dffn_t_ref,
     sums_ref,
+    kept_ref,
+    *refs,
 ):
+    send_refs, held = refs[:-1], refs[-1]
+    depth = held.shape[1]
     tok_count, width = norm_ref.shape
     kept_rows = tok_count // LANES
     left = own_ref[...].astype(F32)
@@ -506,35 +524,44 @@
         d_low = d_res.astype(BF16)
         dres_ref[span, :] = d_res
         dffn_ref[span, :] = d_low
-        dffn_t_ref[:, span] = d_low.T
+        turned = d_low.T
+        for block in range(held.shape[0]):
+            held[block, :, span] = turned[block * depth : (block + 1) * depth, :]
         gain_sum = gain_sum + column_sum(d_out * normed)
         bias_sum = bias_sum + column_sum(d_low.astype(F32))
     sums_ref[0:1, :] = gain_sum
     sums_ref[1:2, :] = shift_sum
     sums_ref[2:3, :] = bias_sum
     sums_ref[3:8, :] = jnp.zeros((5, width), F32)
-
-
-def loss_back(own, pooled_all, place, target, labels, label_cols, normed, rstd, gain):
+    part_blocks(me_ref[0] & 1, held, kept_ref, send_refs)
+
+
+def loss_back(
+    me, own, pooled_all, place, target, labels, label_cols, normed, rstd, gain, wide_count
+):
     tok_count, width = normed.shape
+    half = wide_count // 2
+    depth = width // wide_count
     shapes = (
         ((tok_count, width), F32),
         ((tok_count, width), BF16),
-        ((width, tok_count), BF16),
         ((8, width), F32),
-    )
+        ((half, depth, tok_count), BF16),
+    ) + (((depth, tok_count), BF16, hbm_shape),) * half
     return pl.pallas_call(
         loss_back_kernel,
-        out_shape=[jax.ShapeDtypeStruct(*item) for item in shapes],
-        in_specs=[vmem_spec()] * 9,
+        out_shape=[make_shape(*item) for item in shapes],
+        in_specs=[smem_spec()] + [vmem_spec()] * 9,
         out_specs=[vmem_spec()] * len(shapes),
+        scratch_shapes=[pltpu.VMEM((wide_count, depth, tok_count), BF16)],
         cost_estimate=cost(3),
         compiler_params=params(),
         name="loss_back",
-    )(own, pooled_all, place, target, labels, label_cols, normed, rstd, gain)
+    )(me, own, pooled_all, place, target, labels, label_cols, normed, rstd, gain)
 
 
 def feed_back_kernel(
+    me_ref,
     dffn_ref,
     dres_ref,
     wout_ref,
@@ -544,17 +571,27 @@
     rstd_ref,
     gain_ref,
     wo_ref,
-    dup_t_ref,
     bsum_ref,
     done_ref,
     dattn_t_ref,
     dctx_ref,
     sums_ref,
-    total_ref,
+    kept_ref,
+    *refs,
 ):
+    send_refs, held, total_ref = refs[:-2], refs[-2], refs[-1]
+    count, depth, _ = held.shape
     step = pl.program_id(0)
     d_up = (dot(dffn_ref[...], wout_ref[...], NT) * slope_ref[...].astype(F32)).astype(BF16)
-    dup_t_ref[...] = d_up.T
+    turned = d_up.T
+    for block in range(count):
+        held[block] = turned[block * depth : (block + 1) * depth, :]
+    for at in range(len(send_refs) // (count // 2)):
+
+        @pl.when(step == at)
+        def _():
+            part_blocks(me_ref[0] & 1, held, kept_ref, send_refs, at * (count // 2))
+
     bsum_ref[...] = column_sum(d_up.astype(F32))
     part = dot(d_up, win_ref[...], NT)
 
@@ -591,26 +628,30 @@
         sums_ref[3:8, :] = jnp.zeros((5, width), F32)
 
 
-def feed_back(d_ffn, d_res, w_out, w_in, slope, normed, rstd, gain, w_o):
+def feed_back(me, d_ffn, d_res, w_out, w_in, slope, normed, rstd, gain, w_o, wide_count):
     tok_count, width = d_ffn.shape
     units = w_in.shape[1]
-    tile = 512
+    tile = 768
+    depth = units // wide_count
+    half = wide_count // 2
+    count = tile // depth
     whole = lambda step: (0, 0)
     shapes = (
-        ((units, tok_count), BF16),
         ((1, units), F32),
         ((tok_count, width), F32),
         ((width, tok_count), BF16),
         ((tok_count, width), BF16),
         ((8, width), F32),
-    )
+        ((half, depth, tok_count), BF16),
+    ) + (((depth, tok_count), BF16, hbm_shape),) * half
     return pl.pallas_call(
         feed_back_kernel,
-        out_shape=[jax.ShapeDtypeStruct(*item) for item in shapes],
+        out_shape=[make_shape(*item) for item in shapes],
         grid_spec=pltpu.PrefetchScalarGridSpec(
             num_scalar_prefetch=0,
             grid=(units // tile,),
             in_specs=[
+                smem_spec(),
                 pl.BlockSpec((tok_count, width), whole),
                 pl.BlockSpec((tok_count, width), whole),
                 pl.BlockSpec((tile, width), lambda step: (step, 0)),
@@ -622,37 +663,43 @@
                 pl.BlockSpec((width, width), whole),
             ],
             out_specs=[
-                pl.BlockSpec((tile, tok_count), lambda step: (step, 0)),
                 pl.BlockSpec((1, tile), lambda step: (0, step)),
                 pl.BlockSpec((tok_count, width), whole),
                 pl.BlockSpec((width, tok_count), whole),
                 pl.BlockSpec((tok_count, width), whole),
                 pl.BlockSpec((8, width), whole),
+                pl.BlockSpec((count // 2, depth, tok_count), lambda step: (step, 0, 0)),
+            ]
+            + [pl.BlockSpec((depth, tok_count), whole)] * half,
+            scratch_shapes=[
+                pltpu.VMEM((count, depth, tok_count), BF16),
+                pltpu.VMEM((tok_count, width), F32),
             ],
-            scratch_shapes=[pltpu.VMEM((tok_count, width), F32)],
         ),
         cost_estimate=cost(10),
         compiler_params=params(1),
         name="feed_back",
-    )(d_ffn, d_res, w_out, w_in, slope, normed, rstd, gain, w_o)
+    )(me, d_ffn, d_res, w_out, w_in, slope, normed, rstd, gain, w_o)
 
 
 def attend_back_kernel(
     source_ref,
+    me_ref,
     proj_ref,
     probs_ref,
     dctx_ref,
     done_ref,
     wqkv_ref,
     dattn_t_ref,
-    dmix_t_ref,
     dtok_ref,
     sums_ref,
-    dproj_ref,
+    kept_ref,
+    *refs,
 ):
+    send_refs, held, dproj_ref = refs[:-2], refs[-2], refs[-1]
     row = pl.program_id(0)
     row_len, width = dctx_ref.shape
-    blocks = dmix_t_ref.shape[0]
+    blocks = held.shape[0]
     main = 3 * width // blocks
     scale = 1.0 / math.sqrt(HEAD_DIM)
     lane = lax.broadcasted_iota(jnp.int32, (row_len, LANES), 1)
@@ -686,60 +733,60 @@
             while start < place + LANES:
                 block, offset = divmod(start, main)
                 stop = min(place + LANES, (block + 1) * main)
-                dmix_t_ref[block, offset : offset + stop - start, :] = turned[
+                held[block, offset : offset + stop - start, :] = turned[
                     start - place : stop - place, :
                 ]
                 start = stop
-            summed = column_sum(low.astype(F32))
-
-            @pl.when(row == 0)
-            def _():
-                sums_ref[:, place : place + LANES] = summed
-
-            @pl.when(row > 0)
-            def _():
-                sums_ref[:, place : place + LANES] += summed
+            before = jnp.where(row == 0, 0.0, sums_ref[:, place : place + LANES])
+            sums_ref[:, place : place + LANES] = before + column_sum(low.astype(F32))
 
     rest = width // blocks
     for block in range(blocks):
-        dmix_t_ref[block, main:, :] = dattn_t_ref[block * rest : (block + 1) * rest, :]
+        held[block, main:, :] = dattn_t_ref[block * rest : (block + 1) * rest, :]
+    part_blocks(me_ref[0] & 1, held, kept_ref, send_refs)
     grad = done_ref[...] + dot(dproj_ref[...], wqkv_ref[...], NT)
     dtok_ref[0] = grad.astype(BF16)
 
 
-def attend_back(sources, proj, probs, d_ctx, d_one, w_qkv, d_attn_t, blocks, wide_count):
+def attend_back(sources, me, proj, probs, d_ctx, d_one, w_qkv, d_attn_t, wide_count):
     tok_count, width = d_ctx.shape
     kept_rows = tok_count // LANES
+    half = wide_count // 2
+    depth = 4 * width // wide_count
     shapes = (
-        ((blocks, 4 * width // blocks, tok_count), BF16),
         ((wide_count, LANES, width), BF16),
         ((1, 3 * width), F32),
-    )
+        ((half, depth, tok_count), BF16),
+    ) + (((depth, tok_count), BF16, hbm_shape),) * half
     return pl.pallas_call(
         attend_back_kernel,
-        out_shape=[jax.ShapeDtypeStruct(*item) for item in shapes],
+        out_shape=[make_shape(*item) for item in shapes],
         grid_spec=pltpu.PrefetchScalarGridSpec(
-            num_scalar_prefetch=1,
+            num_scalar_prefetch=2,
             grid=(kept_rows,),
             in_specs=[
-                pl.BlockSpec((LANES, 3 * width), lambda row, src: (row, 0)),
-                pl.BlockSpec((1,) + probs.shape[1:], lambda row, src: (row, 0, 0, 0)),
-                pl.BlockSpec((LANES, width), lambda row, src: (row, 0)),
-                pl.BlockSpec((LANES, width), lambda row, src: (row, 0)),
-                pl.BlockSpec((width, 3 * width), lambda row, src: (0, 0)),
-                pl.BlockSpec((width, LANES), lambda row, src: (0, row)),
+                pl.BlockSpec((LANES, 3 * width), lambda row, src, me: (row, 0)),
+                pl.BlockSpec((1,) + probs.shape[1:], lambda row, src, me: (row, 0, 0, 0)),
+                pl.BlockSpec((LANES, width), lambda row, src, me: (row, 0)),
+                pl.BlockSpec((LANES, width), lambda row, src, me: (row, 0)),
+                pl.BlockSpec((width, 3 * width), lambda row, src, me: (0, 0)),
+                pl.BlockSpec((width, LANES), lambda row, src, me: (0, row)),
             ],
             out_specs=[
-                pl.BlockSpec((blocks, 4 * width // blocks, LANES), lambda row, src: (0, 0, row)),
-                pl.BlockSpec((1, LANES, width), lambda row, src: (src[row], 0, 0)),
-                pl.BlockSpec((1, 3 * width), lambda row, src: (0, 0)),
+                pl.BlockSpec((1, LANES, width), lambda row, src, me: (src[row], 0, 0)),
+                pl.BlockSpec((1, 3 * width), lambda row, src, me: (0, 0)),
+                pl.BlockSpec((half, depth, LANES), lambda row, src, me: (0, 0, row)),
+            ]
+            + [pl.BlockSpec((depth, LANES), lambda row, src, me: (0, row))] * half,
+            scratch_shapes=[
+                pltpu.VMEM((wide_count, depth, LANES), BF16),
+                pltpu.VMEM((LANES, 3 * width), BF16),
             ],
-            scratch_shapes=[pltpu.VMEM((LANES, 3 * width), BF16)],
         ),
         cost_estimate=cost(20),
         compiler_params=params(1),
         name="attend_back",
-    )(sources, proj, probs, d_ctx, d_one, w_qkv, d_attn_t)
+    )(sources, me, proj, probs, d_ctx, d_one, w_qkv, d_attn_t)
 
 
 def home_kernel(dest_ref, rows_ref, out_ref, sems):
@@ -800,7 +847,7 @@
                 kept = ((block >> (bit - 1)) & 1) == side
                 index = jnp.where(kept, rest, rest + blocks // 2)
                 for (start, stop), own_left, recv_left in zip(spans, own_lefts, recv_lefts):
-                    own_left[index] = own_ref[2 * block + (me & 1), start:stop, :]
+                    own_left[index] = own_ref[block, start:stop, :]
                     recv_left[index] = recv_refs[block][start:stop, :]
 
     for term, (start, stop) in enumerate(spans):
@@ -838,7 +885,7 @@
     out_block = (blocks // 2, rows, tile)
     first_spec = pl.BlockSpec(out_block, lambda step: (0, 0, jnp.minimum(step, half - 1)))
     second_spec = pl.BlockSpec(out_block, lambda step: (0, 0, jnp.maximum(step - half, 0)))
-    shape = jax.ShapeDtypeStruct((blocks // 2, rows, columns // 2), BF16)
+    shape = hbm_shape((blocks // 2, rows, columns // 2), BF16)
     whole = lambda step: (0, 0, 0)
     lefts = [pltpu.VMEM((blocks, stop - start, tok_count), BF16) for start, stop in spans]
     return pl.pallas_call(
@@ -877,7 +924,7 @@
 def fold(me, halves, bits, places):
     shapes = []
     for kept, _ in halves:
-        shapes += [jax.ShapeDtypeStruct((kept.shape[0] // 2,) + kept.shape[1:], BF16)] * 2
+        shapes += [hbm_shape((kept.shape[0] // 2,) + kept.shape[1:], BF16)] * 2
     return pl.pallas_call(
         functools.partial(fold_kernel, bits, places),
         out_shape=shapes,
@@ -889,32 +936,81 @@
     )(me, *halves[0], *halves[1])
 
 
-def piece_kernel(turned, *refs):
-    out_ref = refs[4]
-    count = out_ref.shape[0]
-    depth = out_ref.shape[1] if turned else out_ref.shape[2]
+def piece_kernel(turned, me_ref, *refs):
+    outs, held = refs[4:-1], refs[-1]
+    count = len(outs)
+    depth = held.shape[1] if turned else held.shape[2]
     for half in range(2):
         total = add_low(refs[2 * half][0], refs[2 * half + 1][0])
         if turned:
             total = total.T
         for index in range(count // 2):
             span = slice(index * depth, (index + 1) * depth)
-            out_ref[half * (count // 2) + index] = total[span, :] if turned else total[:, span]
-
-
-def narrow_pieces(halves, narrow_count, turned):
+            held[half * (count // 2) + index] = total[span, :] if turned else total[:, span]
+    for step in range(count):
+        outs[step][...] = held[me_ref[0] ^ step]
+
+
+def narrow_pieces(me, halves, narrow_count, turned):
     _, rows, columns = halves[0][0].shape
     depth = 2 * columns // narrow_count
-    shape = (narrow_count,) + ((depth, rows) if turned else (rows, depth))
+    shape = (depth, rows) if turned else (rows, depth)
     return pl.pallas_call(
         functools.partial(piece_kernel, turned),
-        out_shape=jax.ShapeDtypeStruct(shape, BF16),
-        in_specs=[vmem_spec()] * 4,
-        out_specs=vmem_spec(),
+        out_shape=[hbm_shape(shape, BF16)] * narrow_count,
+        in_specs=[smem_spec()] + [vmem_spec()] * 4,
+        out_specs=[vmem_spec()] * narrow_count,
+        scratch_shapes=[pltpu.VMEM((narrow_count,) + shape, BF16)],
         cost_estimate=cost(1),
         compiler_params=params(),
         name="narrow_pieces",
-    )(*halves[0], *halves[1])
+    )(me, *halves[0], *halves[1])
+
+
+def sum_kernel(count, *refs):
+    total = refs[0][...].astype(F32)
+    for ref in refs[1:count]:
+        total = total + ref[...].astype(F32)
+    start = 0
+    for out_ref in refs[count:]:
+        out_ref[...] = total[:, start : start + out_ref.shape[1]]
+        start += out_ref.shape[1]
+
+
+def sum_pieces(pieces, cuts=None):
+    shape = pieces[0].shape
+    outs = [jax.ShapeDtypeStruct((shape[0], cut), F32) for cut in cuts or (shape[1],)]
+    return pl.pallas_call(
+        functools.partial(sum_kernel, len(pieces)),
+        out_shape=outs,
+        in_specs=[vmem_spec()] * len(pieces),
+        out_specs=[vmem_spec()] * len(outs),
+        cost_estimate=cost(1),
+        compiler_params=params(),
+        name="sum_pieces",
+    )(*pieces)
+
+
+def pack_kernel(cuts, *refs):
+    out_ref = refs[-1]
+    place = 0
+    for index, row, start, stop in cuts:
+        for at in range(start, stop, LANES):
+            out_ref[place : place + 1, :] = refs[index][row : row + 1, at : at + LANES]
+            place += 1
+
+
+def pack_vectors(arrays, cuts):
+    lines = sum(stop - start for _, _, start, stop in cuts) // LANES
+    return pl.pallas_call(
+        functools.partial(pack_kernel, cuts),
+        out_shape=jax.ShapeDtypeStruct((lines, LANES), F32),
+        in_specs=[vmem_spec()] * len(arrays),
+        out_specs=vmem_spec(),
+        cost_estimate=cost(0.5),
+        compiler_params=params(),
+        name="pack_vectors",
+    )(*arrays)
 
 
 def swap(values, axis, bit):
@@ -922,6 +1018,14 @@
     return lax.ppermute(values, axis, [(i, i ^ (1 << bit)) for i in range(count)])
 
 
+def trade(pieces):
+    count = len(pieces)
+    got = [pieces[0]]
+    for step in range(1, count):
+        got.append(lax.ppermute(pieces[step], "narrow", [(i, i ^ step) for i in range(count)]))
+    return got
+
+
 def pick(values, dim, index):
     return lax.dynamic_index_in_dim(values, index, dim, keepdims=False)
 
@@ -934,25 +1038,24 @@
     return lax.optimization_barrier((value,) + others)[0]
 
 
-def partner_half(turned, me):
-    blocks, rows, tok_count = turned.shape
-    pairs = turned.reshape(blocks // 2, 2, rows, tok_count)
-    return [swap(pick(pairs[block], 0, 1 - (me & 1)), "wide", 0) for block in range(blocks // 2)]
+def to_partner(blocks):
+    return [swap(block, "wide", 0) for block in blocks]
 
 
 class Folding:
-    def __init__(self, me, outs, orders):
+    def __init__(self, me, outs, orders, *gates):
         self.me = me
         self.orders = orders
         self.left = [sorted(order) for order in orders]
         self.kept = [outs[0], outs[2]]
         self.sent = [outs[1], outs[3]]
         self.level = 0
-        self.exchange()
-
-    def exchange(self):
+        self.exchange(*gates)
+
+    def exchange(self, *gates):
         self.received = [
-            swap(self.sent[half], "wide", self.orders[half][self.level]) for half in range(2)
+            swap(after(self.sent[half], *gates), "wide", self.orders[half][self.level])
+            for half in range(2)
         ]
         for half in range(2):
             self.left[half].remove(self.orders[half][self.level])
@@ -961,34 +1064,25 @@
     def halves(self):
         return [(self.kept[half], self.received[half]) for half in range(2)]
 
-    def step(self):
+    def step(self, *gates):
         bits = [order[self.level] for order in self.orders]
         places = [left.index(bit) for left, bit in zip(self.left, bits)]
         outs = fold(self.me, self.halves(), bits, places)
         self.kept = [outs[0], outs[2]]
         self.sent = [outs[1], outs[3]]
-        self.exchange()
-
-    def finish(self, narrow_count, turned):
+        self.exchange(*gates)
+
+    def gate(self, *others):
+        self.kept[0] = after(self.kept[0], *others)
+
+    def finish(self, me_narrow, narrow_count, turned):
         while self.level < len(self.orders[0]):
             self.step()
-        return narrow_pieces(self.halves(), narrow_count, turned)
-
-
-def sum_pieces(pieces):
-    received = lax.all_to_all(pieces, "narrow", split_axis=0, concat_axis=0, tiled=True)
-    return jnp.sum(received.astype(F32), axis=0)
-
-
-def sum_vectors(values):
-    wide_bits = lax.axis_size("wide").bit_length() - 1
-    narrow_bits = lax.axis_size("narrow").bit_length() - 1
-    steps = [("wide", 0)]
-    steps += [("narrow", bit) for bit in range(narrow_bits)]
-    steps += [("wide", bit) for bit in range(1, wide_bits)]
-    for axis, bit in steps:
-        values = values + swap(values, axis, bit)
-    return values
+        return narrow_pieces(me_narrow, self.halves(), narrow_count, turned)
+
+
+def hop(values, axis, bit):
+    return values + swap(values, axis, bit)
 
 
 def on_device(
@@ -1017,6 +1111,7 @@
     units = w_in.shape[1]
     me = lax.axis_index("wide")
     me_line = me.astype(jnp.int32).reshape(1)
+    me_narrow = lax.axis_index("narrow").astype(jnp.int32).reshape(1)
     line = lambda vector: vector.reshape(1, -1)
 
     sent = build_send(tokens, segments, destination, pair_index, targets, wide_count)
@@ -1048,8 +1143,18 @@
         pooled_copies, "wide", split_axis=0, concat_axis=0, tiled=True
     ).reshape(wide_count * kept_rows * SEG_ROW, width)
     similarity = cosine_pairs(first, second, pooled_all).reshape(-1)
-    d_res_two, d_ffn, d_ffn_t, sums_two = loss_back(
-        pooled, pooled_all, place, target, labels, label_cols, norm_two, rstd_two, line(gain_two)
+    d_res_two, d_ffn, sums_two, own_out, *send_out = loss_back(
+        me_line,
+        pooled,
+        pooled_all,
+        place,
+        target,
+        labels,
+        label_cols,
+        norm_two,
+        rstd_two,
+        line(gain_two),
+        wide_count,
     )
 
     bits = wide_count.bit_length() - 1
@@ -1058,17 +1163,13 @@
     high_first = list(range(middle, bits)) + list(range(1, middle))
     orders = (low_first, high_first)
     first_bits = (low_first[0], high_first[0])
-    tok_count = kept_rows * row_len
-    blocks = lambda turned: turned.reshape(wide_count, -1, tok_count)
-
-    turned_out = blocks(d_ffn_t)
-    rows_out = turned_out.shape[1]
+    rows_out = own_out.shape[1]
     fold_out = Folding(
         me_line,
         grad_terms(
             me_line,
-            turned_out,
-            partner_half(turned_out, me),
+            own_out,
+            to_partner(send_out),
             [(act, None)],
             [(act_recv, None)],
             ((0, rows_out),),
@@ -1077,7 +1178,8 @@
         ),
         orders,
     )
-    d_up_t, sum_b_in, d_one, d_attn_t, d_ctx, sums_one = feed_back(
+    sum_b_in, d_one, d_attn_t, d_ctx, sums_one, own_in, *send_in = feed_back(
+        me_line,
         after(d_ffn, *fold_out.sent),
         d_res_two,
         w_out,
@@ -1087,16 +1189,17 @@
         rstd_one,
         line(gain_one),
         w_o,
-    )
-    turned_in = blocks(d_up_t)
-    rows_in = turned_in.shape[1]
-    recv_in = partner_half(turned_in, me)
+        wide_count,
+    )
+    rows_in = own_in.shape[1]
+    recv_in = to_partner(send_in)
     fold_out.step()
+    pieces_out = fold_out.finish(me_narrow, narrow_count, False)
     fold_in = Folding(
         me_line,
         grad_terms(
             me_line,
-            turned_in,
+            own_in,
             after(tuple(recv_in), *fold_out.sent),
             [(stack, 2)],
             [(stack_recv, 2)],
@@ -1105,63 +1208,81 @@
             width // 2,
         ),
         orders,
-    )
-    turned_mix, d_rows, sums_qkv = attend_back(
+        tuple(pieces_out),
+    )
+    traded_out = trade(pieces_out)
+    d_rows, sums_qkv, own_mix, *send_mix = attend_back(
         sources,
+        me_line,
         proj,
         probs,
-        after(d_ctx, *fold_in.sent),
+        after(d_ctx, tuple(pieces_out), *fold_in.sent),
         d_one,
         w_qkv,
         d_attn_t,
         wide_count,
-        wide_count,
-    )
-    recv_mix = partner_half(turned_mix, me)
+    )
+    recv_mix = to_partner(after(tuple(send_mix), tuple(traded_out)))
+    vectors = pack_vectors(
+        (sums_qkv, sums_one, sum_b_in, sums_two),
+        (
+            (0, 0, 0, width),
+            (0, 0, 2 * width, 3 * width),
+            (1, 2, 0, width),
+            (1, 0, 0, width),
+            (1, 1, 0, width),
+            (2, 0, 0, units),
+            (3, 2, 0, width),
+            (3, 0, 0, width),
+            (3, 1, 0, width),
+        ),
+    )
+    fold_in.gate(d_rows, tuple(traded_out))
     fold_in.step()
-    pieces_out = fold_out.finish(narrow_count, False)
+    home = lax.all_to_all(
+        after(d_rows, *fold_in.sent), "wide", split_axis=0, concat_axis=0, tiled=True
+    )
     cols_qkv = 3 * width // wide_count
-    rows_mix = turned_mix.shape[1]
+    rows_mix = own_mix.shape[1]
+    (grad_w_out,) = sum_pieces(traded_out)
+    grad_w_out = grad_w_out.T
+    outs_mix = grad_terms(
+        me_line,
+        own_mix,
+        after(tuple(recv_mix), *fold_in.sent),
+        [(stack, 0), (stack, 1)],
+        [(stack_recv, 0), (stack_recv, 1)],
+        ((0, cols_qkv), (cols_qkv, rows_mix)),
+        *first_bits,
+        width // 2,
+    )
+    vectors = hop(after(vectors, *outs_mix), "wide", 0)
+    vectors = hop(vectors, "narrow", 0)
     fold_mix = Folding(
         me_line,
-        grad_terms(
-            me_line,
-            turned_mix,
-            after(tuple(recv_mix), pieces_out, *fold_in.sent),
-            [(stack, 0), (stack, 1)],
-            [(stack_recv, 0), (stack_recv, 1)],
-            ((0, cols_qkv), (cols_qkv, rows_mix)),
-            *first_bits,
-            width // 2,
-        ),
+        outs_mix,
         orders,
-    )
-    grad_w_out = sum_pieces(pieces_out).T
-    pieces_in = fold_in.finish(narrow_count, True)
-    grad_w_in = sum_pieces(after(pieces_in, *fold_mix.sent))
+        vectors,
+        grad_w_out,
+        similarity,
+        *fold_in.received,
+    )
+    grad_tokens = home_rows(destination, home)
+    pieces_in = fold_in.finish(me_narrow, narrow_count, True)
+    traded_in = trade(pieces_in)
+    fold_mix.gate(grad_tokens, tuple(traded_in))
     fold_mix.step()
-    home = lax.all_to_all(
-        after(d_rows, *fold_mix.sent), "wide", split_axis=0, concat_axis=0, tiled=True
-    )
-    grad_tokens = home_rows(destination, home)
-    grad_mix = sum_pieces(fold_mix.finish(narrow_count, True))
-    grad_w_qkv = grad_mix[:, :cols_qkv]
-    grad_w_o = grad_mix[:, cols_qkv:]
-
-    vectors = jnp.concatenate(
-        [
-            sums_qkv[0, :width],
-            sums_qkv[0, 2 * width :],
-            sums_one[2],
-            sums_one[0],
-            sums_one[1],
-            sum_b_in[0],
-            sums_two[2],
-            sums_two[0],
-            sums_two[1],
-        ]
-    )
-    vectors = sum_vectors(vectors.reshape(-1, LANES)).reshape(-1)
+    for bit in range(1, narrow_count.bit_length() - 1):
+        vectors = hop(vectors, "narrow", bit)
+    (grad_w_in,) = sum_pieces(traded_in)
+    fold_mix.gate(vectors)
+    pieces_mix = fold_mix.finish(me_narrow, narrow_count, True)
+    for bit in range(1, bits):
+        vectors = hop(vectors if bit > 1 else after(vectors, tuple(pieces_mix)), "wide", bit)
+    grad_w_qkv, grad_w_o = sum_pieces(
+        after(tuple(trade(pieces_mix)), vectors), (cols_qkv, rows_mix - cols_qkv)
+    )
+    vectors = vectors.reshape(-1)
     cuts = (2 * width, width, width, width, units, width, width, width)
     outs = []
     start = 0

time: 268 us -> 241 us (0.90)
  local copies, waits for them, and re-layouts: 57.4 us -> 7.32 us
  Pallas kernels: 90.1 us -> 125 us
  waiting for transfers between devices: 62.8 us -> 47.1 us
  other arithmetic: 4.52 us -> 7.72 us
    unnamed x165 -> x17, local copies, waits for them, and re-layouts: 44.3 us -> 1.41 us
    pallas_call x9 -> x13, Pallas kernels: 57.4 us -> 82.8 us  [the longest x1 17.4 us: feed_back(): pl.pallas_call(feed_back_kernel, out_shape=[make_shape(*item) for item in...]
    ppermute x31, waiting for transfers between devices: 29.1 us -> 9.62 us  [swap(): return lax.ppermute(values, axis, [(i, i ^ 1 << bit) for i in range(count)])]
    all_to_all x4 -> x1, starting transfers between devices: 18.6 us -> 4.43 us  [on_device(): lax.all_to_all(after(d_rows, *fold_in.sent), 'wide', split_axis=0, concat...]
    ppermute x0 -> x9, waiting for transfers between devices: none -> 13.4 us  [trade(): lax.ppermute(pieces[step], 'narrow', [(i, i ^ step) for i in range(count)])]
    ppermute x0 -> x9, starting transfers between devices: none -> 13.2 us  [trade(): lax.ppermute(pieces[step], 'narrow', [(i, i ^ step) for i in range(count)])]
    all_to_all x4 -> x1, waiting for transfers between devices: 9.87 us -> 0.01 us  [on_device(): lax.all_to_all(after(d_rows, *fold_in.sent), 'wide', split_axis=0, concat...]
    add x5, other arithmetic: 0.03 us -> 6.37 us  [hop(): return values + swap(values, axis, bit)]
  transfers between devices with their start and end apart: 37 -> 43, of which waited for: 16 -> 13; matrix products, arithmetic and copies ran while one was open for 8% -> 6% of each run, Pallas kernels for 24% -> 34%
where the time goes in v3:
time: 241 us; the launch traced here: 239 us
  Pallas kernels  125 us (52%)
  starting transfers between devices  50.8 us (21%)
  waiting for transfers between devices  47.1 us (20%)
  other arithmetic  7.72 us (3%)
  local copies, waits for them, and re-layouts  7.32 us (3%)
    pallas_call x3, Pallas kernels, grad_terms(): pl.pallas_call(functools.partial(grad_kernel, first_bit, second_bit, span...  25.1 us
    ppermute x31, starting transfers between devices, swap(): return lax.ppermute(values, axis, [(i, i ^ 1 << bit) for i in range(count)])  23.4 us
    all_to_all x1, waiting for transfers between devices, on_device(): got = lax.all_to_all(sent, 'wide', split_axis=0, concat_axis=0, tiled=True)  19.1 us
    pallas_call x1, Pallas kernels, feed_back(): pl.pallas_call(feed_back_kernel, out_shape=[make_shape(*item) for item in...  17.4 us
    pallas_call x1, Pallas kernels, attend_back(): pl.pallas_call(attend_back_kernel, out_shape=[make_shape(*item) for item...  16.7 us
    pallas_call x1, Pallas kernels, feed_forward(): pl.pallas_call(feed_kernel, out_shape=[make_shape(*item) for item in shap...  14.6 us
    ppermute x9, waiting for transfers between devices, trade(): lax.ppermute(pieces[step], 'narrow', [(i, i ^ step) for i in range(count)])  13.4 us
    ppermute x9, starting transfers between devices, trade(): lax.ppermute(pieces[step], 'narrow', [(i, i ^ step) for i in range(count)])  13.2 us
  transfers between devices with their start and end apart: 43, of which 13 were waited for; matrix products, arithmetic and copies ran while one was open for 6% of the time, Pallas kernels for 34%

profile of v3, /device:TPU:0, one launch (start us, length us, event | category | flops | bytes accessed | tf_op | source)
XLA Modules:
  0.0 239.2 jit_solution(2373524841211968443)
XLA Ops:
  0.6 3.7 %build_send.1 = bf16[8,144,768]{2,1,0:T(8,128)(2,1)} custom-call(s32[8]{0:T(128)} %dest_ref.3, s32[2,32]{1,0:T(2,128)} %bitcast.26, f32[1,32]{1,0:T(1,128)} %bitcast.27, bf16[8,128,768]{2,1,0:T(8,128)(2,1)} %tok_ref.1, s32[8,128]{1,0:T(8,128)} %seg_ref.1), custom_call_target="tpu_custom_call" | custom-call | bytes 9000000 | tf_op jit(solution)/shard_map/build_send/pallas_call | solution.py:126
  4.4 5.5 %all-to-all-start = ((bf16[8,144,768]{2,1,0:T(8,128)(2,1)}), bf16[8,144,768]{2,1,0:T(8,128)(2,1)}, u32[]{:S(2)}, u32[]{:S(2)}) async-start(bf16[8,144,768]{2,1,0:T(8,128)(2,1)} %build_send.1), calls=%async_computation | async-start | bytes 3538944 | tf_op jit(solution)/shard_map/all_to_all | solution.py:1118
  9.9 0.6 reshape.84.bias_ref
  14.1 19.1 %all-to-all-done.got_ref = bf16[8,144,768]{2,1,0:T(8,128)(2,1)} async-done(((bf16[8,144,768]{2,1,0:T(8,128)(2,1)}), bf16[8,144,768]{2,1,0:T(8,128)(2,1)}, u32[]{:S(2)}, u32[]{:S(2)}) %all-to-all-start) | async-done | bytes 1769504 | tf_op jit(solution)/shard_map/all_to_all | solution.py:1118
  33.1 13.1 %attend_forward.1 = (bf16[3,512,768]{2,1,0:T(8,128)(2,1)}, bf16[512,2304]{1,0:T(8,128)(2,1)}, bf16[4,6,256,128]{3,2,1,0:T(8,128)(2,1)}, f32[512,768]{1,0:T(8,128...) custom-call(bf16[8,144,768]{2,1,0:T(8,128)(2,1)} %all-to-all-done.go, ...), custom_call_target="tpu_custom_call" | custom-call | bytes 24000000 | tf_op jit(solution)/shard_map/attend_forward/pallas_call | solution.py:240
  46.2 14.6 %feed_forward.1 = (bf16[512,3072]{1,0:T(8,128)(2,1)}, bf16[512,3072]{1,0:T(8,128)(2,1)}, bf16[512,768]{1,0:T(8,128)(2,1)}, f32[512,768]{1,0:T(8,128)}, f32[512,1...) custom-call(bf16[3,512,768]{2,1,0:T(8,128)(2,1)} %get-tuple-element.127.low_ref.refs_4_.refs_5_, ...), custom_call_target="tpu_custom_call" | custom-call | bytes 30000000 | tf_op jit(solution)/shard_map/feed_forward/pallas_call | solution.py:327
  61.4 4.3 %all-to-all-start.1 = ((bf16[8,32,768]{2,1,0:T(8,128)(2,1)}), bf16[8,32,768]{2,1,0:T(8,128)(2,1)}, u32[]{:S(2)}, u32[]{:S(2)}) async-start(bf16[8,32,768]{2,1,0:T(8,128)(2,1)} %get-tuple-element.134), calls=%async_computation.1 | async-start | bytes 786432 | tf_op jit(solution)/shard_map/all_to_all | solution.py:1142
  65.7 1.4 copy.33.pair_ref
  67.1 1.8 route.1
  68.9 5.0 %all-to-all-done.1 = bf16[8,32,768]{2,1,0:T(8,128)(2,1)} async-done(((bf16[8,32,768]{2,1,0:T(8,128)(2,1)}), bf16[8,32,768]{2,1,0:T(8,128)(2,1)}, u32[]{:S(2)}, u32[]{:S(2)}) %all-to-all-start.1) | async-done | bytes 393248 | tf_op jit(solution)/shard_map/all_to_all | solution.py:1142
  73.8 5.2 %loss_back.1 = (f32[512,768]{1,0:T(8,128)}, bf16[512,768]{1,0:T(8,128)(2,1)}, f32[8,768]{1,0:T(8,128)}, bf16[4,96,512]{2,1,0:T(8,128)(2,1)}, bf16[96,512]{1,0:T(...) custom-call(s32[1]{0:T(128)} %bitcast.4.me_ref, ...), custom_call_target="tpu_custom_call" | custom-call | bytes 9000000 | tf_op jit(solution)/shard_map/loss_back/pallas_call | solution.py:551
  79.6 1.1 collective-permute-done.refs_0_
  81.2 1.1 collective-permute-done.3.refs_3_
  82.3 8.0 %grad_terms.3 = (bf16[2,96,1536]{2,1,0:T(8,128)(2,1)}, bf16[2,96,1536]{2,1,0:T(8,128)(2,1)}, bf16[2,96,1536]{2,1,0:T(8,128)(2,1)}, bf16[2,96,1536]{2,1,0:T(8,128)(2,1)}) custom-call(s32[1]{0:T(128)} %bitcast.4.me_ref, bf16[4,96,512]{2,1,0:T(8,128)(2,1)} %get-tuple-element.145.own_ref, bf16[96,512]{1,0:T(8,128)(2,1)} %collective-permute-done.refs_0_, ...), custom_call_target="tpu_custom_call" | custom-call | bytes 21000000 | tf_op jit(solution)/shard_map/grad_terms/pallas_call | solution.py:891
  91.4 17.4 %feed_back.1 = (f32[1,3072]{1,0:T(1,128)}, f32[512,768]{1,0:T(8,128)}, bf16[768,512]{1,0:T(8,128)(2,1)}, bf16[512,768]{1,0:T(8,128)(2,1)}, f32[8,768]{1,0:T(8,12...) custom-call(s32[1]{0:T(128)} %bitcast.4.me_ref, ...), custom_call_target="tpu_custom_call" | custom-call | bytes 30000000 | tf_op jit(solution)/shard_map/feed_back/pallas_call | solution.py:647
  109.9 2.8 %fold.3 = (bf16[1,96,1536]{2,1,0:T(8,128)(2,1)}, bf16[1,96,1536]{2,1,0:T(8,128)(2,1)}, bf16[1,96,1536]{2,1,0:T(8,128)(2,1)}, bf16[1,96,1536]{2,1,0:T(8,128)(2,1)}) custom-call(s32[1]{0:T(128)} %bitcast.4.me_ref, bf16[2,96,1536]{2,1,0:T(8,128)(2,1)} %get-tuple-element.159.refs_0_, bf16[2,96,1536]{2,1,0:T(8,128)(2,1)} %collective-permute-done.5.refs_1_, ...), custom_call_target="tpu_custom_call" | custom-call | bytes 1500000 | tf_op jit(solution)/shard_map/fold/pallas_call | solution.py:928
  112.7 1.5 collective-permute-start.7
  114.2 1.5 collective-permute-start.8
  115.6 8.2 %grad_terms.4 = (bf16[2,384,384]{2,1,0:T(8,128)(2,1)}, bf16[2,384,384]{2,1,0:T(8,128)(2,1)}, bf16[2,384,384]{2,1,0:T(8,128)(2,1)}, bf16[2,384,384]{2,1,0:T(8,128)(2,1)}) custom-call(s32[1]{0:T(128)} %bitcast.4.me_ref, bf16[4,384,512]{2,1,0:T(8,128)(2,1)} %get-tuple-element.169.own_ref, bf16[384,512]{1,0:T(8,128)(2,1)} %collective-permute-done.9.refs_0_, ...), custom_call_target="tpu_custom_call" | custom-call | bytes 21000000 | tf_op jit(solution)/shard_map/grad_terms/pallas_call | solution.py:891
  123.9 2.3 narrow_pieces.3
  126.2 0.8 collective-permute-start.17
  127.5 2.1 collective-permute-start.14
  129.6 2.2 collective-permute-start.15
  132.0 16.7 %attend_back.1 = (bf16[8,128,768]{2,1,0:T(8,128)(2,1)}, f32[1,2304]{1,0:T(1,128)}, bf16[4,384,512]{2,1,0:T(8,128)(2,1)}, bf16[384,512]{1,0:T(8,128)(2,1)}, bf16[...) custom-call(s32[4]{0:T(128)} %get-tuple-element.135.source_ref, s32[1]{0:T(128)} %bitcast.4.me_ref, ...), custom_call_target="tpu_custom_call" | custom-call | bytes 60000000 | tf_op jit(solution)/shard_map/attend_back/pallas_call | solution.py:761
  148.7 2.7 %fold.4 = (bf16[1,384,384]{2,1,0:T(8,128)(2,1)}, bf16[1,384,384]{2,1,0:T(8,128)(2,1)}, bf16[1,384,384]{2,1,0:T(8,128)(2,1)}, bf16[1,384,384]{2,1,0:T(8,128)(2,1)}) custom-call(s32[1]{0:T(128)} %bitcast.4.me_ref, bf16[2,384,384]{2,1,0:T(8,128)(2,1)} %get-tuple-element.185.refs_0_, bf16[2,384,384]{2,1,0:T(8,128)(2,1)} %collective-permute-done.17.refs_1_, ...), custom_call_target="tpu_custom_call" | custom-call | bytes 1500000 | tf_op jit(solution)/shard_map/fold/pallas_call | solution.py:928
  151.4 4.4 %all-to-all-start.2 = ((bf16[8,128,768]{2,1,0:T(8,128)(2,1)}), bf16[8,128,768]{2,1,0:T(8,128)(2,1)}, u32[]{:S(2)}, u32[]{:S(2)}) async-start(bf16[8,128,768]{2,1,0:T(8,128)(2,1)} %get-tuple-element.191), calls=%async_computation.2 | async-start | bytes 3145728 | tf_op jit(solution)/shard_map/all_to_all | solution.py:1242
  157.0 1.8 collective-permute-start.23
  158.8 1.5 collective-permute-start.24
  160.3 1.4 pack_vectors.1
  161.7 9.0 %grad_terms.5 = (bf16[2,384,384]{2,1,0:T(8,128)(2,1)}, bf16[2,384,384]{2,1,0:T(8,128)(2,1)}, bf16[2,384,384]{2,1,0:T(8,128)(2,1)}, bf16[2,384,384]{2,1,0:T(8,128)(2,1)}) custom-call(s32[1]{0:T(128)} %bitcast.4.me_ref, bf16[4,384,512]{2,1,0:T(8,128)(2,1)} %get-tuple-element.192.own_ref, bf16[384,512]{1,0:T(8,128)(2,1)} %collective-permute-done.19.refs_0_, ...), custom_call_target="tpu_custom_call" | custom-call | bytes 21000000 | tf_op jit(solution)/shard_map/grad_terms/pallas_call | solution.py:891
  170.7 1.4 collective-permute-done.28
  172.1 1.4 add.15
  173.5 1.1 collective-permute-start.29
  174.6 2.0 cosine_pairs.1
  176.7 1.3 reduce
  178.0 1.9 sum_pieces.3
  179.9 1.4 add.16
  181.3 0.9 collective-permute-done.23.refs_1_
  182.3 1.4 collective-permute-start.30
  183.7 0.6 collective-permute-start.31
  184.4 2.3 narrow_pieces.4
  186.6 1.1 collective-permute-start.25
  187.8 3.1 %collective-permute-start.26 = (bf16[192,384]{1,0:T(8,128)(2,1)}, bf16[192,384]{1,0:T(8,128)(2,1)}, u32[]{:S(2)}, u32[]{:S(2)}) collective-permute-start(bf16[192,384]{1,0:T(8,128)(2,1)} %get-tuple-element.210), channel_id=1, source_target_pairs={{0,2},{1,3},{2,0},{3,1},{4,6},{5,7},{6,4},{7,5},{8,10},{9,11},{10,... | collective-permute-start | bytes 442376 | tf_op jit(solution)/shard_map/ppermute | solution.py:1025
  191.0 3.4 %home_rows.1 = bf16[8,128,768]{2,1,0:T(8,128)(2,1)} custom-call(s32[8]{0:T(128)} %dest_ref.3, bf16[8,128,768]{2,1,0:T(8,128)(2,1)} %all-to-all-done.2.rows_ref), custom_call_target="tpu_custom_call" | custom-call | bytes 9000000 | tf_op jit(solution)/shard_map/home_rows/pallas_call | solution.py:812
  194.5 7.6 %collective-permute-done.26.refs_2_ = bf16[192,384]{1,0:T(8,128)(2,1)} collective-permute-done((bf16[192,384]{1,0:T(8,128)(2,1)}, bf16[192,384]{1,0:T(8,128)(2,1)}, u32[]{:S(2)}, u32[]{:S(2)}) %collective-permute-start.26) | collective-permute-done | bytes 147488 | tf_op jit(solution)/shard_map/ppermute | solution.py:1025
  202.1 2.7 %fold.5 = (bf16[1,384,384]{2,1,0:T(8,128)(2,1)}, bf16[1,384,384]{2,1,0:T(8,128)(2,1)}, bf16[1,384,384]{2,1,0:T(8,128)(2,1)}, bf16[1,384,384]{2,1,0:T(8,128)(2,1)}) custom-call(s32[1]{0:T(128)} %bitcast.4.me_ref, bf16[2,384,384]{2,1,0:T(8,128)(2,1)} %get-tuple-element.212.refs_0_, bf16[2,384,384]{2,1,0:T(8,128)(2,1)} %collective-permute-done.30.refs_1_, ...), custom_call_target="tpu_custom_call" | custom-call | bytes 1500000 | tf_op jit(solution)/shard_map/fold/pallas_call | solution.py:928
  204.7 1.6 collective-permute-start.33
  206.7 3.1 %collective-permute-start.32 = (f32[72,128]{1,0:T(8,128)}, f32[72,128]{1,0:T(8,128)S(1)}, u32[]{:S(2)}, u32[]{:S(2)}) collective-permute-start(f32[72,128]{1,0:T(8,128)} %add.16), channel_id=1, source_target_pairs={{0,2},{1,3},{2,0},{3,1},{4,6},{5,7},{6,4},{7,5},{8,10},{9,11},{10,... | collective-permute-start | bytes 110600 | tf_op jit(solution)/shard_map/ppermute | solution.py:1018
  209.8 2.1 collective-permute-done.32
  211.9 1.4 add.17
  213.3 2.2 narrow_pieces.5
  215.6 1.7 collective-permute-start.38
  217.3 2.4 %collective-permute-done.38 = f32[72,128]{1,0:T(8,128)S(1)} collective-permute-done((f32[72,128]{1,0:T(8,128)}, f32[72,128]{1,0:T(8,128)S(1)}, u32[]{:S(2)}, u32[]{:S(2)}) %collective-permute-start.38) | collective-permute-done | bytes 36896 | tf_op jit(solution)/shard_map/ppermute | solution.py:1018
  219.7 1.4 add.18
  221.1 1.3 collective-permute-start.39
  222.5 1.9 sum_pieces.5
  224.4 2.0 collective-permute-start.35
  226.4 0.9 collective-permute-start.36
  227.3 1.5 collective-permute-start.37
  228.8 0.8 add.19
  229.5 0.6 slice_bitcast_fusion.2
  230.2 0.6 slice_bitcast_fusion
  231.6 5.6 %collective-permute-done.36.refs_2_ = bf16[192,384]{1,0:T(8,128)(2,1)} collective-permute-done((bf16[192,384]{1,0:T(8,128)(2,1)}, bf16[192,384]{1,0:T(8,128)(2,1)}, u32[]{:S(2)}, u32[]{:S(2)}) %collective-permute-start.36) | collective-permute-done | bytes 147488 | tf_op jit(solution)/shard_map/ppermute | solution.py:1025
  237.2 1.9 sum_pieces.4
  (80 shorter events, 10.6 us)
Async XLA Ops:
  4.3 5.6 %copy-start = (f32[1536]{0:T(1024)S(1)}, f32[1536]{0:T(1024)}, u32[]{:S(2)}) copy-start(f32[1536]{0:T(1024)} %param.23) | copy-start | bytes 18436
  4.3 6.2 %copy-start.1 = (f32[768]{0:T(1024)S(1)}, f32[768]{0:T(1024)}, u32[]{:S(2)}) copy-start(f32[768]{0:T(1024)} %param.25) | copy-start | bytes 9220
  4.4 6.8 %copy-start.2 = (f32[768]{0:T(1024)S(1)}, f32[768]{0:T(1024)}, u32[]{:S(2)}) copy-start(f32[768]{0:T(1024)} %param.26) | copy-start | bytes 9220
  4.4 7.4 %copy-start.3 = (f32[768]{0:T(1024)S(1)}, f32[768]{0:T(1024)}, u32[]{:S(2)}) copy-start(f32[768]{0:T(1024)} %param.27) | copy-start | bytes 9220
  4.4 7.9 %copy-start.4 = (f32[768]{0:T(1024)S(1)}, f32[768]{0:T(1024)}, u32[]{:S(2)}) copy-start(f32[768]{0:T(1024)} %param.31) | copy-start | bytes 9220
  4.4 8.5 %copy-start.5 = (f32[768]{0:T(1024)S(1)}, f32[768]{0:T(1024)}, u32[]{:S(2)}) copy-start(f32[768]{0:T(1024)} %param.32) | copy-start | bytes 9220
  4.4 9.1 %copy-start.6 = (f32[768]{0:T(1024)S(1)}, f32[768]{0:T(1024)}, u32[]{:S(2)}) copy-start(f32[768]{0:T(1024)} %param.33) | copy-start | bytes 9220
  4.4 28.7 %all-to-all-start = ((bf16[8,144,768]{2,1,0:T(8,128)(2,1)}), bf16[8,144,768]{2,1,0:T(8,128)(2,1)}, u32[]{:S(2)}, u32[]{:S(2)}) async-start(bf16[8,144,768]{2,1,0:T(8,128)(2,1)} %build_send.1), calls=%async_computation | async-start | bytes 3538944 | tf_op jit(solution)/shard_map/all_to_all | solution.py:1118
  60.8 21.5 %collective-permute-start.4 = (bf16[512,3072]{1,0:T(8,128)(2,1)}, bf16[512,3072]{1,0:T(8,128)(2,1)}, u32[]{:S(2)}, u32[]{:S(2)}) collective-permute-start(bf16[512,3072]{1,0:T(8,128)(2,1)} %get-tuple-element.150.refs_4_), channel_id=1, source_target_pairs={{0,4},{4,0},{8,12},{12,8},{16,20},{20,16},{24,28},{28,24},{1,5},{5... | collective-permute-start | bytes 9437192 | tf_op jit(solution)/shard_map/ppermute | solution.py:1018
  60.9 54.7 %collective-permute-start.13 = (bf16[3,512,768]{2,1,0:T(8,128)(2,1)}, bf16[3,512,768]{2,1,0:T(8,128)(2,1)}, u32[]{:S(2)}, u32[]{:S(2)}) collective-permute-start(bf16[3,512,768]{2,1,0:T(8,128)(2,1)} %get-tuple-element.127.low_ref.refs_4_.refs_5_), channel_id=1, source_target_pairs={{0,4},{4,0},{8,12},{12,8},{16,20},{20,16},{24,28},{28,24},{1,5},{5... | collective-permute-start | bytes 7077896 | tf_op jit(solution)/shard_map/ppermute | solution.py:1018
  61.4 12.4 %all-to-all-start.1 = ((bf16[8,32,768]{2,1,0:T(8,128)(2,1)}), bf16[8,32,768]{2,1,0:T(8,128)(2,1)}, u32[]{:S(2)}, u32[]{:S(2)}) async-start(bf16[8,32,768]{2,1,0:T(8,128)(2,1)} %get-tuple-element.134), calls=%async_computation.1 | async-start | bytes 786432 | tf_op jit(solution)/shard_map/all_to_all | solution.py:1142
  79.0 1.6 collective-permute-start
  79.0 1.8 collective-permute-start.1
  79.5 1.6 collective-permute-start.2
  80.6 1.6 collective-permute-start.3
  90.2 19.1 %collective-permute-start.5 = (bf16[2,96,1536]{2,1,0:T(8,128)(2,1)}, bf16[2,96,1536]{2,1,0:T(8,128)(2,1)}, u32[]{:S(2)}, u32[]{:S(2)}) collective-permute-start(bf16[2,96,1536]{2,1,0:T(8,128)(2,1)} %get-tuple-element.151), channel_id=1, source_target_pairs={{0,8},{4,12},{8,0},{12,4},{16,24},{20,28},{24,16},{28,20},{1,9},{5... | collective-permute-start | bytes 1769480 | tf_op jit(solution)/shard_map/ppermute | solution.py:1018
  90.8 18.6 %collective-permute-start.6 = (bf16[2,96,1536]{2,1,0:T(8,128)(2,1)}, bf16[2,96,1536]{2,1,0:T(8,128)(2,1)}, u32[]{:S(2)}, u32[]{:S(2)}) collective-permute-start(bf16[2,96,1536]{2,1,0:T(8,128)(2,1)} %get-tuple-element.152), channel_id=1, source_target_pairs={{0,16},{4,20},{8,24},{12,28},{16,0},{20,4},{24,8},{28,12},{1,17},{... | collective-permute-start | bytes 1769480 | tf_op jit(solution)/shard_map/ppermute | solution.py:1018
  108.8 3.9 %collective-permute-start.9 = (bf16[384,512]{1,0:T(8,128)(2,1)}, bf16[384,512]{1,0:T(8,128)(2,1)}, u32[]{:S(2)}, u32[]{:S(2)}) collective-permute-start(bf16[384,512]{1,0:T(8,128)(2,1)} %get-tuple-element.170), channel_id=1, source_target_pairs={{0,4},{4,0},{8,12},{12,8},{16,20},{20,16},{24,28},{28,24},{1,5},{5... | collective-permute-start | bytes 1179656 | tf_op jit(solution)/shard_map/ppermute | solution.py:1018
  108.9 5.3 %collective-permute-start.10 = (bf16[384,512]{1,0:T(8,128)(2,1)}, bf16[384,512]{1,0:T(8,128)(2,1)}, u32[]{:S(2)}, u32[]{:S(2)}) collective-permute-start(bf16[384,512]{1,0:T(8,128)(2,1)} %get-tuple-element.171), channel_id=1, source_target_pairs={{0,4},{4,0},{8,12},{12,8},{16,20},{20,16},{24,28},{28,24},{1,5},{5... | collective-permute-start | bytes 1179656 | tf_op jit(solution)/shard_map/ppermute | solution.py:1018
  109.4 6.3 %collective-permute-start.11 = (bf16[384,512]{1,0:T(8,128)(2,1)}, bf16[384,512]{1,0:T(8,128)(2,1)}, u32[]{:S(2)}, u32[]{:S(2)}) collective-permute-start(bf16[384,512]{1,0:T(8,128)(2,1)} %get-tuple-element.172), channel_id=1, source_target_pairs={{0,4},{4,0},{8,12},{12,8},{16,20},{20,16},{24,28},{28,24},{1,5},{5... | collective-permute-start | bytes 1179656 | tf_op jit(solution)/shard_map/ppermute | solution.py:1018
  109.4 6.2 %collective-permute-start.12 = (bf16[384,512]{1,0:T(8,128)(2,1)}, bf16[384,512]{1,0:T(8,128)(2,1)}, u32[]{:S(2)}, u32[]{:S(2)}) collective-permute-start(bf16[384,512]{1,0:T(8,128)(2,1)} %get-tuple-element.173), channel_id=1, source_target_pairs={{0,4},{4,0},{8,12},{12,8},{16,20},{20,16},{24,28},{28,24},{1,5},{5... | collective-permute-start | bytes 1179656 | tf_op jit(solution)/shard_map/ppermute | solution.py:1018
  112.7 11.2 %collective-permute-start.7 = (bf16[1,96,1536]{2,1,0:T(8,128)(2,1)}, bf16[1,96,1536]{2,1,0:T(8,128)(2,1)}, u32[]{:S(2)}, u32[]{:S(2)}) collective-permute-start(bf16[1,96,1536]{2,1,0:T(8,128)(2,1)} %get-tuple-element.162), channel_id=1, source_target_pairs={{0,16},{4,20},{8,24},{12,28},{16,0},{20,4},{24,8},{28,12},{1,17},{... | collective-permute-start | bytes 884744 | tf_op jit(solution)/shard_map/ppermute | solution.py:1018
  114.2 9.7 %collective-permute-start.8 = (bf16[1,96,1536]{2,1,0:T(8,128)(2,1)}, bf16[1,96,1536]{2,1,0:T(8,128)(2,1)}, u32[]{:S(2)}, u32[]{:S(2)}) collective-permute-start(bf16[1,96,1536]{2,1,0:T(8,128)(2,1)} %get-tuple-element.164), channel_id=1, source_target_pairs={{0,8},{4,12},{8,0},{12,4},{16,24},{20,28},{24,16},{28,20},{1,9},{5... | collective-permute-start | bytes 884744 | tf_op jit(solution)/shard_map/ppermute | solution.py:1018
  126.2 22.5 %collective-permute-start.17 = (bf16[2,384,384]{2,1,0:T(8,128)(2,1)}, bf16[2,384,384]{2,1,0:T(8,128)(2,1)}, u32[]{:S(2)}, u32[]{:S(2)}) collective-permute-start(bf16[2,384,384]{2,1,0:T(8,128)(2,1)} %get-tuple-element.186), channel_id=1, source_target_pairs={{0,8},{4,12},{8,0},{12,4},{16,24},{20,28},{24,16},{28,20},{1,9},{5... | collective-permute-start | bytes 1769480 | tf_op jit(solution)/shard_map/ppermute | solution.py:1018
  127.0 21.8 %collective-permute-start.18 = (bf16[2,384,384]{2,1,0:T(8,128)(2,1)}, bf16[2,384,384]{2,1,0:T(8,128)(2,1)}, u32[]{:S(2)}, u32[]{:S(2)}) collective-permute-start(bf16[2,384,384]{2,1,0:T(8,128)(2,1)} %get-tuple-element.188), channel_id=1, source_target_pairs={{0,16},{4,20},{8,24},{12,28},{16,0},{20,4},{24,8},{28,12},{1,17},{... | collective-permute-start | bytes 1769480 | tf_op jit(solution)/shard_map/ppermute | solution.py:1018
  127.5 21.2 %collective-permute-start.14 = (bf16[96,768]{1,0:T(8,128)(2,1)}, bf16[96,768]{1,0:T(8,128)(2,1)}, u32[]{:S(2)}, u32[]{:S(2)}) collective-permute-start(bf16[96,768]{1,0:T(8,128)(2,1)} %get-tuple-element.166), channel_id=1, source_target_pairs={{0,1},{1,0},{2,3},{3,2},{4,5},{5,4},{6,7},{7,6},{8,9},{9,8},{10,11... | collective-permute-start | bytes 442376 | tf_op jit(solution)/shard_map/ppermute | solution.py:1025
  129.6 19.1 %collective-permute-start.15 = (bf16[96,768]{1,0:T(8,128)(2,1)}, bf16[96,768]{1,0:T(8,128)(2,1)}, u32[]{:S(2)}, u32[]{:S(2)}) collective-permute-start(bf16[96,768]{1,0:T(8,128)(2,1)} %get-tuple-element.167), channel_id=1, source_target_pairs={{0,2},{1,3},{2,0},{3,1},{4,6},{5,7},{6,4},{7,5},{8,10},{9,11},{10,... | collective-permute-start | bytes 442376 | tf_op jit(solution)/shard_map/ppermute | solution.py:1025
  131.8 16.9 %collective-permute-start.16 = (bf16[96,768]{1,0:T(8,128)(2,1)}, bf16[96,768]{1,0:T(8,128)(2,1)}, u32[]{:S(2)}, u32[]{:S(2)}) collective-permute-start(bf16[96,768]{1,0:T(8,128)(2,1)} %get-tuple-element.168), channel_id=1, source_target_pairs={{0,3},{1,2},{2,1},{3,0},{4,7},{5,6},{6,5},{7,4},{8,11},{9,10},{10,... | collective-permute-start | bytes 442376 | tf_op jit(solution)/shard_map/ppermute | solution.py:1025
  151.4 4.4 %copy-start.7 = (bf16[384,512]{1,0:T(8,128)(2,1)S(1)}, bf16[384,512]{1,0:T(8,128)(2,1)}, u32[]{:S(2)}) copy-start(bf16[384,512]{1,0:T(8,128)(2,1)} %get-tuple-element.197) | copy-start | bytes 1179652
  151.4 39.6 %all-to-all-start.2 = ((bf16[8,128,768]{2,1,0:T(8,128)(2,1)}), bf16[8,128,768]{2,1,0:T(8,128)(2,1)}, u32[]{:S(2)}, u32[]{:S(2)}) async-start(bf16[8,128,768]{2,1,0:T(8,128)(2,1)} %get-tuple-element.191), calls=%async_computation.2 | async-start | bytes 3145728 | tf_op jit(solution)/shard_map/all_to_all | solution.py:1242
  155.9 2.9 %collective-permute-start.19 = (bf16[384,512]{1,0:T(8,128)(2,1)S(1)}, bf16[384,512]{1,0:T(8,128)(2,1)}, u32[]{:S(2)}, u32[]{:S(2)}) collective-permute-start(bf16[384,512]{1,0:T(8,128)(2,1)S(1)} %copy-done.7), channel_id=1, source_target_pairs={{0,4},{4,0},{8,12},{12,8},{16,20},{20,16},{24,28},{28,24},{1,5},{5... | collective-permute-start | bytes 1179656 | tf_op jit(solution)/shard_map/ppermute | solution.py:1018
  156.3 5.5 %collective-permute-start.20 = (bf16[384,512]{1,0:T(8,128)(2,1)}, bf16[384,512]{1,0:T(8,128)(2,1)}, u32[]{:S(2)}, u32[]{:S(2)}) collective-permute-start(bf16[384,512]{1,0:T(8,128)(2,1)} %get-tuple-element.198), channel_id=1, source_target_pairs={{0,4},{4,0},{8,12},{12,8},{16,20},{20,16},{24,28},{28,24},{1,5},{5... | collective-permute-start | bytes 1179656 | tf_op jit(solution)/shard_map/ppermute | solution.py:1018
  156.5 5.3 %collective-permute-start.21 = (bf16[384,512]{1,0:T(8,128)(2,1)}, bf16[384,512]{1,0:T(8,128)(2,1)}, u32[]{:S(2)}, u32[]{:S(2)}) collective-permute-start(bf16[384,512]{1,0:T(8,128)(2,1)} %get-tuple-element.199), channel_id=1, source_target_pairs={{0,4},{4,0},{8,12},{12,8},{16,20},{20,16},{24,28},{28,24},{1,5},{5... | collective-permute-start | bytes 1179656 | tf_op jit(solution)/shard_map/ppermute | solution.py:1018
  156.8 5.0 %collective-permute-start.22 = (bf16[384,512]{1,0:T(8,128)(2,1)}, bf16[384,512]{1,0:T(8,128)(2,1)}, u32[]{:S(2)}, u32[]{:S(2)}) collective-permute-start(bf16[384,512]{1,0:T(8,128)(2,1)} %get-tuple-element.200), channel_id=1, source_target_pairs={{0,4},{4,0},{8,12},{12,8},{16,20},{20,16},{24,28},{28,24},{1,5},{5... | collective-permute-start | bytes 1179656 | tf_op jit(solution)/shard_map/ppermute | solution.py:1018
  157.0 25.3 %collective-permute-start.23 = (bf16[1,384,384]{2,1,0:T(8,128)(2,1)}, bf16[1,384,384]{2,1,0:T(8,128)(2,1)}, u32[]{:S(2)}, u32[]{:S(2)}) collective-permute-start(bf16[1,384,384]{2,1,0:T(8,128)(2,1)} %get-tuple-element.189), channel_id=1, source_target_pairs={{0,16},{4,20},{8,24},{12,28},{16,0},{20,4},{24,8},{28,12},{1,17},{... | collective-permute-start | bytes 884744 | tf_op jit(solution)/shard_map/ppermute | solution.py:1018
  158.8 23.5 %collective-permute-start.24 = (bf16[1,384,384]{2,1,0:T(8,128)(2,1)}, bf16[1,384,384]{2,1,0:T(8,128)(2,1)}, u32[]{:S(2)}, u32[]{:S(2)}) collective-permute-start(bf16[1,384,384]{2,1,0:T(8,128)(2,1)} %get-tuple-element.190), channel_id=1, source_target_pairs={{0,8},{4,12},{8,0},{12,4},{16,24},{20,28},{24,16},{28,20},{1,9},{5... | collective-permute-start | bytes 884744 | tf_op jit(solution)/shard_map/ppermute | solution.py:1018
  170.7 1.4 collective-permute-start.28
  173.5 6.4 %collective-permute-start.29 = (f32[72,128]{1,0:T(8,128)}, f32[72,128]{1,0:T(8,128)}, u32[]{:S(2)}, u32[]{:S(2)}) collective-permute-start(f32[72,128]{1,0:T(8,128)} %add.15), channel_id=1, source_target_pairs={{0,1},{1,0},{2,3},{3,2},{4,5},{5,4},{6,7},{7,6},{8,9},{9,8},{10,11... | collective-permute-start | bytes 110600 | tf_op jit(solution)/shard_map/ppermute | solution.py:1018
  182.3 19.7 %collective-permute-start.30 = (bf16[2,384,384]{2,1,0:T(8,128)(2,1)}, bf16[2,384,384]{2,1,0:T(8,128)(2,1)}, u32[]{:S(2)}, u32[]{:S(2)}) collective-permute-start(bf16[2,384,384]{2,1,0:T(8,128)(2,1)} %get-tuple-element.221), channel_id=1, source_target_pairs={{0,8},{4,12},{8,0},{12,4},{16,24},{20,28},{24,16},{28,20},{1,9},{5... | collective-permute-start | bytes 1769480 | tf_op jit(solution)/shard_map/ppermute | solution.py:1018
  183.7 18.3 %collective-permute-start.31 = (bf16[2,384,384]{2,1,0:T(8,128)(2,1)}, bf16[2,384,384]{2,1,0:T(8,128)(2,1)}, u32[]{:S(2)}, u32[]{:S(2)}) collective-permute-start(bf16[2,384,384]{2,1,0:T(8,128)(2,1)} %get-tuple-element.222), channel_id=1, source_target_pairs={{0,16},{4,20},{8,24},{12,28},{16,0},{20,4},{24,8},{28,12},{1,17},{... | collective-permute-start | bytes 1769480 | tf_op jit(solution)/shard_map/ppermute | solution.py:1018
  186.6 7.9 %collective-permute-start.25 = (bf16[192,384]{1,0:T(8,128)(2,1)}, bf16[192,384]{1,0:T(8,128)(2,1)}, u32[]{:S(2)}, u32[]{:S(2)}) collective-permute-start(bf16[192,384]{1,0:T(8,128)(2,1)} %get-tuple-element.209), channel_id=1, source_target_pairs={{0,1},{1,0},{2,3},{3,2},{4,5},{5,4},{6,7},{7,6},{8,9},{9,8},{10,11... | collective-permute-start | bytes 442376 | tf_op jit(solution)/shard_map/ppermute | solution.py:1025
  187.8 14.3 %collective-permute-start.26 = (bf16[192,384]{1,0:T(8,128)(2,1)}, bf16[192,384]{1,0:T(8,128)(2,1)}, u32[]{:S(2)}, u32[]{:S(2)}) collective-permute-start(bf16[192,384]{1,0:T(8,128)(2,1)} %get-tuple-element.210), channel_id=1, source_target_pairs={{0,2},{1,3},{2,0},{3,1},{4,6},{5,7},{6,4},{7,5},{8,10},{9,11},{10,... | collective-permute-start | bytes 442376 | tf_op jit(solution)/shard_map/ppermute | solution.py:1025
  190.9 11.2 %collective-permute-start.27 = (bf16[192,384]{1,0:T(8,128)(2,1)}, bf16[192,384]{1,0:T(8,128)(2,1)}, u32[]{:S(2)}, u32[]{:S(2)}) collective-permute-start(bf16[192,384]{1,0:T(8,128)(2,1)} %get-tuple-element.211), channel_id=1, source_target_pairs={{0,3},{1,2},{2,1},{3,0},{4,7},{5,6},{6,5},{7,4},{8,11},{9,10},{10,... | collective-permute-start | bytes 442376 | tf_op jit(solution)/shard_map/ppermute | solution.py:1025
  204.7 8.6 %collective-permute-start.33 = (bf16[1,384,384]{2,1,0:T(8,128)(2,1)}, bf16[1,384,384]{2,1,0:T(8,128)(2,1)}, u32[]{:S(2)}, u32[]{:S(2)}) collective-permute-start(bf16[1,384,384]{2,1,0:T(8,128)(2,1)} %get-tuple-element.225), channel_id=1, source_target_pairs={{0,16},{4,20},{8,24},{12,28},{16,0},{20,4},{24,8},{28,12},{1,17},{... | collective-permute-start | bytes 884744 | tf_op jit(solution)/shard_map/ppermute | solution.py:1018
  206.3 7.0 %collective-permute-start.34 = (bf16[1,384,384]{2,1,0:T(8,128)(2,1)}, bf16[1,384,384]{2,1,0:T(8,128)(2,1)}, u32[]{:S(2)}, u32[]{:S(2)}) collective-permute-start(bf16[1,384,384]{2,1,0:T(8,128)(2,1)} %get-tuple-element.227), channel_id=1, source_target_pairs={{0,8},{4,12},{8,0},{12,4},{16,24},{20,28},{24,16},{28,20},{1,9},{5... | collective-permute-start | bytes 884744 | tf_op jit(solution)/shard_map/ppermute | solution.py:1018
  206.7 5.2 %collective-permute-start.32 = (f32[72,128]{1,0:T(8,128)}, f32[72,128]{1,0:T(8,128)S(1)}, u32[]{:S(2)}, u32[]{:S(2)}) collective-permute-start(f32[72,128]{1,0:T(8,128)} %add.16), channel_id=1, source_target_pairs={{0,2},{1,3},{2,0},{3,1},{4,6},{5,7},{6,4},{7,5},{8,10},{9,11},{10,... | collective-permute-start | bytes 110600 | tf_op jit(solution)/shard_map/ppermute | solution.py:1018
  215.6 4.2 %collective-permute-start.38 = (f32[72,128]{1,0:T(8,128)}, f32[72,128]{1,0:T(8,128)S(1)}, u32[]{:S(2)}, u32[]{:S(2)}) collective-permute-start(f32[72,128]{1,0:T(8,128)} %add.17), channel_id=1, source_target_pairs={{0,8},{4,12},{8,0},{12,4},{16,24},{20,28},{24,16},{28,20},{1,9},{5... | collective-permute-start | bytes 110600 | tf_op jit(solution)/shard_map/ppermute | solution.py:1018
  221.1 7.6 %collective-permute-start.39 = (f32[72,128]{1,0:T(8,128)}, f32[72,128]{1,0:T(8,128)}, u32[]{:S(2)}, u32[]{:S(2)}) collective-permute-start(f32[72,128]{1,0:T(8,128)} %add.18), channel_id=1, source_target_pairs={{0,16},{4,20},{8,24},{12,28},{16,0},{20,4},{24,8},{28,12},{1,17},{... | collective-permute-start | bytes 110600 | tf_op jit(solution)/shard_map/ppermute | solution.py:1018
  224.4 7.2 %collective-permute-start.35 = (bf16[192,384]{1,0:T(8,128)(2,1)}, bf16[192,384]{1,0:T(8,128)(2,1)}, u32[]{:S(2)}, u32[]{:S(2)}) collective-permute-start(bf16[192,384]{1,0:T(8,128)(2,1)} %get-tuple-element.229), channel_id=1, source_target_pairs={{0,1},{1,0},{2,3},{3,2},{4,5},{5,4},{6,7},{7,6},{8,9},{9,8},{10,11... | collective-permute-start | bytes 442376 | tf_op jit(solution)/shard_map/ppermute | solution.py:1025
  226.4 10.8 %collective-permute-start.36 = (bf16[192,384]{1,0:T(8,128)(2,1)}, bf16[192,384]{1,0:T(8,128)(2,1)}, u32[]{:S(2)}, u32[]{:S(2)}) collective-permute-start(bf16[192,384]{1,0:T(8,128)(2,1)} %get-tuple-element.230), channel_id=1, source_target_pairs={{0,2},{1,3},{2,0},{3,1},{4,6},{5,7},{6,4},{7,5},{8,10},{9,11},{10,... | collective-permute-start | bytes 442376 | tf_op jit(solution)/shard_map/ppermute | solution.py:1025
  227.3 9.9 %collective-permute-start.37 = (bf16[192,384]{1,0:T(8,128)(2,1)}, bf16[192,384]{1,0:T(8,128)(2,1)}, u32[]{:S(2)}, u32[]{:S(2)}) collective-permute-start(bf16[192,384]{1,0:T(8,128)(2,1)} %get-tuple-element.231), channel_id=1, source_target_pairs={{0,3},{1,2},{2,1},{3,0},{4,7},{5,6},{6,5},{7,4},{8,11},{9,10},{10,... | collective-permute-start | bytes 442376 | tf_op jit(solution)/shard_map/ppermute | solution.py:1025

commit v4 on v3

--- a/solution.py
+++ b/solution.py
@@ -476,7 +476,7 @@
     return rstd * (scaled - row_mean(scaled) - normed * row_mean(scaled * normed))
 
 
-def loss_back_kernel(
+def loss_back_body(
     me_ref,
     own_ref,
     all_ref,
@@ -491,9 +491,9 @@
     dffn_ref,
     sums_ref,
     kept_ref,
-    *refs,
+    send_refs,
+    held,
 ):
-    send_refs, held = refs[:-1], refs[-1]
     depth = held.shape[1]
     tok_count, width = norm_ref.shape
     kept_rows = tok_count // LANES
@@ -536,75 +536,84 @@
     part_blocks(me_ref[0] & 1, held, kept_ref, send_refs)
 
 
-def loss_back(
-    me, own, pooled_all, place, target, labels, label_cols, normed, rstd, gain, wide_count
-):
-    tok_count, width = normed.shape
-    half = wide_count // 2
-    depth = width // wide_count
-    shapes = (
-        ((tok_count, width), F32),
-        ((tok_count, width), BF16),
-        ((8, width), F32),
-        ((half, depth, tok_count), BF16),
-    ) + (((depth, tok_count), BF16, hbm_shape),) * half
-    return pl.pallas_call(
-        loss_back_kernel,
-        out_shape=[make_shape(*item) for item in shapes],
-        in_specs=[smem_spec()] + [vmem_spec()] * 9,
-        out_specs=[vmem_spec()] * len(shapes),
-        scratch_shapes=[pltpu.VMEM((wide_count, depth, tok_count), BF16)],
-        cost_estimate=cost(3),
-        compiler_params=params(),
-        name="loss_back",
-    )(me, own, pooled_all, place, target, labels, label_cols, normed, rstd, gain)
-
-
 def feed_back_kernel(
+    half,
     me_ref,
-    dffn_ref,
-    dres_ref,
+    own_ref,
+    all_ref,
+    place_ref,
+    targ_ref,
+    lab_ref,
+    labcol_ref,
+    norm_two_ref,
+    rstd_two_ref,
+    gain_two_ref,
     wout_ref,
     win_ref,
     slope_ref,
-    norm_ref,
+    norm_src,
     rstd_ref,
     gain_ref,
-    wo_ref,
+    wo_src,
     bsum_ref,
     done_ref,
     dattn_t_ref,
     dctx_ref,
     sums_ref,
+    sums_two_ref,
+    kept_out_ref,
     kept_ref,
     *refs,
 ):
-    send_refs, held, total_ref = refs[:-2], refs[-2], refs[-1]
+    send_out, send_refs, refs = refs[:half], refs[half : 2 * half], refs[2 * half :]
+    held_out, held, dffn_ref, total_ref, norm_ref, wo_ref, sems = refs
     count, depth, _ = held.shape
     step = pl.program_id(0)
+    copies = [
+        pltpu.make_async_copy(norm_src, norm_ref, sems.at[0]),
+        pltpu.make_async_copy(wo_src, wo_ref, sems.at[1]),
+    ]
+
+    @pl.when(step == 0)
+    def _():
+        for copy in copies:
+            copy.start()
+        loss_back_body(
+            me_ref,
+            own_ref,
+            all_ref,
+            place_ref,
+            targ_ref,
+            lab_ref,
+            labcol_ref,
+            norm_two_ref,
+            rstd_two_ref,
+            gain_two_ref,
+            total_ref,
+            dffn_ref,
+            sums_two_ref,
+            kept_out_ref,
+            send_out,
+            held_out,
+        )
+
     d_up = (dot(dffn_ref[...], wout_ref[...], NT) * slope_ref[...].astype(F32)).astype(BF16)
     turned = d_up.T
     for block in range(count):
         held[block] = turned[block * depth : (block + 1) * depth, :]
-    for at in range(len(send_refs) // (count // 2)):
+    for at in range(half // (count // 2)):
 
         @pl.when(step == at)
         def _():
             part_blocks(me_ref[0] & 1, held, kept_ref, send_refs, at * (count // 2))
 
     bsum_ref[...] = column_sum(d_up.astype(F32))
-    part = dot(d_up, win_ref[...], NT)
-
-    @pl.when(step == 0)
-    def _():
-        total_ref[...] = part + dres_ref[...]
-
-    @pl.when(step > 0)
-    def _():
-        total_ref[...] += part
+    total_ref[...] += dot(d_up, win_ref[...], NT)
 
     @pl.when(step == pl.num_programs(0) - 1)
     def _():
+        for copy in copies:
+            copy.wait()
         tok_count, width = total_ref.shape
         kept_rows = tok_count // LANES
         gain_sum = jnp.zeros((1, width), F32)
@@ -628,39 +637,74 @@
         sums_ref[3:8, :] = jnp.zeros((5, width), F32)
 
 
-def feed_back(me, d_ffn, d_res, w_out, w_in, slope, normed, rstd, gain, w_o, wide_count):
-    tok_count, width = d_ffn.shape
+def feed_back(
+    me,
+    own,
+    pooled_all,
+    place,
+    target,
+    labels,
+    label_cols,
+    normed_two,
+    rstd_two,
+    gain_two,
+    w_out,
+    w_in,
+    slope,
+    normed,
+    rstd,
+    gain,
+    w_o,
+    wide_count,
+):
+    tok_count, width = normed.shape
     units = w_in.shape[1]
     tile = 768
     depth = units // wide_count
+    depth_out = width // wide_count
     half = wide_count // 2
     count = tile // depth
     whole = lambda step: (0, 0)
+    fixed = lambda array: pl.BlockSpec(array.shape, whole)
+    hbm = pl.BlockSpec(memory_space=pl.ANY)
     shapes = (
-        ((1, units), F32),
-        ((tok_count, width), F32),
-        ((width, tok_count), BF16),
-        ((tok_count, width), BF16),
-        ((8, width), F32),
-        ((half, depth, tok_count), BF16),
-    ) + (((depth, tok_count), BF16, hbm_shape),) * half
+        (
+            ((1, units), F32),
+            ((tok_count, width), F32),
+            ((width, tok_count), BF16),
+            ((tok_count, width), BF16),
+            ((8, width), F32),
+            ((8, width), F32),
+            ((half, depth_out, tok_count), BF16),
+            ((half, depth, tok_count), BF16),
+        )
+        + (((depth_out, tok_count), BF16, hbm_shape),) * half
+        + (((depth, tok_count), BF16, hbm_shape),) * half
+    )
     return pl.pallas_call(
-        feed_back_kernel,
+        functools.partial(feed_back_kernel, half),
         out_shape=[make_shape(*item) for item in shapes],
         grid_spec=pltpu.PrefetchScalarGridSpec(
             num_scalar_prefetch=0,
             grid=(units // tile,),
             in_specs=[
                 smem_spec(),
-                pl.BlockSpec((tok_count, width), whole),
-                pl.BlockSpec((tok_count, width), whole),
+                fixed(own),
+                fixed(pooled_all),
+                fixed(place),
+                fixed(target),
+                fixed(labels),
+                fixed(label_cols),
+                fixed(normed_two),
+                fixed(rstd_two),
+                fixed(gain_two),
                 pl.BlockSpec((tile, width), lambda step: (step, 0)),
                 pl.BlockSpec((width, tile), lambda step: (0, step)),
                 pl.BlockSpec((tok_count, tile), lambda step: (0, step)),
-                pl.BlockSpec((tok_count, width), whole),
-                pl.BlockSpec((tok_count, 1), whole),
-                pl.BlockSpec((1, width), whole),
-                pl.BlockSpec((width, width), whole),
+                hbm,
+                fixed(rstd),
+                fixed(gain),
+                hbm,
             ],
             out_specs=[
                 pl.BlockSpec((1, tile), lambda step: (0, step)),
@@ -668,18 +712,44 @@
                 pl.BlockSpec((width, tok_count), whole),
                 pl.BlockSpec((tok_count, width), whole),
                 pl.BlockSpec((8, width), whole),
+                pl.BlockSpec((8, width), whole),
+                pl.BlockSpec((half, depth_out, tok_count), lambda step: (0, 0, 0)),
                 pl.BlockSpec((count // 2, depth, tok_count), lambda step: (step, 0, 0)),
             ]
+            + [pl.BlockSpec((depth_out, tok_count), whole)] * half
             + [pl.BlockSpec((depth, tok_count), whole)] * half,
             scratch_shapes=[
+                pltpu.VMEM((wide_count, depth_out, tok_count), BF16),
                 pltpu.VMEM((count, depth, tok_count), BF16),
+                pltpu.VMEM((tok_count, width), BF16),
                 pltpu.VMEM((tok_count, width), F32),
+                pltpu.VMEM((tok_count, width), F32),
+                pltpu.VMEM(w_o.shape, BF16),
+                pltpu.SemaphoreType.DMA((2,)),
             ],
         ),
-        cost_estimate=cost(10),
+        cost_estimate=cost(14),
         compiler_params=params(1),
         name="feed_back",
-    )(me, d_ffn, d_res, w_out, w_in, slope, normed, rstd, gain, w_o)
+    )(
+        me,
+        own,
+        pooled_all,
+        place,
+        target,
+        labels,
+        label_cols,
+        normed_two,
+        rstd_two,
+        gain_two,
+        w_out,
+        w_in,
+        slope,
+        normed,
+        rstd,
+        gain,
+        w_o,
+    )
 
 
 def attend_back_kernel(
@@ -936,9 +1006,9 @@
     )(me, *halves[0], *halves[1])
 
 
-def piece_kernel(turned, me_ref, *refs):
-    outs, held = refs[4:-1], refs[-1]
-    count = len(outs)
+def piece_kernel(turned, stacked, me_ref, *refs):
+    outs, held = (refs[4:], refs[4]) if stacked else (refs[4:-1], refs[-1])
+    count = held.shape[0]
     depth = held.shape[1] if turned else held.shape[2]
     for half in range(2):
         total = add_low(refs[2 * half][0], refs[2 * half + 1][0])
@@ -947,20 +1017,23 @@
         for index in range(count // 2):
             span = slice(index * depth, (index + 1) * depth)
             held[half * (count // 2) + index] = total[span, :] if turned else total[:, span]
-    for step in range(count):
-        outs[step][...] = held[me_ref[0] ^ step]
-
-
-def narrow_pieces(me, halves, narrow_count, turned):
+    if not stacked:
+        for step in range(count):
+            outs[step][...] = held[me_ref[0] ^ step]
+
+
+def narrow_pieces(me, halves, narrow_count, turned, stacked):
     _, rows, columns = halves[0][0].shape
     depth = 2 * columns // narrow_count
     shape = (depth, rows) if turned else (rows, depth)
+    whole = (narrow_count,) + shape
+    outs = [hbm_shape(whole, BF16)] if stacked else [hbm_shape(shape, BF16)] * narrow_count
     return pl.pallas_call(
-        functools.partial(piece_kernel, turned),
-        out_shape=[hbm_shape(shape, BF16)] * narrow_count,
+        functools.partial(piece_kernel, turned, stacked),
+        out_shape=outs,
         in_specs=[smem_spec()] + [vmem_spec()] * 4,
-        out_specs=[vmem_spec()] * narrow_count,
-        scratch_shapes=[pltpu.VMEM((narrow_count,) + shape, BF16)],
+        out_specs=[vmem_spec()] * len(outs),
+        scratch_shapes=[] if stacked else [pltpu.VMEM(whole, BF16)],
         cost_estimate=cost(1),
         compiler_params=params(),
         name="narrow_pieces",
@@ -968,9 +1041,12 @@
 
 
 def sum_kernel(count, *refs):
-    total = refs[0][...].astype(F32)
-    for ref in refs[1:count]:
-        total = total + ref[...].astype(F32)
+    terms = [ref[...] for ref in refs[:count]]
+    if len(terms[0].shape) == 3:
+        terms = [terms[0][place] for place in range(terms[0].shape[0])]
+    total = terms[0].astype(F32)
+    for term in terms[1:]:
+        total = total + term.astype(F32)
     start = 0
     for out_ref in refs[count:]:
         out_ref[...] = total[:, start : start + out_ref.shape[1]]
@@ -978,7 +1054,7 @@
 
 
 def sum_pieces(pieces, cuts=None):
-    shape = pieces[0].shape
+    shape = pieces[0].shape[-2:]
     outs = [jax.ShapeDtypeStruct((shape[0], cut), F32) for cut in cuts or (shape[1],)]
     return pl.pallas_call(
         functools.partial(sum_kernel, len(pieces)),
@@ -1075,10 +1151,10 @@
     def gate(self, *others):
         self.kept[0] = after(self.kept[0], *others)
 
-    def finish(self, me_narrow, narrow_count, turned):
+    def finish(self, me_narrow, narrow_count, turned, stacked=False):
         while self.level < len(self.orders[0]):
             self.step()
-        return narrow_pieces(me_narrow, self.halves(), narrow_count, turned)
+        return narrow_pieces(me_narrow, self.halves(), narrow_count, turned, stacked)
 
 
 def hop(values, axis, bit):
@@ -1143,7 +1219,14 @@
         pooled_copies, "wide", split_axis=0, concat_axis=0, tiled=True
     ).reshape(wide_count * kept_rows * SEG_ROW, width)
     similarity = cosine_pairs(first, second, pooled_all).reshape(-1)
-    d_res_two, d_ffn, sums_two, own_out, *send_out = loss_back(
+    bits = wide_count.bit_length() - 1
+    middle = 1 + (bits - 1) // 2
+    low_first = list(range(1, bits))
+    high_first = list(range(middle, bits)) + list(range(1, middle))
+    orders = (low_first, high_first)
+    first_bits = (low_first[0], high_first[0])
+    half = wide_count // 2
+    sum_b_in, d_one, d_attn_t, d_ctx, sums_one, sums_two, own_out, own_in, *sends = feed_back(
         me_line,
         pooled,
         pooled_all,
@@ -1154,34 +1237,6 @@
         norm_two,
         rstd_two,
         line(gain_two),
-        wide_count,
-    )
-
-    bits = wide_count.bit_length() - 1
-    middle = 1 + (bits - 1) // 2
-    low_first = list(range(1, bits))
-    high_first = list(range(middle, bits)) + list(range(1, middle))
-    orders = (low_first, high_first)
-    first_bits = (low_first[0], high_first[0])
-    rows_out = own_out.shape[1]
-    fold_out = Folding(
-        me_line,
-        grad_terms(
-            me_line,
-            own_out,
-            to_partner(send_out),
-            [(act, None)],
-            [(act_recv, None)],
-            ((0, rows_out),),
-            *first_bits,
-            512,
-        ),
-        orders,
-    )
-    sum_b_in, d_one, d_attn_t, d_ctx, sums_one, own_in, *send_in = feed_back(
-        me_line,
-        after(d_ffn, *fold_out.sent),
-        d_res_two,
         w_out,
         w_in,
         slope,
@@ -1191,38 +1246,49 @@
         w_o,
         wide_count,
     )
+    rows_out = own_out.shape[1]
     rows_in = own_in.shape[1]
-    recv_in = to_partner(send_in)
-    fold_out.step()
-    pieces_out = fold_out.finish(me_narrow, narrow_count, False)
-    fold_in = Folding(
+    recv_out = to_partner(sends[:half])
+    recv_in = to_partner(sends[half:])
+    fold_out = Folding(
         me_line,
         grad_terms(
             me_line,
-            own_in,
-            after(tuple(recv_in), *fold_out.sent),
-            [(stack, 2)],
-            [(stack_recv, 2)],
-            ((0, rows_in),),
+            own_out,
+            recv_out,
+            [(act, None)],
+            [(act_recv, None)],
+            ((0, rows_out),),
             *first_bits,
-            width // 2,
+            512,
         ),
         orders,
-        tuple(pieces_out),
-    )
-    traded_out = trade(pieces_out)
+    )
+    outs_in = grad_terms(
+        me_line,
+        own_in,
+        after(tuple(recv_in), *fold_out.sent),
+        [(stack, 2)],
+        [(stack_recv, 2)],
+        ((0, rows_in),),
+        *first_bits,
+        width // 2,
+    )
+    fold_out.gate(similarity, *outs_in)
+    fold_out.step()
+    fold_in = Folding(me_line, outs_in, orders, *fold_out.sent)
     d_rows, sums_qkv, own_mix, *send_mix = attend_back(
         sources,
         me_line,
         proj,
         probs,
-        after(d_ctx, tuple(pieces_out), *fold_in.sent),
+        after(d_ctx, *fold_out.sent, *fold_in.sent),
         d_one,
         w_qkv,
         d_attn_t,
         wide_count,
     )
-    recv_mix = to_partner(after(tuple(send_mix), tuple(traded_out)))
+    recv_mix = to_partner(send_mix)
     vectors = pack_vectors(
         (sums_qkv, sums_one, sum_b_in, sums_two),
         (
@@ -1237,8 +1303,11 @@
             (3, 1, 0, width),
         ),
     )
-    fold_in.gate(d_rows, tuple(traded_out))
+    fold_in.gate(d_rows, *fold_out.received)
     fold_in.step()
+    fold_out.gate(d_rows)
+    pieces_out = fold_out.finish(me_narrow, narrow_count, False)
+    traded_out = trade(pieces_out)
     home = lax.all_to_all(
         after(d_rows, *fold_in.sent), "wide", split_axis=0, concat_axis=0, tiled=True
     )
@@ -1249,22 +1318,21 @@
     outs_mix = grad_terms(
         me_line,
         own_mix,
-        after(tuple(recv_mix), *fold_in.sent),
+        after(tuple(recv_mix), tuple(pieces_out), *fold_in.sent),
         [(stack, 0), (stack, 1)],
         [(stack_recv, 0), (stack_recv, 1)],
         ((0, cols_qkv), (cols_qkv, rows_mix)),
         *first_bits,
         width // 2,
     )
-    vectors = hop(after(vectors, *outs_mix), "wide", 0)
+    vectors = hop(vectors, "wide", 0)
     vectors = hop(vectors, "narrow", 0)
     fold_mix = Folding(
         me_line,
         outs_mix,
         orders,
         vectors,
-        grad_w_out,
-        similarity,
+        tuple(traded_out),
         *fold_in.received,
     )
     grad_tokens = home_rows(destination, home)
@@ -1272,15 +1340,18 @@
     traded_in = trade(pieces_in)
     fold_mix.gate(grad_tokens, tuple(traded_in))
     fold_mix.step()
+    vectors = after(vectors, *fold_mix.sent)
     for bit in range(1, narrow_count.bit_length() - 1):
         vectors = hop(vectors, "narrow", bit)
     (grad_w_in,) = sum_pieces(traded_in)
     fold_mix.gate(vectors)
-    pieces_mix = fold_mix.finish(me_narrow, narrow_count, True)
+    (pieces_mix,) = fold_mix.finish(me_narrow, narrow_count, True, True)
+    traded_mix = lax.all_to_all(pieces_mix, "narrow", split_axis=0, concat_axis=0, tiled=True)
+    vectors = after(vectors, pieces_mix)
     for bit in range(1, bits):
-        vectors = hop(vectors if bit > 1 else after(vectors, tuple(pieces_mix)), "wide", bit)
+        vectors = hop(vectors, "wide", bit)
     grad_w_qkv, grad_w_o = sum_pieces(
-        after(tuple(trade(pieces_mix)), vectors), (cols_qkv, rows_mix - cols_qkv)
+        (after(traded_mix, vectors),), (cols_qkv, rows_mix - cols_qkv)
     )
     vectors = vectors.reshape(-1)
     cuts = (2 * width, width, width, width, units, width, width, width)

time: 241 us -> 239 us (level)
  Pallas kernels: 125 us -> 121 us
    ppermute x31, waiting for transfers between devices: 9.62 us -> 17.3 us  [swap(): return lax.ppermute(values, axis, [(i, i ^ 1 << bit) for i in range(count)])]
    ppermute x9 -> x6, waiting for transfers between devices: 13.4 us -> 7.13 us  [trade(): lax.ppermute(pieces[step], 'narrow', [(i, i ^ step) for i in range(count)])]
    ppermute x9 -> x6, starting transfers between devices: 13.2 us -> 8.89 us  [trade(): lax.ppermute(pieces[step], 'narrow', [(i, i ^ step) for i in range(count)])]
    pallas_call x5 -> x4, Pallas kernels: 29.4 us -> 25.2 us  [the longest x1 18.4 us: feed_back(): pl.pallas_call(functools.partial(feed_back_kernel, half), out_shape=[make...]
    all_to_all x0 -> x1, starting transfers between devices: none -> 4.19 us  [on_device(): lax.all_to_all(pieces_mix, 'narrow', split_axis=0, concat_axis=0, tiled=T...]
  transfers between devices with their start and end apart: 43 -> 41, of which waited for: 13 -> 15; matrix products, arithmetic and copies ran while one was open for 6% -> 6% of each run, Pallas kernels for 34% -> 33%
where the time goes in v4:
time: 239 us; the launch traced here: 236 us
  Pallas kernels  121 us (51%)
  starting transfers between devices  49.8 us (21%)
  waiting for transfers between devices  49.2 us (21%)
  local copies, waits for them, and re-layouts  8.53 us (4%)
  other arithmetic  7.11 us (3%)
    pallas_call x3, Pallas kernels, grad_terms(): pl.pallas_call(functools.partial(grad_kernel, first_bit, second_bit, span...  25.1 us
    ppermute x31, starting transfers between devices, swap(): return lax.ppermute(values, axis, [(i, i ^ 1 << bit) for i in range(count)])  22.2 us
    all_to_all x1, waiting for transfers between devices, on_device(): got = lax.all_to_all(sent, 'wide', split_axis=0, concat_axis=0, tiled=True)  19.1 us
    pallas_call x1, Pallas kernels, feed_back(): pl.pallas_call(functools.partial(feed_back_kernel, half), out_shape=[make...  18.4 us
    ppermute x31, waiting for transfers between devices, swap(): return lax.ppermute(values, axis, [(i, i ^ 1 << bit) for i in range(count)])  17.3 us
    pallas_call x1, Pallas kernels, attend_back(): pl.pallas_call(attend_back_kernel, out_shape=[make_shape(*item) for item...  16.7 us
    pallas_call x1, Pallas kernels, feed_forward(): pl.pallas_call(feed_kernel, out_shape=[make_shape(*item) for item in shap...  14.6 us
    pallas_call x1, Pallas kernels, attend_forward(): pl.pallas_call(attend_kernel, out_shape=[make_shape(*item) for item in sh...  13.1 us
  transfers between devices with their start and end apart: 41, of which 15 were waited for; matrix products, arithmetic and copies ran while one was open for 6% of the time, Pallas kernels for 33%

profile of v4, /device:TPU:0, one launch (start us, length us, event | category | flops | bytes accessed | tf_op | source)
XLA Modules:
  0.0 236.1 jit_solution(15325550349883402081)
XLA Ops:
  0.6 3.5 %build_send.1 = bf16[8,144,768]{2,1,0:T(8,128)(2,1)} custom-call(s32[8]{0:T(128)} %dest_ref.3, s32[2,32]{1,0:T(2,128)} %bitcast.26, f32[1,32]{1,0:T(1,128)} %bitcast.27, bf16[8,128,768]{2,1,0:T(8,128)(2,1)} %tok_ref.1, s32[8,128]{1,0:T(8,128)} %seg_ref.1), custom_call_target="tpu_custom_call" | custom-call | bytes 9000000 | tf_op jit(solution)/shard_map/build_send/pallas_call | solution.py:126
  4.2 5.7 %all-to-all-start = ((bf16[8,144,768]{2,1,0:T(8,128)(2,1)}), bf16[8,144,768]{2,1,0:T(8,128)(2,1)}, u32[]{:S(2)}, u32[]{:S(2)}) async-start(bf16[8,144,768]{2,1,0:T(8,128)(2,1)} %build_send.1), calls=%async_computation | async-start | bytes 3538944 | tf_op jit(solution)/shard_map/all_to_all | solution.py:1194
  10.0 0.6 reshape.84.bias_ref
  14.1 19.1 %all-to-all-done.got_ref = bf16[8,144,768]{2,1,0:T(8,128)(2,1)} async-done(((bf16[8,144,768]{2,1,0:T(8,128)(2,1)}), bf16[8,144,768]{2,1,0:T(8,128)(2,1)}, u32[]{:S(2)}, u32[]{:S(2)}) %all-to-all-start) | async-done | bytes 1769504 | tf_op jit(solution)/shard_map/all_to_all | solution.py:1194
  33.1 13.1 %attend_forward.1 = (bf16[3,512,768]{2,1,0:T(8,128)(2,1)}, bf16[512,2304]{1,0:T(8,128)(2,1)}, bf16[4,6,256,128]{3,2,1,0:T(8,128)(2,1)}, f32[512,768]{1,0:T(8,128...) custom-call(bf16[8,144,768]{2,1,0:T(8,128)(2,1)} %all-to-all-done.go, ...), custom_call_target="tpu_custom_call" | custom-call | bytes 24000000 | tf_op jit(solution)/shard_map/attend_forward/pallas_call | solution.py:240
  46.2 14.6 %feed_forward.1 = (bf16[512,3072]{1,0:T(8,128)(2,1)}, bf16[512,3072]{1,0:T(8,128)(2,1)}, bf16[512,768]{1,0:T(8,128)(2,1)}, f32[512,768]{1,0:T(8,128)}, f32[512,1...) custom-call(bf16[3,512,768]{2,1,0:T(8,128)(2,1)} %get-tuple-element.115.low_ref.refs_4_.refs_5_, ...), custom_call_target="tpu_custom_call" | custom-call | bytes 30000000 | tf_op jit(solution)/shard_map/feed_forward/pallas_call | solution.py:327
  61.4 4.3 %all-to-all-start.1 = ((bf16[8,32,768]{2,1,0:T(8,128)(2,1)}), bf16[8,32,768]{2,1,0:T(8,128)(2,1)}, u32[]{:S(2)}, u32[]{:S(2)}) async-start(bf16[8,32,768]{2,1,0:T(8,128)(2,1)} %get-tuple-element.122), calls=%async_computation.1 | async-start | bytes 786432 | tf_op jit(solution)/shard_map/all_to_all | solution.py:1218
  65.7 1.4 copy.33.pair_ref
  67.0 1.8 route.1
  68.9 5.0 %all-to-all-done.1 = bf16[8,32,768]{2,1,0:T(8,128)(2,1)} async-done(((bf16[8,32,768]{2,1,0:T(8,128)(2,1)}), bf16[8,32,768]{2,1,0:T(8,128)(2,1)}, u32[]{:S(2)}, u32[]{:S(2)}) %all-to-all-start.1) | async-done | bytes 393248 | tf_op jit(solution)/shard_map/all_to_all | solution.py:1218
  73.8 18.4 %feed_back.1 = (f32[1,3072]{1,0:T(1,128)}, f32[512,768]{1,0:T(8,128)}, bf16[768,512]{1,0:T(8,128)(2,1)}, bf16[512,768]{1,0:T(8,128)(2,1)}, f32[8,768]{1,0:T(8,12...) custom-call(s32[1]{0:T(128)} %bitcast.4.me_ref, ...), custom_call_target="tpu_custom_call" | custom-call | bytes 42000000 | tf_op jit(solution)/shard_map/feed_back/pallas_call | solution.py:684
  92.8 1.1 collective-permute-done.refs_0_
  94.4 1.7 collective-permute-done.2.refs_2_
  96.3 1.5 collective-permute-done.3.refs_3_
  97.8 8.0 %grad_terms.3 = (bf16[2,96,1536]{2,1,0:T(8,128)(2,1)}, bf16[2,96,1536]{2,1,0:T(8,128)(2,1)}, bf16[2,96,1536]{2,1,0:T(8,128)(2,1)}, bf16[2,96,1536]{2,1,0:T(8,128)(2,1)}) custom-call(s32[1]{0:T(128)} %bitcast.4.me_ref, bf16[4,96,512]{2,1,0:T(8,128)(2,1)} %get-tuple-element.136.own_ref, bf16[96,512]{1,0:T(8,128)(2,1)} %collective-permute-done.refs_0_, ...), custom_call_target="tpu_custom_call" | custom-call | bytes 21000000 | tf_op jit(solution)/shard_map/grad_terms/pallas_call | solution.py:961
  107.4 2.0 cosine_pairs.1
  109.4 1.3 reduce
  110.7 8.2 %grad_terms.4 = (bf16[2,384,384]{2,1,0:T(8,128)(2,1)}, bf16[2,384,384]{2,1,0:T(8,128)(2,1)}, bf16[2,384,384]{2,1,0:T(8,128)(2,1)}, bf16[2,384,384]{2,1,0:T(8,128)(2,1)}) custom-call(s32[1]{0:T(128)} %bitcast.4.me_ref, bf16[4,384,512]{2,1,0:T(8,128)(2,1)} %get-tuple-element.143.own_ref, bf16[384,512]{1,0:T(8,128)(2,1)} %collective-permute-done.5.refs_0_, ...), custom_call_target="tpu_custom_call" | custom-call | bytes 21000000 | tf_op jit(solution)/shard_map/grad_terms/pallas_call | solution.py:961
  119.0 2.5 %collective-permute-done.10.refs_1_ = bf16[2,96,1536]{2,1,0:T(8,128)(2,1)} collective-permute-done((bf16[2,96,1536]{2,1,0:T(8,128)(2,1)}, bf16[2,96,1536]{2,1,0:T(8,128)(2,1)}, u32[]{:S(2)}, u32[]{:S(2)}) %collective-permute-start.10) | collective-permute-done | bytes 589856 | tf_op jit(solution)/shard_map/ppermute | solution.py:1094
  121.7 2.8 %fold.3 = (bf16[1,96,1536]{2,1,0:T(8,128)(2,1)}, bf16[1,96,1536]{2,1,0:T(8,128)(2,1)}, bf16[1,96,1536]{2,1,0:T(8,128)(2,1)}, bf16[1,96,1536]{2,1,0:T(8,128)(2,1)}) custom-call(s32[1]{0:T(128)} %bitcast.4.me_ref, bf16[2,96,1536]{2,1,0:T(8,128)(2,1)} %get-tuple-element.158.refs_0_, bf16[2,96,1536]{2,1,0:T(8,128)(2,1)} %collective-permute-done.10.refs_1_, ...), custom_call_target="tpu_custom_call" | custom-call | bytes 1500000 | tf_op jit(solution)/shard_map/fold/pallas_call | solution.py:998
  124.5 1.5 collective-permute-start.14
  126.5 1.5 collective-permute-start.12
  128.6 16.7 %attend_back.1 = (bf16[8,128,768]{2,1,0:T(8,128)(2,1)}, f32[1,2304]{1,0:T(1,128)}, bf16[4,384,512]{2,1,0:T(8,128)(2,1)}, bf16[384,512]{1,0:T(8,128)(2,1)}, bf16[...) custom-call(s32[4]{0:T(128)} %get-tuple-element.123.source_ref, s32[1]{0:T(128)} %bitcast.4.me_ref, ...), custom_call_target="tpu_custom_call" | custom-call | bytes 60000000 | tf_op jit(solution)/shard_map/attend_back/pallas_call | solution.py:831
  145.3 1.3 collective-permute-done.12.refs_1_
  146.6 2.7 %fold.4 = (bf16[1,384,384]{2,1,0:T(8,128)(2,1)}, bf16[1,384,384]{2,1,0:T(8,128)(2,1)}, bf16[1,384,384]{2,1,0:T(8,128)(2,1)}, bf16[1,384,384]{2,1,0:T(8,128)(2,1)}) custom-call(s32[1]{0:T(128)} %bitcast.4.me_ref, bf16[2,384,384]{2,1,0:T(8,128)(2,1)} %get-tuple-element.166.refs_0_, bf16[2,384,384]{2,1,0:T(8,128)(2,1)} %collective-permute-done.14.refs_1_, ...), custom_call_target="tpu_custom_call" | custom-call | bytes 1500000 | tf_op jit(solution)/shard_map/fold/pallas_call | solution.py:998
  149.3 4.5 %all-to-all-start.2 = ((bf16[8,128,768]{2,1,0:T(8,128)(2,1)}), bf16[8,128,768]{2,1,0:T(8,128)(2,1)}, u32[]{:S(2)}, u32[]{:S(2)}) async-start(bf16[8,128,768]{2,1,0:T(8,128)(2,1)} %get-tuple-element.171), calls=%async_computation.2 | async-start | bytes 3145728 | tf_op jit(solution)/shard_map/all_to_all | solution.py:1311
  154.9 1.4 pack_vectors.1
  156.4 1.3 collective-permute-done.25
  157.8 0.8 add.15
  158.5 0.6 copy-done
  159.2 1.9 collective-permute-start.26
  161.0 2.1 collective-permute-done.26
  163.7 1.6 collective-permute-start.20
  165.4 1.5 collective-permute-start.21
  166.8 2.3 narrow_pieces.3
  169.1 1.9 collective-permute-start.27
  171.0 2.5 %collective-permute-start.28 = (bf16[96,768]{1,0:T(8,128)(2,1)}, bf16[96,768]{1,0:T(8,128)(2,1)}, u32[]{:S(2)}, u32[]{:S(2)}) collective-permute-start(bf16[96,768]{1,0:T(8,128)(2,1)} %get-tuple-element.182), channel_id=1, source_target_pairs={{0,2},{1,3},{2,0},{3,1},{4,6},{5,7},{6,4},{7,5},{8,10},{9,11},{10,... | collective-permute-start | bytes 442376 | tf_op jit(solution)/shard_map/ppermute | solution.py:1101
  173.5 1.4 add.16
  174.9 8.9 %grad_terms.5 = (bf16[2,384,384]{2,1,0:T(8,128)(2,1)}, bf16[2,384,384]{2,1,0:T(8,128)(2,1)}, bf16[2,384,384]{2,1,0:T(8,128)(2,1)}, bf16[2,384,384]{2,1,0:T(8,128)(2,1)}) custom-call(s32[1]{0:T(128)} %bitcast.4.me_ref, bf16[4,384,512]{2,1,0:T(8,128)(2,1)} %get-tuple-element.172.own_ref, bf16[384,512]{1,0:T(8,128)(2,1)} %collective-permute-done.16.refs_0_, ...), custom_call_target="tpu_custom_call" | custom-call | bytes 21000000 | tf_op jit(solution)/shard_map/grad_terms/pallas_call | solution.py:961
  183.8 0.6 collective-permute-done.28.refs_2_
  184.5 0.6 collective-permute-start.30
  185.5 2.3 narrow_pieces.4
  187.7 2.1 collective-permute-start.22
  189.8 1.6 collective-permute-start.23
  191.5 0.8 collective-permute-start.24
  192.2 3.3 %home_rows.1 = bf16[8,128,768]{2,1,0:T(8,128)(2,1)} custom-call(s32[8]{0:T(128)} %dest_ref.3, bf16[8,128,768]{2,1,0:T(8,128)(2,1)} %all-to-all-done.2.rows_ref), custom_call_target="tpu_custom_call" | custom-call | bytes 9000000 | tf_op jit(solution)/shard_map/home_rows/pallas_call | solution.py:882
  195.6 6.5 %collective-permute-done.23.refs_2_ = bf16[192,384]{1,0:T(8,128)(2,1)} collective-permute-done((bf16[192,384]{1,0:T(8,128)(2,1)}, bf16[192,384]{1,0:T(8,128)(2,1)}, u32[]{:S(2)}, u32[]{:S(2)}) %collective-permute-start.23) | collective-permute-done | bytes 147488 | tf_op jit(solution)/shard_map/ppermute | solution.py:1101
  202.1 2.7 %fold.5 = (bf16[1,384,384]{2,1,0:T(8,128)(2,1)}, bf16[1,384,384]{2,1,0:T(8,128)(2,1)}, bf16[1,384,384]{2,1,0:T(8,128)(2,1)}, bf16[1,384,384]{2,1,0:T(8,128)(2,1)}) custom-call(s32[1]{0:T(128)} %bitcast.4.me_ref, bf16[2,384,384]{2,1,0:T(8,128)(2,1)} %get-tuple-element.195.refs_0_, bf16[2,384,384]{2,1,0:T(8,128)(2,1)} %collective-permute-done.30.refs_1_, ...), custom_call_target="tpu_custom_call" | custom-call | bytes 1500000 | tf_op jit(solution)/shard_map/fold/pallas_call | solution.py:998
  204.8 1.6 collective-permute-start.33
  206.4 1.5 collective-permute-start.34
  207.9 3.0 %collective-permute-start.32 = (f32[72,128]{1,0:T(8,128)}, f32[72,128]{1,0:T(8,128)S(1)}, u32[]{:S(2)}, u32[]{:S(2)}) collective-permute-start(f32[72,128]{1,0:T(8,128)} %add.16), channel_id=1, source_target_pairs={{0,2},{1,3},{2,0},{3,1},{4,6},{5,7},{6,4},{7,5},{8,10},{9,11},{10,... | collective-permute-start | bytes 110600 | tf_op jit(solution)/shard_map/ppermute | solution.py:1094
  210.9 2.1 collective-permute-done.32
  213.1 1.4 add.17
  214.5 2.3 narrow_pieces.5
  216.7 4.2 %all-to-all-start.3 = ((bf16[4,192,384]{2,1,0:T(8,128)(2,1)}), bf16[4,192,384]{2,1,0:T(8,128)(2,1)}, u32[]{:S(2)}, u32[]{:S(2)}) async-start(bf16[4,192,384]{2,1,0:T(8,128)(2,1)} %narrow_pieces.5), calls=%async_computation.3 | async-start | bytes 1179648 | tf_op jit(solution)/shard_map/all_to_all | solution.py:1349
  220.9 0.9 collective-permute-start.35
  221.8 3.4 %collective-permute-done.35 = f32[72,128]{1,0:T(8,128)S(1)} collective-permute-done((f32[72,128]{1,0:T(8,128)}, f32[72,128]{1,0:T(8,128)S(1)}, u32[]{:S(2)}, u32[]{:S(2)}) %collective-permute-start.35) | collective-permute-done | bytes 36896 | tf_op jit(solution)/shard_map/ppermute | solution.py:1094
  225.2 1.4 add.18
  227.1 1.9 sum_pieces.5
  229.0 1.9 sum_pieces.4
  230.9 0.8 add.19
  232.9 0.6 slice_bitcast_fusion.2
  233.5 0.7 all-to-all-done.3.refs_0_
  234.3 1.9 sum_pieces.3
  (77 shorter events, 12.5 us)
Async XLA Ops:
  4.1 5.8 %copy-start.2 = (f32[1536]{0:T(1024)S(1)}, f32[1536]{0:T(1024)}, u32[]{:S(2)}) copy-start(f32[1536]{0:T(1024)} %param.23) | copy-start | bytes 18436
  4.1 6.4 %copy-start.3 = (f32[768]{0:T(1024)S(1)}, f32[768]{0:T(1024)}, u32[]{:S(2)}) copy-start(f32[768]{0:T(1024)} %param.25) | copy-start | bytes 9220
  4.2 7.0 %copy-start.4 = (f32[768]{0:T(1024)S(1)}, f32[768]{0:T(1024)}, u32[]{:S(2)}) copy-start(f32[768]{0:T(1024)} %param.26) | copy-start | bytes 9220
  4.2 7.6 %copy-start.5 = (f32[768]{0:T(1024)S(1)}, f32[768]{0:T(1024)}, u32[]{:S(2)}) copy-start(f32[768]{0:T(1024)} %param.27) | copy-start | bytes 9220
  4.2 8.1 %copy-start.6 = (f32[768]{0:T(1024)S(1)}, f32[768]{0:T(1024)}, u32[]{:S(2)}) copy-start(f32[768]{0:T(1024)} %param.31) | copy-start | bytes 9220
  4.2 8.7 %copy-start.7 = (f32[768]{0:T(1024)S(1)}, f32[768]{0:T(1024)}, u32[]{:S(2)}) copy-start(f32[768]{0:T(1024)} %param.32) | copy-start | bytes 9220
  4.2 9.3 %copy-start.8 = (f32[768]{0:T(1024)S(1)}, f32[768]{0:T(1024)}, u32[]{:S(2)}) copy-start(f32[768]{0:T(1024)} %param.33) | copy-start | bytes 9220
  4.2 28.9 %all-to-all-start = ((bf16[8,144,768]{2,1,0:T(8,128)(2,1)}), bf16[8,144,768]{2,1,0:T(8,128)(2,1)}, u32[]{:S(2)}, u32[]{:S(2)}) async-start(bf16[8,144,768]{2,1,0:T(8,128)(2,1)} %build_send.1), calls=%async_computation | async-start | bytes 3538944 | tf_op jit(solution)/shard_map/all_to_all | solution.py:1194
  60.8 36.9 %collective-permute-start.4 = (bf16[512,3072]{1,0:T(8,128)(2,1)}, bf16[512,3072]{1,0:T(8,128)(2,1)}, u32[]{:S(2)}, u32[]{:S(2)}) collective-permute-start(bf16[512,3072]{1,0:T(8,128)(2,1)} %get-tuple-element.141.refs_4_), channel_id=1, source_target_pairs={{0,4},{4,0},{8,12},{12,8},{16,20},{20,16},{24,28},{28,24},{1,5},{5... | collective-permute-start | bytes 9437192 | tf_op jit(solution)/shard_map/ppermute | solution.py:1094
  60.9 49.8 %collective-permute-start.9 = (bf16[3,512,768]{2,1,0:T(8,128)(2,1)}, bf16[3,512,768]{2,1,0:T(8,128)(2,1)}, u32[]{:S(2)}, u32[]{:S(2)}) collective-permute-start(bf16[3,512,768]{2,1,0:T(8,128)(2,1)} %get-tuple-element.115.low_ref.refs_4_.refs_5_), channel_id=1, source_target_pairs={{0,4},{4,0},{8,12},{12,8},{16,20},{20,16},{24,28},{28,24},{1,5},{5... | collective-permute-start | bytes 7077896 | tf_op jit(solution)/shard_map/ppermute | solution.py:1094
  61.4 12.4 %all-to-all-start.1 = ((bf16[8,32,768]{2,1,0:T(8,128)(2,1)}), bf16[8,32,768]{2,1,0:T(8,128)(2,1)}, u32[]{:S(2)}, u32[]{:S(2)}) async-start(bf16[8,32,768]{2,1,0:T(8,128)(2,1)} %get-tuple-element.122), calls=%async_computation.1 | async-start | bytes 786432 | tf_op jit(solution)/shard_map/all_to_all | solution.py:1218
  92.2 1.7 collective-permute-start
  92.3 1.8 collective-permute-start.1
  92.8 14.1 %collective-permute-start.5 = (bf16[384,512]{1,0:T(8,128)(2,1)}, bf16[384,512]{1,0:T(8,128)(2,1)}, u32[]{:S(2)}, u32[]{:S(2)}) collective-permute-start(bf16[384,512]{1,0:T(8,128)(2,1)} %get-tuple-element.144), channel_id=1, source_target_pairs={{0,4},{4,0},{8,12},{12,8},{16,20},{20,16},{24,28},{28,24},{1,5},{5... | collective-permute-start | bytes 1179656 | tf_op jit(solution)/shard_map/ppermute | solution.py:1094
  93.9 13.0 %collective-permute-start.6 = (bf16[384,512]{1,0:T(8,128)(2,1)}, bf16[384,512]{1,0:T(8,128)(2,1)}, u32[]{:S(2)}, u32[]{:S(2)}) collective-permute-start(bf16[384,512]{1,0:T(8,128)(2,1)} %get-tuple-element.145), channel_id=1, source_target_pairs={{0,4},{4,0},{8,12},{12,8},{16,20},{20,16},{24,28},{28,24},{1,5},{5... | collective-permute-start | bytes 1179656 | tf_op jit(solution)/shard_map/ppermute | solution.py:1094
  94.1 2.0 collective-permute-start.2
  96.1 1.6 collective-permute-start.3
  105.7 15.7 %collective-permute-start.10 = (bf16[2,96,1536]{2,1,0:T(8,128)(2,1)}, bf16[2,96,1536]{2,1,0:T(8,128)(2,1)}, u32[]{:S(2)}, u32[]{:S(2)}) collective-permute-start(bf16[2,96,1536]{2,1,0:T(8,128)(2,1)} %get-tuple-element.148), channel_id=1, source_target_pairs={{0,8},{4,12},{8,0},{12,4},{16,24},{20,28},{24,16},{28,20},{1,9},{5... | collective-permute-start | bytes 1769480 | tf_op jit(solution)/shard_map/ppermute | solution.py:1094
  106.3 15.4 %collective-permute-start.11 = (bf16[2,96,1536]{2,1,0:T(8,128)(2,1)}, bf16[2,96,1536]{2,1,0:T(8,128)(2,1)}, u32[]{:S(2)}, u32[]{:S(2)}) collective-permute-start(bf16[2,96,1536]{2,1,0:T(8,128)(2,1)} %get-tuple-element.149), channel_id=1, source_target_pairs={{0,16},{4,20},{8,24},{12,28},{16,0},{20,4},{24,8},{28,12},{1,17},{... | collective-permute-start | bytes 1769480 | tf_op jit(solution)/shard_map/ppermute | solution.py:1094
  106.9 3.9 %collective-permute-start.7 = (bf16[384,512]{1,0:T(8,128)(2,1)}, bf16[384,512]{1,0:T(8,128)(2,1)}, u32[]{:S(2)}, u32[]{:S(2)}) collective-permute-start(bf16[384,512]{1,0:T(8,128)(2,1)} %get-tuple-element.146), channel_id=1, source_target_pairs={{0,4},{4,0},{8,12},{12,8},{16,20},{20,16},{24,28},{28,24},{1,5},{5... | collective-permute-start | bytes 1179656 | tf_op jit(solution)/shard_map/ppermute | solution.py:1094
  106.9 3.9 %collective-permute-start.8 = (bf16[384,512]{1,0:T(8,128)(2,1)}, bf16[384,512]{1,0:T(8,128)(2,1)}, u32[]{:S(2)}, u32[]{:S(2)}) collective-permute-start(bf16[384,512]{1,0:T(8,128)(2,1)} %get-tuple-element.147), channel_id=1, source_target_pairs={{0,4},{4,0},{8,12},{12,8},{16,20},{20,16},{24,28},{28,24},{1,5},{5... | collective-permute-start | bytes 1179656 | tf_op jit(solution)/shard_map/ppermute | solution.py:1094
  124.5 22.1 %collective-permute-start.14 = (bf16[2,384,384]{2,1,0:T(8,128)(2,1)}, bf16[2,384,384]{2,1,0:T(8,128)(2,1)}, u32[]{:S(2)}, u32[]{:S(2)}) collective-permute-start(bf16[2,384,384]{2,1,0:T(8,128)(2,1)} %get-tuple-element.167), channel_id=1, source_target_pairs={{0,8},{4,12},{8,0},{12,4},{16,24},{20,28},{24,16},{28,20},{1,9},{5... | collective-permute-start | bytes 1769480 | tf_op jit(solution)/shard_map/ppermute | solution.py:1094
  126.0 20.6 %collective-permute-start.15 = (bf16[2,384,384]{2,1,0:T(8,128)(2,1)}, bf16[2,384,384]{2,1,0:T(8,128)(2,1)}, u32[]{:S(2)}, u32[]{:S(2)}) collective-permute-start(bf16[2,384,384]{2,1,0:T(8,128)(2,1)} %get-tuple-element.168), channel_id=1, source_target_pairs={{0,16},{4,20},{8,24},{12,28},{16,0},{20,4},{24,8},{28,12},{1,17},{... | collective-permute-start | bytes 1769480 | tf_op jit(solution)/shard_map/ppermute | solution.py:1094
  126.5 20.1 %collective-permute-start.12 = (bf16[1,96,1536]{2,1,0:T(8,128)(2,1)}, bf16[1,96,1536]{2,1,0:T(8,128)(2,1)}, u32[]{:S(2)}, u32[]{:S(2)}) collective-permute-start(bf16[1,96,1536]{2,1,0:T(8,128)(2,1)} %get-tuple-element.160), channel_id=1, source_target_pairs={{0,16},{4,20},{8,24},{12,28},{16,0},{20,4},{24,8},{28,12},{1,17},{... | collective-permute-start | bytes 884744 | tf_op jit(solution)/shard_map/ppermute | solution.py:1094
  128.0 18.6 %collective-permute-start.13 = (bf16[1,96,1536]{2,1,0:T(8,128)(2,1)}, bf16[1,96,1536]{2,1,0:T(8,128)(2,1)}, u32[]{:S(2)}, u32[]{:S(2)}) collective-permute-start(bf16[1,96,1536]{2,1,0:T(8,128)(2,1)} %get-tuple-element.161), channel_id=1, source_target_pairs={{0,8},{4,12},{8,0},{12,4},{16,24},{20,28},{24,16},{28,20},{1,9},{5... | collective-permute-start | bytes 884744 | tf_op jit(solution)/shard_map/ppermute | solution.py:1094
  149.3 42.9 %all-to-all-start.2 = ((bf16[8,128,768]{2,1,0:T(8,128)(2,1)}), bf16[8,128,768]{2,1,0:T(8,128)(2,1)}, u32[]{:S(2)}, u32[]{:S(2)}) async-start(bf16[8,128,768]{2,1,0:T(8,128)(2,1)} %get-tuple-element.171), calls=%async_computation.2 | async-start | bytes 3145728 | tf_op jit(solution)/shard_map/all_to_all | solution.py:1311
  153.8 11.5 %collective-permute-start.16 = (bf16[384,512]{1,0:T(8,128)(2,1)}, bf16[384,512]{1,0:T(8,128)(2,1)}, u32[]{:S(2)}, u32[]{:S(2)}) collective-permute-start(bf16[384,512]{1,0:T(8,128)(2,1)} %get-tuple-element.173), channel_id=1, source_target_pairs={{0,4},{4,0},{8,12},{12,8},{16,20},{20,16},{24,28},{28,24},{1,5},{5... | collective-permute-start | bytes 1179656 | tf_op jit(solution)/shard_map/ppermute | solution.py:1094
  154.0 15.1 %collective-permute-start.17 = (bf16[384,512]{1,0:T(8,128)(2,1)}, bf16[384,512]{1,0:T(8,128)(2,1)}, u32[]{:S(2)}, u32[]{:S(2)}) collective-permute-start(bf16[384,512]{1,0:T(8,128)(2,1)} %get-tuple-element.174), channel_id=1, source_target_pairs={{0,4},{4,0},{8,12},{12,8},{16,20},{20,16},{24,28},{28,24},{1,5},{5... | collective-permute-start | bytes 1179656 | tf_op jit(solution)/shard_map/ppermute | solution.py:1094
  154.4 16.6 %collective-permute-start.18 = (bf16[384,512]{1,0:T(8,128)(2,1)}, bf16[384,512]{1,0:T(8,128)(2,1)}, u32[]{:S(2)}, u32[]{:S(2)}) collective-permute-start(bf16[384,512]{1,0:T(8,128)(2,1)} %get-tuple-element.175), channel_id=1, source_target_pairs={{0,4},{4,0},{8,12},{12,8},{16,20},{20,16},{24,28},{28,24},{1,5},{5... | collective-permute-start | bytes 1179656 | tf_op jit(solution)/shard_map/ppermute | solution.py:1094
  154.5 19.0 %collective-permute-start.19 = (bf16[384,512]{1,0:T(8,128)(2,1)}, bf16[384,512]{1,0:T(8,128)(2,1)}, u32[]{:S(2)}, u32[]{:S(2)}) collective-permute-start(bf16[384,512]{1,0:T(8,128)(2,1)} %get-tuple-element.176), channel_id=1, source_target_pairs={{0,4},{4,0},{8,12},{12,8},{16,20},{20,16},{24,28},{28,24},{1,5},{5... | collective-permute-start | bytes 1179656 | tf_op jit(solution)/shard_map/ppermute | solution.py:1094
  156.3 1.4 collective-permute-start.25
  158.5 0.6 copy-start
  159.2 4.0 %collective-permute-start.26 = (f32[72,128]{1,0:T(8,128)S(1)}, f32[72,128]{1,0:T(8,128)S(1)}, u32[]{:S(2)}, u32[]{:S(2)}) collective-permute-start(f32[72,128]{1,0:T(8,128)S(1)} %add.15), channel_id=1, source_target_pairs={{0,1},{1,0},{2,3},{3,2},{4,5},{5,4},{6,7},{7,6},{8,9},{9,8},{10,11... | collective-permute-start | bytes 110600 | tf_op jit(solution)/shard_map/ppermute | solution.py:1094
  163.1 0.6 copy-start.1
  163.7 20.7 %collective-permute-start.20 = (bf16[1,384,384]{2,1,0:T(8,128)(2,1)}, bf16[1,384,384]{2,1,0:T(8,128)(2,1)}, u32[]{:S(2)}, u32[]{:S(2)}) collective-permute-start(bf16[1,384,384]{2,1,0:T(8,128)(2,1)} %get-tuple-element.169), channel_id=1, source_target_pairs={{0,16},{4,20},{8,24},{12,28},{16,0},{20,4},{24,8},{28,12},{1,17},{... | collective-permute-start | bytes 884744 | tf_op jit(solution)/shard_map/ppermute | solution.py:1094
  165.4 19.1 %collective-permute-start.21 = (bf16[1,384,384]{2,1,0:T(8,128)(2,1)}, bf16[1,384,384]{2,1,0:T(8,128)(2,1)}, u32[]{:S(2)}, u32[]{:S(2)}) collective-permute-start(bf16[1,384,384]{2,1,0:T(8,128)(2,1)} %get-tuple-element.170), channel_id=1, source_target_pairs={{0,8},{4,12},{8,0},{12,4},{16,24},{20,28},{24,16},{28,20},{1,9},{5... | collective-permute-start | bytes 884744 | tf_op jit(solution)/shard_map/ppermute | solution.py:1094
  169.1 14.7 %collective-permute-start.27 = (bf16[96,768]{1,0:T(8,128)(2,1)}, bf16[96,768]{1,0:T(8,128)(2,1)}, u32[]{:S(2)}, u32[]{:S(2)}) collective-permute-start(bf16[96,768]{1,0:T(8,128)(2,1)} %get-tuple-element.181), channel_id=1, source_target_pairs={{0,1},{1,0},{2,3},{3,2},{4,5},{5,4},{6,7},{7,6},{8,9},{9,8},{10,11... | collective-permute-start | bytes 442376 | tf_op jit(solution)/shard_map/ppermute | solution.py:1101
  171.0 13.4 %collective-permute-start.28 = (bf16[96,768]{1,0:T(8,128)(2,1)}, bf16[96,768]{1,0:T(8,128)(2,1)}, u32[]{:S(2)}, u32[]{:S(2)}) collective-permute-start(bf16[96,768]{1,0:T(8,128)(2,1)} %get-tuple-element.182), channel_id=1, source_target_pairs={{0,2},{1,3},{2,0},{3,1},{4,6},{5,7},{6,4},{7,5},{8,10},{9,11},{10,... | collective-permute-start | bytes 442376 | tf_op jit(solution)/shard_map/ppermute | solution.py:1101
  173.5 11.0 %collective-permute-start.29 = (bf16[96,768]{1,0:T(8,128)(2,1)}, bf16[96,768]{1,0:T(8,128)(2,1)}, u32[]{:S(2)}, u32[]{:S(2)}) collective-permute-start(bf16[96,768]{1,0:T(8,128)(2,1)} %get-tuple-element.183), channel_id=1, source_target_pairs={{0,3},{1,2},{2,1},{3,0},{4,7},{5,6},{6,5},{7,4},{8,11},{9,10},{10,... | collective-permute-start | bytes 442376 | tf_op jit(solution)/shard_map/ppermute | solution.py:1101
  184.5 17.6 %collective-permute-start.30 = (bf16[2,384,384]{2,1,0:T(8,128)(2,1)}, bf16[2,384,384]{2,1,0:T(8,128)(2,1)}, u32[]{:S(2)}, u32[]{:S(2)}) collective-permute-start(bf16[2,384,384]{2,1,0:T(8,128)(2,1)} %get-tuple-element.201), channel_id=1, source_target_pairs={{0,8},{4,12},{8,0},{12,4},{16,24},{20,28},{24,16},{28,20},{1,9},{5... | collective-permute-start | bytes 1769480 | tf_op jit(solution)/shard_map/ppermute | solution.py:1094
  185.1 17.0 %collective-permute-start.31 = (bf16[2,384,384]{2,1,0:T(8,128)(2,1)}, bf16[2,384,384]{2,1,0:T(8,128)(2,1)}, u32[]{:S(2)}, u32[]{:S(2)}) collective-permute-start(bf16[2,384,384]{2,1,0:T(8,128)(2,1)} %get-tuple-element.204), channel_id=1, source_target_pairs={{0,16},{4,20},{8,24},{12,28},{16,0},{20,4},{24,8},{28,12},{1,17},{... | collective-permute-start | bytes 1769480 | tf_op jit(solution)/shard_map/ppermute | solution.py:1094
  187.7 7.8 %collective-permute-start.22 = (bf16[192,384]{1,0:T(8,128)(2,1)}, bf16[192,384]{1,0:T(8,128)(2,1)}, u32[]{:S(2)}, u32[]{:S(2)}) collective-permute-start(bf16[192,384]{1,0:T(8,128)(2,1)} %get-tuple-element.192), channel_id=1, source_target_pairs={{0,1},{1,0},{2,3},{3,2},{4,5},{5,4},{6,7},{7,6},{8,9},{9,8},{10,11... | collective-permute-start | bytes 442376 | tf_op jit(solution)/shard_map/ppermute | solution.py:1101
  189.8 12.2 %collective-permute-start.23 = (bf16[192,384]{1,0:T(8,128)(2,1)}, bf16[192,384]{1,0:T(8,128)(2,1)}, u32[]{:S(2)}, u32[]{:S(2)}) collective-permute-start(bf16[192,384]{1,0:T(8,128)(2,1)} %get-tuple-element.193), channel_id=1, source_target_pairs={{0,2},{1,3},{2,0},{3,1},{4,6},{5,7},{6,4},{7,5},{8,10},{9,11},{10,... | collective-permute-start | bytes 442376 | tf_op jit(solution)/shard_map/ppermute | solution.py:1101
  191.5 10.6 %collective-permute-start.24 = (bf16[192,384]{1,0:T(8,128)(2,1)}, bf16[192,384]{1,0:T(8,128)(2,1)}, u32[]{:S(2)}, u32[]{:S(2)}) collective-permute-start(bf16[192,384]{1,0:T(8,128)(2,1)} %get-tuple-element.194), channel_id=1, source_target_pairs={{0,3},{1,2},{2,1},{3,0},{4,7},{5,6},{6,5},{7,4},{8,11},{9,10},{10,... | collective-permute-start | bytes 442376 | tf_op jit(solution)/shard_map/ppermute | solution.py:1101
  204.8 9.7 %collective-permute-start.33 = (bf16[1,384,384]{2,1,0:T(8,128)(2,1)}, bf16[1,384,384]{2,1,0:T(8,128)(2,1)}, u32[]{:S(2)}, u32[]{:S(2)}) collective-permute-start(bf16[1,384,384]{2,1,0:T(8,128)(2,1)} %get-tuple-element.206), channel_id=1, source_target_pairs={{0,16},{4,20},{8,24},{12,28},{16,0},{20,4},{24,8},{28,12},{1,17},{... | collective-permute-start | bytes 884744 | tf_op jit(solution)/shard_map/ppermute | solution.py:1094
  206.4 8.1 %collective-permute-start.34 = (bf16[1,384,384]{2,1,0:T(8,128)(2,1)}, bf16[1,384,384]{2,1,0:T(8,128)(2,1)}, u32[]{:S(2)}, u32[]{:S(2)}) collective-permute-start(bf16[1,384,384]{2,1,0:T(8,128)(2,1)} %get-tuple-element.207), channel_id=1, source_target_pairs={{0,8},{4,12},{8,0},{12,4},{16,24},{20,28},{24,16},{28,20},{1,9},{5... | collective-permute-start | bytes 884744 | tf_op jit(solution)/shard_map/ppermute | solution.py:1094
  207.9 5.2 %collective-permute-start.32 = (f32[72,128]{1,0:T(8,128)}, f32[72,128]{1,0:T(8,128)S(1)}, u32[]{:S(2)}, u32[]{:S(2)}) collective-permute-start(f32[72,128]{1,0:T(8,128)} %add.16), channel_id=1, source_target_pairs={{0,2},{1,3},{2,0},{3,1},{4,6},{5,7},{6,4},{7,5},{8,10},{9,11},{10,... | collective-permute-start | bytes 110600 | tf_op jit(solution)/shard_map/ppermute | solution.py:1094
  216.7 17.5 %all-to-all-start.3 = ((bf16[4,192,384]{2,1,0:T(8,128)(2,1)}), bf16[4,192,384]{2,1,0:T(8,128)(2,1)}, u32[]{:S(2)}, u32[]{:S(2)}) async-start(bf16[4,192,384]{2,1,0:T(8,128)(2,1)} %narrow_pieces.5), calls=%async_computation.3 | async-start | bytes 1179648 | tf_op jit(solution)/shard_map/all_to_all | solution.py:1349
  220.9 4.2 %collective-permute-start.35 = (f32[72,128]{1,0:T(8,128)}, f32[72,128]{1,0:T(8,128)S(1)}, u32[]{:S(2)}, u32[]{:S(2)}) collective-permute-start(f32[72,128]{1,0:T(8,128)} %add.17), channel_id=1, source_target_pairs={{0,8},{4,12},{8,0},{12,4},{16,24},{20,28},{24,16},{28,20},{1,9},{5... | collective-permute-start | bytes 110600 | tf_op jit(solution)/shard_map/ppermute | solution.py:1094
  226.5 4.4 %collective-permute-start.36 = (f32[72,128]{1,0:T(8,128)}, f32[72,128]{1,0:T(8,128)}, u32[]{:S(2)}, u32[]{:S(2)}) collective-permute-start(f32[72,128]{1,0:T(8,128)} %add.18), channel_id=1, source_target_pairs={{0,16},{4,20},{8,24},{12,28},{16,0},{20,4},{24,8},{28,12},{1,17},{... | collective-permute-start | bytes 110600 | tf_op jit(solution)/shard_map/ppermute | solution.py:1094

commit v5 on v4

--- a/solution.py
+++ b/solution.py
@@ -135,49 +135,82 @@
     )(destination, pair_index.T, targets.reshape(1, -1), tokens, segments)
 
 
-def attend_kernel(
+def attend_body(
     got_ref,
-    wqkv_ref,
+    wqkv_src,
     bias_ref,
-    wo_ref,
+    wo_src,
     bo_ref,
     gain_ref,
     shift_ref,
-    stack_ref,
-    proj_ref,
-    probs_ref,
-    hid_ref,
-    norm_ref,
     rstd_ref,
     lab_ref,
     labcol_ref,
     meta_ref,
     source_ref,
+    stack_ref,
+    proj_ref,
+    probs_ref,
+    norm_ref,
+    hid_ref,
+    wqkv_ref,
+    wo_ref,
+    sems,
 ):
     x_ref, ctx_ref, low_ref = stack_ref.at[0], stack_ref.at[1], stack_ref.at[2]
     wide_count = got_ref.shape[0]
     tok_count, width = hid_ref.shape
     row_len = got_ref.shape[1] - META_ROWS
     kept_rows = tok_count // row_len
+    total_cols = proj_ref.shape[1]
+    parts = total_cols // width
+    get_meta = pltpu.make_async_copy(
+        got_ref.at[:, pl.ds(row_len, META_ROWS), pl.ds(0, LANES)], meta_ref, sems.at[0]
+    )
+    get_meta.start()
+    get_weights = []
+    for part in range(parts):
+        span = pl.ds(part * width, width)
+        get_weights.append(
+            pltpu.make_async_copy(
+                wqkv_src.at[:, span], wqkv_ref.at[:, span], sems.at[1 + part]
+            )
+        )
+    get_wo = pltpu.make_async_copy(wo_src, wo_ref, sems.at[1 + parts])
+    get_weights[0].start()
+    get_meta.wait()
     seen = jnp.int32(0)
     sources = [jnp.int32(0)] * kept_rows
     for slot in range(wide_count):
-        top = jnp.max(got_ref[slot, row_len : row_len + 1, :LANES].astype(F32))
-        live = top >= 0.0
+        live = jnp.max(meta_ref[slot, 0:1, :].astype(F32)) >= 0.0
         for row in range(kept_rows):
             sources[row] = jnp.where(live & (seen == row), slot, sources[row])
         seen = seen + live.astype(jnp.int32)
-    meta_ref[...] = got_ref[:, row_len:, :LANES]
+    get_rows = []
     for row in range(kept_rows):
         source_ref[row] = sources[row]
         span = pl.ds(row * row_len, row_len)
-        x_ref[span, :] = got_ref[sources[row], :row_len, :]
-        tag = got_ref[sources[row], row_len : row_len + 1, :LANES].astype(F32)
+        get_rows.append(
+            pltpu.make_async_copy(
+                got_ref.at[sources[row], pl.ds(0, row_len), :],
+                x_ref.at[span, :],
+                sems.at[2 + parts + row],
+            )
+        )
+        get_rows[row].start()
+    for copy in get_weights[1:] + [get_wo]:
+        copy.start()
+    for row in range(kept_rows):
+        span = pl.ds(row * row_len, row_len)
+        tag = meta_ref[sources[row], 0:1, :].astype(F32)
         lab_ref[row : row + 1, :] = tag
         labcol_ref[span, :] = jnp.broadcast_to(tag, (LANES, LANES)).T
-    total_cols = proj_ref.shape[1]
+    for copy in get_rows:
+        copy.wait()
     tile = 256
     for start in range(0, total_cols, tile):
+        if start % width == 0:
+            get_weights[start // width].wait()
         cols = slice(start, start + tile)
         proj_ref[:, cols] = (dot(x_ref[...], wqkv_ref[:, cols]) + bias_ref[:, cols]).astype(BF16)
 
@@ -208,6 +241,7 @@
         return carry
 
     lax.fori_loop(0, kept_rows, attend_row, 0)
+    get_wo.wait()
     for row in range(kept_rows):
         span = pl.ds(row * row_len, row_len)
         total = x_ref[span, :].astype(F32) + dot(ctx_ref[span, :], wo_ref[...]) + bo_ref[...]
@@ -221,68 +255,95 @@
         low_ref[span, :] = hidden.astype(BF16)
 
 
-def attend_forward(got, w_qkv, bias, w_o, b_o, gain, shift, kept_rows):
-    wide_count, slot_len, width = got.shape
-    row_len = slot_len - META_ROWS
-    tok_count = kept_rows * row_len
-    shapes = (
-        ((3, tok_count, width), BF16),
-        ((tok_count, 3 * width), BF16),
-        ((kept_rows, width // LANES, 2 * row_len, row_len), BF16),
-        ((tok_count, width), F32),
-        ((tok_count, width), F32),
-        ((tok_count, 1), F32),
-        ((8, LANES), F32),
-        ((tok_count, LANES), F32),
-        ((wide_count, META_ROWS, LANES), BF16),
-        ((kept_rows,), jnp.int32),
-    )
-    return pl.pallas_call(
-        attend_kernel,
-        out_shape=[make_shape(*item) for item in shapes],
-        in_specs=[vmem_spec()] * 7,
-        out_specs=[vmem_spec()] * (len(shapes) - 1) + [smem_spec()],
-        cost_estimate=cost(8),
-        compiler_params=params(),
-        name="attend_forward",
-    )(got, w_qkv, bias, w_o, b_o, gain, shift)
-
-
-def feed_kernel(
-    low_ref,
-    hid_ref,
+def forward_kernel(
+    got_ref,
+    wqkv_src,
+    bias_ref,
+    wo_src,
+    bo_ref,
+    gain_ref,
+    shift_ref,
     win_ref,
     bin_ref,
     wout_ref,
     bout_ref,
-    gain_ref,
-    shift_ref,
+    gain_two_ref,
+    shift_two_ref,
+    stack_out,
+    proj_out,
+    probs_out,
+    norm_out,
+    rstd_ref,
     lab_ref,
+    labcol_ref,
+    meta_ref,
+    source_ref,
     act_ref,
     slope_ref,
     enc_ref,
-    norm_ref,
-    rstd_ref,
+    norm_two_ref,
+    rstd_two_ref,
     pooled_ref,
     copies_ref,
+    stack_ref,
+    proj_ref,
+    probs_ref,
+    norm_ref,
+    hid_ref,
     total_ref,
+    wqkv_ref,
+    wo_ref,
+    sems,
+    out_sems,
 ):
     step = pl.program_id(0)
-    up = dot(low_ref[...], win_ref[...]) + bin_ref[...]
+    puts = [
+        pltpu.make_async_copy(held, out, out_sems.at[index])
+        for index, (held, out) in enumerate(
+            (
+                (stack_ref, stack_out),
+                (proj_ref, proj_out),
+                (probs_ref, probs_out),
+                (norm_ref, norm_out),
+            )
+        )
+    ]
+
+    @pl.when(step == 0)
+    def _():
+        attend_body(
+            got_ref,
+            wqkv_src,
+            bias_ref,
+            wo_src,
+            bo_ref,
+            gain_ref,
+            shift_ref,
+            rstd_ref,
+            lab_ref,
+            labcol_ref,
+            meta_ref,
+            source_ref,
+            stack_ref,
+            proj_ref,
+            probs_ref,
+            norm_ref,
+            hid_ref,
+            wqkv_ref,
+            wo_ref,
+            sems,
+        )
+        for put in puts:
+            put.start()
+        total_ref[...] = hid_ref[...] + bout_ref[...]
+
+    up = dot(stack_ref[2], win_ref[...]) + bin_ref[...]
     phi = 0.5 * (1.0 + lax.erf(up * (1.0 / math.sqrt(2.0))))
     density = jnp.exp(-0.5 * up * up) * (1.0 / math.sqrt(2.0 * math.pi))
     act = (up * phi).astype(BF16)
     act_ref[...] = act
     slope_ref[...] = (phi + up * density).astype(BF16)
-    part = dot(act, wout_ref[...])
-
-    @pl.when(step == 0)
-    def _():
-        total_ref[...] = part + (hid_ref[...] + bout_ref[...])
-
-    @pl.when(step > 0)
-    def _():
-        total_ref[...] += part
+    total_ref[...] += dot(act, wout_ref[...])
 
     @pl.when(step == pl.num_programs(0) - 1)
     def _():
@@ -294,9 +355,9 @@
             centered = total - row_mean(total)
             rstd = lax.rsqrt(row_mean(centered * centered) + NORM_EPS)
             normed = centered * rstd
-            out = normed * gain_ref[...] + shift_ref[...]
-            norm_ref[span, :] = normed
-            rstd_ref[span, :] = rstd
+            out = normed * gain_two_ref[...] + shift_two_ref[...]
+            norm_two_ref[span, :] = normed
+            rstd_two_ref[span, :] = rstd
             enc_ref[span, :] = out.astype(BF16)
             segment = lax.broadcasted_iota(jnp.int32, (SEG_ROW, LANES), 0).astype(F32)
             onehot = (lab_ref[row : row + 1, :] == segment).astype(F32)
@@ -307,55 +368,128 @@
             pooled_ref[row * SEG_ROW : (row + 1) * SEG_ROW, :] = (summed / count).astype(BF16)
         for owner in range(copies_ref.shape[0]):
             copies_ref[owner] = pooled_ref[...]
-
-
-def feed_forward(stack, hidden, w_in, b_in, w_out, b_out, gain, shift, labels, wide_count):
-    _, tok_count, width = stack.shape
+        for put in puts:
+            put.wait()
+
+
+def forward(
+    got,
+    w_qkv,
+    bias,
+    w_o,
+    b_o,
+    gain,
+    shift,
+    w_in,
+    b_in,
+    w_out,
+    b_out,
+    gain_two,
+    shift_two,
+    kept_rows,
+):
+    wide_count, slot_len, width = got.shape
+    row_len = slot_len - META_ROWS
+    tok_count = kept_rows * row_len
     units = w_in.shape[1]
-    tile = 512
-    kept_rows = tok_count // LANES
+    tile = 768
     whole = lambda step: (0, 0)
+    hbm = pl.BlockSpec(memory_space=pl.ANY)
+    wide_vector = pl.BlockSpec((1, 3 * width), whole)
+    vector = pl.BlockSpec((1, width), whole)
+    stack = (3, tok_count, width)
+    proj = (tok_count, 3 * width)
+    probs = (kept_rows, width // LANES, 2 * row_len, row_len)
+    flat = (tok_count, width)
+    own = (kept_rows * SEG_ROW, width)
     shapes = (
+        (stack, BF16, hbm_shape),
+        (proj, BF16, hbm_shape),
+        (probs, BF16, hbm_shape),
+        (flat, F32, hbm_shape),
+        ((tok_count, 1), F32),
+        ((8, LANES), F32),
+        ((tok_count, LANES), F32),
+        ((wide_count, META_ROWS, LANES), BF16),
+        ((kept_rows,), jnp.int32),
         ((tok_count, units), BF16),
         ((tok_count, units), BF16),
-        ((tok_count, width), BF16),
-        ((tok_count, width), F32),
+        (flat, BF16),
+        (flat, F32),
         ((tok_count, 1), F32),
-        ((kept_rows * SEG_ROW, width), BF16),
-        ((wide_count, kept_rows * SEG_ROW, width), BF16),
+        (own, BF16),
+        ((wide_count,) + own, BF16),
     )
     return pl.pallas_call(
-        feed_kernel,
+        forward_kernel,
         out_shape=[make_shape(*item) for item in shapes],
         grid_spec=pltpu.PrefetchScalarGridSpec(
             num_scalar_prefetch=0,
             grid=(units // tile,),
             in_specs=[
-                pl.BlockSpec((pl.Squeezed(), tok_count, width), lambda step: (2, 0, 0)),
-                pl.BlockSpec((tok_count, width), whole),
+                hbm,
+                hbm,
+                wide_vector,
+                hbm,
+                vector,
+                vector,
+                vector,
                 pl.BlockSpec((width, tile), lambda step: (0, step)),
                 pl.BlockSpec((1, tile), lambda step: (0, step)),
                 pl.BlockSpec((tile, width), lambda step: (step, 0)),
-                pl.BlockSpec((1, width), whole),
-                pl.BlockSpec((1, width), whole),
-                pl.BlockSpec((1, width), whole),
-                pl.BlockSpec((8, LANES), whole),
+                vector,
+                vector,
+                vector,
             ],
             out_specs=[
+                hbm,
+                hbm,
+                hbm,
+                hbm,
+                pl.BlockSpec((tok_count, 1), whole),
+                pl.BlockSpec((8, LANES), whole),
+                pl.BlockSpec((tok_count, LANES), whole),
+                pl.BlockSpec((wide_count, META_ROWS, LANES), lambda step: (0, 0, 0)),
+                smem_spec(),
                 pl.BlockSpec((tok_count, tile), lambda step: (0, step)),
                 pl.BlockSpec((tok_count, tile), lambda step: (0, step)),
-                pl.BlockSpec((tok_count, width), whole),
-                pl.BlockSpec((tok_count, width), whole),
+                pl.BlockSpec(flat, whole),
+                pl.BlockSpec(flat, whole),
                 pl.BlockSpec((tok_count, 1), whole),
-                pl.BlockSpec((kept_rows * SEG_ROW, width), whole),
-                pl.BlockSpec((wide_count, kept_rows * SEG_ROW, width), lambda step: (0, 0, 0)),
+                pl.BlockSpec(own, whole),
+                pl.BlockSpec((wide_count,) + own, lambda step: (0, 0, 0)),
             ],
-            scratch_shapes=[pltpu.VMEM((tok_count, width), F32)],
+            scratch_shapes=[
+                pltpu.VMEM(stack, BF16),
+                pltpu.VMEM(proj, BF16),
+                pltpu.VMEM(probs, BF16),
+                pltpu.VMEM(flat, F32),
+                pltpu.VMEM(flat, F32),
+                pltpu.VMEM(flat, F32),
+                pltpu.VMEM(w_qkv.shape, BF16),
+                pltpu.VMEM(w_o.shape, BF16),
+                pltpu.SemaphoreType.DMA((5 + kept_rows,)),
+                pltpu.SemaphoreType.DMA((4,)),
+            ],
         ),
-        cost_estimate=cost(10),
+        cost_estimate=cost(20),
         compiler_params=params(1),
-        name="feed_forward",
-    )(stack, hidden, w_in, b_in, w_out, b_out, gain, shift, labels)
+        name="forward",
+    )(
+        got,
+        w_qkv,
+        bias,
+        w_o,
+        b_o,
+        gain,
+        shift,
+        w_in,
+        b_in,
+        w_out,
+        b_out,
+        gain_two,
+        shift_two,
+    )
 
 
 def route_kernel(me_ref, meta_ref, pair_ref, place_ref, targ_ref, first_ref, second_ref):
@@ -1195,24 +1329,40 @@
     full_bias = jnp.concatenate(
         [b_qv[:width], jnp.zeros((width,), F32), b_qv[width:]]
     ).reshape(1, 3 * width)
-    stack, proj, probs, hidden, norm_one, rstd_one, labels, label_cols, meta, sources = (
-        attend_forward(
-            got, w_qkv, full_bias, w_o, line(b_o), line(gain_one), line(shift_one), kept_rows
-        )
-    )
-    stack_recv = swap(stack, "wide", 0)
-    act, slope, encoded, norm_two, rstd_two, pooled, pooled_copies = feed_forward(
+    (
         stack,
-        hidden,
+        proj,
+        probs,
+        norm_one,
+        rstd_one,
+        labels,
+        label_cols,
+        meta,
+        sources,
+        act,
+        slope,
+        encoded,
+        norm_two,
+        rstd_two,
+        pooled,
+        pooled_copies,
+    ) = forward(
+        got,
+        w_qkv,
+        full_bias,
+        w_o,
+        line(b_o),
+        line(gain_one),
+        line(shift_one),
         w_in,
         line(b_in),
         w_out,
         line(b_out),
         line(gain_two),
         line(shift_two),
-        labels,
-        wide_count,
-    )
+        kept_rows,
+    )
+    stack_recv = swap(stack, "wide", 0)
     act_recv = swap(act, "wide", 0)
     place, target, first, second = route(me_line, meta, pair_index, kept_rows)
     pooled_all = lax.all_to_all(
@@ -1249,7 +1399,7 @@
     rows_out = own_out.shape[1]
     rows_in = own_in.shape[1]
     recv_out = to_partner(sends[:half])
-    recv_in = to_partner(sends[half:])
+    recv_in = to_partner(after(tuple(sends[half:]), tuple(recv_out)))
     fold_out = Folding(
         me_line,
         grad_terms(

time: 239 us -> 233 us (0.975)
  Pallas kernels: 121 us -> 117 us
    pallas_call x2 -> x1, Pallas kernels: 27.7 us -> 24.4 us  [forward(): pl.pallas_call(forward_kernel, out_shape=[make_shape(*item) for item in s...]
where the time goes in v5:
time: 233 us; the launch traced here: 232 us
  Pallas kernels  117 us (50%)
  starting transfers between devices  50.6 us (22%)
  waiting for transfers between devices  47.5 us (20%)
  local copies, waits for them, and re-layouts  8.54 us (4%)
  other arithmetic  7.11 us (3%)
    pallas_call x3, Pallas kernels, grad_terms(): pl.pallas_call(functools.partial(grad_kernel, first_bit, second_bit, span...  25.1 us
    pallas_call x1, Pallas kernels, forward(): pl.pallas_call(forward_kernel, out_shape=[make_shape(*item) for item in s...  24.4 us
    ppermute x31, starting transfers between devices, swap(): return lax.ppermute(values, axis, [(i, i ^ 1 << bit) for i in range(count)])  22.6 us
    all_to_all x1, waiting for transfers between devices, on_device(): got = lax.all_to_all(sent, 'wide', split_axis=0, concat_axis=0, tiled=True)  19.1 us
    pallas_call x1, Pallas kernels, feed_back(): pl.pallas_call(functools.partial(feed_back_kernel, half), out_shape=[make...  18.3 us
    pallas_call x1, Pallas kernels, attend_back(): pl.pallas_call(attend_back_kernel, out_shape=[make_shape(*item) for item...  16.7 us
    ppermute x31, waiting for transfers between devices, swap(): return lax.ppermute(values, axis, [(i, i ^ 1 << bit) for i in range(count)])  15.3 us
    ppermute x6, starting transfers between devices, trade(): lax.ppermute(pieces[step], 'narrow', [(i, i ^ step) for i in range(count)])  9.52 us
  transfers between devices with their start and end apart: 41, of which 15 were waited for; matrix products, arithmetic and copies ran while one was open for 6% of the time, Pallas kernels for 33%

profile of v5, /device:TPU:0, one launch (start us, length us, event | category | flops | bytes accessed | tf_op | source)
XLA Modules:
  0.0 231.9 jit_solution(6141900410130311628)
XLA Ops:
  0.6 3.5 %build_send.1 = bf16[8,144,768]{2,1,0:T(8,128)(2,1)} custom-call(s32[8]{0:T(128)} %dest_ref.3, s32[2,32]{1,0:T(2,128)} %bitcast.26, f32[1,32]{1,0:T(1,128)} %bitcast.27, bf16[8,128,768]{2,1,0:T(8,128)(2,1)} %tok_ref.1, s32[8,128]{1,0:T(8,128)} %seg_ref.1), custom_call_target="tpu_custom_call" | custom-call | bytes 9000000 | tf_op jit(solution)/shard_map/build_send/pallas_call | solution.py:126
  4.2 5.5 %all-to-all-start = ((bf16[8,144,768]{2,1,0:T(8,128)(2,1)}), bf16[8,144,768]{2,1,0:T(8,128)(2,1)}, u32[]{:S(2)}, u32[]{:S(2)}) async-start(bf16[8,144,768]{2,1,0:T(8,128)(2,1)} %build_send.1), calls=%async_computation | async-start | bytes 3538944 | tf_op jit(solution)/shard_map/all_to_all | solution.py:1328
  9.7 0.6 reshape.84.bias_ref
  13.9 19.1 %all-to-all-done.got_ref = bf16[8,144,768]{2,1,0:T(8,128)(2,1)} async-done(((bf16[8,144,768]{2,1,0:T(8,128)(2,1)}), bf16[8,144,768]{2,1,0:T(8,128)(2,1)}, u32[]{:S(2)}, u32[]{:S(2)}) %all-to-all-start) | async-done | bytes 1769504 | tf_op jit(solution)/shard_map/all_to_all | solution.py:1328
  32.9 24.4 %forward.1 = (bf16[3,512,768]{2,1,0:T(8,128)(2,1)}, bf16[512,2304]{1,0:T(8,128)(2,1)}, bf16[4,6,256,128]{3,2,1,0:T(8,128)(2,1)}, f32[512,768]{1,0:T(8,128)}, f32...) custom-call(bf16[8,144,768]{2,1,0:T(8,128)(2,1)} %all-to-all-done.go, ...), custom_call_target="tpu_custom_call" | custom-call | bytes 60000000 | tf_op jit(solution)/shard_map/forward/pallas_call | solution.py:423
  57.9 4.3 %all-to-all-start.1 = ((bf16[8,32,768]{2,1,0:T(8,128)(2,1)}), bf16[8,32,768]{2,1,0:T(8,128)(2,1)}, u32[]{:S(2)}, u32[]{:S(2)}) async-start(bf16[8,32,768]{2,1,0:T(8,128)(2,1)} %get-tuple-element.122), calls=%async_computation.1 | async-start | bytes 786432 | tf_op jit(solution)/shard_map/all_to_all | solution.py:1368
  62.1 1.4 copy.33.pair_ref
  63.5 1.8 route.1
  65.3 5.0 %all-to-all-done.1 = bf16[8,32,768]{2,1,0:T(8,128)(2,1)} async-done(((bf16[8,32,768]{2,1,0:T(8,128)(2,1)}), bf16[8,32,768]{2,1,0:T(8,128)(2,1)}, u32[]{:S(2)}, u32[]{:S(2)}) %all-to-all-start.1) | async-done | bytes 393248 | tf_op jit(solution)/shard_map/all_to_all | solution.py:1368
  70.3 18.3 %feed_back.1 = (f32[1,3072]{1,0:T(1,128)}, f32[512,768]{1,0:T(8,128)}, bf16[768,512]{1,0:T(8,128)(2,1)}, bf16[512,768]{1,0:T(8,128)(2,1)}, f32[8,768]{1,0:T(8,12...) custom-call(s32[1]{0:T(128)} %bitcast.4.me_ref, ...), custom_call_target="tpu_custom_call" | custom-call | bytes 42000000 | tf_op jit(solution)/shard_map/feed_back/pallas_call | solution.py:818
  89.3 1.1 collective-permute-done.refs_0_
  90.9 1.1 collective-permute-done.3.refs_3_
  92.5 8.0 %grad_terms.3 = (bf16[2,96,1536]{2,1,0:T(8,128)(2,1)}, bf16[2,96,1536]{2,1,0:T(8,128)(2,1)}, bf16[2,96,1536]{2,1,0:T(8,128)(2,1)}, bf16[2,96,1536]{2,1,0:T(8,128)(2,1)}) custom-call(s32[1]{0:T(128)} %bitcast.4.me_ref, bf16[4,96,512]{2,1,0:T(8,128)(2,1)} %get-tuple-element.137.own_ref, bf16[96,512]{1,0:T(8,128)(2,1)} %collective-permute-done.refs_0_, ...), custom_call_target="tpu_custom_call" | custom-call | bytes 21000000 | tf_op jit(solution)/shard_map/grad_terms/pallas_call | solution.py:1095
  102.1 2.0 cosine_pairs.1
  104.1 1.3 reduce
  105.5 8.2 %grad_terms.4 = (bf16[2,384,384]{2,1,0:T(8,128)(2,1)}, bf16[2,384,384]{2,1,0:T(8,128)(2,1)}, bf16[2,384,384]{2,1,0:T(8,128)(2,1)}, bf16[2,384,384]{2,1,0:T(8,128)(2,1)}) custom-call(s32[1]{0:T(128)} %bitcast.4.me_ref, bf16[4,384,512]{2,1,0:T(8,128)(2,1)} %get-tuple-element.144.own_ref, bf16[384,512]{1,0:T(8,128)(2,1)} %collective-permute-done.5.refs_0_, ...), custom_call_target="tpu_custom_call" | custom-call | bytes 21000000 | tf_op jit(solution)/shard_map/grad_terms/pallas_call | solution.py:1095
  113.7 2.5 %collective-permute-done.10.refs_1_ = bf16[2,96,1536]{2,1,0:T(8,128)(2,1)} collective-permute-done((bf16[2,96,1536]{2,1,0:T(8,128)(2,1)}, bf16[2,96,1536]{2,1,0:T(8,128)(2,1)}, u32[]{:S(2)}, u32[]{:S(2)}) %collective-permute-start.10) | collective-permute-done | bytes 589856 | tf_op jit(solution)/shard_map/ppermute | solution.py:1228
  116.5 2.8 %fold.3 = (bf16[1,96,1536]{2,1,0:T(8,128)(2,1)}, bf16[1,96,1536]{2,1,0:T(8,128)(2,1)}, bf16[1,96,1536]{2,1,0:T(8,128)(2,1)}, bf16[1,96,1536]{2,1,0:T(8,128)(2,1)}) custom-call(s32[1]{0:T(128)} %bitcast.4.me_ref, bf16[2,96,1536]{2,1,0:T(8,128)(2,1)} %get-tuple-element.164.refs_0_, bf16[2,96,1536]{2,1,0:T(8,128)(2,1)} %collective-permute-done.10.refs_1_, ...), custom_call_target="tpu_custom_call" | custom-call | bytes 1500000 | tf_op jit(solution)/shard_map/fold/pallas_call | solution.py:1132
  119.3 1.5 collective-permute-start.14
  121.3 1.5 collective-permute-start.12
  123.3 16.7 %attend_back.1 = (bf16[8,128,768]{2,1,0:T(8,128)(2,1)}, f32[1,2304]{1,0:T(1,128)}, bf16[4,384,512]{2,1,0:T(8,128)(2,1)}, bf16[384,512]{1,0:T(8,128)(2,1)}, bf16[...) custom-call(s32[4]{0:T(128)} %get-tuple-element.123.source_ref, s32[1]{0:T(128)} %bitcast.4.me_ref, ...), custom_call_target="tpu_custom_call" | custom-call | bytes 60000000 | tf_op jit(solution)/shard_map/attend_back/pallas_call | solution.py:965
  140.0 1.3 collective-permute-done.12.refs_1_
  141.4 2.7 %fold.4 = (bf16[1,384,384]{2,1,0:T(8,128)(2,1)}, bf16[1,384,384]{2,1,0:T(8,128)(2,1)}, bf16[1,384,384]{2,1,0:T(8,128)(2,1)}, bf16[1,384,384]{2,1,0:T(8,128)(2,1)}) custom-call(s32[1]{0:T(128)} %bitcast.4.me_ref, bf16[2,384,384]{2,1,0:T(8,128)(2,1)} %get-tuple-element.172.refs_0_, bf16[2,384,384]{2,1,0:T(8,128)(2,1)} %collective-permute-done.14.refs_1_, ...), custom_call_target="tpu_custom_call" | custom-call | bytes 1500000 | tf_op jit(solution)/shard_map/fold/pallas_call | solution.py:1132
  144.1 4.5 %all-to-all-start.2 = ((bf16[8,128,768]{2,1,0:T(8,128)(2,1)}), bf16[8,128,768]{2,1,0:T(8,128)(2,1)}, u32[]{:S(2)}, u32[]{:S(2)}) async-start(bf16[8,128,768]{2,1,0:T(8,128)(2,1)} %get-tuple-element.177), calls=%async_computation.2 | async-start | bytes 3145728 | tf_op jit(solution)/shard_map/all_to_all | solution.py:1461
  149.7 1.4 pack_vectors.1
  151.2 1.3 collective-permute-done.25
  152.5 0.8 add.15
  153.3 0.6 copy-done
  153.9 2.0 collective-permute-start.26
  155.9 2.0 collective-permute-done.26
  157.9 0.6 copy-done.1
  158.5 1.6 collective-permute-start.20
  160.1 1.5 collective-permute-start.21
  161.6 2.3 %narrow_pieces.3 = (bf16[96,768]{1,0:T(8,128)(2,1)}, bf16[96,768]{1,0:T(8,128)(2,1)}, bf16[96,768]{1,0:T(8,128)(2,1)}, bf16[96,768]{1,0:T(8,128)(2,1)}) custom-call(s32[1]{0:T(128)} %bitcast.6.me_ref, bf16[1,96,1536]{2,1,0:T(8,128)(2,1)} %get-tuple-element.184.refs_0_, bf16[1,96,1536]{2,1,0:T(8,128)(2,1)} %collective-permute-done.12.refs_1_, ...), custom_call_target="tpu_custom_call" | custom-call | bytes 3000000 | tf_op jit(solution)/shard_map/narrow_pieces/pallas_call | solution.py:1165
  163.9 2.0 collective-permute-start.27
  165.9 2.9 %collective-permute-start.28 = (bf16[96,768]{1,0:T(8,128)(2,1)}, bf16[96,768]{1,0:T(8,128)(2,1)}, u32[]{:S(2)}, u32[]{:S(2)}) collective-permute-start(bf16[96,768]{1,0:T(8,128)(2,1)} %get-tuple-element.188), channel_id=1, source_target_pairs={{0,2},{1,3},{2,0},{3,1},{4,6},{5,7},{6,4},{7,5},{8,10},{9,11},{10,... | collective-permute-start | bytes 442376 | tf_op jit(solution)/shard_map/ppermute | solution.py:1235
  168.9 1.4 add.16
  170.3 8.9 %grad_terms.5 = (bf16[2,384,384]{2,1,0:T(8,128)(2,1)}, bf16[2,384,384]{2,1,0:T(8,128)(2,1)}, bf16[2,384,384]{2,1,0:T(8,128)(2,1)}, bf16[2,384,384]{2,1,0:T(8,128)(2,1)}) custom-call(s32[1]{0:T(128)} %bitcast.4.me_ref, bf16[4,384,512]{2,1,0:T(8,128)(2,1)} %get-tuple-element.178.own_ref, bf16[384,512]{1,0:T(8,128)(2,1)} %collective-permute-done.16.refs_0_, ...), custom_call_target="tpu_custom_call" | custom-call | bytes 21000000 | tf_op jit(solution)/shard_map/grad_terms/pallas_call | solution.py:1095
  179.6 0.6 collective-permute-start.30
  180.6 2.3 narrow_pieces.4
  182.9 2.2 collective-permute-start.22
  185.1 1.8 collective-permute-start.23
  186.9 0.6 collective-permute-start.24
  187.5 3.3 %home_rows.1 = bf16[8,128,768]{2,1,0:T(8,128)(2,1)} custom-call(s32[8]{0:T(128)} %dest_ref.3, bf16[8,128,768]{2,1,0:T(8,128)(2,1)} %all-to-all-done.2.rows_ref), custom_call_target="tpu_custom_call" | custom-call | bytes 9000000 | tf_op jit(solution)/shard_map/home_rows/pallas_call | solution.py:1016
  190.9 6.5 %collective-permute-done.23.refs_2_ = bf16[192,384]{1,0:T(8,128)(2,1)} collective-permute-done((bf16[192,384]{1,0:T(8,128)(2,1)}, bf16[192,384]{1,0:T(8,128)(2,1)}, u32[]{:S(2)}, u32[]{:S(2)}) %collective-permute-start.23) | collective-permute-done | bytes 147488 | tf_op jit(solution)/shard_map/ppermute | solution.py:1235
  197.4 2.7 %fold.5 = (bf16[1,384,384]{2,1,0:T(8,128)(2,1)}, bf16[1,384,384]{2,1,0:T(8,128)(2,1)}, bf16[1,384,384]{2,1,0:T(8,128)(2,1)}, bf16[1,384,384]{2,1,0:T(8,128)(2,1)}) custom-call(s32[1]{0:T(128)} %bitcast.4.me_ref, bf16[2,384,384]{2,1,0:T(8,128)(2,1)} %get-tuple-element.201.refs_0_, bf16[2,384,384]{2,1,0:T(8,128)(2,1)} %collective-permute-done.30.refs_1_, ...), custom_call_target="tpu_custom_call" | custom-call | bytes 1500000 | tf_op jit(solution)/shard_map/fold/pallas_call | solution.py:1132
  200.1 1.6 collective-permute-start.33
  201.7 1.5 collective-permute-start.34
  203.2 3.1 %collective-permute-start.32 = (f32[72,128]{1,0:T(8,128)}, f32[72,128]{1,0:T(8,128)S(1)}, u32[]{:S(2)}, u32[]{:S(2)}) collective-permute-start(f32[72,128]{1,0:T(8,128)} %add.16), channel_id=1, source_target_pairs={{0,2},{1,3},{2,0},{3,1},{4,6},{5,7},{6,4},{7,5},{8,10},{9,11},{10,... | collective-permute-start | bytes 110600 | tf_op jit(solution)/shard_map/ppermute | solution.py:1228
  206.3 2.1 collective-permute-done.32
  208.4 1.4 add.17
  209.8 2.3 narrow_pieces.5
  212.1 4.2 %all-to-all-start.3 = ((bf16[4,192,384]{2,1,0:T(8,128)(2,1)}), bf16[4,192,384]{2,1,0:T(8,128)(2,1)}, u32[]{:S(2)}, u32[]{:S(2)}) async-start(bf16[4,192,384]{2,1,0:T(8,128)(2,1)} %narrow_pieces.5), calls=%async_computation.3 | async-start | bytes 1179648 | tf_op jit(solution)/shard_map/all_to_all | solution.py:1499
  216.3 1.1 collective-permute-start.35
  217.4 3.1 %collective-permute-done.35 = f32[72,128]{1,0:T(8,128)S(1)} collective-permute-done((f32[72,128]{1,0:T(8,128)}, f32[72,128]{1,0:T(8,128)S(1)}, u32[]{:S(2)}, u32[]{:S(2)}) %collective-permute-start.35) | collective-permute-done | bytes 36896 | tf_op jit(solution)/shard_map/ppermute | solution.py:1228
  220.5 1.4 add.18
  222.4 1.9 sum_pieces.5
  224.3 1.9 sum_pieces.4
  226.2 0.8 add.19
  227.0 0.6 slice_bitcast_fusion.1
  227.6 0.6 slice_bitcast_fusion
  228.2 0.6 slice_bitcast_fusion.2
  228.8 1.2 all-to-all-done.3.refs_0_
  230.0 1.9 sum_pieces.3
  (76 shorter events, 11.4 us)
Async XLA Ops:
  4.1 5.6 %copy-start.2 = (f32[1536]{0:T(1024)S(1)}, f32[1536]{0:T(1024)}, u32[]{:S(2)}) copy-start(f32[1536]{0:T(1024)} %param.23) | copy-start | bytes 18436
  4.1 6.2 %copy-start.3 = (f32[768]{0:T(1024)S(1)}, f32[768]{0:T(1024)}, u32[]{:S(2)}) copy-start(f32[768]{0:T(1024)} %param.25) | copy-start | bytes 9220
  4.2 6.8 %copy-start.4 = (f32[768]{0:T(1024)S(1)}, f32[768]{0:T(1024)}, u32[]{:S(2)}) copy-start(f32[768]{0:T(1024)} %param.26) | copy-start | bytes 9220
  4.2 7.4 %copy-start.5 = (f32[768]{0:T(1024)S(1)}, f32[768]{0:T(1024)}, u32[]{:S(2)}) copy-start(f32[768]{0:T(1024)} %param.27) | copy-start | bytes 9220
  4.2 7.9 %copy-start.6 = (f32[768]{0:T(1024)S(1)}, f32[768]{0:T(1024)}, u32[]{:S(2)}) copy-start(f32[768]{0:T(1024)} %param.31) | copy-start | bytes 9220
  4.2 8.5 %copy-start.7 = (f32[768]{0:T(1024)S(1)}, f32[768]{0:T(1024)}, u32[]{:S(2)}) copy-start(f32[768]{0:T(1024)} %param.32) | copy-start | bytes 9220
  4.2 9.1 %copy-start.8 = (f32[768]{0:T(1024)S(1)}, f32[768]{0:T(1024)}, u32[]{:S(2)}) copy-start(f32[768]{0:T(1024)} %param.33) | copy-start | bytes 9220
  4.2 28.7 %all-to-all-start = ((bf16[8,144,768]{2,1,0:T(8,128)(2,1)}), bf16[8,144,768]{2,1,0:T(8,128)(2,1)}, u32[]{:S(2)}, u32[]{:S(2)}) async-start(bf16[8,144,768]{2,1,0:T(8,128)(2,1)} %build_send.1), calls=%async_computation | async-start | bytes 3538944 | tf_op jit(solution)/shard_map/all_to_all | solution.py:1328
  57.3 35.2 %collective-permute-start.4 = (bf16[512,3072]{1,0:T(8,128)(2,1)}, bf16[512,3072]{1,0:T(8,128)(2,1)}, u32[]{:S(2)}, u32[]{:S(2)}) collective-permute-start(bf16[512,3072]{1,0:T(8,128)(2,1)} %get-tuple-element.142.refs_4_), channel_id=1, source_target_pairs={{0,4},{4,0},{8,12},{12,8},{16,20},{20,16},{24,28},{28,24},{1,5},{5... | collective-permute-start | bytes 9437192 | tf_op jit(solution)/shard_map/ppermute | solution.py:1228
  57.4 48.1 %collective-permute-start.9 = (bf16[3,512,768]{2,1,0:T(8,128)(2,1)}, bf16[3,512,768]{2,1,0:T(8,128)(2,1)}, u32[]{:S(2)}, u32[]{:S(2)}) collective-permute-start(bf16[3,512,768]{2,1,0:T(8,128)(2,1)} %get-tuple-element.159.refs_4_.refs_5_), channel_id=1, source_target_pairs={{0,4},{4,0},{8,12},{12,8},{16,20},{20,16},{24,28},{28,24},{1,5},{5... | collective-permute-start | bytes 7077896 | tf_op jit(solution)/shard_map/ppermute | solution.py:1228
  57.9 12.4 %all-to-all-start.1 = ((bf16[8,32,768]{2,1,0:T(8,128)(2,1)}), bf16[8,32,768]{2,1,0:T(8,128)(2,1)}, u32[]{:S(2)}, u32[]{:S(2)}) async-start(bf16[8,32,768]{2,1,0:T(8,128)(2,1)} %get-tuple-element.122), calls=%async_computation.1 | async-start | bytes 786432 | tf_op jit(solution)/shard_map/all_to_all | solution.py:1368
  88.6 1.7 collective-permute-start
  88.7 1.8 collective-permute-start.1
  89.2 1.6 collective-permute-start.2
  90.4 1.6 collective-permute-start.3
  92.0 9.6 %collective-permute-start.5 = (bf16[384,512]{1,0:T(8,128)(2,1)}, bf16[384,512]{1,0:T(8,128)(2,1)}, u32[]{:S(2)}, u32[]{:S(2)}) collective-permute-start(bf16[384,512]{1,0:T(8,128)(2,1)} %get-tuple-element.149), channel_id=1, source_target_pairs={{0,4},{4,0},{8,12},{12,8},{16,20},{20,16},{24,28},{28,24},{1,5},{5... | collective-permute-start | bytes 1179656 | tf_op jit(solution)/shard_map/ppermute | solution.py:1228
  92.1 9.4 %collective-permute-start.6 = (bf16[384,512]{1,0:T(8,128)(2,1)}, bf16[384,512]{1,0:T(8,128)(2,1)}, u32[]{:S(2)}, u32[]{:S(2)}) collective-permute-start(bf16[384,512]{1,0:T(8,128)(2,1)} %get-tuple-element.150), channel_id=1, source_target_pairs={{0,4},{4,0},{8,12},{12,8},{16,20},{20,16},{24,28},{28,24},{1,5},{5... | collective-permute-start | bytes 1179656 | tf_op jit(solution)/shard_map/ppermute | solution.py:1228
  100.5 15.7 %collective-permute-start.10 = (bf16[2,96,1536]{2,1,0:T(8,128)(2,1)}, bf16[2,96,1536]{2,1,0:T(8,128)(2,1)}, u32[]{:S(2)}, u32[]{:S(2)}) collective-permute-start(bf16[2,96,1536]{2,1,0:T(8,128)(2,1)} %get-tuple-element.153), channel_id=1, source_target_pairs={{0,8},{4,12},{8,0},{12,4},{16,24},{20,28},{24,16},{28,20},{1,9},{5... | collective-permute-start | bytes 1769480 | tf_op jit(solution)/shard_map/ppermute | solution.py:1228
  101.0 15.4 %collective-permute-start.11 = (bf16[2,96,1536]{2,1,0:T(8,128)(2,1)}, bf16[2,96,1536]{2,1,0:T(8,128)(2,1)}, u32[]{:S(2)}, u32[]{:S(2)}) collective-permute-start(bf16[2,96,1536]{2,1,0:T(8,128)(2,1)} %get-tuple-element.154), channel_id=1, source_target_pairs={{0,16},{4,20},{8,24},{12,28},{16,0},{20,4},{24,8},{28,12},{1,17},{... | collective-permute-start | bytes 1769480 | tf_op jit(solution)/shard_map/ppermute | solution.py:1228
  101.6 3.9 %collective-permute-start.7 = (bf16[384,512]{1,0:T(8,128)(2,1)}, bf16[384,512]{1,0:T(8,128)(2,1)}, u32[]{:S(2)}, u32[]{:S(2)}) collective-permute-start(bf16[384,512]{1,0:T(8,128)(2,1)} %get-tuple-element.151), channel_id=1, source_target_pairs={{0,4},{4,0},{8,12},{12,8},{16,20},{20,16},{24,28},{28,24},{1,5},{5... | collective-permute-start | bytes 1179656 | tf_op jit(solution)/shard_map/ppermute | solution.py:1228
  101.6 3.9 %collective-permute-start.8 = (bf16[384,512]{1,0:T(8,128)(2,1)}, bf16[384,512]{1,0:T(8,128)(2,1)}, u32[]{:S(2)}, u32[]{:S(2)}) collective-permute-start(bf16[384,512]{1,0:T(8,128)(2,1)} %get-tuple-element.152), channel_id=1, source_target_pairs={{0,4},{4,0},{8,12},{12,8},{16,20},{20,16},{24,28},{28,24},{1,5},{5... | collective-permute-start | bytes 1179656 | tf_op jit(solution)/shard_map/ppermute | solution.py:1228
  119.3 22.1 %collective-permute-start.14 = (bf16[2,384,384]{2,1,0:T(8,128)(2,1)}, bf16[2,384,384]{2,1,0:T(8,128)(2,1)}, u32[]{:S(2)}, u32[]{:S(2)}) collective-permute-start(bf16[2,384,384]{2,1,0:T(8,128)(2,1)} %get-tuple-element.173), channel_id=1, source_target_pairs={{0,8},{4,12},{8,0},{12,4},{16,24},{20,28},{24,16},{28,20},{1,9},{5... | collective-permute-start | bytes 1769480 | tf_op jit(solution)/shard_map/ppermute | solution.py:1228
  120.7 20.6 %collective-permute-start.15 = (bf16[2,384,384]{2,1,0:T(8,128)(2,1)}, bf16[2,384,384]{2,1,0:T(8,128)(2,1)}, u32[]{:S(2)}, u32[]{:S(2)}) collective-permute-start(bf16[2,384,384]{2,1,0:T(8,128)(2,1)} %get-tuple-element.174), channel_id=1, source_target_pairs={{0,16},{4,20},{8,24},{12,28},{16,0},{20,4},{24,8},{28,12},{1,17},{... | collective-permute-start | bytes 1769480 | tf_op jit(solution)/shard_map/ppermute | solution.py:1228
  121.3 20.1 %collective-permute-start.12 = (bf16[1,96,1536]{2,1,0:T(8,128)(2,1)}, bf16[1,96,1536]{2,1,0:T(8,128)(2,1)}, u32[]{:S(2)}, u32[]{:S(2)}) collective-permute-start(bf16[1,96,1536]{2,1,0:T(8,128)(2,1)} %get-tuple-element.166), channel_id=1, source_target_pairs={{0,16},{4,20},{8,24},{12,28},{16,0},{20,4},{24,8},{28,12},{1,17},{... | collective-permute-start | bytes 884744 | tf_op jit(solution)/shard_map/ppermute | solution.py:1228
  122.8 18.6 %collective-permute-start.13 = (bf16[1,96,1536]{2,1,0:T(8,128)(2,1)}, bf16[1,96,1536]{2,1,0:T(8,128)(2,1)}, u32[]{:S(2)}, u32[]{:S(2)}) collective-permute-start(bf16[1,96,1536]{2,1,0:T(8,128)(2,1)} %get-tuple-element.167), channel_id=1, source_target_pairs={{0,8},{4,12},{8,0},{12,4},{16,24},{20,28},{24,16},{28,20},{1,9},{5... | collective-permute-start | bytes 884744 | tf_op jit(solution)/shard_map/ppermute | solution.py:1228
  144.1 43.4 %all-to-all-start.2 = ((bf16[8,128,768]{2,1,0:T(8,128)(2,1)}), bf16[8,128,768]{2,1,0:T(8,128)(2,1)}, u32[]{:S(2)}, u32[]{:S(2)}) async-start(bf16[8,128,768]{2,1,0:T(8,128)(2,1)} %get-tuple-element.177), calls=%async_computation.2 | async-start | bytes 3145728 | tf_op jit(solution)/shard_map/all_to_all | solution.py:1461
  148.6 11.5 %collective-permute-start.16 = (bf16[384,512]{1,0:T(8,128)(2,1)}, bf16[384,512]{1,0:T(8,128)(2,1)}, u32[]{:S(2)}, u32[]{:S(2)}) collective-permute-start(bf16[384,512]{1,0:T(8,128)(2,1)} %get-tuple-element.179), channel_id=1, source_target_pairs={{0,4},{4,0},{8,12},{12,8},{16,20},{20,16},{24,28},{28,24},{1,5},{5... | collective-permute-start | bytes 1179656 | tf_op jit(solution)/shard_map/ppermute | solution.py:1228
  148.8 15.2 %collective-permute-start.17 = (bf16[384,512]{1,0:T(8,128)(2,1)}, bf16[384,512]{1,0:T(8,128)(2,1)}, u32[]{:S(2)}, u32[]{:S(2)}) collective-permute-start(bf16[384,512]{1,0:T(8,128)(2,1)} %get-tuple-element.180), channel_id=1, source_target_pairs={{0,4},{4,0},{8,12},{12,8},{16,20},{20,16},{24,28},{28,24},{1,5},{5... | collective-permute-start | bytes 1179656 | tf_op jit(solution)/shard_map/ppermute | solution.py:1228
  149.2 16.7 %collective-permute-start.18 = (bf16[384,512]{1,0:T(8,128)(2,1)}, bf16[384,512]{1,0:T(8,128)(2,1)}, u32[]{:S(2)}, u32[]{:S(2)}) collective-permute-start(bf16[384,512]{1,0:T(8,128)(2,1)} %get-tuple-element.181), channel_id=1, source_target_pairs={{0,4},{4,0},{8,12},{12,8},{16,20},{20,16},{24,28},{28,24},{1,5},{5... | collective-permute-start | bytes 1179656 | tf_op jit(solution)/shard_map/ppermute | solution.py:1228
  149.3 19.6 %collective-permute-start.19 = (bf16[384,512]{1,0:T(8,128)(2,1)}, bf16[384,512]{1,0:T(8,128)(2,1)}, u32[]{:S(2)}, u32[]{:S(2)}) collective-permute-start(bf16[384,512]{1,0:T(8,128)(2,1)} %get-tuple-element.182), channel_id=1, source_target_pairs={{0,4},{4,0},{8,12},{12,8},{16,20},{20,16},{24,28},{28,24},{1,5},{5... | collective-permute-start | bytes 1179656 | tf_op jit(solution)/shard_map/ppermute | solution.py:1228
  151.1 1.4 collective-permute-start.25
  153.3 0.6 copy-start
  153.9 4.0 %collective-permute-start.26 = (f32[72,128]{1,0:T(8,128)S(1)}, f32[72,128]{1,0:T(8,128)S(1)}, u32[]{:S(2)}, u32[]{:S(2)}) collective-permute-start(f32[72,128]{1,0:T(8,128)S(1)} %add.15), channel_id=1, source_target_pairs={{0,1},{1,0},{2,3},{3,2},{4,5},{5,4},{6,7},{7,6},{8,9},{9,8},{10,11... | collective-permute-start | bytes 110600 | tf_op jit(solution)/shard_map/ppermute | solution.py:1228
  157.9 0.6 copy-start.1
  158.5 21.1 %collective-permute-start.20 = (bf16[1,384,384]{2,1,0:T(8,128)(2,1)}, bf16[1,384,384]{2,1,0:T(8,128)(2,1)}, u32[]{:S(2)}, u32[]{:S(2)}) collective-permute-start(bf16[1,384,384]{2,1,0:T(8,128)(2,1)} %get-tuple-element.175), channel_id=1, source_target_pairs={{0,16},{4,20},{8,24},{12,28},{16,0},{20,4},{24,8},{28,12},{1,17},{... | collective-permute-start | bytes 884744 | tf_op jit(solution)/shard_map/ppermute | solution.py:1228
  160.1 19.5 %collective-permute-start.21 = (bf16[1,384,384]{2,1,0:T(8,128)(2,1)}, bf16[1,384,384]{2,1,0:T(8,128)(2,1)}, u32[]{:S(2)}, u32[]{:S(2)}) collective-permute-start(bf16[1,384,384]{2,1,0:T(8,128)(2,1)} %get-tuple-element.176), channel_id=1, source_target_pairs={{0,8},{4,12},{8,0},{12,4},{16,24},{20,28},{24,16},{28,20},{1,9},{5... | collective-permute-start | bytes 884744 | tf_op jit(solution)/shard_map/ppermute | solution.py:1228
  163.9 15.2 %collective-permute-start.27 = (bf16[96,768]{1,0:T(8,128)(2,1)}, bf16[96,768]{1,0:T(8,128)(2,1)}, u32[]{:S(2)}, u32[]{:S(2)}) collective-permute-start(bf16[96,768]{1,0:T(8,128)(2,1)} %get-tuple-element.187), channel_id=1, source_target_pairs={{0,1},{1,0},{2,3},{3,2},{4,5},{5,4},{6,7},{7,6},{8,9},{9,8},{10,11... | collective-permute-start | bytes 442376 | tf_op jit(solution)/shard_map/ppermute | solution.py:1235
  165.9 13.7 %collective-permute-start.28 = (bf16[96,768]{1,0:T(8,128)(2,1)}, bf16[96,768]{1,0:T(8,128)(2,1)}, u32[]{:S(2)}, u32[]{:S(2)}) collective-permute-start(bf16[96,768]{1,0:T(8,128)(2,1)} %get-tuple-element.188), channel_id=1, source_target_pairs={{0,2},{1,3},{2,0},{3,1},{4,6},{5,7},{6,4},{7,5},{8,10},{9,11},{10,... | collective-permute-start | bytes 442376 | tf_op jit(solution)/shard_map/ppermute | solution.py:1235
  168.8 10.7 %collective-permute-start.29 = (bf16[96,768]{1,0:T(8,128)(2,1)}, bf16[96,768]{1,0:T(8,128)(2,1)}, u32[]{:S(2)}, u32[]{:S(2)}) collective-permute-start(bf16[96,768]{1,0:T(8,128)(2,1)} %get-tuple-element.189), channel_id=1, source_target_pairs={{0,3},{1,2},{2,1},{3,0},{4,7},{5,6},{6,5},{7,4},{8,11},{9,10},{10,... | collective-permute-start | bytes 442376 | tf_op jit(solution)/shard_map/ppermute | solution.py:1235
  179.6 17.8 %collective-permute-start.30 = (bf16[2,384,384]{2,1,0:T(8,128)(2,1)}, bf16[2,384,384]{2,1,0:T(8,128)(2,1)}, u32[]{:S(2)}, u32[]{:S(2)}) collective-permute-start(bf16[2,384,384]{2,1,0:T(8,128)(2,1)} %get-tuple-element.207), channel_id=1, source_target_pairs={{0,8},{4,12},{8,0},{12,4},{16,24},{20,28},{24,16},{28,20},{1,9},{5... | collective-permute-start | bytes 1769480 | tf_op jit(solution)/shard_map/ppermute | solution.py:1228
  180.2 17.2 %collective-permute-start.31 = (bf16[2,384,384]{2,1,0:T(8,128)(2,1)}, bf16[2,384,384]{2,1,0:T(8,128)(2,1)}, u32[]{:S(2)}, u32[]{:S(2)}) collective-permute-start(bf16[2,384,384]{2,1,0:T(8,128)(2,1)} %get-tuple-element.210), channel_id=1, source_target_pairs={{0,16},{4,20},{8,24},{12,28},{16,0},{20,4},{24,8},{28,12},{1,17},{... | collective-permute-start | bytes 1769480 | tf_op jit(solution)/shard_map/ppermute | solution.py:1228
  182.9 8.0 %collective-permute-start.22 = (bf16[192,384]{1,0:T(8,128)(2,1)}, bf16[192,384]{1,0:T(8,128)(2,1)}, u32[]{:S(2)}, u32[]{:S(2)}) collective-permute-start(bf16[192,384]{1,0:T(8,128)(2,1)} %get-tuple-element.198), channel_id=1, source_target_pairs={{0,1},{1,0},{2,3},{3,2},{4,5},{5,4},{6,7},{7,6},{8,9},{9,8},{10,11... | collective-permute-start | bytes 442376 | tf_op jit(solution)/shard_map/ppermute | solution.py:1235
  185.1 12.3 %collective-permute-start.23 = (bf16[192,384]{1,0:T(8,128)(2,1)}, bf16[192,384]{1,0:T(8,128)(2,1)}, u32[]{:S(2)}, u32[]{:S(2)}) collective-permute-start(bf16[192,384]{1,0:T(8,128)(2,1)} %get-tuple-element.199), channel_id=1, source_target_pairs={{0,2},{1,3},{2,0},{3,1},{4,6},{5,7},{6,4},{7,5},{8,10},{9,11},{10,... | collective-permute-start | bytes 442376 | tf_op jit(solution)/shard_map/ppermute | solution.py:1235
  186.9 10.5 %collective-permute-start.24 = (bf16[192,384]{1,0:T(8,128)(2,1)}, bf16[192,384]{1,0:T(8,128)(2,1)}, u32[]{:S(2)}, u32[]{:S(2)}) collective-permute-start(bf16[192,384]{1,0:T(8,128)(2,1)} %get-tuple-element.200), channel_id=1, source_target_pairs={{0,3},{1,2},{2,1},{3,0},{4,7},{5,6},{6,5},{7,4},{8,11},{9,10},{10,... | collective-permute-start | bytes 442376 | tf_op jit(solution)/shard_map/ppermute | solution.py:1235
  200.1 9.7 %collective-permute-start.33 = (bf16[1,384,384]{2,1,0:T(8,128)(2,1)}, bf16[1,384,384]{2,1,0:T(8,128)(2,1)}, u32[]{:S(2)}, u32[]{:S(2)}) collective-permute-start(bf16[1,384,384]{2,1,0:T(8,128)(2,1)} %get-tuple-element.212), channel_id=1, source_target_pairs={{0,16},{4,20},{8,24},{12,28},{16,0},{20,4},{24,8},{28,12},{1,17},{... | collective-permute-start | bytes 884744 | tf_op jit(solution)/shard_map/ppermute | solution.py:1228
  201.7 8.1 %collective-permute-start.34 = (bf16[1,384,384]{2,1,0:T(8,128)(2,1)}, bf16[1,384,384]{2,1,0:T(8,128)(2,1)}, u32[]{:S(2)}, u32[]{:S(2)}) collective-permute-start(bf16[1,384,384]{2,1,0:T(8,128)(2,1)} %get-tuple-element.213), channel_id=1, source_target_pairs={{0,8},{4,12},{8,0},{12,4},{16,24},{20,28},{24,16},{28,20},{1,9},{5... | collective-permute-start | bytes 884744 | tf_op jit(solution)/shard_map/ppermute | solution.py:1228
  203.2 5.2 %collective-permute-start.32 = (f32[72,128]{1,0:T(8,128)}, f32[72,128]{1,0:T(8,128)S(1)}, u32[]{:S(2)}, u32[]{:S(2)}) collective-permute-start(f32[72,128]{1,0:T(8,128)} %add.16), channel_id=1, source_target_pairs={{0,2},{1,3},{2,0},{3,1},{4,6},{5,7},{6,4},{7,5},{8,10},{9,11},{10,... | collective-permute-start | bytes 110600 | tf_op jit(solution)/shard_map/ppermute | solution.py:1228
  212.1 17.9 %all-to-all-start.3 = ((bf16[4,192,384]{2,1,0:T(8,128)(2,1)}), bf16[4,192,384]{2,1,0:T(8,128)(2,1)}, u32[]{:S(2)}, u32[]{:S(2)}) async-start(bf16[4,192,384]{2,1,0:T(8,128)(2,1)} %narrow_pieces.5), calls=%async_computation.3 | async-start | bytes 1179648 | tf_op jit(solution)/shard_map/all_to_all | solution.py:1499
  216.3 4.2 %collective-permute-start.35 = (f32[72,128]{1,0:T(8,128)}, f32[72,128]{1,0:T(8,128)S(1)}, u32[]{:S(2)}, u32[]{:S(2)}) collective-permute-start(f32[72,128]{1,0:T(8,128)} %add.17), channel_id=1, source_target_pairs={{0,8},{4,12},{8,0},{12,4},{16,24},{20,28},{24,16},{28,20},{1,9},{5... | collective-permute-start | bytes 110600 | tf_op jit(solution)/shard_map/ppermute | solution.py:1228
  221.9 4.4 %collective-permute-start.36 = (f32[72,128]{1,0:T(8,128)}, f32[72,128]{1,0:T(8,128)}, u32[]{:S(2)}, u32[]{:S(2)}) collective-permute-start(f32[72,128]{1,0:T(8,128)} %add.18), channel_id=1, source_target_pairs={{0,16},{4,20},{8,24},{12,28},{16,0},{20,4},{24,8},{28,12},{1,17},{... | collective-permute-start | bytes 110600 | tf_op jit(solution)/shard_map/ppermute | solution.py:1228

commit v6 on v5

--- a/solution.py
+++ b/solution.py
@@ -1410,7 +1410,7 @@
             [(act_recv, None)],
             ((0, rows_out),),
             *first_bits,
-            512,
+            768,
         ),
         orders,
     )

time: 233 us -> 234 us (level)
  no operation moved by 1% of the time
where the time goes in v6:
time: 234 us; the launch traced here: 231 us
  Pallas kernels  117 us (50%)
  starting transfers between devices  50.6 us (22%)
  waiting for transfers between devices  47.6 us (20%)
  local copies, waits for them, and re-layouts  8.54 us (4%)
  other arithmetic  7.11 us (3%)
    pallas_call x1, Pallas kernels, forward(): pl.pallas_call(forward_kernel, out_shape=[make_shape(*item) for item in s...  24.4 us
    pallas_call x3, Pallas kernels, grad_terms(): pl.pallas_call(functools.partial(grad_kernel, first_bit, second_bit, span...  24.2 us
    ppermute x31, starting transfers between devices, swap(): return lax.ppermute(values, axis, [(i, i ^ 1 << bit) for i in range(count)])  23.2 us
    all_to_all x1, waiting for transfers between devices, on_device(): got = lax.all_to_all(sent, 'wide', split_axis=0, concat_axis=0, tiled=True)  19.1 us
    pallas_call x1, Pallas kernels, feed_back(): pl.pallas_call(functools.partial(feed_back_kernel, half), out_shape=[make...  18.3 us
    pallas_call x1, Pallas kernels, attend_back(): pl.pallas_call(attend_back_kernel, out_shape=[make_shape(*item) for item...  16.7 us
    ppermute x31, waiting for transfers between devices, swap(): return lax.ppermute(values, axis, [(i, i ^ 1 << bit) for i in range(count)])  14.8 us
    ppermute x6, starting transfers between devices, trade(): lax.ppermute(pieces[step], 'narrow', [(i, i ^ step) for i in range(count)])  9.31 us
  transfers between devices with their start and end apart: 41, of which 15 were waited for; matrix products, arithmetic and copies ran while one was open for 6% of the time, Pallas kernels for 33%

profile of v6, /device:TPU:0, one launch (start us, length us, event | category | flops | bytes accessed | tf_op | source)
XLA Modules:
  0.0 231.5 jit_solution(3754109804710275012)
XLA Ops:
  0.6 3.7 %build_send.1 = bf16[8,144,768]{2,1,0:T(8,128)(2,1)} custom-call(s32[8]{0:T(128)} %dest_ref.3, s32[2,32]{1,0:T(2,128)} %bitcast.26, f32[1,32]{1,0:T(1,128)} %bitcast.27, bf16[8,128,768]{2,1,0:T(8,128)(2,1)} %tok_ref.1, s32[8,128]{1,0:T(8,128)} %seg_ref.1), custom_call_target="tpu_custom_call" | custom-call | bytes 9000000 | tf_op jit(solution)/shard_map/build_send/pallas_call | solution.py:126
  4.4 5.1 %all-to-all-start = ((bf16[8,144,768]{2,1,0:T(8,128)(2,1)}), bf16[8,144,768]{2,1,0:T(8,128)(2,1)}, u32[]{:S(2)}, u32[]{:S(2)}) async-start(bf16[8,144,768]{2,1,0:T(8,128)(2,1)} %build_send.1), calls=%async_computation | async-start | bytes 3538944 | tf_op jit(solution)/shard_map/all_to_all | solution.py:1328
  9.6 0.6 reshape.84.bias_ref
  13.7 19.1 %all-to-all-done.got_ref = bf16[8,144,768]{2,1,0:T(8,128)(2,1)} async-done(((bf16[8,144,768]{2,1,0:T(8,128)(2,1)}), bf16[8,144,768]{2,1,0:T(8,128)(2,1)}, u32[]{:S(2)}, u32[]{:S(2)}) %all-to-all-start) | async-done | bytes 1769504 | tf_op jit(solution)/shard_map/all_to_all | solution.py:1328
  32.8 24.4 %forward.1 = (bf16[3,512,768]{2,1,0:T(8,128)(2,1)}, bf16[512,2304]{1,0:T(8,128)(2,1)}, bf16[4,6,256,128]{3,2,1,0:T(8,128)(2,1)}, f32[512,768]{1,0:T(8,128)}, f32...) custom-call(bf16[8,144,768]{2,1,0:T(8,128)(2,1)} %all-to-all-done.go, ...), custom_call_target="tpu_custom_call" | custom-call | bytes 60000000 | tf_op jit(solution)/shard_map/forward/pallas_call | solution.py:423
  57.7 4.3 %all-to-all-start.1 = ((bf16[8,32,768]{2,1,0:T(8,128)(2,1)}), bf16[8,32,768]{2,1,0:T(8,128)(2,1)}, u32[]{:S(2)}, u32[]{:S(2)}) async-start(bf16[8,32,768]{2,1,0:T(8,128)(2,1)} %get-tuple-element.122), calls=%async_computation.1 | async-start | bytes 786432 | tf_op jit(solution)/shard_map/all_to_all | solution.py:1368
  62.0 1.4 copy.33.pair_ref
  63.4 1.8 route.1
  65.2 5.0 %all-to-all-done.1 = bf16[8,32,768]{2,1,0:T(8,128)(2,1)} async-done(((bf16[8,32,768]{2,1,0:T(8,128)(2,1)}), bf16[8,32,768]{2,1,0:T(8,128)(2,1)}, u32[]{:S(2)}, u32[]{:S(2)}) %all-to-all-start.1) | async-done | bytes 393248 | tf_op jit(solution)/shard_map/all_to_all | solution.py:1368
  70.1 18.3 %feed_back.1 = (f32[1,3072]{1,0:T(1,128)}, f32[512,768]{1,0:T(8,128)}, bf16[768,512]{1,0:T(8,128)(2,1)}, bf16[512,768]{1,0:T(8,128)(2,1)}, f32[8,768]{1,0:T(8,12...) custom-call(s32[1]{0:T(128)} %bitcast.4.me_ref, ...), custom_call_target="tpu_custom_call" | custom-call | bytes 42000000 | tf_op jit(solution)/shard_map/feed_back/pallas_call | solution.py:818
  89.2 1.1 collective-permute-done.refs_0_
  90.7 1.1 collective-permute-done.3.refs_3_
  92.4 7.1 %grad_terms.3 = (bf16[2,96,1536]{2,1,0:T(8,128)(2,1)}, bf16[2,96,1536]{2,1,0:T(8,128)(2,1)}, bf16[2,96,1536]{2,1,0:T(8,128)(2,1)}, bf16[2,96,1536]{2,1,0:T(8,128)(2,1)}) custom-call(s32[1]{0:T(128)} %bitcast.4.me_ref, bf16[4,96,512]{2,1,0:T(8,128)(2,1)} %get-tuple-element.137.own_ref, bf16[96,512]{1,0:T(8,128)(2,1)} %collective-permute-done.refs_0_, ...), custom_call_target="tpu_custom_call" | custom-call | bytes 21000000 | tf_op jit(solution)/shard_map/grad_terms/pallas_call | solution.py:1095
  101.1 2.0 cosine_pairs.1
  103.1 1.3 reduce
  104.4 8.2 %grad_terms.4 = (bf16[2,384,384]{2,1,0:T(8,128)(2,1)}, bf16[2,384,384]{2,1,0:T(8,128)(2,1)}, bf16[2,384,384]{2,1,0:T(8,128)(2,1)}, bf16[2,384,384]{2,1,0:T(8,128)(2,1)}) custom-call(s32[1]{0:T(128)} %bitcast.4.me_ref, bf16[4,384,512]{2,1,0:T(8,128)(2,1)} %get-tuple-element.144.own_ref, bf16[384,512]{1,0:T(8,128)(2,1)} %collective-permute-done.5.refs_0_, ...), custom_call_target="tpu_custom_call" | custom-call | bytes 21000000 | tf_op jit(solution)/shard_map/grad_terms/pallas_call | solution.py:1095
  112.6 2.5 %collective-permute-done.10.refs_1_ = bf16[2,96,1536]{2,1,0:T(8,128)(2,1)} collective-permute-done((bf16[2,96,1536]{2,1,0:T(8,128)(2,1)}, bf16[2,96,1536]{2,1,0:T(8,128)(2,1)}, u32[]{:S(2)}, u32[]{:S(2)}) %collective-permute-start.10) | collective-permute-done | bytes 589856 | tf_op jit(solution)/shard_map/ppermute | solution.py:1228
  115.4 2.8 %fold.3 = (bf16[1,96,1536]{2,1,0:T(8,128)(2,1)}, bf16[1,96,1536]{2,1,0:T(8,128)(2,1)}, bf16[1,96,1536]{2,1,0:T(8,128)(2,1)}, bf16[1,96,1536]{2,1,0:T(8,128)(2,1)}) custom-call(s32[1]{0:T(128)} %bitcast.4.me_ref, bf16[2,96,1536]{2,1,0:T(8,128)(2,1)} %get-tuple-element.164.refs_0_, bf16[2,96,1536]{2,1,0:T(8,128)(2,1)} %collective-permute-done.10.refs_1_, ...), custom_call_target="tpu_custom_call" | custom-call | bytes 1500000 | tf_op jit(solution)/shard_map/fold/pallas_call | solution.py:1132
  118.3 1.5 collective-permute-start.14
  120.3 1.5 collective-permute-start.12
  122.3 16.7 %attend_back.1 = (bf16[8,128,768]{2,1,0:T(8,128)(2,1)}, f32[1,2304]{1,0:T(1,128)}, bf16[4,384,512]{2,1,0:T(8,128)(2,1)}, bf16[384,512]{1,0:T(8,128)(2,1)}, bf16[...) custom-call(s32[4]{0:T(128)} %get-tuple-element.123.source_ref, s32[1]{0:T(128)} %bitcast.4.me_ref, ...), custom_call_target="tpu_custom_call" | custom-call | bytes 60000000 | tf_op jit(solution)/shard_map/attend_back/pallas_call | solution.py:965
  139.0 1.3 collective-permute-done.12.refs_1_
  140.3 2.7 %fold.4 = (bf16[1,384,384]{2,1,0:T(8,128)(2,1)}, bf16[1,384,384]{2,1,0:T(8,128)(2,1)}, bf16[1,384,384]{2,1,0:T(8,128)(2,1)}, bf16[1,384,384]{2,1,0:T(8,128)(2,1)}) custom-call(s32[1]{0:T(128)} %bitcast.4.me_ref, bf16[2,384,384]{2,1,0:T(8,128)(2,1)} %get-tuple-element.172.refs_0_, bf16[2,384,384]{2,1,0:T(8,128)(2,1)} %collective-permute-done.14.refs_1_, ...), custom_call_target="tpu_custom_call" | custom-call | bytes 1500000 | tf_op jit(solution)/shard_map/fold/pallas_call | solution.py:1132
  143.0 4.5 %all-to-all-start.2 = ((bf16[8,128,768]{2,1,0:T(8,128)(2,1)}), bf16[8,128,768]{2,1,0:T(8,128)(2,1)}, u32[]{:S(2)}, u32[]{:S(2)}) async-start(bf16[8,128,768]{2,1,0:T(8,128)(2,1)} %get-tuple-element.177), calls=%async_computation.2 | async-start | bytes 3145728 | tf_op jit(solution)/shard_map/all_to_all | solution.py:1461
  148.6 1.4 pack_vectors.1
  150.2 1.3 collective-permute-done.25
  151.5 0.8 add.15
  152.3 0.6 copy-done
  152.9 2.1 collective-permute-start.26
  155.0 1.9 collective-permute-done.26
  156.9 0.6 copy-done.1
  157.5 1.6 collective-permute-start.20
  159.2 1.5 collective-permute-start.21
  160.6 2.3 %narrow_pieces.3 = (bf16[96,768]{1,0:T(8,128)(2,1)}, bf16[96,768]{1,0:T(8,128)(2,1)}, bf16[96,768]{1,0:T(8,128)(2,1)}, bf16[96,768]{1,0:T(8,128)(2,1)}) custom-call(s32[1]{0:T(128)} %bitcast.6.me_ref, bf16[1,96,1536]{2,1,0:T(8,128)(2,1)} %get-tuple-element.184.refs_0_, bf16[1,96,1536]{2,1,0:T(8,128)(2,1)} %collective-permute-done.12.refs_1_, ...), custom_call_target="tpu_custom_call" | custom-call | bytes 3000000 | tf_op jit(solution)/shard_map/narrow_pieces/pallas_call | solution.py:1165
  163.0 2.0 collective-permute-start.27
  165.0 2.7 %collective-permute-start.28 = (bf16[96,768]{1,0:T(8,128)(2,1)}, bf16[96,768]{1,0:T(8,128)(2,1)}, u32[]{:S(2)}, u32[]{:S(2)}) collective-permute-start(bf16[96,768]{1,0:T(8,128)(2,1)} %get-tuple-element.188), channel_id=1, source_target_pairs={{0,2},{1,3},{2,0},{3,1},{4,6},{5,7},{6,4},{7,5},{8,10},{9,11},{10,... | collective-permute-start | bytes 442376 | tf_op jit(solution)/shard_map/ppermute | solution.py:1235
  167.7 1.4 add.16
  169.1 8.9 %grad_terms.5 = (bf16[2,384,384]{2,1,0:T(8,128)(2,1)}, bf16[2,384,384]{2,1,0:T(8,128)(2,1)}, bf16[2,384,384]{2,1,0:T(8,128)(2,1)}, bf16[2,384,384]{2,1,0:T(8,128)(2,1)}) custom-call(s32[1]{0:T(128)} %bitcast.4.me_ref, bf16[4,384,512]{2,1,0:T(8,128)(2,1)} %get-tuple-element.178.own_ref, bf16[384,512]{1,0:T(8,128)(2,1)} %collective-permute-done.16.refs_0_, ...), custom_call_target="tpu_custom_call" | custom-call | bytes 21000000 | tf_op jit(solution)/shard_map/grad_terms/pallas_call | solution.py:1095
  178.6 0.6 collective-permute-start.30
  179.6 2.3 narrow_pieces.4
  181.8 2.1 collective-permute-start.22
  183.9 1.8 collective-permute-start.23
  185.7 0.7 collective-permute-start.24
  186.4 3.4 %home_rows.1 = bf16[8,128,768]{2,1,0:T(8,128)(2,1)} custom-call(s32[8]{0:T(128)} %dest_ref.3, bf16[8,128,768]{2,1,0:T(8,128)(2,1)} %all-to-all-done.2.rows_ref), custom_call_target="tpu_custom_call" | custom-call | bytes 9000000 | tf_op jit(solution)/shard_map/home_rows/pallas_call | solution.py:1016
  189.9 6.3 %collective-permute-done.23.refs_2_ = bf16[192,384]{1,0:T(8,128)(2,1)} collective-permute-done((bf16[192,384]{1,0:T(8,128)(2,1)}, bf16[192,384]{1,0:T(8,128)(2,1)}, u32[]{:S(2)}, u32[]{:S(2)}) %collective-permute-start.23) | collective-permute-done | bytes 147488 | tf_op jit(solution)/shard_map/ppermute | solution.py:1235
  196.2 2.7 %fold.5 = (bf16[1,384,384]{2,1,0:T(8,128)(2,1)}, bf16[1,384,384]{2,1,0:T(8,128)(2,1)}, bf16[1,384,384]{2,1,0:T(8,128)(2,1)}, bf16[1,384,384]{2,1,0:T(8,128)(2,1)}) custom-call(s32[1]{0:T(128)} %bitcast.4.me_ref, bf16[2,384,384]{2,1,0:T(8,128)(2,1)} %get-tuple-element.201.refs_0_, bf16[2,384,384]{2,1,0:T(8,128)(2,1)} %collective-permute-done.30.refs_1_, ...), custom_call_target="tpu_custom_call" | custom-call | bytes 1500000 | tf_op jit(solution)/shard_map/fold/pallas_call | solution.py:1132
  198.9 1.6 collective-permute-start.33
  200.5 1.5 collective-permute-start.34
  202.0 3.1 %collective-permute-start.32 = (f32[72,128]{1,0:T(8,128)}, f32[72,128]{1,0:T(8,128)S(1)}, u32[]{:S(2)}, u32[]{:S(2)}) collective-permute-start(f32[72,128]{1,0:T(8,128)} %add.16), channel_id=1, source_target_pairs={{0,2},{1,3},{2,0},{3,1},{4,6},{5,7},{6,4},{7,5},{8,10},{9,11},{10,... | collective-permute-start | bytes 110600 | tf_op jit(solution)/shard_map/ppermute | solution.py:1228
  205.1 2.1 collective-permute-done.32
  207.3 1.4 add.17
  208.7 2.3 narrow_pieces.5
  210.9 4.2 %all-to-all-start.3 = ((bf16[4,192,384]{2,1,0:T(8,128)(2,1)}), bf16[4,192,384]{2,1,0:T(8,128)(2,1)}, u32[]{:S(2)}, u32[]{:S(2)}) async-start(bf16[4,192,384]{2,1,0:T(8,128)(2,1)} %narrow_pieces.5), calls=%async_computation.3 | async-start | bytes 1179648 | tf_op jit(solution)/shard_map/all_to_all | solution.py:1499
  215.1 1.4 collective-permute-start.35
  216.6 2.8 %collective-permute-done.35 = f32[72,128]{1,0:T(8,128)S(1)} collective-permute-done((f32[72,128]{1,0:T(8,128)}, f32[72,128]{1,0:T(8,128)S(1)}, u32[]{:S(2)}, u32[]{:S(2)}) %collective-permute-start.35) | collective-permute-done | bytes 36896 | tf_op jit(solution)/shard_map/ppermute | solution.py:1228
  219.3 1.4 add.18
  221.3 1.9 sum_pieces.5
  223.2 1.9 sum_pieces.4
  225.1 0.8 add.19
  225.9 0.6 slice_bitcast_fusion.1
  226.5 0.6 slice_bitcast_fusion
  227.1 0.6 slice_bitcast_fusion.2
  227.7 1.9 all-to-all-done.3.refs_0_
  229.6 1.9 sum_pieces.3
  (76 shorter events, 11.5 us)
Async XLA Ops:
  4.4 5.2 %copy-start.2 = (f32[1536]{0:T(1024)S(1)}, f32[1536]{0:T(1024)}, u32[]{:S(2)}) copy-start(f32[1536]{0:T(1024)} %param.23) | copy-start | bytes 18436
  4.4 5.8 %copy-start.3 = (f32[768]{0:T(1024)S(1)}, f32[768]{0:T(1024)}, u32[]{:S(2)}) copy-start(f32[768]{0:T(1024)} %param.25) | copy-start | bytes 9220
  4.4 6.4 %copy-start.4 = (f32[768]{0:T(1024)S(1)}, f32[768]{0:T(1024)}, u32[]{:S(2)}) copy-start(f32[768]{0:T(1024)} %param.26) | copy-start | bytes 9220
  4.4 7.0 %copy-start.5 = (f32[768]{0:T(1024)S(1)}, f32[768]{0:T(1024)}, u32[]{:S(2)}) copy-start(f32[768]{0:T(1024)} %param.27) | copy-start | bytes 9220
  4.4 7.6 %copy-start.6 = (f32[768]{0:T(1024)S(1)}, f32[768]{0:T(1024)}, u32[]{:S(2)}) copy-start(f32[768]{0:T(1024)} %param.31) | copy-start | bytes 9220
  4.4 8.1 %copy-start.7 = (f32[768]{0:T(1024)S(1)}, f32[768]{0:T(1024)}, u32[]{:S(2)}) copy-start(f32[768]{0:T(1024)} %param.32) | copy-start | bytes 9220
  4.4 8.7 %copy-start.8 = (f32[768]{0:T(1024)S(1)}, f32[768]{0:T(1024)}, u32[]{:S(2)}) copy-start(f32[768]{0:T(1024)} %param.33) | copy-start | bytes 9220
  4.4 28.3 %all-to-all-start = ((bf16[8,144,768]{2,1,0:T(8,128)(2,1)}), bf16[8,144,768]{2,1,0:T(8,128)(2,1)}, u32[]{:S(2)}, u32[]{:S(2)}) async-start(bf16[8,144,768]{2,1,0:T(8,128)(2,1)} %build_send.1), calls=%async_computation | async-start | bytes 3538944 | tf_op jit(solution)/shard_map/all_to_all | solution.py:1328
  57.1 35.2 %collective-permute-start.4 = (bf16[512,3072]{1,0:T(8,128)(2,1)}, bf16[512,3072]{1,0:T(8,128)(2,1)}, u32[]{:S(2)}, u32[]{:S(2)}) collective-permute-start(bf16[512,3072]{1,0:T(8,128)(2,1)} %get-tuple-element.142.refs_4_), channel_id=1, source_target_pairs={{0,4},{4,0},{8,12},{12,8},{16,20},{20,16},{24,28},{28,24},{1,5},{5... | collective-permute-start | bytes 9437192 | tf_op jit(solution)/shard_map/ppermute | solution.py:1228
  57.2 47.2 %collective-permute-start.9 = (bf16[3,512,768]{2,1,0:T(8,128)(2,1)}, bf16[3,512,768]{2,1,0:T(8,128)(2,1)}, u32[]{:S(2)}, u32[]{:S(2)}) collective-permute-start(bf16[3,512,768]{2,1,0:T(8,128)(2,1)} %get-tuple-element.159.refs_4_.refs_5_), channel_id=1, source_target_pairs={{0,4},{4,0},{8,12},{12,8},{16,20},{20,16},{24,28},{28,24},{1,5},{5... | collective-permute-start | bytes 7077896 | tf_op jit(solution)/shard_map/ppermute | solution.py:1228
  57.7 12.4 %all-to-all-start.1 = ((bf16[8,32,768]{2,1,0:T(8,128)(2,1)}), bf16[8,32,768]{2,1,0:T(8,128)(2,1)}, u32[]{:S(2)}, u32[]{:S(2)}) async-start(bf16[8,32,768]{2,1,0:T(8,128)(2,1)} %get-tuple-element.122), calls=%async_computation.1 | async-start | bytes 786432 | tf_op jit(solution)/shard_map/all_to_all | solution.py:1368
  88.5 1.7 collective-permute-start
  88.6 1.8 collective-permute-start.1
  89.1 1.6 collective-permute-start.2
  90.2 1.6 collective-permute-start.3
  91.9 8.7 %collective-permute-start.5 = (bf16[384,512]{1,0:T(8,128)(2,1)}, bf16[384,512]{1,0:T(8,128)(2,1)}, u32[]{:S(2)}, u32[]{:S(2)}) collective-permute-start(bf16[384,512]{1,0:T(8,128)(2,1)} %get-tuple-element.149), channel_id=1, source_target_pairs={{0,4},{4,0},{8,12},{12,8},{16,20},{20,16},{24,28},{28,24},{1,5},{5... | collective-permute-start | bytes 1179656 | tf_op jit(solution)/shard_map/ppermute | solution.py:1228
  92.0 8.6 %collective-permute-start.6 = (bf16[384,512]{1,0:T(8,128)(2,1)}, bf16[384,512]{1,0:T(8,128)(2,1)}, u32[]{:S(2)}, u32[]{:S(2)}) collective-permute-start(bf16[384,512]{1,0:T(8,128)(2,1)} %get-tuple-element.150), channel_id=1, source_target_pairs={{0,4},{4,0},{8,12},{12,8},{16,20},{20,16},{24,28},{28,24},{1,5},{5... | collective-permute-start | bytes 1179656 | tf_op jit(solution)/shard_map/ppermute | solution.py:1228
  99.4 15.7 %collective-permute-start.10 = (bf16[2,96,1536]{2,1,0:T(8,128)(2,1)}, bf16[2,96,1536]{2,1,0:T(8,128)(2,1)}, u32[]{:S(2)}, u32[]{:S(2)}) collective-permute-start(bf16[2,96,1536]{2,1,0:T(8,128)(2,1)} %get-tuple-element.153), channel_id=1, source_target_pairs={{0,8},{4,12},{8,0},{12,4},{16,24},{20,28},{24,16},{28,20},{1,9},{5... | collective-permute-start | bytes 1769480 | tf_op jit(solution)/shard_map/ppermute | solution.py:1228
  100.0 15.4 %collective-permute-start.11 = (bf16[2,96,1536]{2,1,0:T(8,128)(2,1)}, bf16[2,96,1536]{2,1,0:T(8,128)(2,1)}, u32[]{:S(2)}, u32[]{:S(2)}) collective-permute-start(bf16[2,96,1536]{2,1,0:T(8,128)(2,1)} %get-tuple-element.154), channel_id=1, source_target_pairs={{0,16},{4,20},{8,24},{12,28},{16,0},{20,4},{24,8},{28,12},{1,17},{... | collective-permute-start | bytes 1769480 | tf_op jit(solution)/shard_map/ppermute | solution.py:1228
  100.6 3.9 %collective-permute-start.7 = (bf16[384,512]{1,0:T(8,128)(2,1)}, bf16[384,512]{1,0:T(8,128)(2,1)}, u32[]{:S(2)}, u32[]{:S(2)}) collective-permute-start(bf16[384,512]{1,0:T(8,128)(2,1)} %get-tuple-element.151), channel_id=1, source_target_pairs={{0,4},{4,0},{8,12},{12,8},{16,20},{20,16},{24,28},{28,24},{1,5},{5... | collective-permute-start | bytes 1179656 | tf_op jit(solution)/shard_map/ppermute | solution.py:1228
  100.6 3.9 %collective-permute-start.8 = (bf16[384,512]{1,0:T(8,128)(2,1)}, bf16[384,512]{1,0:T(8,128)(2,1)}, u32[]{:S(2)}, u32[]{:S(2)}) collective-permute-start(bf16[384,512]{1,0:T(8,128)(2,1)} %get-tuple-element.152), channel_id=1, source_target_pairs={{0,4},{4,0},{8,12},{12,8},{16,20},{20,16},{24,28},{28,24},{1,5},{5... | collective-permute-start | bytes 1179656 | tf_op jit(solution)/shard_map/ppermute | solution.py:1228
  118.3 22.1 %collective-permute-start.14 = (bf16[2,384,384]{2,1,0:T(8,128)(2,1)}, bf16[2,384,384]{2,1,0:T(8,128)(2,1)}, u32[]{:S(2)}, u32[]{:S(2)}) collective-permute-start(bf16[2,384,384]{2,1,0:T(8,128)(2,1)} %get-tuple-element.173), channel_id=1, source_target_pairs={{0,8},{4,12},{8,0},{12,4},{16,24},{20,28},{24,16},{28,20},{1,9},{5... | collective-permute-start | bytes 1769480 | tf_op jit(solution)/shard_map/ppermute | solution.py:1228
  119.7 20.6 %collective-permute-start.15 = (bf16[2,384,384]{2,1,0:T(8,128)(2,1)}, bf16[2,384,384]{2,1,0:T(8,128)(2,1)}, u32[]{:S(2)}, u32[]{:S(2)}) collective-permute-start(bf16[2,384,384]{2,1,0:T(8,128)(2,1)} %get-tuple-element.174), channel_id=1, source_target_pairs={{0,16},{4,20},{8,24},{12,28},{16,0},{20,4},{24,8},{28,12},{1,17},{... | collective-permute-start | bytes 1769480 | tf_op jit(solution)/shard_map/ppermute | solution.py:1228
  120.3 20.0 %collective-permute-start.12 = (bf16[1,96,1536]{2,1,0:T(8,128)(2,1)}, bf16[1,96,1536]{2,1,0:T(8,128)(2,1)}, u32[]{:S(2)}, u32[]{:S(2)}) collective-permute-start(bf16[1,96,1536]{2,1,0:T(8,128)(2,1)} %get-tuple-element.166), channel_id=1, source_target_pairs={{0,16},{4,20},{8,24},{12,28},{16,0},{20,4},{24,8},{28,12},{1,17},{... | collective-permute-start | bytes 884744 | tf_op jit(solution)/shard_map/ppermute | solution.py:1228
  121.7 18.6 %collective-permute-start.13 = (bf16[1,96,1536]{2,1,0:T(8,128)(2,1)}, bf16[1,96,1536]{2,1,0:T(8,128)(2,1)}, u32[]{:S(2)}, u32[]{:S(2)}) collective-permute-start(bf16[1,96,1536]{2,1,0:T(8,128)(2,1)} %get-tuple-element.167), channel_id=1, source_target_pairs={{0,8},{4,12},{8,0},{12,4},{16,24},{20,28},{24,16},{28,20},{1,9},{5... | collective-permute-start | bytes 884744 | tf_op jit(solution)/shard_map/ppermute | solution.py:1228
  143.0 43.4 %all-to-all-start.2 = ((bf16[8,128,768]{2,1,0:T(8,128)(2,1)}), bf16[8,128,768]{2,1,0:T(8,128)(2,1)}, u32[]{:S(2)}, u32[]{:S(2)}) async-start(bf16[8,128,768]{2,1,0:T(8,128)(2,1)} %get-tuple-element.177), calls=%async_computation.2 | async-start | bytes 3145728 | tf_op jit(solution)/shard_map/all_to_all | solution.py:1461
  147.6 11.6 %collective-permute-start.16 = (bf16[384,512]{1,0:T(8,128)(2,1)}, bf16[384,512]{1,0:T(8,128)(2,1)}, u32[]{:S(2)}, u32[]{:S(2)}) collective-permute-start(bf16[384,512]{1,0:T(8,128)(2,1)} %get-tuple-element.179), channel_id=1, source_target_pairs={{0,4},{4,0},{8,12},{12,8},{16,20},{20,16},{24,28},{28,24},{1,5},{5... | collective-permute-start | bytes 1179656 | tf_op jit(solution)/shard_map/ppermute | solution.py:1228
  147.7 15.3 %collective-permute-start.17 = (bf16[384,512]{1,0:T(8,128)(2,1)}, bf16[384,512]{1,0:T(8,128)(2,1)}, u32[]{:S(2)}, u32[]{:S(2)}) collective-permute-start(bf16[384,512]{1,0:T(8,128)(2,1)} %get-tuple-element.180), channel_id=1, source_target_pairs={{0,4},{4,0},{8,12},{12,8},{16,20},{20,16},{24,28},{28,24},{1,5},{5... | collective-permute-start | bytes 1179656 | tf_op jit(solution)/shard_map/ppermute | solution.py:1228
  148.1 16.9 %collective-permute-start.18 = (bf16[384,512]{1,0:T(8,128)(2,1)}, bf16[384,512]{1,0:T(8,128)(2,1)}, u32[]{:S(2)}, u32[]{:S(2)}) collective-permute-start(bf16[384,512]{1,0:T(8,128)(2,1)} %get-tuple-element.181), channel_id=1, source_target_pairs={{0,4},{4,0},{8,12},{12,8},{16,20},{20,16},{24,28},{28,24},{1,5},{5... | collective-permute-start | bytes 1179656 | tf_op jit(solution)/shard_map/ppermute | solution.py:1228
  148.2 19.5 %collective-permute-start.19 = (bf16[384,512]{1,0:T(8,128)(2,1)}, bf16[384,512]{1,0:T(8,128)(2,1)}, u32[]{:S(2)}, u32[]{:S(2)}) collective-permute-start(bf16[384,512]{1,0:T(8,128)(2,1)} %get-tuple-element.182), channel_id=1, source_target_pairs={{0,4},{4,0},{8,12},{12,8},{16,20},{20,16},{24,28},{28,24},{1,5},{5... | collective-permute-start | bytes 1179656 | tf_op jit(solution)/shard_map/ppermute | solution.py:1228
  150.1 1.4 collective-permute-start.25
  152.3 0.6 copy-start
  152.9 4.0 %collective-permute-start.26 = (f32[72,128]{1,0:T(8,128)S(1)}, f32[72,128]{1,0:T(8,128)S(1)}, u32[]{:S(2)}, u32[]{:S(2)}) collective-permute-start(f32[72,128]{1,0:T(8,128)S(1)} %add.15), channel_id=1, source_target_pairs={{0,1},{1,0},{2,3},{3,2},{4,5},{5,4},{6,7},{7,6},{8,9},{9,8},{10,11... | collective-permute-start | bytes 110600 | tf_op jit(solution)/shard_map/ppermute | solution.py:1228
  156.9 0.6 copy-start.1
  157.5 21.0 %collective-permute-start.20 = (bf16[1,384,384]{2,1,0:T(8,128)(2,1)}, bf16[1,384,384]{2,1,0:T(8,128)(2,1)}, u32[]{:S(2)}, u32[]{:S(2)}) collective-permute-start(bf16[1,384,384]{2,1,0:T(8,128)(2,1)} %get-tuple-element.175), channel_id=1, source_target_pairs={{0,16},{4,20},{8,24},{12,28},{16,0},{20,4},{24,8},{28,12},{1,17},{... | collective-permute-start | bytes 884744 | tf_op jit(solution)/shard_map/ppermute | solution.py:1228
  159.2 19.4 %collective-permute-start.21 = (bf16[1,384,384]{2,1,0:T(8,128)(2,1)}, bf16[1,384,384]{2,1,0:T(8,128)(2,1)}, u32[]{:S(2)}, u32[]{:S(2)}) collective-permute-start(bf16[1,384,384]{2,1,0:T(8,128)(2,1)} %get-tuple-element.176), channel_id=1, source_target_pairs={{0,8},{4,12},{8,0},{12,4},{16,24},{20,28},{24,16},{28,20},{1,9},{5... | collective-permute-start | bytes 884744 | tf_op jit(solution)/shard_map/ppermute | solution.py:1228
  163.0 15.0 %collective-permute-start.27 = (bf16[96,768]{1,0:T(8,128)(2,1)}, bf16[96,768]{1,0:T(8,128)(2,1)}, u32[]{:S(2)}, u32[]{:S(2)}) collective-permute-start(bf16[96,768]{1,0:T(8,128)(2,1)} %get-tuple-element.187), channel_id=1, source_target_pairs={{0,1},{1,0},{2,3},{3,2},{4,5},{5,4},{6,7},{7,6},{8,9},{9,8},{10,11... | collective-permute-start | bytes 442376 | tf_op jit(solution)/shard_map/ppermute | solution.py:1235
  165.0 13.5 %collective-permute-start.28 = (bf16[96,768]{1,0:T(8,128)(2,1)}, bf16[96,768]{1,0:T(8,128)(2,1)}, u32[]{:S(2)}, u32[]{:S(2)}) collective-permute-start(bf16[96,768]{1,0:T(8,128)(2,1)} %get-tuple-element.188), channel_id=1, source_target_pairs={{0,2},{1,3},{2,0},{3,1},{4,6},{5,7},{6,4},{7,5},{8,10},{9,11},{10,... | collective-permute-start | bytes 442376 | tf_op jit(solution)/shard_map/ppermute | solution.py:1235
  167.7 10.8 %collective-permute-start.29 = (bf16[96,768]{1,0:T(8,128)(2,1)}, bf16[96,768]{1,0:T(8,128)(2,1)}, u32[]{:S(2)}, u32[]{:S(2)}) collective-permute-start(bf16[96,768]{1,0:T(8,128)(2,1)} %get-tuple-element.189), channel_id=1, source_target_pairs={{0,3},{1,2},{2,1},{3,0},{4,7},{5,6},{6,5},{7,4},{8,11},{9,10},{10,... | collective-permute-start | bytes 442376 | tf_op jit(solution)/shard_map/ppermute | solution.py:1235
  178.6 17.6 %collective-permute-start.30 = (bf16[2,384,384]{2,1,0:T(8,128)(2,1)}, bf16[2,384,384]{2,1,0:T(8,128)(2,1)}, u32[]{:S(2)}, u32[]{:S(2)}) collective-permute-start(bf16[2,384,384]{2,1,0:T(8,128)(2,1)} %get-tuple-element.207), channel_id=1, source_target_pairs={{0,8},{4,12},{8,0},{12,4},{16,24},{20,28},{24,16},{28,20},{1,9},{5... | collective-permute-start | bytes 1769480 | tf_op jit(solution)/shard_map/ppermute | solution.py:1228
  179.2 17.0 %collective-permute-start.31 = (bf16[2,384,384]{2,1,0:T(8,128)(2,1)}, bf16[2,384,384]{2,1,0:T(8,128)(2,1)}, u32[]{:S(2)}, u32[]{:S(2)}) collective-permute-start(bf16[2,384,384]{2,1,0:T(8,128)(2,1)} %get-tuple-element.210), channel_id=1, source_target_pairs={{0,16},{4,20},{8,24},{12,28},{16,0},{20,4},{24,8},{28,12},{1,17},{... | collective-permute-start | bytes 1769480 | tf_op jit(solution)/shard_map/ppermute | solution.py:1228
  181.8 8.0 %collective-permute-start.22 = (bf16[192,384]{1,0:T(8,128)(2,1)}, bf16[192,384]{1,0:T(8,128)(2,1)}, u32[]{:S(2)}, u32[]{:S(2)}) collective-permute-start(bf16[192,384]{1,0:T(8,128)(2,1)} %get-tuple-element.198), channel_id=1, source_target_pairs={{0,1},{1,0},{2,3},{3,2},{4,5},{5,4},{6,7},{7,6},{8,9},{9,8},{10,11... | collective-permute-start | bytes 442376 | tf_op jit(solution)/shard_map/ppermute | solution.py:1235
  183.9 12.3 %collective-permute-start.23 = (bf16[192,384]{1,0:T(8,128)(2,1)}, bf16[192,384]{1,0:T(8,128)(2,1)}, u32[]{:S(2)}, u32[]{:S(2)}) collective-permute-start(bf16[192,384]{1,0:T(8,128)(2,1)} %get-tuple-element.199), channel_id=1, source_target_pairs={{0,2},{1,3},{2,0},{3,1},{4,6},{5,7},{6,4},{7,5},{8,10},{9,11},{10,... | collective-permute-start | bytes 442376 | tf_op jit(solution)/shard_map/ppermute | solution.py:1235
  185.7 10.5 %collective-permute-start.24 = (bf16[192,384]{1,0:T(8,128)(2,1)}, bf16[192,384]{1,0:T(8,128)(2,1)}, u32[]{:S(2)}, u32[]{:S(2)}) collective-permute-start(bf16[192,384]{1,0:T(8,128)(2,1)} %get-tuple-element.200), channel_id=1, source_target_pairs={{0,3},{1,2},{2,1},{3,0},{4,7},{5,6},{6,5},{7,4},{8,11},{9,10},{10,... | collective-permute-start | bytes 442376 | tf_op jit(solution)/shard_map/ppermute | solution.py:1235
  198.9 9.8 %collective-permute-start.33 = (bf16[1,384,384]{2,1,0:T(8,128)(2,1)}, bf16[1,384,384]{2,1,0:T(8,128)(2,1)}, u32[]{:S(2)}, u32[]{:S(2)}) collective-permute-start(bf16[1,384,384]{2,1,0:T(8,128)(2,1)} %get-tuple-element.212), channel_id=1, source_target_pairs={{0,16},{4,20},{8,24},{12,28},{16,0},{20,4},{24,8},{28,12},{1,17},{... | collective-permute-start | bytes 884744 | tf_op jit(solution)/shard_map/ppermute | solution.py:1228
  200.5 8.2 %collective-permute-start.34 = (bf16[1,384,384]{2,1,0:T(8,128)(2,1)}, bf16[1,384,384]{2,1,0:T(8,128)(2,1)}, u32[]{:S(2)}, u32[]{:S(2)}) collective-permute-start(bf16[1,384,384]{2,1,0:T(8,128)(2,1)} %get-tuple-element.213), channel_id=1, source_target_pairs={{0,8},{4,12},{8,0},{12,4},{16,24},{20,28},{24,16},{28,20},{1,9},{5... | collective-permute-start | bytes 884744 | tf_op jit(solution)/shard_map/ppermute | solution.py:1228
  202.0 5.3 %collective-permute-start.32 = (f32[72,128]{1,0:T(8,128)}, f32[72,128]{1,0:T(8,128)S(1)}, u32[]{:S(2)}, u32[]{:S(2)}) collective-permute-start(f32[72,128]{1,0:T(8,128)} %add.16), channel_id=1, source_target_pairs={{0,2},{1,3},{2,0},{3,1},{4,6},{5,7},{6,4},{7,5},{8,10},{9,11},{10,... | collective-permute-start | bytes 110600 | tf_op jit(solution)/shard_map/ppermute | solution.py:1228
  210.9 18.6 %all-to-all-start.3 = ((bf16[4,192,384]{2,1,0:T(8,128)(2,1)}), bf16[4,192,384]{2,1,0:T(8,128)(2,1)}, u32[]{:S(2)}, u32[]{:S(2)}) async-start(bf16[4,192,384]{2,1,0:T(8,128)(2,1)} %narrow_pieces.5), calls=%async_computation.3 | async-start | bytes 1179648 | tf_op jit(solution)/shard_map/all_to_all | solution.py:1499
  215.1 4.2 %collective-permute-start.35 = (f32[72,128]{1,0:T(8,128)}, f32[72,128]{1,0:T(8,128)S(1)}, u32[]{:S(2)}, u32[]{:S(2)}) collective-permute-start(f32[72,128]{1,0:T(8,128)} %add.17), channel_id=1, source_target_pairs={{0,8},{4,12},{8,0},{12,4},{16,24},{20,28},{24,16},{28,20},{1,9},{5... | collective-permute-start | bytes 110600 | tf_op jit(solution)/shard_map/ppermute | solution.py:1228
  220.7 4.4 %collective-permute-start.36 = (f32[72,128]{1,0:T(8,128)}, f32[72,128]{1,0:T(8,128)}, u32[]{:S(2)}, u32[]{:S(2)}) collective-permute-start(f32[72,128]{1,0:T(8,128)} %add.18), channel_id=1, source_target_pairs={{0,16},{4,20},{8,24},{12,28},{16,0},{20,4},{24,8},{28,12},{1,17},{... | collective-permute-start | bytes 110600 | tf_op jit(solution)/shard_map/ppermute | solution.py:1228
